TPU v7x, 32 devices: a whole 2x2x4 slice. The times are simulated.
32 devices in a mesh: row: 8 (over z, core), col: 4 (over y, x).
Axes of the slice: x: 2, y: 2, z: 4, core: 2. Of those that a mesh axis runs over, the one named last changes fastest.
Arguments:
- hidden: bfloat16 [16384, 2560], P(('row', 'col')), may hold values from -6 to 6
- in_gain: bfloat16 [2560], P('col'), may hold values from 0.5 to 1.5
- w_gate: bfloat16 [2560, 5120], P('row', 'col'), may hold values from -0.125 to 0.125
- w_value: bfloat16 [2560, 5120], P('row', 'col'), may hold values from -0.125 to 0.125
- w_bc: bfloat16 [2560, 256], P('row', 'col'), may hold values from -0.125 to 0.125
- w_step: bfloat16 [2560, 80], P('row', 'col'), may hold values from -0.125 to 0.125
- conv_value: float32 [4, 5120], P(None, 'col'), may hold values from -3 to 3
- conv_value_bias: float32 [5120], P('col'), may hold values from -0.5 to 0.5
- conv_bc: float32 [4, 256], P(None, 'col'), may hold values from -3 to 3
- conv_bc_bias: float32 [256], P('col'), may hold values from -0.5 to 0.5
- step_bias: float32 [80], P('col'), may hold values from -6 to -2
- decay_log: float32 [80], P('col'), may hold values from 0 to 2.5
- skip_gain: float32 [80], P('col'), may hold values from 0.5 to 1.5
- norm_gain: float32 [5120], P('col'), may hold values from 0.5 to 1.5
- w_out: bfloat16 [5120, 2560], P('col', 'row'), may hold values from -0.078125 to 0.078125
- grad_out: bfloat16 [16384, 2560], P(('row', 'col')), may hold values from -6 to 6
Outputs:
- out: bfloat16 [16384, 2560], P(('row', 'col'))
- grad_hidden: float32 [16384, 2560], P(('row', 'col'))
- grad_in_gain: float32 [2560], P('col')
- grad_w_gate: float32 [2560, 5120], P('row', 'col')
- grad_w_value: float32 [2560, 5120], P('row', 'col')
- grad_w_bc: float32 [2560, 256], P('row', 'col')
- grad_w_step: float32 [2560, 80], P('row', 'col')
- grad_conv_value: float32 [4, 5120], P(None, 'col')
- grad_conv_value_bias: float32 [5120], P('col')
- grad_conv_bc: float32 [4, 256], P(None, 'col')
- grad_conv_bc_bias: float32 [256], P('col')
- grad_step_bias: float32 [80], P('col')
- grad_decay_log: float32 [80], P('col')
- grad_skip_gain: float32 [80], P('col')
- grad_norm_gain: float32 [5120], P('col')
- grad_w_out: float32 [5120, 2560], P('col', 'row')
All inputs are finite; a program needn't handle non-finite values.
Results may differ from a plain program's by a relative error of at most 0.018.
Values may be sent and summed in bfloat16 or wider, within the bound.
No kernel may reach another device: no remote copies, remote signals or barrier semaphores. Data moves between devices by JAX's collectives and lax.ppermute only.
A program may use at most 256 MiB of HBM per device.

v0:
```python
import jax
import jax.numpy as jnp
from jax import lax
from jax.sharding import PartitionSpec as P

P_SIZE = 64
N = 128
E = 5120
GROUP = 256


EPSILON = 1e-05
HIGH = lax.Precision.HIGHEST


def swish(value_in):
    return value_in * jax.nn.sigmoid(value_in)


def row_scale(tokens):
    return lax.rsqrt(jnp.mean(tokens * tokens, axis=1, keepdims=True) + EPSILON)


def norm_rows(tokens, gain_vec):
    return tokens * row_scale(tokens) * gain_vec


def causal_conv(values, taps, offsets):
    tap_count = taps.shape[0]
    length = values.shape[0]
    padded = jnp.pad(values, ((tap_count - 1, 0), (0, 0)))
    summed = offsets[None, :] + taps[0][None, :] * padded[0:length]
    for offset in range(1, tap_count):
        summed = summed + taps[offset][None, :] * padded[offset : offset + length]
    return summed


def block_scan(inner_vals, step_sizes, decay_rates, b_rows, c_rows, skips, block_len):
    length, head_num, head_dim = inner_vals.shape
    blocks = length // block_len
    state_dim = b_rows.shape[1]
    causal = jnp.tril(jnp.ones((block_len, block_len), jnp.float32))
    split_vals = inner_vals.reshape(blocks, block_len, head_num, head_dim)
    split_steps = step_sizes.reshape(blocks, block_len, head_num)
    split_b = b_rows.reshape(blocks, block_len, state_dim)
    split_c = c_rows.reshape(blocks, block_len, state_dim)

    def block_step(carried, pieces):
        values_in, steps_here, b_here, c_here = pieces
        log_sums = jnp.cumsum(steps_here * decay_rates[None, :], axis=0)
        gaps = log_sums[:, None, :] - log_sums[None, :, :]
        decays = jnp.exp(jnp.where(causal[:, :, None] > 0, gaps, 0.0)) * causal[:, :, None]
        scores = jnp.dot(c_here, b_here.T, precision=HIGH)
        mixing = scores[:, :, None] * decays * steps_here[None, :, :]
        inside = jnp.einsum("tsh,shp->thp", mixing, values_in, precision=HIGH)
        across = (
            jnp.einsum("tn,hpn->thp", c_here, carried, precision=HIGH)
            * jnp.exp(log_sums)[:, :, None]
        )
        block_end = log_sums[-1]
        carry_weight = jnp.exp(block_end[None, :] - log_sums) * steps_here
        updated = carried * jnp.exp(block_end)[:, None, None] + jnp.einsum(
            "sh,shp,sn->hpn", carry_weight, values_in, b_here, precision=HIGH
        )
        return (updated, inside + across + skips[None, :, None] * values_in)

    start_state = jnp.zeros((head_num, head_dim, state_dim), jnp.float32)
    last_state, results = lax.scan(
        jax.checkpoint(block_step), start_state, (split_vals, split_steps, split_b, split_c)
    )
    return results.reshape(length, head_num, head_dim)


def body(
    hidden,
    in_gain,
    w_gate,
    w_value,
    w_bc,
    w_step,
    conv_value,
    conv_value_bias,
    conv_bc,
    conv_bc_bias,
    step_bias,
    decay_log,
    skip_gain,
    norm_gain,
    w_out,
    grad_out,
):
    head_local = step_bias.shape[0]
    full_rows, full_gain = (
        lax.all_gather(hidden, "col", axis=0, tiled=True),
        lax.all_gather(in_gain, "col", axis=0, tiled=True),
    )
    row_count = full_rows.shape[0]
    rows_float = full_rows.astype(jnp.float32)
    gain_float = full_gain.astype(jnp.float32)
    normal_in = norm_rows(rows_float, gain_float).astype(jnp.bfloat16)
    pieces = (
        lax.all_gather(w_gate, "row", axis=0, tiled=True),
        lax.all_gather(w_value, "row", axis=0, tiled=True),
        lax.all_gather(w_bc, "row", axis=0, tiled=True),
        lax.all_gather(w_step, "row", axis=0, tiled=True),
    )
    gate_pre, value_pre, bc_pre, step_pre = tuple(
        (
            jnp.dot(normal_in, weight_piece, preferred_element_type=jnp.float32)
            for weight_piece in pieces
        )
    )

    def state_branch(pre_vals, conv_weight, conv_offset):
        return swish(causal_conv(pre_vals, conv_weight, conv_offset))

    state_local, state_back = jax.vjp(state_branch, bc_pre, conv_bc, conv_bc_bias)
    state_full = lax.all_gather(state_local.astype(jnp.bfloat16), "col", axis=1, tiled=True)

    def mixer(
        gate_in, value_in, step_in, state_in, conv_weight, conv_offset, bias_in, decay_in, skip_in
    ):
        inner_vals = swish(causal_conv(value_in, conv_weight, conv_offset))
        step_sizes = jax.nn.softplus(step_in + bias_in)
        decay_rates = -jnp.exp(decay_in)
        heads_out = block_scan(
            inner_vals.reshape(row_count, head_local, P_SIZE),
            step_sizes,
            decay_rates,
            state_in[:, :N],
            state_in[:, N:],
            skip_in,
            GROUP,
        )
        return heads_out.reshape(row_count, head_local * P_SIZE) * swish(gate_in)

    gated_vals, mixer_back = jax.vjp(
        mixer,
        gate_pre,
        value_pre,
        step_pre,
        state_full.astype(jnp.float32),
        conv_value,
        conv_value_bias,
        step_bias,
        decay_log,
        skip_gain,
    )
    squares = lax.psum(jnp.sum(gated_vals * gated_vals, axis=1), "col")
    gated_scale = lax.rsqrt(squares / E + EPSILON)[:, None]
    normed = (gated_vals * gated_scale * norm_gain).astype(jnp.bfloat16)
    out_terms = jnp.dot(
        normed, lax.all_gather(w_out, "row", axis=1, tiled=True), preferred_element_type=jnp.float32
    )
    branch_out = lax.psum_scatter(
        out_terms.astype(jnp.bfloat16), "col", scatter_dimension=0, tiled=True
    ).astype(jnp.float32)
    result = (hidden.astype(jnp.float32) + branch_out).astype(jnp.bfloat16)
    grad_full = lax.all_gather(grad_out, "col", axis=0, tiled=True)
    d_normed = lax.dot_general(
        grad_full,
        lax.all_gather(w_out, "row", axis=1, tiled=True),
        (((1,), (1,)), ((), ())),
        preferred_element_type=jnp.float32,
    )
    grad_out_t = lax.dot_general(
        grad_full, normed, (((0,), (0,)), ((), ())), preferred_element_type=jnp.float32
    )
    scaled_grad = d_normed * norm_gain
    gated_dots = lax.psum(jnp.sum(gated_vals * scaled_grad, axis=1), "col")[:, None]
    d_gated = (
        gated_scale * scaled_grad
        - gated_vals * gated_scale * gated_scale * gated_scale * gated_dots / E
    )
    grad_norm_gain = jnp.sum(d_normed * gated_vals * gated_scale, axis=0)
    (
        d_gate_pre,
        d_value_pre,
        d_step_pre,
        d_state_part,
        g_conv_value,
        g_conv_value_bias,
        g_step_bias,
        g_decay_log,
        g_skip_gain,
    ) = mixer_back(d_gated)
    d_state_local = lax.psum_scatter(
        d_state_part.astype(jnp.bfloat16), "col", scatter_dimension=1, tiled=True
    ).astype(jnp.float32)
    d_bc_pre, g_conv_bc, g_conv_bc_bias = state_back(d_state_local)
    grads_pre = (
        d_gate_pre.astype(jnp.bfloat16),
        d_value_pre.astype(jnp.bfloat16),
        d_bc_pre.astype(jnp.bfloat16),
        d_step_pre.astype(jnp.bfloat16),
    )
    pieces = lax.all_gather((w_gate, w_value, w_bc, w_step), "row", axis=0, tiled=True)
    product = lax.dot_general(
        grads_pre[0], pieces[0], (((1,), (1,)), ((), ())), preferred_element_type=jnp.float32
    )
    for back_grad_piece, weight_piece in zip(grads_pre[1:], pieces[1:]):
        product = product + lax.dot_general(
            back_grad_piece,
            weight_piece,
            (((1,), (1,)), ((), ())),
            preferred_element_type=jnp.float32,
        )
    weight_grads = tuple(
        (
            lax.dot_general(
                normal_in, grad_piece, (((0,), (0,)), ((), ())), preferred_element_type=jnp.float32
            )
            for grad_piece in grads_pre
        )
    )
    col_count = lax.axis_size("col")
    norm_value, norm_back = jax.vjp(norm_rows, rows_float, gain_float)
    d_rows_part, d_gain_part = norm_back(product)
    d_rows_local, d_gain_local = (
        lax.psum_scatter(
            d_rows_part.astype(jnp.bfloat16), "col", scatter_dimension=0, tiled=True
        ).astype(jnp.float32),
        lax.psum_scatter(
            d_gain_part.reshape(col_count, -1).astype(jnp.bfloat16),
            "col",
            scatter_dimension=0,
            tiled=True,
        ).astype(jnp.float32),
    )
    grad_hidden = grad_out.astype(jnp.float32) + d_rows_local
    spread = lax.axis_size("row")

    def tiled(vector):
        return jnp.broadcast_to(vector[None], (spread,) + vector.shape)

    summed_all = (
        lax.psum_scatter(
            weight_grads[0].astype(jnp.bfloat16), "row", scatter_dimension=0, tiled=True
        ).astype(jnp.float32),
        lax.psum_scatter(
            weight_grads[1].astype(jnp.bfloat16), "row", scatter_dimension=0, tiled=True
        ).astype(jnp.float32),
        lax.psum_scatter(
            weight_grads[2].astype(jnp.bfloat16), "row", scatter_dimension=0, tiled=True
        ).astype(jnp.float32),
        lax.psum_scatter(
            weight_grads[3].astype(jnp.bfloat16), "row", scatter_dimension=0, tiled=True
        ).astype(jnp.float32),
        lax.psum_scatter(
            grad_out_t.astype(jnp.bfloat16), "row", scatter_dimension=0, tiled=True
        ).astype(jnp.float32),
        lax.psum_scatter(
            tiled(d_gain_local[0]).astype(jnp.bfloat16), "row", scatter_dimension=0, tiled=True
        ).astype(jnp.float32),
        lax.psum_scatter(
            tiled(g_conv_value).astype(jnp.bfloat16), "row", scatter_dimension=0, tiled=True
        ).astype(jnp.float32),
        lax.psum_scatter(
            tiled(g_conv_value_bias).astype(jnp.bfloat16), "row", scatter_dimension=0, tiled=True
        ).astype(jnp.float32),
        lax.psum_scatter(
            tiled(g_conv_bc).astype(jnp.bfloat16), "row", scatter_dimension=0, tiled=True
        ).astype(jnp.float32),
        lax.psum_scatter(
            tiled(g_conv_bc_bias).astype(jnp.bfloat16), "row", scatter_dimension=0, tiled=True
        ).astype(jnp.float32),
        lax.psum_scatter(
            tiled(g_step_bias).astype(jnp.bfloat16), "row", scatter_dimension=0, tiled=True
        ).astype(jnp.float32),
        lax.psum_scatter(
            tiled(g_decay_log).astype(jnp.bfloat16), "row", scatter_dimension=0, tiled=True
        ).astype(jnp.float32),
        lax.psum_scatter(
            tiled(g_skip_gain).astype(jnp.bfloat16), "row", scatter_dimension=0, tiled=True
        ).astype(jnp.float32),
        lax.psum_scatter(
            tiled(grad_norm_gain).astype(jnp.bfloat16), "row", scatter_dimension=0, tiled=True
        ).astype(jnp.float32),
    )
    return (
        result,
        grad_hidden,
        summed_all[5][0],
        summed_all[0],
        summed_all[1],
        summed_all[2],
        summed_all[3],
        summed_all[6][0],
        summed_all[7][0],
        summed_all[8][0],
        summed_all[9][0],
        summed_all[10][0],
        summed_all[11][0],
        summed_all[12][0],
        summed_all[13][0],
        summed_all[4].T,
    )


def solution(mesh):
    placed = (
        P(("row", "col"), None),
        P("col"),
        P("row", "col"),
        P("row", "col"),
        P("row", "col"),
        P("row", "col"),
        P(None, "col"),
        P("col"),
        P(None, "col"),
        P("col"),
        P("col"),
        P("col"),
        P("col"),
        P("col"),
        P("col", "row"),
        P(("row", "col"), None),
    )
    return jax.shard_map(
        body,
        mesh=mesh,
        in_specs=placed,
        out_specs=(
            P(("row", "col"), None),
            P(("row", "col"), None),
            P("col"),
            P("row", "col"),
            P("row", "col"),
            P("row", "col"),
            P("row", "col"),
            P(None, "col"),
            P("col"),
            P(None, "col"),
            P("col"),
            P("col"),
            P("col"),
            P("col"),
            P("col"),
            P("col", "row"),
        ),
        check_vma=False,
    )
```

profile of v0, /device:TPU:0, one launch (start us, length us, event | category | flops | bytes accessed | tf_op | source)
XLA Modules:
  0.0 2432.6 jit_solution(16471768909405806578)
XLA Ops:
  35.6 81.9 %all-gather.10.cloned.1.call-done = bf16[2048,2560]{1,0:T(8,128)(2,1)} async-done(((bf16[512,2560]{1,0:T(8,128)(2,1)}), bf16[2048,2560]{1,0:T(8,128)(2,1)}) %all-gather.10.cloned.1.call-update) | async-done | bytes 10485776 | tf_op jit(solution)/shard_map/all_gather | solution.py:94
  155.5 31.6 %all-gather.12.cloned.1.call-done = bf16[2560,1280]{1,0:T(8,128)(2,1)} async-done(((bf16[320,1280]{1,0:T(8,128)(2,1)}), bf16[2560,1280]{1,0:T(8,128)(2,1)}) %all-gather.12.cloned.1.call-update) | async-done | bytes 6553616 | tf_op jit(solution)/shard_map/all_gather | solution.py:103
  206.5 27.0 %fusion.122 = (f32[2048,1280]{1,0:T(8,128)}, f32[2048,1280]{1,0:T(8,128)}) fusion(f32[2048,1280]{1,0:T(8,128)} %fusion.160, f32[1280]{0:T(1024)S(1)} %get-tuple-element.858, f32[1280]{0:T(1024)S(1)} %get-tuple-element.859, f32[1280]{0:T(1024)S(1)} %get-tuple-element.857, f32[1280]{0:T(1024)S(1)} %get-tuple-element.856, f32[1280]{0:T(1024)S(1)} %copy-done.43), kind=kLoop, calls=%fused_computation.185 | loop fusion | flops 31457280 | bytes 31482880 | tf_op jit(solution)/shard_map/jvp()/mul | solution.py:17
  283.5 391.7 %while.43 = (s32[]{:T(128)}, f32[20,64,128]{2,1,0:T(8,128)S(1)}, f32[8,256,20,64]{1,0,3,2:T(8,128)}, f32[8,20,64,128]{3,2,1,0:T(8,128)}, f32[8,256,20]{1,0,2:T(8...) while((s32[]{:T(128)}, f32[20,64,128]{2,1,0:T(8,128)S(1)}, ...), condition=%wide.region_4.5_spmd.clone, body=%wide.region_1.4_spmd.clone.sunk | while | flops 2123742208 | bytes 18647428 | solution.py:68
  298.8 30.2 %dynamic_update_slice.67 = f32[8,256,20,64]{1,0,3,2:T(8,128)} dynamic-update-slice(f32[8,256,20,64]{1,0,3,2:T(8,128)} %get-tuple-element.1212, f32[1,256,20,64]{1,0,3,2:T(1,128)S(1)} %copy.352, s32[]{:T(128)} %get-tuple-element.1210, s32[]{:T(128)} %constant.122.clone.1..sunk, s32[]{:T(128)} %constant.122.clone.1..sunk, s32[]{:T(128)} %constant.122.clone.1..sunk) | dynamic-update-slice | bytes 2621444 | tf_op jit(solution)/shard_map/jvp()/while/body/jit(dynamic_update_index_in_dim)/dynamic_update_slice | solution.py:68
  347.7 30.3 %dynamic_update_slice.67 = f32[8,256,20,64]{1,0,3,2:T(8,128)} dynamic-update-slice(f32[8,256,20,64]{1,0,3,2:T(8,128)} %get-tuple-element.1212, f32[1,256,20,64]{1,0,3,2:T(1,128)S(1)} %copy.352, s32[]{:T(128)} %get-tuple-element.1210, s32[]{:T(128)} %constant.122.clone.1..sunk, s32[]{:T(128)} %constant.122.clone.1..sunk, s32[]{:T(128)} %constant.122.clone.1..sunk) | dynamic-update-slice | bytes 2621444 | tf_op jit(solution)/shard_map/jvp()/while/body/jit(dynamic_update_index_in_dim)/dynamic_update_slice | solution.py:68
  396.8 30.3 %dynamic_update_slice.67 = f32[8,256,20,64]{1,0,3,2:T(8,128)} dynamic-update-slice(f32[8,256,20,64]{1,0,3,2:T(8,128)} %get-tuple-element.1212, f32[1,256,20,64]{1,0,3,2:T(1,128)S(1)} %copy.352, s32[]{:T(128)} %get-tuple-element.1210, s32[]{:T(128)} %constant.122.clone.1..sunk, s32[]{:T(128)} %constant.122.clone.1..sunk, s32[]{:T(128)} %constant.122.clone.1..sunk) | dynamic-update-slice | bytes 2621444 | tf_op jit(solution)/shard_map/jvp()/while/body/jit(dynamic_update_index_in_dim)/dynamic_update_slice | solution.py:68
  445.8 30.1 %dynamic_update_slice.67 = f32[8,256,20,64]{1,0,3,2:T(8,128)} dynamic-update-slice(f32[8,256,20,64]{1,0,3,2:T(8,128)} %get-tuple-element.1212, f32[1,256,20,64]{1,0,3,2:T(1,128)S(1)} %copy.352, s32[]{:T(128)} %get-tuple-element.1210, s32[]{:T(128)} %constant.122.clone.1..sunk, s32[]{:T(128)} %constant.122.clone.1..sunk, s32[]{:T(128)} %constant.122.clone.1..sunk) | dynamic-update-slice | bytes 2621444 | tf_op jit(solution)/shard_map/jvp()/while/body/jit(dynamic_update_index_in_dim)/dynamic_update_slice | solution.py:68
  494.6 30.1 %dynamic_update_slice.67 = f32[8,256,20,64]{1,0,3,2:T(8,128)} dynamic-update-slice(f32[8,256,20,64]{1,0,3,2:T(8,128)} %get-tuple-element.1212, f32[1,256,20,64]{1,0,3,2:T(1,128)S(1)} %copy.352, s32[]{:T(128)} %get-tuple-element.1210, s32[]{:T(128)} %constant.122.clone.1..sunk, s32[]{:T(128)} %constant.122.clone.1..sunk, s32[]{:T(128)} %constant.122.clone.1..sunk) | dynamic-update-slice | bytes 2621444 | tf_op jit(solution)/shard_map/jvp()/while/body/jit(dynamic_update_index_in_dim)/dynamic_update_slice | solution.py:68
  543.5 30.1 %dynamic_update_slice.67 = f32[8,256,20,64]{1,0,3,2:T(8,128)} dynamic-update-slice(f32[8,256,20,64]{1,0,3,2:T(8,128)} %get-tuple-element.1212, f32[1,256,20,64]{1,0,3,2:T(1,128)S(1)} %copy.352, s32[]{:T(128)} %get-tuple-element.1210, s32[]{:T(128)} %constant.122.clone.1..sunk, s32[]{:T(128)} %constant.122.clone.1..sunk, s32[]{:T(128)} %constant.122.clone.1..sunk) | dynamic-update-slice | bytes 2621444 | tf_op jit(solution)/shard_map/jvp()/while/body/jit(dynamic_update_index_in_dim)/dynamic_update_slice | solution.py:68
  592.3 30.1 %dynamic_update_slice.67 = f32[8,256,20,64]{1,0,3,2:T(8,128)} dynamic-update-slice(f32[8,256,20,64]{1,0,3,2:T(8,128)} %get-tuple-element.1212, f32[1,256,20,64]{1,0,3,2:T(1,128)S(1)} %copy.352, s32[]{:T(128)} %get-tuple-element.1210, s32[]{:T(128)} %constant.122.clone.1..sunk, s32[]{:T(128)} %constant.122.clone.1..sunk, s32[]{:T(128)} %constant.122.clone.1..sunk) | dynamic-update-slice | bytes 2621444 | tf_op jit(solution)/shard_map/jvp()/while/body/jit(dynamic_update_index_in_dim)/dynamic_update_slice | solution.py:68
  641.1 30.1 %dynamic_update_slice.67 = f32[8,256,20,64]{1,0,3,2:T(8,128)} dynamic-update-slice(f32[8,256,20,64]{1,0,3,2:T(8,128)} %get-tuple-element.1212, f32[1,256,20,64]{1,0,3,2:T(1,128)S(1)} %copy.352, s32[]{:T(128)} %get-tuple-element.1210, s32[]{:T(128)} %constant.122.clone.1..sunk, s32[]{:T(128)} %constant.122.clone.1..sunk, s32[]{:T(128)} %constant.122.clone.1..sunk) | dynamic-update-slice | bytes 2621444 | tf_op jit(solution)/shard_map/jvp()/while/body/jit(dynamic_update_index_in_dim)/dynamic_update_slice | solution.py:68
  699.6 24.6 %multiply_reduce_fusion.10 = (f32[2048]{0:T(1024)S(1)}, f32[2048,1280]{1,0:T(8,128)}, f32[2048,1280]{1,0:T(8,128)}) fusion(f32[2048,1280]{1,0:T(8,128)} %copy.231, bf16[2048,2560]{1,0:T(8,128)(2,1)} %copy-done, bf16[2560,1280]{1,0:T(8,128)(2,1)} %all-gather.16.cloned.1.call-done), kind=kOutput, calls=%fused_computation.181 | convolution fusion | flops 13440120832 | bytes 48504832 | tf_op jit(solution)/shard_map/dot_general | solution.py:109
  734.4 23.3 multiply_reduce_fusion.4
  818.7 994.8 %while.44 = (s32[]{:T(128)}, f32[20]{0:T(128)}, f32[20]{0:T(128)}, f32[20,64,128]{2,1,0:T(8,128)}, f32[8,256,20,64]{1,0,3,2:T(8,128)}, /*index=5*/f32[8,256,20]{...) while((s32[]{:T(128)}, f32[20]{0:T(128)}, f32[20]{0:T(128)}, ...), condition=%wide.region_24.25_spmd.clone, body=%wide.region_10.24_spmd.clone.sunk | while | flops 4864715776 | bytes 43812472 | solution.py:68
  906.9 30.0 %dynamic_update_slice.71 = f32[8,256,20,64]{1,0,3,2:T(8,128)} dynamic-update-slice(f32[8,256,20,64]{1,0,3,2:T(8,128)} %get-tuple-element.1262, f32[1,256,20,64]{1,0,3,2:T(1,128)S(1)} %copy.368, s32[]{:T(128)S(6)} %sub.267, s32[]{:T(128)} %constant.122.clone.1..sunk.1, s32[]{:T(128)} %constant.122.clone.1..sunk.1, s32[]{:T(128)} %constant.122.clone.1..sunk.1) | dynamic-update-slice | bytes 2621444 | tf_op jit(solution)/shard_map/transpose(jvp())/while/body/jit(dynamic_update_index_in_dim)/dynamic_update_slice | solution.py:68
  1030.8 30.0 %dynamic_update_slice.71 = f32[8,256,20,64]{1,0,3,2:T(8,128)} dynamic-update-slice(f32[8,256,20,64]{1,0,3,2:T(8,128)} %get-tuple-element.1262, f32[1,256,20,64]{1,0,3,2:T(1,128)S(1)} %copy.368, s32[]{:T(128)S(6)} %sub.267, s32[]{:T(128)} %constant.122.clone.1..sunk.1, s32[]{:T(128)} %constant.122.clone.1..sunk.1, s32[]{:T(128)} %constant.122.clone.1..sunk.1) | dynamic-update-slice | bytes 2621444 | tf_op jit(solution)/shard_map/transpose(jvp())/while/body/jit(dynamic_update_index_in_dim)/dynamic_update_slice | solution.py:68
  1155.3 30.0 %dynamic_update_slice.71 = f32[8,256,20,64]{1,0,3,2:T(8,128)} dynamic-update-slice(f32[8,256,20,64]{1,0,3,2:T(8,128)} %get-tuple-element.1262, f32[1,256,20,64]{1,0,3,2:T(1,128)S(1)} %copy.368, s32[]{:T(128)S(6)} %sub.267, s32[]{:T(128)} %constant.122.clone.1..sunk.1, s32[]{:T(128)} %constant.122.clone.1..sunk.1, s32[]{:T(128)} %constant.122.clone.1..sunk.1) | dynamic-update-slice | bytes 2621444 | tf_op jit(solution)/shard_map/transpose(jvp())/while/body/jit(dynamic_update_index_in_dim)/dynamic_update_slice | solution.py:68
  1279.8 30.0 %dynamic_update_slice.71 = f32[8,256,20,64]{1,0,3,2:T(8,128)} dynamic-update-slice(f32[8,256,20,64]{1,0,3,2:T(8,128)} %get-tuple-element.1262, f32[1,256,20,64]{1,0,3,2:T(1,128)S(1)} %copy.368, s32[]{:T(128)S(6)} %sub.267, s32[]{:T(128)} %constant.122.clone.1..sunk.1, s32[]{:T(128)} %constant.122.clone.1..sunk.1, s32[]{:T(128)} %constant.122.clone.1..sunk.1) | dynamic-update-slice | bytes 2621444 | tf_op jit(solution)/shard_map/transpose(jvp())/while/body/jit(dynamic_update_index_in_dim)/dynamic_update_slice | solution.py:68
  1404.3 30.0 %dynamic_update_slice.71 = f32[8,256,20,64]{1,0,3,2:T(8,128)} dynamic-update-slice(f32[8,256,20,64]{1,0,3,2:T(8,128)} %get-tuple-element.1262, f32[1,256,20,64]{1,0,3,2:T(1,128)S(1)} %copy.368, s32[]{:T(128)S(6)} %sub.267, s32[]{:T(128)} %constant.122.clone.1..sunk.1, s32[]{:T(128)} %constant.122.clone.1..sunk.1, s32[]{:T(128)} %constant.122.clone.1..sunk.1) | dynamic-update-slice | bytes 2621444 | tf_op jit(solution)/shard_map/transpose(jvp())/while/body/jit(dynamic_update_index_in_dim)/dynamic_update_slice | solution.py:68
  1528.8 30.0 %dynamic_update_slice.71 = f32[8,256,20,64]{1,0,3,2:T(8,128)} dynamic-update-slice(f32[8,256,20,64]{1,0,3,2:T(8,128)} %get-tuple-element.1262, f32[1,256,20,64]{1,0,3,2:T(1,128)S(1)} %copy.368, s32[]{:T(128)S(6)} %sub.267, s32[]{:T(128)} %constant.122.clone.1..sunk.1, s32[]{:T(128)} %constant.122.clone.1..sunk.1, s32[]{:T(128)} %constant.122.clone.1..sunk.1) | dynamic-update-slice | bytes 2621444 | tf_op jit(solution)/shard_map/transpose(jvp())/while/body/jit(dynamic_update_index_in_dim)/dynamic_update_slice | solution.py:68
  1653.3 30.0 %dynamic_update_slice.71 = f32[8,256,20,64]{1,0,3,2:T(8,128)} dynamic-update-slice(f32[8,256,20,64]{1,0,3,2:T(8,128)} %get-tuple-element.1262, f32[1,256,20,64]{1,0,3,2:T(1,128)S(1)} %copy.368, s32[]{:T(128)S(6)} %sub.267, s32[]{:T(128)} %constant.122.clone.1..sunk.1, s32[]{:T(128)} %constant.122.clone.1..sunk.1, s32[]{:T(128)} %constant.122.clone.1..sunk.1) | dynamic-update-slice | bytes 2621444 | tf_op jit(solution)/shard_map/transpose(jvp())/while/body/jit(dynamic_update_index_in_dim)/dynamic_update_slice | solution.py:68
  1777.8 30.0 %dynamic_update_slice.71 = f32[8,256,20,64]{1,0,3,2:T(8,128)} dynamic-update-slice(f32[8,256,20,64]{1,0,3,2:T(8,128)} %get-tuple-element.1262, f32[1,256,20,64]{1,0,3,2:T(1,128)S(1)} %copy.368, s32[]{:T(128)S(6)} %sub.267, s32[]{:T(128)} %constant.122.clone.1..sunk.1, s32[]{:T(128)} %constant.122.clone.1..sunk.1, s32[]{:T(128)} %constant.122.clone.1..sunk.1) | dynamic-update-slice | bytes 2621444 | tf_op jit(solution)/shard_map/transpose(jvp())/while/body/jit(dynamic_update_index_in_dim)/dynamic_update_slice | solution.py:68
  1842.1 26.5 %multiply_reduce_fusion.8 = (f32[1280]{0:T(1024)S(1)}, f32[1280]{0:T(1024)S(1)}, f32[1280]{0:T(1024)S(1)}, f32[1280]{0:T(1024)S(1)}, bf16[1280]{0:T(1024)(128)(2,1)}, /*index=5*/f32[2048,1280]{1,0:T(8,128)}) fusion(f32[2048,1280]{1,0:T(8,128)} %fusion.160, f32[2048,1280]{1,0:T(8,128)} %get-tuple-element.933, f32[2048,1280]{1,0:T(8,128)} %copy.241), kind=kLoop, calls=%fused_computation.177 | loop fusion | flops 47179520 | bytes 41966080 | tf_op jit(solution)/shard_map/transpose(jvp())/reduce_sum | solution.py:34
  1888.3 21.9 fusion.123
  1989.5 21.8 convolution_convert_fusion
  2021.2 20.6 fusion.163
  2058.7 32.5 %fusion.111 = (bf16[2560]{0:T(1024)(128)(2,1)S(1)}, f32[2048]{0:T(1024)S(1)}, f32[2048,2560]{1,0:T(8,128)}) fusion(bf16[2048,2560]{1,0:T(8,128)(2,1)} %all-gather.10.cloned.1.call-done, f32[2048]{0:T(1024)S(1)} %copy-done.21, f32[2560]{0:T(1024)S(1)} %copy-done.19, f32[2048,2560]{1,0:T(8,128)} %fusion.133, bf16[2048,64]{0,1:T(8,128)(2,1)S(1)} %copy-done.8, ...), kind=kOutput, calls=%fused_computation.153 | convolution fusion | flops 723512832 | bytes 94993408 | tf_op jit(solution)/shard_map/dot_general | solution.py:202
  2124.2 28.7 %all-reduce.31 = (bf16[8,640]{1,0:T(8,128)(2,1)S(1)}, bf16[8,1280]{1,0:T(8,128)(2,1)S(1)}, bf16[8,4,64]{2,1,0:T(4,128)(2,1)S(1)}, bf16[8,64]{1,0:T(8,128)(2,1)S(...) all-reduce(bf16[8,640]{1,0:T(8,128)(2,1)S(1)} %broadcast_in_dim.217, ...), channel_id=6, replica_groups=mesh['row'=8,'col'=4] {'row'}, use_global_device_ids=true, to_apply=%region_30.31.clone | all-reduce | flops 28640 | bytes 114560
  2171.9 38.1 %reduce-scatter.21.cloned.1.call-done = bf16[320,1280]{1,0:T(8,128)(2,1)} async-done(((bf16[2560,1280]{1,0:T(8,128)(2,1)}), bf16[320,1280]{1,0:T(8,128)(2,1)}) %reduce-scatter.21.cloned.1.call-update) | async-done | bytes 819216 | tf_op jit(solution)/shard_map/reduce_scatter | solution.py:237
  2212.4 102.1 %reduce-scatter.15.cloned.1.call-done = bf16[512,2560]{1,0:T(8,128)(2,1)} async-done(((bf16[2048,2560]{1,0:T(8,128)(2,1)}), bf16[512,2560]{1,0:T(8,128)(2,1)}) %reduce-scatter.15.cloned.1.call-update) | async-done | bytes 2621456 | tf_op jit(solution)/shard_map/reduce_scatter | solution.py:155
  2319.2 101.8 %reduce-scatter.19.cloned.1.call-done = bf16[512,2560]{1,0:T(8,128)(2,1)} async-done(((bf16[2048,2560]{1,0:T(8,128)(2,1)}), bf16[512,2560]{1,0:T(8,128)(2,1)}) %reduce-scatter.19.cloned.1.call-update) | async-done | bytes 2621456 | tf_op jit(solution)/shard_map/reduce_scatter | solution.py:220
  (996 shorter events, 1350.5 us)
Async XLA Ops:
  7.2 110.3 %all-gather.10.cloned.1.call-start = ((), (), s32[]{:S(2)}) async-start(), calls=%async_computation.8 | async-start | bytes 13107200 | tf_op jit(solution)/shard_map/all_gather | solution.py:94
  7.9 179.2 %all-gather.12.cloned.1.call-start = ((), (), s32[]{:S(2)}) async-start(), calls=%async_computation.9 | async-start | bytes 7372800 | tf_op jit(solution)/shard_map/all_gather | solution.py:103
  8.7 265.7 %all-gather.14.cloned.1.call-start = ((), (), s32[]{:S(2)}) async-start(), calls=%async_computation.10 | async-start | bytes 1310720 | tf_op jit(solution)/shard_map/all_gather | solution.py:118
  19.1 108.7 %copy-start.18 = (f32[2560]{0:T(1024)}, f32[2560]{0:T(1024)S(1)}, u32[]{:S(2)}) copy-start(f32[2560]{0:T(1024)S(1)} %reshape.358) | copy-start | bytes 30724
  34.7 93.1 %copy-start.9 = (bf16[2560,64]{0,1:T(8,128)(2,1)}, bf16[2560,64]{0,1:T(8,128)(2,1)S(1)}, u32[]{:S(2)}) copy-start(bf16[2560,64]{0,1:T(8,128)(2,1)S(1)} %reshape.357) | copy-start | bytes 983044
  35.6 99.5 %copy-start.48 = (f32[64]{0:T(128)}, f32[64]{0:T(128)S(1)}, u32[]{:S(2)}) copy-start(f32[64]{0:T(128)S(1)} %get-tuple-element.957) | copy-start | bytes 772
  35.6 99.5 %copy-start.50 = (f32[64]{0:T(128)}, f32[64]{0:T(128)S(1)}, u32[]{:S(2)}) copy-start(f32[64]{0:T(128)S(1)} %get-tuple-element.958) | copy-start | bytes 772
  35.6 99.5 %copy-start.52 = (f32[64]{0:T(128)}, f32[64]{0:T(128)S(1)}, u32[]{:S(2)}) copy-start(f32[64]{0:T(128)S(1)} %get-tuple-element.959) | copy-start | bytes 772
  35.6 99.5 %copy-start.54 = (f32[64]{0:T(128)}, f32[64]{0:T(128)S(1)}, u32[]{:S(2)}) copy-start(f32[64]{0:T(128)S(1)} %get-tuple-element.960) | copy-start | bytes 772
  137.3 562.4 %all-gather.16.cloned.1.call-start = ((), (), s32[]{:S(2)}) async-start(), calls=%async_computation.11 | async-start | bytes 7372800 | tf_op jit(solution)/shard_map/all_gather | solution.py:102
  137.9 596.5 %all-gather.18.cloned.1.call-start = ((), (), s32[]{:S(2)}) async-start(), calls=%async_computation.12 | async-start | bytes 7372800 | tf_op jit(solution)/shard_map/all_gather | solution.py:153
  138.4 596.0 %all-gather.20.cloned.1.call-start = ((), (), s32[]{:S(2)}) async-start(), calls=%async_computation.14 | async-start | bytes 13107200 | tf_op jit(solution)/shard_map/all_gather | solution.py:159
  139.0 1738.5 %reduce-scatter.17.cloned.1.call-start = ((), (), s32[]{:S(2)}) async-start(), calls=%async_computation.15 | async-start | bytes 1310720 | tf_op jit(solution)/shard_map/reduce_scatter | solution.py:187
  139.2 67.2 %copy-start.24 = (f32[1280]{0:T(1024)}, f32[1280]{0:T(1024)S(1)}, u32[]{:S(2)}) copy-start(f32[1280]{0:T(1024)S(1)} %get-tuple-element.856) | copy-start | bytes 15364
  139.2 67.2 %copy-start.26 = (f32[1280]{0:T(1024)}, f32[1280]{0:T(1024)S(1)}, u32[]{:S(2)}) copy-start(f32[1280]{0:T(1024)S(1)} %get-tuple-element.857) | copy-start | bytes 15364
  139.3 67.2 %copy-start.28 = (f32[1280]{0:T(1024)}, f32[1280]{0:T(1024)S(1)}, u32[]{:S(2)}) copy-start(f32[1280]{0:T(1024)S(1)} %get-tuple-element.858) | copy-start | bytes 15364
  139.3 67.2 %copy-start.30 = (f32[1280]{0:T(1024)}, f32[1280]{0:T(1024)S(1)}, u32[]{:S(2)}) copy-start(f32[1280]{0:T(1024)S(1)} %get-tuple-element.859) | copy-start | bytes 15364
  155.0 115.1 %copy-start.13 = (bf16[2560,20]{0,1:T(8,128)(2,1)}, bf16[2560,20]{0,1:T(8,128)(2,1)S(1)}, u32[]{:S(2)}) copy-start(bf16[2560,20]{0,1:T(8,128)(2,1)S(1)} %reshape.355) | copy-start | bytes 307204
  155.5 51.0 %copy-start.43 = (f32[1280]{0:T(1024)S(1)}, f32[1280]{0:T(1024)}, u32[]{:S(2)}) copy-start(f32[1280]{0:T(1024)} %param.27) | copy-start | bytes 15364
  894.1 47.2 %copy-start.33 = (f32[20]{0:T(128)S(1)}, f32[20]{0:T(128)}, u32[]{:S(2)}) copy-start(f32[20]{0:T(128)} %get-tuple-element.1189) | copy-start | bytes 244 | tf_op jit(solution)/shard_map/transpose(jvp())/while
  1142.4 47.2 %copy-start.33 = (f32[20]{0:T(128)S(1)}, f32[20]{0:T(128)}, u32[]{:S(2)}) copy-start(f32[20]{0:T(128)} %get-tuple-element.1189) | copy-start | bytes 244 | tf_op jit(solution)/shard_map/transpose(jvp())/while
  1515.9 47.2 %copy-start.33 = (f32[20]{0:T(128)S(1)}, f32[20]{0:T(128)}, u32[]{:S(2)}) copy-start(f32[20]{0:T(128)} %get-tuple-element.1189) | copy-start | bytes 244 | tf_op jit(solution)/shard_map/transpose(jvp())/while
  1640.5 47.2 %copy-start.33 = (f32[20]{0:T(128)S(1)}, f32[20]{0:T(128)}, u32[]{:S(2)}) copy-start(f32[20]{0:T(128)} %get-tuple-element.1189) | copy-start | bytes 244 | tf_op jit(solution)/shard_map/transpose(jvp())/while
  1817.8 292.3 %all-reduce.34.cloned.1.call-start = ((), (), s32[]{:S(2)}) async-start(), calls=%async_computation.22 | async-start | bytes 163840
  1870.6 241.5 %reduce-scatter.27.cloned.1.call-start = ((), (), s32[]{:S(2)}) async-start(), calls=%async_computation.20 | async-start | bytes 737280
  1877.3 282.9 %reduce-scatter.25.cloned.1.call-start = ((), (), s32[]{:S(2)}) async-start(), calls=%async_computation.19 | async-start | bytes 737280
  1888.2 273.5 %reduce-scatter.29.cloned.1.call-start = ((), (), s32[]{:S(2)}) async-start(), calls=%async_computation.21 | async-start | bytes 7372800
  1919.8 249.7 %reduce-scatter.23.cloned.1.call-start = ((), (), s32[]{:S(2)}) async-start(), calls=%async_computation.18 | async-start | bytes 7372800 | tf_op jit(solution)/shard_map/reduce_scatter | solution.py:240
  1968.8 241.2 %reduce-scatter.21.cloned.1.call-start = ((), (), s32[]{:S(2)}) async-start(), calls=%async_computation.17 | async-start | bytes 7372800 | tf_op jit(solution)/shard_map/reduce_scatter | solution.py:237
  1989.3 325.2 %reduce-scatter.15.cloned.1.call-start = ((), (), s32[]{:S(2)}) async-start(), calls=%async_computation.13 | async-start | bytes 13107200 | tf_op jit(solution)/shard_map/reduce_scatter | solution.py:155
  2011.3 409.6 %reduce-scatter.19.cloned.1.call-start = ((), (), s32[]{:S(2)}) async-start(), calls=%async_computation.16 | async-start | bytes 13107200 | tf_op jit(solution)/shard_map/reduce_scatter | solution.py:220
  2161.8 259.2 %copy-start.3 = (bf16[512,2560]{1,0:T(8,128)(2,1)S(1)}, bf16[512,2560]{1,0:T(8,128)(2,1)}, u32[]{:S(2)}) copy-start(bf16[512,2560]{1,0:T(8,128)(2,1)} %param.35) | copy-start | bytes 7864324
  (96 other events, 1587.0 us)
Sparse Core Ops, SparseCore 0:
  9.8 107.6 all-gather.9
  119.2 67.9 all-gather.11
  189.6 25.1 all-gather.13
  216.2 66.8 all-gather.15
  284.6 65.5 all-gather.17
  351.9 103.5 all-gather.19
  1817.9 25.9 reduce-scatter.16
  1870.7 48.7 all-reduce.33
  1922.4 35.0 reduce-scatter.26
  1960.2 29.7 reduce-scatter.24
  1992.3 70.3 reduce-scatter.28
  2064.9 71.1 reduce-scatter.22
  2138.5 71.4 reduce-scatter.20
  2213.0 101.5 reduce-scatter.14
  2317.5 103.4 reduce-scatter.18
where the time goes:
time: 2470 us; the launch traced here: 2430 us
  local copies, waits for them, and re-layouts  942 us (38%)
  matrix products  668 us (27%)
  waiting for transfers between devices  359 us (15%)
  other arithmetic  347 us (14%)
  blocking collectives  96.7 us (4%)
    dynamic_update_slice x40, local copies, waits for them, and re-layouts, block_scan(): lax.scan(jax.checkpoint(block_step), start_state, (split_vals, split_step...  515 us
    dot_general x24, matrix products, block_step(): inside = jnp.einsum('tsh,shp->thp', mixing, values_in, precision=HIGH)  192 us
    reduce_scatter x1, waiting for transfers between devices, body(): lax.psum_scatter(out_terms.astype(jnp.bfloat16), 'col', scatter_dimension...  102 us
    reduce_scatter x1, waiting for transfers between devices, body(): lax.psum_scatter(d_rows_part.astype(jnp.bfloat16), 'col', scatter_dimensi...  102 us
    unnamed x166, local copies, waits for them, and re-layouts  95.5 us
    dot_general x32, matrix products, block_step(): jnp.einsum('tn,hpn->thp', c_here, carried, precision=HIGH)  92.6 us
    another operation x82, other arithmetic  89.5 us
    all_gather x1, waiting for transfers between devices, body(): lax.all_gather(hidden, 'col', axis=0, tiled=True)  81.9 us
  transfers between devices with their start and end apart: 15, of which 5 were waited for; matrix products, arithmetic and copies ran while one was open for 36% of the time, Pallas kernels for 0%

commit v1 on v0

v1 whole, which is shorter than its diff:
```python
import functools
import jax
import jax.numpy as jnp
from jax import lax
from jax.experimental import pallas as pl
from jax.experimental.pallas import tpu as pltpu
from jax.sharding import PartitionSpec as P

P_SIZE = 64
N = 128
Q = 128
LANES = 128
NEG = -1e30
HIGH = lax.Precision.HIGHEST
F32 = jnp.float32
BF16 = jnp.bfloat16


def sigmoid(v):
    return 0.5 * jnp.tanh(0.5 * v) + 0.5


def nt_dot(a, b):
    return lax.dot_general(a, b, (((1,), (1,)), ((), ())), preferred_element_type=F32)


def mm(a, b):
    return jnp.dot(a, b, preferred_element_type=F32)


def mm_exact(a, b):
    return jnp.dot(a, b, precision=HIGH, preferred_element_type=F32)


def turned(m):
    return m.astype(F32).T.astype(BF16)


def pair_cols(low_half, cols, first):
    return jnp.where(low_half, cols[:, first : first + 1], cols[:, first + 1 : first + 2])


def halves(low_half, v):
    zero = jnp.zeros_like(v)
    return jnp.concatenate([jnp.where(low_half, v, zero), jnp.where(low_half, zero, v)], axis=0)


def conv_at(halo, taps_ref, bias_ref, cols, start):
    total = bias_ref[:, cols] + taps_ref[0:1, cols] * halo[start : start + Q, cols]
    for k in range(1, 4):
        total = total + taps_ref[k : k + 1, cols] * halo[start + k : start + k + Q, cols]
    return total


def scan_forward(
    seat_ref, vp_ref, bc_ref, st_ref, taps_ref, bias_ref, rate_ref, skip_ref,
    y_ref, hold_ref, state, halo, *, pairs
):
    @pl.when(pl.program_id(0) == 0)
    def _():
        state[...] = jnp.zeros_like(state)
        halo[0:8, :] = jnp.zeros_like(halo[0:8, :])

    halo[8 : 8 + Q, :] = vp_ref[...].astype(F32)
    rows = lax.broadcasted_iota(jnp.int32, (Q, Q), 0)
    lanes = lax.broadcasted_iota(jnp.int32, (Q, Q), 1)
    causal = rows >= lanes
    low_half = lanes < P_SIZE
    steps = st_ref[...]
    lam = mm_exact(causal.astype(F32), steps * rate_ref[...])
    source_t = (lam - jnp.log(steps)).T
    grown = jnp.exp(lam)
    last = lam[Q - 1 : Q, :]
    weight = jnp.exp(last - lam) * steps
    fade = jnp.exp(last)
    b_rows = bc_ref[:, :N]
    c_rows = bc_ref[:, N:]
    b_t = turned(b_rows)
    scores = nt_dot(c_rows, b_rows)
    for pair in range(pairs):
        cols = slice(pair * LANES, (pair + 1) * LANES)
        first = 2 * pair
        conv = conv_at(halo, taps_ref, bias_ref, cols, 5)
        x = conv * sigmoid(conv)
        mixing = []
        for h in (first, first + 1):
            gap = jnp.where(causal, lam[:, h : h + 1] - source_t[h : h + 1, :], NEG)
            mixing.append((scores * jnp.exp(gap)).astype(BF16))
        y = mm(jnp.concatenate(mixing, axis=1), halves(low_half, x).astype(BF16))
        held = state[:, cols]
        held_low = held.astype(BF16)
        y = y + mm(c_rows, held_low) * pair_cols(low_half, grown, first)
        y = y + skip_ref[:, cols] * x
        y_ref[:, cols] = y.astype(y_ref.dtype)
        hold_ref[0, :, cols] = held_low
        fed = (x * pair_cols(low_half, weight, first)).astype(BF16)
        state[:, cols] = held * pair_cols(low_half[0:1], fade, first) + mm(b_t, fed)
    halo[0:8, :] = halo[Q : Q + 8, :]


def scan_backward(
    seat_ref, vp_ref, before_ref, dy_ref, bc_ref, st_ref, hold_ref, taps_ref, bias_ref, rate_ref, skip_ref, pick_ref,
    dvp_ref, dbc_ref, dst_ref, gconv_ref, gdecay_ref,
    halo, gbuf, ds, ds_low, across, r_cols, w_rows, state_terms, inter_terms, fed_all, dyl_all, e_rows, *, pairs, blocks
):
    step_id = pl.program_id(0)

    @pl.when(step_id == 0)
    def _():
        ds[...] = jnp.zeros_like(ds)
        gbuf[Q : Q + 8, :] = jnp.zeros_like(gbuf[Q : Q + 8, :])
        gconv_ref[...] = jnp.zeros_like(gconv_ref)
        gdecay_ref[...] = jnp.zeros_like(gdecay_ref)
        r_cols[...] = jnp.zeros_like(r_cols)
        w_rows[...] = jnp.zeros_like(w_rows)
        e_rows[...] = jnp.zeros_like(e_rows)

    halo[16 : 16 + Q, :] = vp_ref[...].astype(F32)

    @pl.when(step_id < blocks - 1)
    def _():
        halo[0:16, :] = before_ref[...].astype(F32)

    @pl.when(step_id == blocks - 1)
    def _():
        halo[0:16, :] = jnp.zeros_like(halo[0:16, :])

    rows = lax.broadcasted_iota(jnp.int32, (Q, Q), 0)
    lanes = lax.broadcasted_iota(jnp.int32, (Q, Q), 1)
    causal = rows >= lanes
    later = lanes >= rows
    low_half = lanes < P_SIZE
    steps = st_ref[...]
    rate = rate_ref[...]
    lam = mm_exact(causal.astype(F32), steps * rate)
    lam_t = lam.T
    grown = jnp.exp(lam)
    last = lam[Q - 1 : Q, :]
    reach = jnp.exp(last - lam)
    fade = jnp.exp(last)
    b_rows = bc_ref[:, :N]
    c_rows = bc_ref[:, N:]
    c_t = turned(c_rows)
    scores_t = nt_dot(b_rows, c_rows)
    for pair in range(pairs):
        cols = slice(pair * LANES, (pair + 1) * LANES)
        first = 2 * pair
        conv = conv_at(halo, taps_ref, bias_ref, cols, 13)
        gate = sigmoid(conv)
        x = conv * gate
        dy = dy_ref[:, cols]
        dy_wide = dy.astype(F32)
        q_t = nt_dot(halves(low_half, x).astype(BF16), dy)
        mixing = []
        crossed = None
        for at, h in enumerate((first, first + 1)):
            step_col = steps[:, h : h + 1]
            decay = jnp.exp(jnp.where(later, lam_t[h : h + 1, :] - lam[:, h : h + 1], NEG))
            seen = decay * q_t[at * Q : (at + 1) * Q]
            stepped = seen * step_col
            crossed = stepped if crossed is None else crossed + stepped
            r_cols[:, h : h + 1] = jnp.sum(seen * scores_t, axis=1, keepdims=True)
            w_rows[h : h + 1, :] = jnp.sum(stepped * scores_t, axis=0, keepdims=True)
            mixing.append((decay * scores_t).astype(BF16))
        if pair == 0:
            across[...] = crossed
        else:
            across[...] += crossed
        dx = mm(jnp.concatenate(mixing, axis=1), halves(low_half, dy_wide).astype(BF16))
        d_state = ds[:, cols]
        d_state_low = d_state.astype(BF16)
        ds_low[:, cols] = d_state_low
        step_pair = pair_cols(low_half, steps, first)
        reach_pair = pair_cols(low_half, reach, first)
        carried = reach_pair * mm(b_rows, d_state_low)
        dx = step_pair * (dx + carried) + skip_ref[:, cols] * dy_wide
        state_terms[:, cols] = (x * carried).astype(BF16)
        fed_all[:, cols] = (x * (reach_pair * step_pair)).astype(BF16)
        held = hold_ref[0, :, cols]
        dyl = dy_wide * pair_cols(low_half, grown, first)
        dyl_low = dyl.astype(BF16)
        dyl_all[:, cols] = dyl_low
        inter_terms[:, cols] = (dyl * mm(c_rows, held)).astype(BF16)
        e_rows[0:1, cols] = jnp.sum(d_state * held.astype(F32), axis=0, keepdims=True)
        ds[:, cols] = d_state * pair_cols(low_half[0:1], fade, first) + mm(c_t, dyl_low)
        g = dx * (gate * (1.0 + conv * (1.0 - gate)))
        gbuf[0:Q, cols] = g
        for k in range(4):
            gconv_ref[k : k + 1, cols] += jnp.sum(g * halo[13 + k : 13 + k + Q, cols], axis=0, keepdims=True)
        gconv_ref[4:5, cols] += jnp.sum(g, axis=0, keepdims=True)
        gconv_ref[5:6, cols] += jnp.sum(dy_wide * x, axis=0, keepdims=True)
        d_pre = taps_ref[3:4, cols] * g
        for k in range(1, 4):
            d_pre = d_pre + taps_ref[3 - k : 4 - k, cols] * gbuf[k : k + Q, cols]
        dvp_ref[:, cols] = d_pre.astype(dvp_ref.dtype)
        gbuf[Q : Q + 8, cols] = g[0:8]
    if dvp_ref.shape[1] > pairs * LANES:
        dvp_ref[:, pairs * LANES :] = jnp.zeros_like(dvp_ref[:, pairs * LANES :])
    cross = across[...]
    d_b = mm(cross.astype(BF16), c_rows) + nt_dot(fed_all[...], ds_low[...])
    d_c = mm(turned(cross), b_rows) + nt_dot(dyl_all[...], hold_ref[0])
    dbc_ref[:, :N] = d_b.astype(dbc_ref.dtype)
    dbc_ref[:, N:] = d_c.astype(dbc_ref.dtype)
    pick = pick_ref[...]
    from_state = mm(state_terms[...], pick)
    from_carry = mm(inter_terms[...], pick)
    e_high = e_rows[...].astype(BF16)
    e_rest = (e_rows[...] - e_high.astype(F32)).astype(BF16)
    through = (mm(e_high, pick) + mm(e_rest, pick))[0:1]
    r_all = r_cols[...]
    d_lam = w_rows[...].T - steps * r_all + from_carry
    d_log = (
        mm_exact(later.astype(F32), d_lam)
        + mm_exact((rows > lanes).astype(F32), steps * from_state)
        + fade * through
    )
    dst_ref[...] = r_all + from_state + rate * d_log
    gdecay_ref[...] += jnp.sum(steps * d_log, axis=0, keepdims=True)


def chunk_of(i, seat, per):
    return (lax.div(i, per) ^ seat[0]) * per + lax.rem(i, per)


def run_forward(seat, pre, states_in, steps, taps, bias, rate, skip, shards):
    tokens = steps.shape[0]
    width = taps.shape[1]
    blocks = tokens // Q
    per = blocks // shards
    fixed = lambda i, seat: (0, 0)
    plain = lambda i, seat: (i, 0)
    moved = lambda i, seat: (chunk_of(i, seat, per), 0)
    return pl.pallas_call(
        functools.partial(scan_forward, pairs=width // LANES),
        out_shape=(
            jax.ShapeDtypeStruct((tokens, width), BF16),
            jax.ShapeDtypeStruct((blocks, N, width), BF16),
        ),
        grid_spec=pltpu.PrefetchScalarGridSpec(
            num_scalar_prefetch=1,
            grid=(blocks,),
            in_specs=[
                pl.BlockSpec((Q, width), moved),
                pl.BlockSpec((Q, 2 * N), plain),
                pl.BlockSpec((Q, LANES), plain),
                pl.BlockSpec((4, width), fixed),
                pl.BlockSpec((1, width), fixed),
                pl.BlockSpec((1, LANES), fixed),
                pl.BlockSpec((1, width), fixed),
            ],
            out_specs=[
                pl.BlockSpec((Q, width), moved),
                pl.BlockSpec((1, N, width), lambda i, seat: (i, 0, 0)),
            ],
            scratch_shapes=[pltpu.VMEM((N, width), F32), pltpu.VMEM((Q + 8, width), F32)],
        ),
        cost_estimate=pl.CostEstimate(
            flops=tokens * width * 1200, bytes_accessed=tokens * width * 10, transcendentals=tokens * width * 3
        ),
        name="scan_forward",
    )(seat, pre, states_in, steps, taps, bias, rate, skip)


def run_backward(seat, pre, dy, states_in, steps, held, taps, bias, rate, skip, pick, shards, out_width):
    tokens = steps.shape[0]
    width = taps.shape[1]
    blocks = tokens // Q
    per = blocks // shards
    fixed = lambda i, seat: (0, 0)
    plain = lambda i, seat: (blocks - 1 - i, 0)
    moved = lambda i, seat: (chunk_of(blocks - 1 - i, seat, per), 0)

    def before(i, seat):
        chunk = jnp.maximum(blocks - 2 - i, 0)
        return (chunk_of(chunk, seat, per) * (Q // 16) + Q // 16 - 1, 0)

    return pl.pallas_call(
        functools.partial(scan_backward, pairs=width // LANES, blocks=blocks),
        out_shape=(
            jax.ShapeDtypeStruct((tokens, out_width), BF16),
            jax.ShapeDtypeStruct((tokens, 2 * N), BF16),
            jax.ShapeDtypeStruct((tokens, LANES), F32),
            jax.ShapeDtypeStruct((8, width), F32),
            jax.ShapeDtypeStruct((1, LANES), F32),
        ),
        grid_spec=pltpu.PrefetchScalarGridSpec(
            num_scalar_prefetch=1,
            grid=(blocks,),
            in_specs=[
                pl.BlockSpec((Q, width), moved),
                pl.BlockSpec((16, width), before),
                pl.BlockSpec((Q, width), moved),
                pl.BlockSpec((Q, 2 * N), plain),
                pl.BlockSpec((Q, LANES), plain),
                pl.BlockSpec((1, N, width), lambda i, seat: (blocks - 1 - i, 0, 0)),
                pl.BlockSpec((4, width), fixed),
                pl.BlockSpec((1, width), fixed),
                pl.BlockSpec((1, LANES), fixed),
                pl.BlockSpec((1, width), fixed),
                pl.BlockSpec((width, LANES), fixed),
            ],
            out_specs=[
                pl.BlockSpec((Q, out_width), moved),
                pl.BlockSpec((Q, 2 * N), plain),
                pl.BlockSpec((Q, LANES), plain),
                pl.BlockSpec((8, width), fixed),
                pl.BlockSpec((1, LANES), fixed),
            ],
            scratch_shapes=[
                pltpu.VMEM((Q + 16, width), F32),
                pltpu.VMEM((Q + 8, width), F32),
                pltpu.VMEM((N, width), F32),
                pltpu.VMEM((N, width), BF16),
                pltpu.VMEM((Q, Q), F32),
                pltpu.VMEM((Q, LANES), F32),
                pltpu.VMEM((LANES, Q), F32),
                pltpu.VMEM((Q, width), BF16),
                pltpu.VMEM((Q, width), BF16),
                pltpu.VMEM((Q, width), BF16),
                pltpu.VMEM((Q, width), BF16),
                pltpu.VMEM((8, width), F32),
            ],
        ),
        cost_estimate=pl.CostEstimate(
            flops=tokens * width * 3000, bytes_accessed=tokens * width * 14, transcendentals=tokens * width * 4
        ),
        name="scan_backward",
    )(seat, pre, pre, dy, states_in, steps, held, taps, bias, rate, skip, pick)


EPSILON = 1e-05


def swish(v):
    return v * sigmoid(v)


def tn_dot(a, b):
    return lax.dot_general(a, b, (((0,), (0,)), ((), ())), preferred_element_type=F32)


def causal_conv(values, taps, offsets):
    tap_count = taps.shape[0]
    length = values.shape[0]
    padded = jnp.pad(values, ((tap_count - 1, 0), (0, 0)))
    summed = offsets[None, :] + taps[0][None, :] * padded[0:length]
    for offset in range(1, tap_count):
        summed = summed + taps[offset][None, :] * padded[offset : offset + length]
    return summed


def swap(v, bit, axis="col"):
    size = lax.axis_size(axis)
    return lax.ppermute(v, axis, [(i, i ^ bit) for i in range(size)])


def row_sum(v):
    bit = 1
    while bit < lax.axis_size("row"):
        v = v + swap(v, bit, "row")
        bit *= 2
    return v


class Square:
    shards = 4

    def __init__(self):
        self.place = lax.axis_index("col")
        self.x = lax.rem(self.place, 2) == 1
        self.y = lax.div(self.place, 2) == 1
        self.seat = jnp.reshape(self.place, (1,)).astype(jnp.int32)

    def settle(self, v):
        parts = v.reshape((2, 2, v.shape[0] // 4) + v.shape[1:])
        parts = jnp.where(self.y, parts[::-1], parts)
        parts = jnp.where(self.x, parts[:, ::-1], parts)
        return parts.reshape(v.shape)

    def gather(self, v):
        half = v.shape[0] // 2
        from_x = swap(v, 1)
        from_y = swap(v, 2)
        return [v, from_x, from_y, swap(from_x[:half], 2), swap(from_y[half:], 1)]

    def gather_flat(self, v):
        return self.settle(jnp.concatenate(self.gather(v)))

    def token_sum(self, v):
        parts = v.reshape(2, 2, -1)
        parts = parts + swap(parts, 1)[:, ::-1]
        parts = parts + swap(parts, 2)[::-1]
        return parts.reshape(v.shape)

    def total(self, v):
        v = v + swap(v, 1)
        return v + swap(v, 2)

    def scatter(self, piece_of):
        far = piece_of(3).astype(BF16)
        half = far.shape[0] // 2
        beside = piece_of(1)
        above = piece_of(2)
        across_x = swap(far[:half], 1).astype(F32)
        across_y = swap(far[half:], 2).astype(F32)
        x_top = swap(beside[:half].astype(BF16), 1)
        y_low = swap(above[half:].astype(BF16), 2)
        own = piece_of(0)
        x_low = swap((beside[half:] + across_y).astype(BF16), 1)
        y_top = swap((above[:half] + across_x).astype(BF16), 2)
        top = own[:half] + x_top.astype(F32) + y_top.astype(F32)
        low = own[half:] + x_low.astype(F32) + y_low.astype(F32)
        return jnp.concatenate([top, low])

    def gather_states(self, s):
        pair = jnp.concatenate([s, swap(s, 1)], axis=1)
        other = swap(pair, 2)
        return jnp.concatenate([jnp.where(self.y, other, pair), jnp.where(self.y, pair, other)], axis=1)

    def scatter_states(self, d):
        first, second = d[:, :N], d[:, N:]
        kept = jnp.where(self.y, second, first).astype(F32)
        kept = kept + swap(jnp.where(self.y, first, second), 2).astype(F32)
        half = N // 2
        return kept[:, :half] + swap(kept[:, half:].astype(BF16), 1).astype(F32)

    def own_slice(self, v):
        width = v.shape[0] // 4
        return lax.dynamic_slice(v, (self.place * width,), (width,))


class Line:
    shards = 1

    def __init__(self):
        self.seat = jnp.zeros((1,), jnp.int32)

    def settle(self, v):
        return v

    def gather(self, v):
        return [lax.all_gather(v, "col", axis=0, tiled=True)]

    def gather_flat(self, v):
        return lax.all_gather(v, "col", axis=0, tiled=True)

    def token_sum(self, v):
        return lax.psum(v, "col")

    def total(self, v):
        return lax.psum(v, "col")

    def scatter(self, piece_of):
        return lax.psum_scatter(
            piece_of(None).astype(BF16), "col", scatter_dimension=0, tiled=True
        ).astype(F32)

    def gather_states(self, s):
        return lax.all_gather(s, "col", axis=1, tiled=True)

    def scatter_states(self, d):
        return lax.psum_scatter(d.astype(BF16), "col", scatter_dimension=1, tiled=True).astype(F32)

    def own_slice(self, v):
        width = v.shape[0] // lax.axis_size("col")
        return lax.dynamic_slice(v, (lax.axis_index("col") * width,), (width,))


def widened(v, width):
    return v if v.shape[-1] == width else jnp.pad(v, [(0, 0)] * (v.ndim - 1) + [(0, width - v.shape[-1])])


def row_scatter(v):
    return lax.psum_scatter(v.astype(BF16), "row", scatter_dimension=0, tiled=True).astype(F32)


def body(
    hidden,
    in_gain,
    w_gate,
    w_value,
    w_bc,
    w_step,
    conv_value,
    conv_value_bias,
    conv_bc,
    conv_bc_bias,
    step_bias,
    decay_log,
    skip_gain,
    norm_gain,
    w_out,
    grad_out,
):
    lines = Square() if lax.axis_size("col") == 4 else Line()
    heads = step_bias.shape[0]
    channels = w_value.shape[1]
    inner_width = lax.axis_size("col") * channels
    bc_width = w_bc.shape[1]
    wide = -(-channels // LANES) * LANES
    full_width = wide + LANES
    step_at = wide + bc_width
    piece_rows = hidden.shape[0]

    def rows_of(v, piece):
        return v if piece is None else v[piece * piece_rows : (piece + 1) * piece_rows]

    w_cat = lax.all_gather(
        widened(jnp.concatenate([widened(w_value, wide), w_bc, w_step], axis=1), full_width),
        "row", axis=0, tiled=True,
    )
    w_gate_full = lax.all_gather(w_gate, "row", axis=0, tiled=True)
    w_out_t = lax.all_gather(w_out.T, "row", axis=0, tiled=True)
    full_gain = lines.gather_flat(in_gain).astype(F32)

    def normalized(rows):
        rows = rows.astype(F32)
        scale = lax.rsqrt(jnp.mean(rows * rows, axis=1, keepdims=True) + EPSILON)
        return (rows * scale * full_gain).astype(BF16)

    normal_in = jnp.concatenate([normalized(piece) for piece in lines.gather(hidden)])
    grad_full = jnp.concatenate(lines.gather(grad_out))

    pre = mm(normal_in, w_cat)
    bc_pre = lines.settle(pre[:, wide : wide + bc_width])
    step_sum = lines.settle(pre[:, step_at : step_at + heads]) + step_bias

    def state_branch(pre_vals, conv_weight, conv_offset):
        return swish(causal_conv(pre_vals, conv_weight, conv_offset))

    state_local, state_back = jax.vjp(state_branch, bc_pre, conv_bc, conv_bc_bias)
    states = lines.gather_states(state_local.astype(BF16))
    steps = widened(jax.nn.softplus(step_sum), LANES)
    rate = widened(-jnp.exp(decay_log), LANES)[None]
    skip = widened(jnp.repeat(skip_gain, P_SIZE), wide)[None]
    taps = widened(conv_value, wide)
    offsets = widened(conv_value_bias, wide)[None]
    pick = (jnp.arange(wide)[:, None] // P_SIZE == jnp.arange(LANES)[None]).astype(BF16)
    heads_out, held = run_forward(lines.seat, pre, states, steps, taps, offsets, rate, skip, lines.shards)

    gate_pre = mm(normal_in, w_gate_full).astype(BF16)
    ho = heads_out[:, :channels].astype(F32)
    gate = gate_pre.astype(F32)
    gated = ho * swish(gate)
    squares = lines.token_sum(jnp.sum(gated * gated, axis=1))
    mix = lax.rsqrt(squares / inner_width + EPSILON)[:, None]
    normed = (gated * mix * norm_gain).astype(BF16)

    branch_out = lines.scatter(lambda piece: nt_dot(rows_of(normed, piece), w_out_t))
    result = (hidden.astype(F32) + branch_out).astype(BF16)

    d_normed = mm(grad_full, w_out_t).astype(BF16).astype(F32)
    scaled = d_normed * norm_gain
    dots = lines.token_sum(jnp.sum(gated * scaled, axis=1))[:, None]
    g_out_t = row_scatter(tn_dot(grad_full, normed))
    d_gated = mix * scaled - gated * (mix * mix * mix * dots / inner_width)
    g_norm_gain = jnp.sum(d_normed * gated * mix, axis=0)
    open_gate = sigmoid(gate)
    d_heads = (d_gated * gate * open_gate).astype(BF16)
    d_gate = (d_gated * ho * (open_gate * (1.0 + gate * (1.0 - open_gate)))).astype(BF16)
    g_gate_part = tn_dot(normal_in, d_gate).astype(BF16)
    g_gate = row_scatter(g_gate_part)

    d_cat, d_states, d_steps, g_conv, g_decay = run_backward(
        lines.seat, pre, widened(d_heads, wide), states, steps, held, taps, offsets, rate, skip, pick,
        lines.shards, full_width,
    )
    d_bc_pre, g_conv_bc, g_conv_bc_bias = state_back(lines.scatter_states(d_states))
    d_step = d_steps[:, :heads] * sigmoid(step_sum)
    small = lines.settle(widened(jnp.concatenate([d_bc_pre, d_step], axis=1), LANES)).astype(BF16)
    d_cat = lax.dynamic_update_slice(d_cat, small, (0, wide))
    g_cat_part = tn_dot(normal_in, d_cat).astype(BF16)
    g_cat = row_scatter(g_cat_part)

    d_rows = lines.scatter(
        lambda piece: nt_dot(rows_of(d_gate, piece), w_gate_full) + nt_dot(rows_of(d_cat, piece), w_cat)
    )
    tokens = hidden.astype(F32)
    scale = lax.rsqrt(jnp.mean(tokens * tokens, axis=1, keepdims=True) + EPSILON)
    scaled_rows = d_rows * full_gain
    grad_hidden = grad_out.astype(F32) + scale * (
        scaled_rows - tokens * (scale * scale * jnp.mean(tokens * scaled_rows, axis=1, keepdims=True))
    )

    g_in_gain = (
        jnp.sum(w_gate_full.astype(F32) * g_gate_part.astype(F32), axis=1)
        + jnp.sum(w_cat.astype(F32) * g_cat_part.astype(F32), axis=1)
    ) / full_gain
    g_in_gain = row_sum(lines.own_slice(lines.total(g_in_gain)))
    parts = (
        g_conv[:4, :channels],
        g_conv[4, :channels],
        g_conv_bc,
        g_conv_bc_bias,
        jnp.sum(d_step, axis=0),
        (g_decay * rate)[0, :heads],
        jnp.sum(g_conv[5, :channels].reshape(heads, P_SIZE), axis=1),
        g_norm_gain,
    )
    packed = row_sum(jnp.concatenate([part.reshape(-1) for part in parts]))
    summed = []
    at = 0
    for part in parts:
        summed.append(packed[at : at + part.size].reshape(part.shape))
        at += part.size
    return (
        result,
        grad_hidden,
        g_in_gain,
        g_gate,
        g_cat[:, :channels],
        g_cat[:, wide : wide + bc_width],
        g_cat[:, step_at : step_at + heads],
        *summed,
        g_out_t.T,
    )


def solution(mesh):
    over_tokens = P(("row", "col"), None)
    square = P("row", "col")
    across = P(None, "col")
    vector = P("col")
    return jax.shard_map(
        body,
        mesh=mesh,
        in_specs=(
            over_tokens, vector, square, square, square, square, across, vector, across, vector,
            vector, vector, vector, vector, P("col", "row"), over_tokens,
        ),
        out_specs=(
            over_tokens, over_tokens, vector, square, square, square, square, across, vector, across,
            vector, vector, vector, vector, vector, P("col", "row"),
        ),
        check_vma=False,
    )
```

time: 2470 us -> 880 us (0.36); the launches traced: 2430 us -> 868 us
  local copies, waits for them, and re-layouts: 942 us -> 121 us
  matrix products: 668 us -> 219 us
  other arithmetic: 347 us -> 71.2 us
  Pallas kernels: 0 us -> 123 us
  blocking collectives: 96.7 us -> 0 us
  waiting for transfers between devices: 359 us -> 273 us
  starting transfers between devices: 1.92 us -> 46 us
    dynamic_update_slice x40 -> x1, local copies, waits for them, and re-layouts: 515 us -> 0.85 us  [body(): d_cat = lax.dynamic_update_slice(d_cat, small, (0, wide))]
    dot_general x127 -> x18, matrix products: 668 us -> 219 us  [the longest x12 89.9 us: nt_dot(): lax.dot_general(a, b, (((1,), (1,)), ((), ())), preferred_element_type=F32)]
    ppermute x0 -> x40, waiting for transfers between devices: none -> 272 us  [swap(): return lax.ppermute(v, axis, [(i, i ^ bit) for i in range(size)])]
    reduce_scatter x5 -> x1, waiting for transfers between devices: 242 us -> 0.01 us  [row_scatter(): lax.psum_scatter(v.astype(BF16), 'row', scatter_dimension=0, tiled=True)]
    pallas_call x0 -> x2, Pallas kernels: none -> 123 us  [the longest x1 88.1 us: run_backward(): pl.pallas_call(functools.partial(scan_backward, pairs=width // LANES, blo...]
    all_gather x6 -> x3, waiting for transfers between devices: 114 us -> 0.02 us  [the longest x1 0.02 us: body(): w_out_t = lax.all_gather(w_out.T, 'row', axis=0, tiled=True)]
    another operation x90 -> x0, other arithmetic: 97.8 us -> none
    another operation x124 -> x2, local copies, waits for them, and re-layouts: 90.2 us -> 0.75 us  [the longest x1 0.68 us: body(): skip = widened(jnp.repeat(skip_gain, P_SIZE), wide)[None]]
  transfers between devices with their start and end apart: 15 -> 46, of which waited for: 5 -> 14; matrix products, arithmetic and copies ran while one was open for 36% -> 37% of each run, Pallas kernels for 0% -> 14%
where the time goes in v1:
time: 880 us; the launch traced here: 868 us
  waiting for transfers between devices  273 us (31%)
  matrix products  219 us (25%)
  Pallas kernels  123 us (14%)
  local copies, waits for them, and re-layouts  121 us (14%)
  other arithmetic  71.2 us (8%)
  starting transfers between devices  46 us (5%)
  between operations  15.6 us (2%)
    ppermute x40, waiting for transfers between devices, swap(): return lax.ppermute(v, axis, [(i, i ^ bit) for i in range(size)])  272 us
    dot_general x12, matrix products, nt_dot(): lax.dot_general(a, b, (((1,), (1,)), ((), ())), preferred_element_type=F32)  89.9 us
    pallas_call x1, Pallas kernels, run_backward(): pl.pallas_call(functools.partial(scan_backward, pairs=width // LANES, blo...  88.1 us
    dot_general x3, matrix products, mm(): return jnp.dot(a, b, preferred_element_type=F32)  65.7 us
    dot_general x3, matrix products, tn_dot(): lax.dot_general(a, b, (((0,), (0,)), ((), ())), preferred_element_type=F32)  63.4 us
    unnamed x138, local copies, waits for them, and re-layouts  50.5 us
    ppermute x40, starting transfers between devices, swap(): return lax.ppermute(v, axis, [(i, i ^ bit) for i in range(size)])  45.7 us
    pallas_call x1, Pallas kernels, run_forward(): pl.pallas_call(functools.partial(scan_forward, pairs=width // LANES), out...  34.7 us
  transfers between devices with their start and end apart: 46, of which 14 were waited for; matrix products, arithmetic and copies ran while one was open for 37% of the time, Pallas kernels for 14%

profile of v1, /device:TPU:0, one launch (start us, length us, event | category | flops | bytes accessed | tf_op | source)
XLA Modules:
  0.0 868.0 jit_solution(12369538145904890750)
XLA Ops:
  25.0 104.8 %collective-permute-done = bf16[640]{0:T(1024)(128)(2,1)S(1)} collective-permute-done((bf16[640]{0:T(1024)(128)(2,1)S(1)}, bf16[640]{0:T(1024)(128)(2,1)S(1)}, u32[]{:S(2)}, u32[]{:S(2)}) %collective-permute-start) | collective-permute-done | bytes 1312 | tf_op jit(solution)/shard_map/ppermute | solution.py:354
  182.7 20.0 %fusion.82 = f32[2048,1408]{0,1:T(8,128)S(1)} fusion(bf16[2048,2560]{1,0:T(8,128)(2,1)} %fusion.55, bf16[2560,1408]{1,0:T(8,128)(2,1)} %all-gather.4.cloned.1.call-done), kind=kOutput, calls=%fused_computation.202 | convolution fusion | flops 14763950080 | bytes 29229056 | tf_op jit(solution)/shard_map/dot_general | solution.py:28
  213.6 6.3 collective-permute-done.8
  221.4 12.3 %copy.50.vp_ref.before_ref = f32[2048,1408]{1,0:T(8,128)} copy(f32[2048,1408]{0,1:T(8,128)} %copy-done.4) | data formatting | bytes 23068672 | tf_op jit(solution)/shard_map/dot_general | solution.py:28
  237.9 34.7 %scan_forward.1 = (bf16[2048,1280]{1,0:T(8,128)(2,1)}, bf16[16,128,1280]{2,1,0:T(8,128)(2,1)}) custom-call(s32[1]{0:T(128)} %bitcast.seat_ref, f32[2048,1408]{1,0:T(8,128)} %copy.50.vp_ref.before_ref, bf16[2048,256]{1,0:T(8,128)(2,1)} %pad_maximum_fusion.bc_ref, f32[2048,128]{1,0:T(8,128)} %pad.51.st_ref, f32[4,1280]{1,0:T(4,128)} %taps_ref.3, ...), custom_call_target="tpu_custom_call" | custom-call | flops 3145728000 | bytes 26214400 | tf_op jit(solution)/shard_map/scan_forward/pallas_call | solution.py:233
  272.6 21.5 %multiply_reduce_fusion.2 = (f32[2048]{0:T(1024)S(1)}, bf16[2048,1280]{1,0:T(8,128)(2,1)}) fusion(bf16[2048,1280]{1,0:T(8,128)(2,1)} %get-tuple-element.23, bf16[2048,2560]{1,0:T(8,128)(2,1)} %fusion.55, bf16[2560,1280]{1,0:T(8,128)(2,1)} %all-gather.6.cloned.1.call-done), kind=kOutput, calls=%fused_computation.30 | convolution fusion | flops 13447985152 | bytes 27533312 | tf_op jit(solution)/shard_map/dot_general | solution.py:28
  302.4 24.2 %fusion.7 = (f32[1280]{0:T(1024)S(1)}, f32[2048]{0:T(1024)S(1)}, bf16[2048,1280]{1,0:T(8,128)(2,1)}) fusion(f32[2048]{0:T(1024)S(1)} %bitcast.90, bf16[2048,1280]{1,0:T(8,128)(2,1)} %get-tuple-element.105, bf16[2048,1280]{1,0:T(8,128)(2,1)} %get-tuple-element.23, f32[1280]{0:T(1024)S(1)} %copy-done.24, ...), kind=kOutput, calls=%fused_computation.20 | convolution fusion | flops 13461091328 | bytes 32794624 | tf_op jit(solution)/shard_map/dot_general | solution.py:28
  332.0 9.5 %copy.54 = bf16[2560,1280]{0,1:T(8,128)(2,1)} copy(bf16[2560,1280]{1,0:T(8,128)(2,1)} %all-gather.6.cloned.1.call-done) | data formatting | bytes 13107200 | tf_op jit(solution)/shard_map/all_gather | solution.py:512
  341.5 16.4 %fusion.5 = (bf16[2048,1280]{1,0:T(8,128)(2,1)}, bf16[2048,1280]{1,0:T(8,128)(2,1)}, bf16[2048,1280]{1,0:T(8,128)(2,1)}) fusion(bf16[2048,1280]{1,0:T(8,128)(2,1)} %get-tuple-element.23, bf16[2048,1280]{1,0:T(8,128)(2,1)} %get-tuple-element.105, bf16[2048,1280]{1,0:T(8,128)(2,1)} %get-tuple-element.106, f32[2048]{0:T(1024)S(1)} %fusion.71, ...), kind=kLoop, calls=%fused_computation.18 | loop fusion | flops 65536000 | bytes 31478784 | tf_op jit(solution)/shard_map/convert_element_type | solution.py:560
  357.9 20.4 %multiply_reduce_fusion.1 = (f32[2560]{0:T(1024)S(1)}, bf16[2560,1280]{0,1:T(8,128)(2,1)}) fusion(bf16[2560,1280]{0,1:T(8,128)(2,1)S(1)} %copy-done.8, bf16[2048,2560]{1,0:T(8,128)(2,1)} %fusion.55, bf16[2048,1280]{1,0:T(8,128)(2,1)} %get-tuple-element.76), kind=kOutput, calls=%fused_computation.5 | convolution fusion | flops 13438154752 | bytes 28846080 | tf_op jit(solution)/shard_map/dot_general | solution.py:339
  378.3 9.4 %copy.59 = bf16[2560,1280]{1,0:T(8,128)(2,1)} copy(bf16[2560,1280]{0,1:T(8,128)(2,1)} %get-tuple-element.108) | data formatting | bytes 13107200
  387.8 20.1 %convolution_convert_fusion.1 = bf16[2560,1280]{1,0:T(8,128)(2,1)} fusion(bf16[2048,2560]{1,0:T(8,128)(2,1)} %constant_dynamic-update-slice_fusion, bf16[2048,1280]{1,0:T(8,128)(2,1)} %get-tuple-element.78), kind=kOutput, calls=%fused_computation.13 | convolution fusion | flops 13425049600 | bytes 22282240 | tf_op jit(solution)/shard_map/dot_general | solution.py:339
  409.0 10.4 %copy.55 = bf16[2560,1408]{0,1:T(8,128)(2,1)} copy(bf16[2560,1408]{1,0:T(8,128)(2,1)} %all-gather.4.cloned.1.call-done) | data formatting | bytes 14417920 | tf_op jit(solution)/shard_map/all_gather | solution.py:508
  419.4 88.1 %scan_backward.1 = (bf16[2048,1408]{1,0:T(8,128)(2,1)}, bf16[2048,256]{1,0:T(8,128)(2,1)}, f32[2048,128]{1,0:T(8,128)}, f32[8,1280]{1,0:T(8,128)}, f32[1,128]{1,0:T(1,128)}) custom-call(s32[1]{0:T(128)} %bitcast.seat_ref, f32[2048,1408]{1,0:T(8,128)} %copy.50.vp_ref.before_ref, f32[2048,1408]{1,0:T(8,128)} %copy.50.vp_ref.before_ref, ...), custom_call_target="tpu_custom_call" | custom-call | flops 7864320000 | bytes 36700160 | tf_op jit(solution)/shard_map/scan_backward/pallas_call | solution.py:277
  510.9 6.9 convolution_convert_fusion.5
  522.1 6.7 fusion.64
  536.4 5.5 fusion.66
  549.3 29.3 %collective-permute-done.25 = bf16[2048,64]{1,0:T(8,128)(2,1)S(1)} collective-permute-done((bf16[2048,64]{1,0:T(8,128)(2,1)S(1)}, bf16[2048,64]{1,0:T(8,128)(2,1)S(1)}, u32[]{:S(2)}, u32[]{:S(2)}) %collective-permute-start.25) | collective-permute-done | bytes 262176 | tf_op jit(solution)/shard_map/ppermute | solution.py:354
  582.3 22.9 %multiply_reduce_fusion = (f32[2560]{0:T(1024)S(1)}, bf16[2560,1408]{0,1:T(8,128)(2,1)}) fusion(bf16[2560,1408]{0,1:T(8,128)(2,1)} %copy.55, bf16[2048,2560]{1,0:T(8,128)(2,1)} %fusion.55, bf16[2048,1408]{1,0:T(8,128)(2,1)} %constant_dynamic-update-slice_fusion.5), kind=kOutput, calls=%fused_computation.4 | convolution fusion | flops 14781970432 | bytes 30681088 | tf_op jit(solution)/shard_map/dot_general | solution.py:339
  605.6 10.4 %copy.61 = bf16[2560,1408]{1,0:T(8,128)(2,1)} copy(bf16[2560,1408]{0,1:T(8,128)(2,1)} %get-tuple-element.110) | data formatting | bytes 14417920
  616.0 10.2 %fusion.51 = f32[512,2560]{1,0:T(8,128)} fusion(bf16[2560,1408]{1,0:T(8,128)(2,1)} %all-gather.4.cloned.1.call-done, bf16[2048,1408]{1,0:T(8,128)(2,1)} %constant_dynamic-update-slice_fusion.5), kind=kOutput, calls=%fused_computation.107 | convolution fusion | flops 3690987520 | bytes 13893632 | tf_op jit(solution)/shard_map/dot_general | solution.py:24
  626.2 10.8 %convolution_add_fusion.1 = f32[512,2560]{1,0:T(8,128)} fusion(f32[512,2560]{1,0:T(8,128)} %fusion.51, bf16[2560,1280]{1,0:T(8,128)(2,1)} %all-gather.6.cloned.1.call-done, bf16[2048,1280]{1,0:T(8,128)(2,1)} %get-tuple-element.76), kind=kOutput, calls=%fused_computation.59 | convolution fusion | flops 3356753920 | bytes 18350080 | tf_op jit(solution)/shard_map/dot_general | solution.py:24
  637.1 7.5 fusion.47
  644.7 6.7 add_convert_fusion
  651.4 7.4 fusion.49
  660.4 7.1 convolution_add_fusion
  667.7 7.3 fusion.53
  677.2 8.2 convolution_add_fusion.2
  703.4 47.8 %collective-permute-done.29 = bf16[256,2560]{1,0:T(8,128)(2,1)S(1)} collective-permute-done((bf16[256,2560]{1,0:T(8,128)(2,1)S(1)}, bf16[256,2560]{1,0:T(8,128)(2,1)S(1)}, u32[]{:S(2)}, u32[]{:S(2)}) %collective-permute-start.29) | collective-permute-done | bytes 1310752 | tf_op jit(solution)/shard_map/ppermute | solution.py:354
  759.8 23.4 %collective-permute-done.14 = bf16[256,2560]{1,0:T(8,128)(2,1)} collective-permute-done((bf16[256,2560]{1,0:T(8,128)(2,1)}, bf16[256,2560]{1,0:T(8,128)(2,1)}, u32[]{:S(2)}, u32[]{:S(2)}) %collective-permute-start.14) | collective-permute-done | bytes 1310752 | tf_op jit(solution)/shard_map/ppermute | solution.py:354
  788.2 23.0 %collective-permute-done.31 = bf16[256,2560]{1,0:T(8,128)(2,1)} collective-permute-done((bf16[256,2560]{1,0:T(8,128)(2,1)}, bf16[256,2560]{1,0:T(8,128)(2,1)}, u32[]{:S(2)}, u32[]{:S(2)}) %collective-permute-start.31) | collective-permute-done | bytes 1310752 | tf_op jit(solution)/shard_map/ppermute | solution.py:354
  811.2 25.4 %collective-permute-done.28 = bf16[256,2560]{1,0:T(8,128)(2,1)} collective-permute-done((bf16[256,2560]{1,0:T(8,128)(2,1)S(1)}, bf16[256,2560]{1,0:T(8,128)(2,1)}, u32[]{:S(2)}, u32[]{:S(2)}) %collective-permute-start.28) | collective-permute-done | bytes 1310752 | tf_op jit(solution)/shard_map/ppermute | solution.py:354
  (354 shorter events, 187.5 us)
Async XLA Ops:
  7.2 175.5 %all-gather.4.cloned.1.call-start = ((), (), s32[]{:S(2)}) async-start(), calls=%async_computation.3 | async-start | bytes 8110080 | tf_op jit(solution)/shard_map/all_gather | solution.py:508
  12.8 259.9 %all-gather.6.cloned.1.call-start = ((), (), s32[]{:S(2)}) async-start(), calls=%async_computation.4 | async-start | bytes 7372800 | tf_op jit(solution)/shard_map/all_gather | solution.py:512
  13.5 288.9 %all-gather.8.cloned.1.call-start = ((), (), s32[]{:S(2)}) async-start(), calls=%async_computation.5 | async-start | bytes 7372800 | tf_op jit(solution)/shard_map/all_gather | solution.py:513
  13.6 129.5 %collective-permute-start.4 = (bf16[512,2560]{1,0:T(8,128)(2,1)S(1)}, bf16[512,2560]{1,0:T(8,128)(2,1)}, u32[]{:S(2)}, u32[]{:S(2)}) collective-permute-start(bf16[512,2560]{1,0:T(8,128)(2,1)S(1)} %copy-done), channel_id=1, source_target_pairs={{0,1},{1,0},{2,3},{3,2},{4,5},{5,4},{6,7},{7,6},{8,9},{9,8},{10,11... | collective-permute-start | bytes 7864328 | tf_op jit(solution)/shard_map/ppermute | solution.py:354
  16.6 129.7 %collective-permute-start.5 = (bf16[512,2560]{1,0:T(8,128)(2,1)S(1)}, bf16[512,2560]{1,0:T(8,128)(2,1)}, u32[]{:S(2)}, u32[]{:S(2)}) collective-permute-start(bf16[512,2560]{1,0:T(8,128)(2,1)S(1)} %copy-done), channel_id=1, source_target_pairs={{0,2},{1,3},{2,0},{3,1},{4,6},{5,7},{6,4},{7,5},{8,10},{9,11},{10,... | collective-permute-start | bytes 7864328 | tf_op jit(solution)/shard_map/ppermute | solution.py:354
  18.1 131.2 %collective-permute-start.18 = (bf16[512,2560]{1,0:T(8,128)(2,1)}, bf16[512,2560]{1,0:T(8,128)(2,1)}, u32[]{:S(2)}, u32[]{:S(2)}) collective-permute-start(bf16[512,2560]{1,0:T(8,128)(2,1)} %param.31), channel_id=1, source_target_pairs={{0,1},{1,0},{2,3},{3,2},{4,5},{5,4},{6,7},{7,6},{8,9},{9,8},{10,11... | collective-permute-start | bytes 7864328 | tf_op jit(solution)/shard_map/ppermute | solution.py:354
  18.7 136.0 %collective-permute-start.19 = (bf16[512,2560]{1,0:T(8,128)(2,1)}, bf16[512,2560]{1,0:T(8,128)(2,1)}, u32[]{:S(2)}, u32[]{:S(2)}) collective-permute-start(bf16[512,2560]{1,0:T(8,128)(2,1)} %param.31), channel_id=1, source_target_pairs={{0,2},{1,3},{2,0},{3,1},{4,6},{5,7},{6,4},{7,5},{8,10},{9,11},{10,... | collective-permute-start | bytes 7864328 | tf_op jit(solution)/shard_map/ppermute | solution.py:354
  18.7 111.1 %collective-permute-start = (bf16[640]{0:T(1024)(128)(2,1)S(1)}, bf16[640]{0:T(1024)(128)(2,1)S(1)}, u32[]{:S(2)}, u32[]{:S(2)}) collective-permute-start(bf16[640]{0:T(1024)(128)(2,1)S(1)} %copy-done.35), channel_id=1, source_target_pairs={{0,1},{1,0},{2,3},{3,2},{4,5},{5,4},{6,7},{7,6},{8,9},{9,8},{10,11... | collective-permute-start | bytes 3848 | tf_op jit(solution)/shard_map/ppermute | solution.py:354
  20.7 825.3 %reduce-scatter.10.cloned.1.call-start = ((), (), s32[]{:S(2)}) async-start(), calls=%async_computation.7 | async-start | bytes 7372800
  144.5 31.7 %collective-permute-start.6 = (bf16[256,2560]{1,0:T(8,128)(2,1)S(1)}, bf16[256,2560]{1,0:T(8,128)(2,1)S(1)}, u32[]{:S(2)}, u32[]{:S(2)}) collective-permute-start(bf16[256,2560]{1,0:T(8,128)(2,1)S(1)} %slice.259), channel_id=1, source_target_pairs={{0,2},{1,3},{2,0},{3,1},{4,6},{5,7},{6,4},{7,5},{8,10},{9,11},{10,... | collective-permute-start | bytes 3932168 | tf_op jit(solution)/shard_map/ppermute | solution.py:354
  147.7 31.7 %collective-permute-start.7 = (bf16[256,2560]{1,0:T(8,128)(2,1)S(1)}, bf16[256,2560]{1,0:T(8,128)(2,1)S(1)}, u32[]{:S(2)}, u32[]{:S(2)}) collective-permute-start(bf16[256,2560]{1,0:T(8,128)(2,1)S(1)} %slice.260), channel_id=1, source_target_pairs={{0,1},{1,0},{2,3},{3,2},{4,5},{5,4},{6,7},{7,6},{8,9},{9,8},{10,11... | collective-permute-start | bytes 3932168 | tf_op jit(solution)/shard_map/ppermute | solution.py:354
  151.7 144.2 %collective-permute-start.20 = (bf16[256,2560]{1,0:T(8,128)(2,1)}, bf16[256,2560]{1,0:T(8,128)(2,1)}, u32[]{:S(2)}, u32[]{:S(2)}) collective-permute-start(bf16[256,2560]{1,0:T(8,128)(2,1)} %slice.275), channel_id=1, source_target_pairs={{0,2},{1,3},{2,0},{3,1},{4,6},{5,7},{6,4},{7,5},{8,10},{9,11},{10,... | collective-permute-start | bytes 3932168 | tf_op jit(solution)/shard_map/ppermute | solution.py:354
  157.1 143.1 %collective-permute-start.21 = (bf16[256,2560]{1,0:T(8,128)(2,1)}, bf16[256,2560]{1,0:T(8,128)(2,1)S(1)}, u32[]{:S(2)}, u32[]{:S(2)}) collective-permute-start(bf16[256,2560]{1,0:T(8,128)(2,1)} %slice.276), channel_id=1, source_target_pairs={{0,1},{1,0},{2,3},{3,2},{4,5},{5,4},{6,7},{7,6},{8,9},{9,8},{10,11... | collective-permute-start | bytes 3932168 | tf_op jit(solution)/shard_map/ppermute | solution.py:354
  221.0 14.4 %collective-permute-start.9 = (bf16[2048,128]{1,0:T(8,128)(2,1)}, bf16[2048,128]{1,0:T(8,128)(2,1)}, u32[]{:S(2)}, u32[]{:S(2)}) collective-permute-start(bf16[2048,128]{1,0:T(8,128)(2,1)} %pad_maximum_fusion.1), channel_id=1, source_target_pairs={{0,2},{1,3},{2,0},{3,1},{4,6},{5,7},{6,4},{7,5},{8,10},{9,11},{10,... | collective-permute-start | bytes 1572872 | tf_op jit(solution)/shard_map/ppermute | solution.py:354
  387.8 461.3 %reduce-scatter.8.cloned.1.call-start = ((), (), s32[]{:S(2)}) async-start(), calls=%async_computation.6 | async-start | bytes 7372800 | tf_op jit(solution)/shard_map/reduce_scatter | solution.py:474
  408.0 443.5 %reduce-scatter.12.cloned.1.call-start = ((), (), s32[]{:S(2)}) async-start(), calls=%async_computation.8 | async-start | bytes 8110080
  509.5 36.8 %collective-permute-start.24 = (bf16[2048,128]{1,0:T(8,128)(2,1)}, bf16[2048,128]{1,0:T(8,128)(2,1)}, u32[]{:S(2)}, u32[]{:S(2)}) collective-permute-start(bf16[2048,128]{1,0:T(8,128)(2,1)} %broadcast_select_fusion), channel_id=1, source_target_pairs={{0,2},{1,3},{2,0},{3,1},{4,6},{5,7},{6,4},{7,5},{8,10},{9,11},{10,... | collective-permute-start | bytes 1572872 | tf_op jit(solution)/shard_map/ppermute | solution.py:354
  519.4 176.4 %collective-permute-start.15 = (bf16[256,2560]{1,0:T(8,128)(2,1)}, bf16[256,2560]{1,0:T(8,128)(2,1)}, u32[]{:S(2)}, u32[]{:S(2)}) collective-permute-start(bf16[256,2560]{1,0:T(8,128)(2,1)} %get-tuple-element.88), channel_id=1, source_target_pairs={{0,2},{1,3},{2,0},{3,1},{4,6},{5,7},{6,4},{7,5},{8,10},{9,11},{10,... | collective-permute-start | bytes 3932168 | tf_op jit(solution)/shard_map/ppermute | solution.py:354
  521.0 179.2 %collective-permute-start.13 = (bf16[256,2560]{1,0:T(8,128)(2,1)}, bf16[256,2560]{1,0:T(8,128)(2,1)}, u32[]{:S(2)}, u32[]{:S(2)}) collective-permute-start(bf16[256,2560]{1,0:T(8,128)(2,1)} %get-tuple-element.87), channel_id=1, source_target_pairs={{0,1},{1,0},{2,3},{3,2},{4,5},{5,4},{6,7},{7,6},{8,9},{9,8},{10,11... | collective-permute-start | bytes 3932168 | tf_op jit(solution)/shard_map/ppermute | solution.py:354
  530.1 224.0 %collective-permute-start.12 = (bf16[256,2560]{1,0:T(8,128)(2,1)}, bf16[256,2560]{1,0:T(8,128)(2,1)}, u32[]{:S(2)}, u32[]{:S(2)}) collective-permute-start(bf16[256,2560]{1,0:T(8,128)(2,1)} %slice.389), channel_id=1, source_target_pairs={{0,1},{1,0},{2,3},{3,2},{4,5},{5,4},{6,7},{7,6},{8,9},{9,8},{10,11... | collective-permute-start | bytes 3932168 | tf_op jit(solution)/shard_map/ppermute | solution.py:354
  547.8 30.9 %collective-permute-start.25 = (bf16[2048,64]{1,0:T(8,128)(2,1)S(1)}, bf16[2048,64]{1,0:T(8,128)(2,1)S(1)}, u32[]{:S(2)}, u32[]{:S(2)}) collective-permute-start(bf16[2048,64]{1,0:T(8,128)(2,1)S(1)} %slice.390), channel_id=1, source_target_pairs={{0,1},{1,0},{2,3},{3,2},{4,5},{5,4},{6,7},{7,6},{8,9},{9,8},{10,11... | collective-permute-start | bytes 786440 | tf_op jit(solution)/shard_map/ppermute | solution.py:354
  580.1 95.6 %collective-permute-start.37 = (f32[8060]{0:T(1024)S(1)}, f32[8060]{0:T(1024)S(1)}, u32[]{:S(2)}, u32[]{:S(2)}) collective-permute-start(f32[8060]{0:T(1024)S(1)} %concatenate.39), channel_id=1, source_target_pairs={{0,4},{4,0},{8,12},{12,8},{16,20},{20,16},{24,28},{28,24},{1,5},{5... | collective-permute-start | bytes 96728 | tf_op jit(solution)/shard_map/ppermute | solution.py:354
  605.2 53.5 %collective-permute-start.32 = (f32[2560]{0:T(1024)S(1)}, f32[2560]{0:T(1024)S(1)}, u32[]{:S(2)}, u32[]{:S(2)}) collective-permute-start(f32[2560]{0:T(1024)S(1)} %add_divide_fusion), channel_id=1, source_target_pairs={{0,1},{1,0},{2,3},{3,2},{4,5},{5,4},{6,7},{7,6},{8,9},{9,8},{10,11... | collective-permute-start | bytes 30728 | tf_op jit(solution)/shard_map/ppermute | solution.py:354
  693.2 62.4 %collective-permute-start.17 = (bf16[256,2560]{1,0:T(8,128)(2,1)S(1)}, bf16[256,2560]{1,0:T(8,128)(2,1)S(1)}, u32[]{:S(2)}, u32[]{:S(2)}) collective-permute-start(bf16[256,2560]{1,0:T(8,128)(2,1)S(1)} %copy-done.13), channel_id=1, source_target_pairs={{0,2},{1,3},{2,0},{3,1},{4,6},{5,7},{6,4},{7,5},{8,10},{9,11},{10,... | collective-permute-start | bytes 3932168 | tf_op jit(solution)/shard_map/ppermute | solution.py:354
  694.2 57.0 %collective-permute-start.29 = (bf16[256,2560]{1,0:T(8,128)(2,1)S(1)}, bf16[256,2560]{1,0:T(8,128)(2,1)S(1)}, u32[]{:S(2)}, u32[]{:S(2)}) collective-permute-start(bf16[256,2560]{1,0:T(8,128)(2,1)S(1)} %get-tuple-element.86), channel_id=1, source_target_pairs={{0,2},{1,3},{2,0},{3,1},{4,6},{5,7},{6,4},{7,5},{8,10},{9,11},{10,... | collective-permute-start | bytes 3932168 | tf_op jit(solution)/shard_map/ppermute | solution.py:354
  695.9 56.2 %collective-permute-start.27 = (bf16[256,2560]{1,0:T(8,128)(2,1)S(1)}, bf16[256,2560]{1,0:T(8,128)(2,1)S(1)}, u32[]{:S(2)}, u32[]{:S(2)}) collective-permute-start(bf16[256,2560]{1,0:T(8,128)(2,1)S(1)} %get-tuple-element.85), channel_id=1, source_target_pairs={{0,1},{1,0},{2,3},{3,2},{4,5},{5,4},{6,7},{7,6},{8,9},{9,8},{10,11... | collective-permute-start | bytes 3932168 | tf_op jit(solution)/shard_map/ppermute | solution.py:354
  700.1 56.0 %collective-permute-start.16 = (bf16[256,2560]{1,0:T(8,128)(2,1)S(1)}, bf16[256,2560]{1,0:T(8,128)(2,1)S(1)}, u32[]{:S(2)}, u32[]{:S(2)}) collective-permute-start(bf16[256,2560]{1,0:T(8,128)(2,1)S(1)} %fusion.43), channel_id=1, source_target_pairs={{0,1},{1,0},{2,3},{3,2},{4,5},{5,4},{6,7},{7,6},{8,9},{9,8},{10,11... | collective-permute-start | bytes 3932168 | tf_op jit(solution)/shard_map/ppermute | solution.py:354
  751.2 32.0 %collective-permute-start.14 = (bf16[256,2560]{1,0:T(8,128)(2,1)}, bf16[256,2560]{1,0:T(8,128)(2,1)}, u32[]{:S(2)}, u32[]{:S(2)}) collective-permute-start(bf16[256,2560]{1,0:T(8,128)(2,1)} %fusion.45), channel_id=1, source_target_pairs={{0,2},{1,3},{2,0},{3,1},{4,6},{5,7},{6,4},{7,5},{8,10},{9,11},{10,... | collective-permute-start | bytes 3932168 | tf_op jit(solution)/shard_map/ppermute | solution.py:354
  752.0 36.1 %collective-permute-start.26 = (bf16[256,2560]{1,0:T(8,128)(2,1)}, bf16[256,2560]{1,0:T(8,128)(2,1)}, u32[]{:S(2)}, u32[]{:S(2)}) collective-permute-start(bf16[256,2560]{1,0:T(8,128)(2,1)} %slice.387), channel_id=1, source_target_pairs={{0,1},{1,0},{2,3},{3,2},{4,5},{5,4},{6,7},{7,6},{8,9},{9,8},{10,11... | collective-permute-start | bytes 3932168 | tf_op jit(solution)/shard_map/ppermute | solution.py:354
  754.1 57.1 %collective-permute-start.31 = (bf16[256,2560]{1,0:T(8,128)(2,1)}, bf16[256,2560]{1,0:T(8,128)(2,1)}, u32[]{:S(2)}, u32[]{:S(2)}) collective-permute-start(bf16[256,2560]{1,0:T(8,128)(2,1)} %slice.386), channel_id=1, source_target_pairs={{0,2},{1,3},{2,0},{3,1},{4,6},{5,7},{6,4},{7,5},{8,10},{9,11},{10,... | collective-permute-start | bytes 3932168 | tf_op jit(solution)/shard_map/ppermute | solution.py:354
  755.6 55.6 %collective-permute-start.30 = (bf16[256,2560]{1,0:T(8,128)(2,1)S(1)}, bf16[256,2560]{1,0:T(8,128)(2,1)}, u32[]{:S(2)}, u32[]{:S(2)}) collective-permute-start(bf16[256,2560]{1,0:T(8,128)(2,1)S(1)} %fusion.39), channel_id=1, source_target_pairs={{0,1},{1,0},{2,3},{3,2},{4,5},{5,4},{6,7},{7,6},{8,9},{9,8},{10,11... | collective-permute-start | bytes 3932168 | tf_op jit(solution)/shard_map/ppermute | solution.py:354
  756.1 80.6 %collective-permute-start.28 = (bf16[256,2560]{1,0:T(8,128)(2,1)S(1)}, bf16[256,2560]{1,0:T(8,128)(2,1)}, u32[]{:S(2)}, u32[]{:S(2)}) collective-permute-start(bf16[256,2560]{1,0:T(8,128)(2,1)S(1)} %fusion.41), channel_id=1, source_target_pairs={{0,2},{1,3},{2,0},{3,1},{4,6},{5,7},{6,4},{7,5},{8,10},{9,11},{10,... | collective-permute-start | bytes 3932168 | tf_op jit(solution)/shard_map/ppermute | solution.py:354
  (75 other events, 2382.1 us)
Sparse Core Ops, SparseCore 0:
  12.9 74.9 all-gather.3
  89.6 65.4 all-gather.5
  156.7 65.4 all-gather.7
  387.9 72.1 reduce-scatter.9
  462.3 70.6 reduce-scatter.7
  616.1 81.2 reduce-scatter.11

commit v2 on v1

--- a/solution.py
+++ b/solution.py
@@ -4,7 +4,9 @@
 from jax import lax
 from jax.experimental import pallas as pl
 from jax.experimental.pallas import tpu as pltpu
+from jax.experimental.layout import Layout, with_layout_constraint
 from jax.sharding import PartitionSpec as P
+
 
 P_SIZE = 64
 N = 128
@@ -339,6 +341,93 @@
     return lax.dot_general(a, b, (((0,), (0,)), ((), ())), preferred_element_type=F32)
 
 
+def fill_kernel(x_ref, w_ref, *refs):
+    refs[-1][...] = mm(x_ref[...], w_ref[...])
+
+
+def run_fill(x, w, into, rows, first, block):
+    depth, width = w.shape
+    return pl.pallas_call(
+        fill_kernel,
+        out_shape=jax.ShapeDtypeStruct((rows, width), F32),
+        grid=(x.shape[0] // block,),
+        in_specs=[
+            pl.BlockSpec((block, depth), lambda i: (i, 0)),
+            pl.BlockSpec((depth, width), lambda i: (0, 0), pipeline_mode=pl.Buffered(1)),
+        ]
+        + [pl.BlockSpec(memory_space=pl.ANY)] * len(into),
+        out_specs=pl.BlockSpec((block, width), lambda i: (i + first, 0)),
+        input_output_aliases={2: 0} if into else {},
+        cost_estimate=pl.CostEstimate(
+            flops=2 * x.shape[0] * depth * width,
+            bytes_accessed=2 * (x.shape[0] + width) * depth + 4 * x.shape[0] * width,
+            transcendentals=0,
+        ),
+        name="value_product",
+    )(x, w, *into)
+
+
+def split_kernel(x_ref, w_ref, *out_refs):
+    rows = out_refs[0].shape[0]
+    for at, out_ref in enumerate(out_refs):
+        out_ref[...] = nt_dot(x_ref[at * rows : (at + 1) * rows], w_ref[...]).astype(BF16)
+
+
+def run_split(x, w, parts, block):
+    tokens, depth = x.shape
+    width = w.shape[0]
+    rows = tokens // parts
+    return pl.pallas_call(
+        split_kernel,
+        out_shape=[jax.ShapeDtypeStruct((rows, width), BF16)] * parts,
+        grid=(width // block,),
+        in_specs=[
+            pl.BlockSpec((tokens, depth), lambda i: (0, 0), pipeline_mode=pl.Buffered(1)),
+            pl.BlockSpec((block, depth), lambda i: (i, 0)),
+        ],
+        out_specs=[pl.BlockSpec((rows, block), lambda i: (0, i))] * parts,
+        cost_estimate=pl.CostEstimate(
+            flops=2 * tokens * depth * width, bytes_accessed=2 * (tokens + width) * depth + 2 * tokens * width, transcendentals=0
+        ),
+        name="split_product",
+    )(x, w)
+
+
+def rows_kernel(gate_ref, value_ref, small_ref, w_gate_ref, w_cat_ref, top_ref, low_ref):
+    wide = value_ref.shape[1]
+    rows = top_ref.shape[0]
+    for at, out_ref in enumerate((top_ref, low_ref)):
+        here = slice(at * rows, (at + 1) * rows)
+        total = nt_dot(gate_ref[here], w_gate_ref[...])
+        total = total + nt_dot(value_ref[here], w_cat_ref[:, :wide])
+        total = total + nt_dot(small_ref[here], w_cat_ref[:, wide:])
+        out_ref[...] = total.astype(BF16)
+
+
+def run_rows(piece, d_gate, d_value, d_small, w_gate, w_cat, rows, block):
+    width = w_gate.shape[0]
+    depth = w_gate.shape[1] + w_cat.shape[1]
+    mine = lambda i: (piece, 0)
+    once = pl.Buffered(1)
+    return pl.pallas_call(
+        rows_kernel,
+        out_shape=[jax.ShapeDtypeStruct((rows // 2, width), BF16)] * 2,
+        grid=(width // block,),
+        in_specs=[
+            pl.BlockSpec((rows, d_gate.shape[1]), mine, pipeline_mode=once),
+            pl.BlockSpec((rows, d_value.shape[1]), mine, pipeline_mode=once),
+            pl.BlockSpec((rows, d_small.shape[1]), mine, pipeline_mode=once),
+            pl.BlockSpec((block, w_gate.shape[1]), lambda i: (i, 0)),
+            pl.BlockSpec((block, w_cat.shape[1]), lambda i: (i, 0)),
+        ],
+        out_specs=[pl.BlockSpec((rows // 2, block), lambda i: (0, i))] * 2,
+        cost_estimate=pl.CostEstimate(
+            flops=2 * rows * depth * width, bytes_accessed=2 * (rows + width) * depth + 2 * rows * width, transcendentals=0
+        ),
+        name="rows_product",
+    )(d_gate, d_value, d_small, w_gate, w_cat)
+
+
 def causal_conv(values, taps, offsets):
     tap_count = taps.shape[0]
     length = values.shape[0]
@@ -377,14 +466,15 @@
         parts = jnp.where(self.x, parts[:, ::-1], parts)
         return parts.reshape(v.shape)
 
-    def gather(self, v):
-        half = v.shape[0] // 2
-        from_x = swap(v, 1)
-        from_y = swap(v, 2)
-        return [v, from_x, from_y, swap(from_x[:half], 2), swap(from_y[half:], 1)]
+    def gather_begin(self, v):
+        return [v, swap(v, 1), swap(v, 2)]
+
+    def gather_end(self, pieces):
+        half = pieces[0].shape[0] // 2
+        return pieces + [swap(pieces[1][:half], 2), swap(pieces[2][half:], 1)]
 
     def gather_flat(self, v):
-        return self.settle(jnp.concatenate(self.gather(v)))
+        return self.settle(jnp.concatenate([v, swap(v, 1), swap(v, 2), swap(v, 3)]))
 
     def token_sum(self, v):
         parts = v.reshape(2, 2, -1)
@@ -396,33 +486,44 @@
         v = v + swap(v, 1)
         return v + swap(v, 2)
 
-    def scatter(self, piece_of):
-        far = piece_of(3).astype(BF16)
-        half = far.shape[0] // 2
-        beside = piece_of(1)
-        above = piece_of(2)
-        across_x = swap(far[:half], 1).astype(F32)
-        across_y = swap(far[half:], 2).astype(F32)
-        x_top = swap(beside[:half].astype(BF16), 1)
-        y_low = swap(above[half:].astype(BF16), 2)
-        own = piece_of(0)
-        x_low = swap((beside[half:] + across_y).astype(BF16), 1)
-        y_top = swap((above[:half] + across_x).astype(BF16), 2)
-        top = own[:half] + x_top.astype(F32) + y_top.astype(F32)
-        low = own[half:] + x_low.astype(F32) + y_low.astype(F32)
-        return jnp.concatenate([top, low])
+    def scatter_begin(self, halves_of):
+        top, low, x_top, x_low, y_top, y_low, far_top, far_low = halves_of
+        came = []
+        for part, bit in ((far_top, 1), (far_low, 2), (x_top, 1), (y_low, 2)):
+            came.append(swap(part, bit))
+        return [x_low, y_top, top, low], came
+
+    def scatter_relay(self, kept, came):
+        beside, above, top, low = kept
+        across_x, across_y, x_top, y_low = came
+        x_low = (beside.astype(F32) + across_y.astype(F32)).astype(BF16)
+        y_top = (above.astype(F32) + across_x.astype(F32)).astype(BF16)
+        return [x_low, y_top], [top, low, x_top, y_low]
+
+    def scatter_end(self, sent, came):
+        x_low = swap(sent[0], 1)
+        y_top = swap(sent[1], 2)
+        top, low, x_top, y_low = (v.astype(F32) for v in came)
+        return jnp.concatenate([top + x_top + y_top.astype(F32), low + x_low.astype(F32) + y_low])
 
     def gather_states(self, s):
         pair = jnp.concatenate([s, swap(s, 1)], axis=1)
-        other = swap(pair, 2)
+        other = jnp.concatenate([swap(s, 2), swap(s, 3)], axis=1)
         return jnp.concatenate([jnp.where(self.y, other, pair), jnp.where(self.y, pair, other)], axis=1)
 
-    def scatter_states(self, d):
+    def split_states(self, d):
         first, second = d[:, :N], d[:, N:]
-        kept = jnp.where(self.y, second, first).astype(F32)
-        kept = kept + swap(jnp.where(self.y, first, second), 2).astype(F32)
+        kept = jnp.where(self.y, second, first)
+        given = jnp.where(self.y, first, second)
         half = N // 2
-        return kept[:, :half] + swap(kept[:, half:].astype(BF16), 1).astype(F32)
+        return [kept[:, :half], kept[:, half:], given[:, :half], given[:, half:]]
+
+    def scatter_states(self, parts):
+        own = parts[0].astype(F32)
+        for bit in (1, 2, 3):
+            came = swap(parts[bit], bit)
+            own = own + came.astype(F32)
+        return own
 
     def own_slice(self, v):
         width = v.shape[0] // 4
@@ -438,8 +539,11 @@
     def settle(self, v):
         return v
 
-    def gather(self, v):
+    def gather_begin(self, v):
         return [lax.all_gather(v, "col", axis=0, tiled=True)]
+
+    def gather_end(self, pieces):
+        return pieces
 
     def gather_flat(self, v):
         return lax.all_gather(v, "col", axis=0, tiled=True)
@@ -450,16 +554,23 @@
     def total(self, v):
         return lax.psum(v, "col")
 
-    def scatter(self, piece_of):
-        return lax.psum_scatter(
-            piece_of(None).astype(BF16), "col", scatter_dimension=0, tiled=True
-        ).astype(F32)
+    def scatter_begin(self, halves_of):
+        return [], list(halves_of)
+
+    def scatter_relay(self, kept, came):
+        return came, []
+
+    def scatter_end(self, sent, came):
+        return lax.psum_scatter(sent[0], "col", scatter_dimension=0, tiled=True).astype(F32)
 
     def gather_states(self, s):
         return lax.all_gather(s, "col", axis=1, tiled=True)
 
-    def scatter_states(self, d):
-        return lax.psum_scatter(d.astype(BF16), "col", scatter_dimension=1, tiled=True).astype(F32)
+    def split_states(self, d):
+        return [d]
+
+    def scatter_states(self, parts):
+        return lax.psum_scatter(parts[0].astype(BF16), "col", scatter_dimension=1, tiled=True).astype(F32)
 
     def own_slice(self, v):
         width = v.shape[0] // lax.axis_size("col")
@@ -468,6 +579,27 @@
 
 def widened(v, width):
     return v if v.shape[-1] == width else jnp.pad(v, [(0, 0)] * (v.ndim - 1) + [(0, width - v.shape[-1])])
+
+
+def tied(*values):
+    return lax.optimization_barrier(values)
+
+
+def row_major(v):
+    return with_layout_constraint(v, Layout(major_to_minor=(0, 1)))
+
+
+def row_scatter_small(v):
+    bit = lax.axis_size("row") // 2
+    place = lax.axis_index("row")
+    while bit:
+        half = v.shape[0] // 2
+        upper = lax.rem(lax.div(place, bit), 2) == 1
+        kept = jnp.where(upper, v[half:], v[:half])
+        given = jnp.where(upper, v[:half], v[half:])
+        v = kept + swap(given.astype(BF16), bit, "row").astype(F32)
+        bit //= 2
+    return v
 
 
 def row_scatter(v):
@@ -502,9 +634,6 @@
     step_at = wide + bc_width
     piece_rows = hidden.shape[0]
 
-    def rows_of(v, piece):
-        return v if piece is None else v[piece * piece_rows : (piece + 1) * piece_rows]
-
     w_cat = lax.all_gather(
         widened(jnp.concatenate([widened(w_value, wide), w_bc, w_step], axis=1), full_width),
         "row", axis=0, tiled=True,
@@ -518,10 +647,21 @@
         scale = lax.rsqrt(jnp.mean(rows * rows, axis=1, keepdims=True) + EPSILON)
         return (rows * scale * full_gain).astype(BF16)
 
-    normal_in = jnp.concatenate([normalized(piece) for piece in lines.gather(hidden)])
-    grad_full = jnp.concatenate(lines.gather(grad_out))
-
-    pre = mm(normal_in, w_cat)
+    hidden_pieces = lines.gather_end(lines.gather_begin(hidden))
+    near = jnp.concatenate([normalized(piece) for piece in hidden_pieces[:3]])
+    far = [normalized(piece) for piece in hidden_pieces[3:]]
+    grad_source, _ = tied(grad_out, hidden_pieces[-1])
+    grad_pieces = lines.gather_begin(grad_source)
+
+    if far:
+        far = jnp.concatenate(far)
+        tokens_here = near.shape[0] + far.shape[0]
+        pre = run_fill(near, w_cat, (), tokens_here, 0, 256)
+        pre = run_fill(far, w_cat, (pre,), tokens_here, near.shape[0] // 256, 256)
+        normal_in = jnp.concatenate([near, far])
+    else:
+        normal_in = near
+        pre = mm(normal_in, w_cat)
     bc_pre = lines.settle(pre[:, wide : wide + bc_width])
     step_sum = lines.settle(pre[:, step_at : step_at + heads]) + step_bias
 
@@ -538,6 +678,8 @@
     pick = (jnp.arange(wide)[:, None] // P_SIZE == jnp.arange(LANES)[None]).astype(BF16)
     heads_out, held = run_forward(lines.seat, pre, states, steps, taps, offsets, rate, skip, lines.shards)
 
+    heads_out, *grad_pieces = tied(heads_out, *grad_pieces)
+    grad_pieces = lines.gather_end(grad_pieces)
     gate_pre = mm(normal_in, w_gate_full).astype(BF16)
     ho = heads_out[:, :channels].astype(F32)
     gate = gate_pre.astype(F32)
@@ -545,48 +687,58 @@
     squares = lines.token_sum(jnp.sum(gated * gated, axis=1))
     mix = lax.rsqrt(squares / inner_width + EPSILON)[:, None]
     normed = (gated * mix * norm_gain).astype(BF16)
-
-    branch_out = lines.scatter(lambda piece: nt_dot(rows_of(normed, piece), w_out_t))
-    result = (hidden.astype(F32) + branch_out).astype(BF16)
-
+    normed, *grad_pieces = tied(normed, *grad_pieces)
+    grad_full = jnp.concatenate(grad_pieces)
+
+    g_out_part = row_major(tn_dot(grad_full, normed).astype(BF16))
+    w_out_t, g_out_part = tied(w_out_t, g_out_part)
+    g_out_t = row_scatter(g_out_part)
     d_normed = mm(grad_full, w_out_t).astype(BF16).astype(F32)
     scaled = d_normed * norm_gain
-    dots = lines.token_sum(jnp.sum(gated * scaled, axis=1))[:, None]
-    g_out_t = row_scatter(tn_dot(grad_full, normed))
+    dots = jnp.sum(gated * scaled, axis=1)
+    w_out_t, dots = tied(w_out_t, dots)
+    if lines.shards == 4:
+        out_parts = run_split(normed, w_out_t, 8, 512)
+    else:
+        out_parts = [nt_dot(normed, w_out_t).astype(BF16)]
+    kept, came = lines.scatter_begin(out_parts)
+    dots = lines.token_sum(dots)[:, None]
     d_gated = mix * scaled - gated * (mix * mix * mix * dots / inner_width)
     g_norm_gain = jnp.sum(d_normed * gated * mix, axis=0)
     open_gate = sigmoid(gate)
     d_heads = (d_gated * gate * open_gate).astype(BF16)
     d_gate = (d_gated * ho * (open_gate * (1.0 + gate * (1.0 - open_gate)))).astype(BF16)
-    g_gate_part = tn_dot(normal_in, d_gate).astype(BF16)
+    g_gate_part = row_major(tn_dot(normal_in, d_gate).astype(BF16))
+    sent, came = lines.scatter_relay(kept, came)
+    d_heads, g_gate_part, *sent = tied(d_heads, g_gate_part, *sent)
     g_gate = row_scatter(g_gate_part)
 
-    d_cat, d_states, d_steps, g_conv, g_decay = run_backward(
+    d_value, d_states, d_steps, g_conv, g_decay = run_backward(
         lines.seat, pre, widened(d_heads, wide), states, steps, held, taps, offsets, rate, skip, pick,
-        lines.shards, full_width,
+        lines.shards, wide,
     )
-    d_bc_pre, g_conv_bc, g_conv_bc_bias = state_back(lines.scatter_states(d_states))
+    state_parts = lines.split_states(d_states)
+    normal_in, *state_parts = tied(normal_in, *state_parts)
+    g_value_part = row_major(tn_dot(normal_in, d_value).astype(BF16))
+    g_value = row_scatter(g_value_part)
+    branch_out = lines.scatter_end(sent, came)
+    result = (hidden.astype(F32) + branch_out).astype(BF16)
+    d_state_local, result, g_value_part = tied(lines.scatter_states(state_parts), result, g_value_part)
+    d_bc_pre, g_conv_bc, g_conv_bc_bias = state_back(d_state_local)
     d_step = d_steps[:, :heads] * sigmoid(step_sum)
     small = lines.settle(widened(jnp.concatenate([d_bc_pre, d_step], axis=1), LANES)).astype(BF16)
-    d_cat = lax.dynamic_update_slice(d_cat, small, (0, wide))
-    g_cat_part = tn_dot(normal_in, d_cat).astype(BF16)
-    g_cat = row_scatter(g_cat_part)
-
-    d_rows = lines.scatter(
-        lambda piece: nt_dot(rows_of(d_gate, piece), w_gate_full) + nt_dot(rows_of(d_cat, piece), w_cat)
-    )
-    tokens = hidden.astype(F32)
-    scale = lax.rsqrt(jnp.mean(tokens * tokens, axis=1, keepdims=True) + EPSILON)
-    scaled_rows = d_rows * full_gain
-    grad_hidden = grad_out.astype(F32) + scale * (
-        scaled_rows - tokens * (scale * scale * jnp.mean(tokens * scaled_rows, axis=1, keepdims=True))
-    )
-
-    g_in_gain = (
-        jnp.sum(w_gate_full.astype(F32) * g_gate_part.astype(F32), axis=1)
-        + jnp.sum(w_cat.astype(F32) * g_cat_part.astype(F32), axis=1)
-    ) / full_gain
-    g_in_gain = row_sum(lines.own_slice(lines.total(g_in_gain)))
+    small, d_value, g_value_part = tied(small, d_value, g_value_part)
+    if lines.shards == 4:
+        pieces = {}
+        turn = d_value
+        for piece in (3, 1, 2, 0):
+            pieces[piece] = run_rows(piece, d_gate, turn, small, w_gate_full, w_cat, piece_rows, 512)
+            turn, last_part = tied(turn, pieces[piece][0])
+        row_parts = [half for piece in range(4) for half in pieces[piece]]
+    else:
+        d_cat = jnp.concatenate([d_value, small], axis=1)
+        row_parts = [(nt_dot(d_gate, w_gate_full) + nt_dot(d_cat, w_cat)).astype(BF16)]
+    sent, came = lines.scatter_relay(*lines.scatter_begin(row_parts))
     parts = (
         g_conv[:4, :channels],
         g_conv[4, :channels],
@@ -597,7 +749,23 @@
         jnp.sum(g_conv[5, :channels].reshape(heads, P_SIZE), axis=1),
         g_norm_gain,
     )
-    packed = row_sum(jnp.concatenate([part.reshape(-1) for part in parts]))
+    packed = jnp.concatenate([part.reshape(-1) for part in parts])
+    packed, last_part, normal_in, g_gate_part, g_value_part, *sent = tied(
+        packed, row_parts[0], normal_in, g_gate_part, g_value_part, *sent
+    )
+    d_rows = lines.scatter_end(sent, came)
+    packed = row_sum(packed)
+    g_small_part = tn_dot(normal_in, small)
+    g_small = row_scatter_small(g_small_part)
+    tokens = hidden.astype(F32)
+    scale = lax.rsqrt(jnp.mean(tokens * tokens, axis=1, keepdims=True) + EPSILON)
+    scaled_rows = d_rows * full_gain
+    grad_hidden = grad_out.astype(F32) + scale * (
+        scaled_rows - tokens * (scale * scale * jnp.mean(tokens * scaled_rows, axis=1, keepdims=True))
+    )
+
+    g_in_gain = gain_sums(w_gate_full, g_gate_part, w_cat, g_value_part, g_small_part) / full_gain
+    g_in_gain = row_sum(lines.own_slice(lines.total(g_in_gain)))
     summed = []
     at = 0
     for part in parts:
@@ -608,11 +776,20 @@
         grad_hidden,
         g_in_gain,
         g_gate,
-        g_cat[:, :channels],
-        g_cat[:, wide : wide + bc_width],
-        g_cat[:, step_at : step_at + heads],
+        g_value[:, :channels],
+        g_small[:, :bc_width],
+        g_small[:, bc_width : bc_width + heads],
         *summed,
         g_out_t.T,
+    )
+
+
+def gain_sums(w_gate, g_gate, w_cat, g_value, g_small):
+    wide = g_value.shape[1]
+    return (
+        jnp.sum(w_gate.astype(F32) * g_gate.astype(F32), axis=1)
+        + jnp.sum(w_cat[:, :wide].astype(F32) * g_value.astype(F32), axis=1)
+        + jnp.sum(w_cat[:, wide:].astype(F32) * g_small, axis=1)
     )
 
 

time: 880 us -> 782 us (0.89)
  matrix products: 219 us -> 107 us
  Pallas kernels: 123 us -> 218 us
  local copies, waits for them, and re-layouts: 121 us -> 40.5 us
  other arithmetic: 71.2 us -> 98.7 us
  waiting for transfers between devices: 273 us -> 246 us
    pallas_call x0 -> x7, Pallas kernels: none -> 94.3 us  [the longest x4 48.8 us: run_rows(): pl.pallas_call(rows_kernel, out_shape=[jax.ShapeDtypeStruct((rows // 2, w...]
    dot_general x12 -> x0, matrix products: 89.9 us -> none  [nt_dot(): lax.dot_general(a, b, (((1,), (1,)), ((), ())), preferred_element_type=F32)]
    unnamed x138 -> x112, local copies, waits for them, and re-layouts: 50.5 us -> 21.2 us
    ppermute x40 -> x44, waiting for transfers between devices: 272 us -> 245 us  [swap(): return lax.ppermute(v, axis, [(i, i ^ bit) for i in range(size)])]
    dot_general x3 -> x2, matrix products: 65.7 us -> 45.6 us  [mm(): return jnp.dot(a, b, preferred_element_type=F32)]
    all_gather x2 -> x0, local copies, waits for them, and re-layouts: 19.9 us -> none  [the longest x1 10.4 us: body(): lax.all_gather(widened(jnp.concatenate([widened(w_value, wide), w_bc, w_s...]
    convert_element_type x4 -> x11, other arithmetic: 5.94 us -> 25.3 us  [the longest x1 7.13 us: body(): normed = (gated * mix * norm_gain).astype(BF16)]
    slice x16 -> x6, local copies, waits for them, and re-layouts: 23 us -> 7.17 us  [the longest x4 5.61 us: gather_end(): return pieces + [swap(pieces[1][:half], 2), swap(pieces[2][half:], 1)]]
  transfers between devices with their start and end apart: 46 -> 50, of which waited for: 14 -> 20; matrix products, arithmetic and copies ran while one was open for 37% -> 26% of each run, Pallas kernels for 14% -> 28%
where the time goes in v2:
time: 782 us; the launch traced here: 771 us
  waiting for transfers between devices  246 us (31%)
  Pallas kernels  218 us (28%)
  matrix products  107 us (14%)
  other arithmetic  98.7 us (13%)
  starting transfers between devices  45.7 us (6%)
  local copies, waits for them, and re-layouts  40.5 us (5%)
  between operations  15.7 us (2%)
    ppermute x44, waiting for transfers between devices, swap(): return lax.ppermute(v, axis, [(i, i ^ bit) for i in range(size)])  245 us
    pallas_call x1, Pallas kernels, run_backward(): pl.pallas_call(functools.partial(scan_backward, pairs=width // LANES, blo...  88.3 us
    dot_general x4, matrix products, tn_dot(): lax.dot_general(a, b, (((0,), (0,)), ((), ())), preferred_element_type=F32)  61.4 us
    pallas_call x4, Pallas kernels, run_rows(): pl.pallas_call(rows_kernel, out_shape=[jax.ShapeDtypeStruct((rows // 2, w...  48.8 us
    dot_general x2, matrix products, mm(): return jnp.dot(a, b, preferred_element_type=F32)  45.6 us
    ppermute x44, starting transfers between devices, swap(): return lax.ppermute(v, axis, [(i, i ^ bit) for i in range(size)])  45.3 us
    pallas_call x1, Pallas kernels, run_forward(): pl.pallas_call(functools.partial(scan_forward, pairs=width // LANES), out...  35 us
    pallas_call x2, Pallas kernels, run_fill(): pl.pallas_call(fill_kernel, out_shape=jax.ShapeDtypeStruct((rows, width),...  27 us
  transfers between devices with their start and end apart: 50, of which 20 were waited for; matrix products, arithmetic and copies ran while one was open for 26% of the time, Pallas kernels for 28%

profile of v2, /device:TPU:0, one launch (start us, length us, event | category | flops | bytes accessed | tf_op | source)
XLA Modules:
  0.0 771.0 jit_solution(15231812088748865585)
XLA Ops:
  24.3 49.3 %collective-permute-done = bf16[640]{0:T(1024)(128)(2,1)S(1)} collective-permute-done((bf16[640]{0:T(1024)(128)(2,1)S(1)}, bf16[640]{0:T(1024)(128)(2,1)S(1)}, u32[]{:S(2)}, u32[]{:S(2)}) %collective-permute-start) | collective-permute-done | bytes 1312 | tf_op jit(solution)/shard_map/ppermute | solution.py:443
  90.4 3.9 pad_maximum_fusion.x_ref
  94.3 19.2 %collective-permute-done.6 = bf16[256,2560]{1,0:T(8,128)(2,1)S(1)} collective-permute-done((bf16[256,2560]{1,0:T(8,128)(2,1)S(1)}, bf16[256,2560]{1,0:T(8,128)(2,1)S(1)}, u32[]{:S(2)}, u32[]{:S(2)}) %collective-permute-start.6) | collective-permute-done | bytes 1310752 | tf_op jit(solution)/shard_map/ppermute | solution.py:443
  123.5 17.9 %value_product.2.refs_0_ = f32[2048,1408]{1,0:T(8,128)} custom-call(bf16[1536,2560]{1,0:T(8,128)(2,1)} %pad_maximum_fusion.x_ref, bf16[2560,1408]{1,0:T(8,128)(2,1)} %all-gather.4.cloned.1.call-done.w_ref.w_cat_ref), custom_call_target="tpu_custom_call" | custom-call | flops 11072962560 | bytes 23724032 | tf_op jit(solution)/shard_map/value_product/pallas_call | solution.py:350
  141.4 9.0 %value_product.3.vp_ref.before_ref = f32[2048,1408]{1,0:T(8,128)} custom-call(bf16[512,2560]{1,0:T(8,128)(2,1)} %pad_maximum_fusion.1.x_ref, bf16[2560,1408]{1,0:T(8,128)(2,1)} %all-gather.4.cloned.1.call-done.w_ref.w_cat_ref, f32[2048,1408]{1,0:T(8,128)} %value_product.2.refs_0_), custom_call_target="tpu_custom_call", output_to_operand_aliasing={{}: (2, {})} | custom-call | flops 3690987520 | bytes 12713984 | tf_op jit(solution)/shard_map/value_product/pallas_call | solution.py:350
  160.7 33.2 %collective-permute-done.7 = bf16[2048,64]{1,0:T(8,128)(2,1)S(1)} collective-permute-done((bf16[2048,64]{1,0:T(8,128)(2,1)S(1)}, bf16[2048,64]{1,0:T(8,128)(2,1)S(1)}, u32[]{:S(2)}, u32[]{:S(2)}) %collective-permute-start.7) | collective-permute-done | bytes 262176 | tf_op jit(solution)/shard_map/ppermute | solution.py:443
  195.7 35.0 %scan_forward.1 = (bf16[2048,1280]{1,0:T(8,128)(2,1)}, bf16[16,128,1280]{2,1,0:T(8,128)(2,1)}) custom-call(s32[1]{0:T(128)} %bitcast.seat_ref, f32[2048,1408]{1,0:T(8,128)} %value_product.3.vp_ref.before_ref, bf16[2048,256]{1,0:T(8,128)(2,1)} %pad_maximum_fusion.2.bc_ref, f32[2048,128]{1,0:T(8,128)} %pad.51.st_ref, f32[4,1280]{1,0:T(4,128)} %taps_ref.3, ...), custom_call_target="tpu_custom_call" | custom-call | flops 3145728000 | bytes 26214400 | tf_op jit(solution)/shard_map/scan_forward/pallas_call | solution.py:235
  230.7 21.5 %multiply_reduce_fusion.2 = (f32[2048]{0:T(1024)S(1)}, bf16[2048,1280]{1,0:T(8,128)(2,1)}) fusion(bf16[2048,1280]{1,0:T(8,128)(2,1)} %get-tuple-element.80, bf16[2048,2560]{1,0:T(8,128)(2,1)} %copy-done.20, bf16[2560,1280]{1,0:T(8,128)(2,1)} %all-gather.6.cloned.1.call-done.w_gate_ref), kind=kOutput, calls=%fused_computation.30 | convolution fusion | flops 13447985152 | bytes 27533312 | tf_op jit(solution)/shard_map/dot_general | solution.py:30
  261.6 7.1 multiply_convert_fusion.x_ref
  268.8 16.8 %collective-permute-done.14 = bf16[256,2560]{1,0:T(8,128)(2,1)S(1)} collective-permute-done((bf16[256,2560]{1,0:T(8,128)(2,1)S(1)}, bf16[256,2560]{1,0:T(8,128)(2,1)S(1)}, u32[]{:S(2)}, u32[]{:S(2)}) %collective-permute-start.14) | collective-permute-done | bytes 1310752 | tf_op jit(solution)/shard_map/ppermute | solution.py:443
  291.3 3.9 copy-done.21
  295.2 16.3 %convolution_convert_fusion.2 = bf16[2560,1280]{1,0:T(8,128)(2,1)} fusion(bf16[2048,2560]{1,0:T(8,128)(2,1)S(1)} %constant_dynamic-update-slice_fusion.5, bf16[2048,1280]{1,0:T(8,128)(2,1)S(1)} %multiply_convert_fusion.x_ref), kind=kOutput, calls=%fused_computation.14 | convolution fusion | flops 13425049600 | bytes 22282240 | tf_op jit(solution)/shard_map/dot_general | solution.py:341
  311.6 24.1 %fusion.7 = (f32[1280]{0:T(1024)S(1)}, f32[2048]{0:T(1024)S(1)}, bf16[2048,1280]{1,0:T(8,128)(2,1)}) fusion(f32[2048]{0:T(1024)S(1)} %bitcast.69, bf16[2048,1280]{1,0:T(8,128)(2,1)} %get-tuple-element.204, bf16[2048,1280]{1,0:T(8,128)(2,1)} %get-tuple-element.80, f32[1280]{0:T(1024)S(1)} %copy-done.23, bf16[2048,2560]{1,0:T(8,128)(2,1)} %copy-done.21, ...), kind=kOutput, calls=%fused_computation.20 | convolution fusion | flops 13461091328 | bytes 32794624 | tf_op jit(solution)/shard_map/dot_general | solution.py:30
  341.3 18.4 %split_product.1 = (bf16[256,2560]{1,0:T(8,128)(2,1)}, bf16[256,2560]{1,0:T(8,128)(2,1)}, bf16[256,2560]{1,0:T(8,128)(2,1)}, bf16[256,2560]{1,0:T(8,128)(2,1)}, ...) custom-call(bf16[2048,1280]{1,0:T(8,128)(2,1)} %copy-done.9, ...), custom_call_target="tpu_custom_call" | custom-call | flops 13421772800 | bytes 22282240 | tf_op jit(solution)/shard_map/split_product/pallas_call | solution.py:380
  360.8 13.1 %fusion.5 = (bf16[2048,1280]{1,0:T(8,128)(2,1)S(1)}, bf16[2048,1280]{1,0:T(8,128)(2,1)}) fusion(bf16[2048,1280]{1,0:T(8,128)(2,1)} %get-tuple-element.80, bf16[2048,1280]{1,0:T(8,128)(2,1)} %get-tuple-element.204, bf16[2048,1280]{1,0:T(8,128)(2,1)} %get-tuple-element.205, f32[2048]{0:T(1024)S(1)} %fusion.39, f32[1280]{0:T(1024)S(1)} %copy-done.23, ...), kind=kLoop, calls=%fused_computation.18 | loop fusion | flops 57671680 | bytes 26235904 | tf_op jit(solution)/shard_map/convert_element_type | solution.py:710
  376.3 18.6 %convolution_convert_fusion.1 = bf16[2560,1280]{1,0:T(8,128)(2,1)} fusion(bf16[2048,2560]{1,0:T(8,128)(2,1)} %copy-done.20, bf16[2048,1280]{1,0:T(8,128)(2,1)S(1)} %get-tuple-element.180.gate_ref), kind=kOutput, calls=%fused_computation.13 | convolution fusion | flops 13425049600 | bytes 22282240 | tf_op jit(solution)/shard_map/dot_general | solution.py:341
  400.7 88.3 %scan_backward.1 = (bf16[2048,1280]{1,0:T(8,128)(2,1)}, bf16[2048,256]{1,0:T(8,128)(2,1)}, f32[2048,128]{1,0:T(8,128)}, f32[8,1280]{1,0:T(8,128)}, f32[1,128]{1,0:T(1,128)}) custom-call(s32[1]{0:T(128)} %bitcast.seat_ref, f32[2048,1408]{1,0:T(8,128)} %value_product.3.vp_ref.before_ref, f32[2048,1408]{1,0:T(8,128)} %value_product.3.vp_ref.before_ref, ...), custom_call_target="tpu_custom_call" | custom-call | flops 7864320000 | bytes 36700160 | tf_op jit(solution)/shard_map/scan_backward/pallas_call | solution.py:279
  492.1 18.9 %convolution_convert_fusion = bf16[2560,1280]{1,0:T(8,128)(2,1)} fusion(bf16[2048,2560]{1,0:T(8,128)(2,1)} %copy-done.20, bf16[2048,1280]{1,0:T(8,128)(2,1)S(1)} %copy-done.44), kind=kOutput, calls=%fused_computation.12 | convolution fusion | flops 13425049600 | bytes 22282240 | tf_op jit(solution)/shard_map/dot_general | solution.py:341
  520.1 34.2 %collective-permute-done.20 = bf16[2048,64]{1,0:T(8,128)(2,1)S(1)} collective-permute-done((bf16[2048,64]{1,0:T(8,128)(2,1)}, bf16[2048,64]{1,0:T(8,128)(2,1)S(1)}, u32[]{:S(2)}, u32[]{:S(2)}) %collective-permute-start.20) | collective-permute-done | bytes 262176 | tf_op jit(solution)/shard_map/ppermute | solution.py:443
  556.0 9.0 %collective-permute-done.21 = bf16[2048,64]{1,0:T(8,128)(2,1)} collective-permute-done((bf16[2048,64]{1,0:T(8,128)(2,1)}, bf16[2048,64]{1,0:T(8,128)(2,1)}, u32[]{:S(2)}, u32[]{:S(2)}) %collective-permute-start.21) | collective-permute-done | bytes 262176 | tf_op jit(solution)/shard_map/ppermute | solution.py:443
  570.6 15.6 %collective-permute-done.26 = bf16[256,2560]{1,0:T(8,128)(2,1)S(1)} collective-permute-done((bf16[256,2560]{1,0:T(8,128)(2,1)}, bf16[256,2560]{1,0:T(8,128)(2,1)S(1)}, u32[]{:S(2)}, u32[]{:S(2)}) %collective-permute-start.26) | collective-permute-done | bytes 1310752 | tf_op jit(solution)/shard_map/ppermute | solution.py:443
  592.4 12.1 %rows_product.4 = (bf16[256,2560]{1,0:T(8,128)(2,1)}, bf16[256,2560]{1,0:T(8,128)(2,1)}) custom-call(bf16[2048,1280]{1,0:T(8,128)(2,1)} %copy-done.10, bf16[2048,1280]{1,0:T(8,128)(2,1)} %get-tuple-element.123.value_ref, bf16[2048,128]{1,0:T(8,128)(2,1)} %bitcast.63, bf16[2560,1280]{1,0:T(8,128)(2,1)} %all-gather.6.cloned.1.call-done.w_gate_ref, ...), custom_call_target="tpu_custom_call" | custom-call | flops 7046430720 | bytes 19136512 | tf_op jit(solution)/shard_map/rows_product/pallas_call | solution.py:412
  605.3 12.2 %rows_product.5 = (bf16[256,2560]{1,0:T(8,128)(2,1)}, bf16[256,2560]{1,0:T(8,128)(2,1)}) custom-call(bf16[2048,1280]{1,0:T(8,128)(2,1)} %copy-done.10, bf16[2048,1280]{1,0:T(8,128)(2,1)} %get-tuple-element.123.value_ref, bf16[2048,128]{1,0:T(8,128)(2,1)} %bitcast.64, bf16[2560,1280]{1,0:T(8,128)(2,1)} %all-gather.6.cloned.1.call-done.w_gate_ref, ...), custom_call_target="tpu_custom_call" | custom-call | flops 7046430720 | bytes 19136512 | tf_op jit(solution)/shard_map/rows_product/pallas_call | solution.py:412
  619.0 12.2 %rows_product.6 = (bf16[256,2560]{1,0:T(8,128)(2,1)}, bf16[256,2560]{1,0:T(8,128)(2,1)}) custom-call(bf16[2048,1280]{1,0:T(8,128)(2,1)} %copy-done.10, bf16[2048,1280]{1,0:T(8,128)(2,1)} %get-tuple-element.123.value_ref, bf16[2048,128]{1,0:T(8,128)(2,1)} %bitcast.65, bf16[2560,1280]{1,0:T(8,128)(2,1)} %all-gather.6.cloned.1.call-done.w_gate_ref, ...), custom_call_target="tpu_custom_call" | custom-call | flops 7046430720 | bytes 19136512 | tf_op jit(solution)/shard_map/rows_product/pallas_call | solution.py:412
  631.4 12.4 %rows_product.7 = (bf16[256,2560]{1,0:T(8,128)(2,1)}, bf16[256,2560]{1,0:T(8,128)(2,1)}) custom-call(bf16[2048,1280]{1,0:T(8,128)(2,1)} %copy-done.10, bf16[2048,1280]{1,0:T(8,128)(2,1)} %get-tuple-element.123.value_ref, bf16[2048,128]{1,0:T(8,128)(2,1)} %bitcast.66, bf16[2560,1280]{1,0:T(8,128)(2,1)} %all-gather.6.cloned.1.call-done.w_gate_ref, ...), custom_call_target="tpu_custom_call" | custom-call | flops 7046430720 | bytes 19136512 | tf_op jit(solution)/shard_map/rows_product/pallas_call | solution.py:412
  650.0 7.6 multiply_reduce_fusion.3
  659.6 4.7 multiply_reduce_fusion
  664.4 6.5 multiply_reduce_fusion.1
  695.0 4.3 collective-permute-done.39
  703.4 14.8 %collective-permute-done.27 = bf16[256,2560]{1,0:T(8,128)(2,1)} collective-permute-done((bf16[256,2560]{1,0:T(8,128)(2,1)}, bf16[256,2560]{1,0:T(8,128)(2,1)}, u32[]{:S(2)}, u32[]{:S(2)}) %collective-permute-start.27) | collective-permute-done | bytes 1310752 | tf_op jit(solution)/shard_map/ppermute | solution.py:443
  718.3 26.9 %collective-permute-done.30 = bf16[256,2560]{1,0:T(8,128)(2,1)} collective-permute-done((bf16[256,2560]{1,0:T(8,128)(2,1)}, bf16[256,2560]{1,0:T(8,128)(2,1)}, u32[]{:S(2)}, u32[]{:S(2)}) %collective-permute-start.30) | collective-permute-done | bytes 1310752 | tf_op jit(solution)/shard_map/ppermute | solution.py:443
  751.7 4.8 fusion.29
  (322 shorter events, 163.2 us)
Async XLA Ops:
  7.2 116.2 %all-gather.4.cloned.1.call-start = ((), (), s32[]{:S(2)}) async-start(), calls=%async_computation.3 | async-start | bytes 8110080 | tf_op jit(solution)/shard_map/all_gather | solution.py:637
  12.8 217.9 %all-gather.6.cloned.1.call-start = ((), (), s32[]{:S(2)}) async-start(), calls=%async_computation.4 | async-start | bytes 7372800 | tf_op jit(solution)/shard_map/all_gather | solution.py:641
  13.5 298.0 %all-gather.8.cloned.1.call-start = ((), (), s32[]{:S(2)}) async-start(), calls=%async_computation.5 | async-start | bytes 7372800 | tf_op jit(solution)/shard_map/all_gather | solution.py:642
  13.6 62.3 %collective-permute-start.3 = (bf16[512,2560]{1,0:T(8,128)(2,1)S(1)}, bf16[512,2560]{1,0:T(8,128)(2,1)}, u32[]{:S(2)}, u32[]{:S(2)}) collective-permute-start(bf16[512,2560]{1,0:T(8,128)(2,1)S(1)} %copy-done), channel_id=1, source_target_pairs={{0,1},{1,0},{2,3},{3,2},{4,5},{5,4},{6,7},{7,6},{8,9},{9,8},{10,11... | collective-permute-start | bytes 7864328 | tf_op jit(solution)/shard_map/ppermute | solution.py:443
  16.6 57.0 %collective-permute-start = (bf16[640]{0:T(1024)(128)(2,1)S(1)}, bf16[640]{0:T(1024)(128)(2,1)S(1)}, u32[]{:S(2)}, u32[]{:S(2)}) collective-permute-start(bf16[640]{0:T(1024)(128)(2,1)S(1)} %copy-done.40), channel_id=1, source_target_pairs={{0,1},{1,0},{2,3},{3,2},{4,5},{5,4},{6,7},{7,6},{8,9},{9,8},{10,11... | collective-permute-start | bytes 3848 | tf_op jit(solution)/shard_map/ppermute | solution.py:443
  16.7 56.9 %collective-permute-start.1 = (bf16[640]{0:T(1024)(128)(2,1)S(1)}, bf16[640]{0:T(1024)(128)(2,1)S(1)}, u32[]{:S(2)}, u32[]{:S(2)}) collective-permute-start(bf16[640]{0:T(1024)(128)(2,1)S(1)} %copy-done.40), channel_id=1, source_target_pairs={{0,2},{1,3},{2,0},{3,1},{4,6},{5,7},{6,4},{7,5},{8,10},{9,11},{10,... | collective-permute-start | bytes 3848 | tf_op jit(solution)/shard_map/ppermute | solution.py:443
  18.7 56.2 %collective-permute-start.2 = (bf16[640]{0:T(1024)(128)(2,1)S(1)}, bf16[640]{0:T(1024)(128)(2,1)S(1)}, u32[]{:S(2)}, u32[]{:S(2)}) collective-permute-start(bf16[640]{0:T(1024)(128)(2,1)S(1)} %copy-done.40), channel_id=1, source_target_pairs={{0,3},{1,2},{2,1},{3,0},{4,7},{5,6},{6,5},{7,4},{8,11},{9,10},{10,... | collective-permute-start | bytes 3848 | tf_op jit(solution)/shard_map/ppermute | solution.py:443
  20.1 58.1 %collective-permute-start.4 = (bf16[512,2560]{1,0:T(8,128)(2,1)S(1)}, bf16[512,2560]{1,0:T(8,128)(2,1)}, u32[]{:S(2)}, u32[]{:S(2)}) collective-permute-start(bf16[512,2560]{1,0:T(8,128)(2,1)S(1)} %copy-done), channel_id=1, source_target_pairs={{0,2},{1,3},{2,0},{3,1},{4,6},{5,7},{6,4},{7,5},{8,10},{9,11},{10,... | collective-permute-start | bytes 7864328 | tf_op jit(solution)/shard_map/ppermute | solution.py:443
  21.7 734.8 %reduce-scatter.8.cloned.1.call-start = ((), (), s32[]{:S(2)}) async-start(), calls=%async_computation.8 | async-start | bytes 7372800 | tf_op jit(solution)/shard_map/reduce_scatter | solution.py:606
  82.0 34.5 %collective-permute-start.5 = (bf16[256,2560]{1,0:T(8,128)(2,1)S(1)}, bf16[256,2560]{1,0:T(8,128)(2,1)S(1)}, u32[]{:S(2)}, u32[]{:S(2)}) collective-permute-start(bf16[256,2560]{1,0:T(8,128)(2,1)S(1)} %slice.176), channel_id=1, source_target_pairs={{0,2},{1,3},{2,0},{3,1},{4,6},{5,7},{6,4},{7,5},{8,10},{9,11},{10,... | collective-permute-start | bytes 3932168 | tf_op jit(solution)/shard_map/ppermute | solution.py:443
  113.5 117.2 %collective-permute-start.10 = (bf16[512,2560]{1,0:T(8,128)(2,1)S(1)}, bf16[512,2560]{1,0:T(8,128)(2,1)}, u32[]{:S(2)}, u32[]{:S(2)}) collective-permute-start(bf16[512,2560]{1,0:T(8,128)(2,1)S(1)} %copy-done.5), channel_id=1, source_target_pairs={{0,1},{1,0},{2,3},{3,2},{4,5},{5,4},{6,7},{7,6},{8,9},{9,8},{10,11... | collective-permute-start | bytes 7864328 | tf_op jit(solution)/shard_map/ppermute | solution.py:443
  115.0 115.7 %collective-permute-start.11 = (bf16[512,2560]{1,0:T(8,128)(2,1)S(1)}, bf16[512,2560]{1,0:T(8,128)(2,1)}, u32[]{:S(2)}, u32[]{:S(2)}) collective-permute-start(bf16[512,2560]{1,0:T(8,128)(2,1)S(1)} %copy-done.5), channel_id=1, source_target_pairs={{0,2},{1,3},{2,0},{3,1},{4,6},{5,7},{6,4},{7,5},{8,10},{9,11},{10,... | collective-permute-start | bytes 7864328 | tf_op jit(solution)/shard_map/ppermute | solution.py:443
  153.7 40.2 %collective-permute-start.7 = (bf16[2048,64]{1,0:T(8,128)(2,1)S(1)}, bf16[2048,64]{1,0:T(8,128)(2,1)S(1)}, u32[]{:S(2)}, u32[]{:S(2)}) collective-permute-start(bf16[2048,64]{1,0:T(8,128)(2,1)S(1)} %get-tuple-element.168), channel_id=1, source_target_pairs={{0,2},{1,3},{2,0},{3,1},{4,6},{5,7},{6,4},{7,5},{8,10},{9,11},{10,... | collective-permute-start | bytes 786440 | tf_op jit(solution)/shard_map/ppermute | solution.py:443
  154.3 39.6 %collective-permute-start.8 = (bf16[2048,64]{1,0:T(8,128)(2,1)S(1)}, bf16[2048,64]{1,0:T(8,128)(2,1)S(1)}, u32[]{:S(2)}, u32[]{:S(2)}) collective-permute-start(bf16[2048,64]{1,0:T(8,128)(2,1)S(1)} %get-tuple-element.168), channel_id=1, source_target_pairs={{0,3},{1,2},{2,1},{3,0},{4,7},{5,6},{6,5},{7,4},{8,11},{9,10},{10,... | collective-permute-start | bytes 786440 | tf_op jit(solution)/shard_map/ppermute | solution.py:443
  155.8 38.1 %collective-permute-start.9 = (bf16[2048,64]{1,0:T(8,128)(2,1)S(1)}, bf16[2048,64]{1,0:T(8,128)(2,1)S(1)}, u32[]{:S(2)}, u32[]{:S(2)}) collective-permute-start(bf16[2048,64]{1,0:T(8,128)(2,1)S(1)} %get-tuple-element.168), channel_id=1, source_target_pairs={{0,1},{1,0},{2,3},{3,2},{4,5},{5,4},{6,7},{7,6},{8,9},{9,8},{10,11... | collective-permute-start | bytes 786440 | tf_op jit(solution)/shard_map/ppermute | solution.py:443
  337.3 421.6 %reduce-scatter.6.cloned.1.call-start = ((), (), s32[]{:S(2)}) async-start(), calls=%async_computation.7 | async-start | bytes 7372800 | tf_op jit(solution)/shard_map/reduce_scatter | solution.py:606
  359.8 35.2 %collective-permute-start.19 = (bf16[256,2560]{1,0:T(8,128)(2,1)}, bf16[256,2560]{1,0:T(8,128)(2,1)S(1)}, u32[]{:S(2)}, u32[]{:S(2)}) collective-permute-start(bf16[256,2560]{1,0:T(8,128)(2,1)} %get-tuple-element.96), channel_id=1, source_target_pairs={{0,1},{1,0},{2,3},{3,2},{4,5},{5,4},{6,7},{7,6},{8,9},{9,8},{10,11... | collective-permute-start | bytes 3932168 | tf_op jit(solution)/shard_map/ppermute | solution.py:443
  360.4 37.7 %collective-permute-start.18 = (bf16[256,2560]{1,0:T(8,128)(2,1)}, bf16[256,2560]{1,0:T(8,128)(2,1)}, u32[]{:S(2)}, u32[]{:S(2)}) collective-permute-start(bf16[256,2560]{1,0:T(8,128)(2,1)} %get-tuple-element.94), channel_id=1, source_target_pairs={{0,2},{1,3},{2,0},{3,1},{4,6},{5,7},{6,4},{7,5},{8,10},{9,11},{10,... | collective-permute-start | bytes 3932168 | tf_op jit(solution)/shard_map/ppermute | solution.py:443
  511.0 250.4 %reduce-scatter.4.cloned.1.call-start = ((), (), s32[]{:S(2)}) async-start(), calls=%async_computation.6 | async-start | bytes 7372800 | tf_op jit(solution)/shard_map/reduce_scatter | solution.py:606
  511.2 57.0 %collective-permute-start.23 = (bf16[256,2560]{1,0:T(8,128)(2,1)}, bf16[256,2560]{1,0:T(8,128)(2,1)}, u32[]{:S(2)}, u32[]{:S(2)}) collective-permute-start(bf16[256,2560]{1,0:T(8,128)(2,1)} %get-tuple-element.105), channel_id=1, source_target_pairs={{0,1},{1,0},{2,3},{3,2},{4,5},{5,4},{6,7},{7,6},{8,9},{9,8},{10,11... | collective-permute-start | bytes 3932168 | tf_op jit(solution)/shard_map/ppermute | solution.py:443
  512.7 55.5 %collective-permute-start.24 = (bf16[256,2560]{1,0:T(8,128)(2,1)S(1)}, bf16[256,2560]{1,0:T(8,128)(2,1)}, u32[]{:S(2)}, u32[]{:S(2)}) collective-permute-start(bf16[256,2560]{1,0:T(8,128)(2,1)S(1)} %add_convert_fusion.2), channel_id=1, source_target_pairs={{0,2},{1,3},{2,0},{3,1},{4,6},{5,7},{6,4},{7,5},{8,10},{9,11},{10,... | collective-permute-start | bytes 3932168 | tf_op jit(solution)/shard_map/ppermute | solution.py:443
  514.4 40.0 %collective-permute-start.20 = (bf16[2048,64]{1,0:T(8,128)(2,1)}, bf16[2048,64]{1,0:T(8,128)(2,1)S(1)}, u32[]{:S(2)}, u32[]{:S(2)}) collective-permute-start(bf16[2048,64]{1,0:T(8,128)(2,1)} %get-tuple-element.101), channel_id=1, source_target_pairs={{0,1},{1,0},{2,3},{3,2},{4,5},{5,4},{6,7},{7,6},{8,9},{9,8},{10,11... | collective-permute-start | bytes 786440 | tf_op jit(solution)/shard_map/ppermute | solution.py:443
  515.0 50.0 %collective-permute-start.21 = (bf16[2048,64]{1,0:T(8,128)(2,1)}, bf16[2048,64]{1,0:T(8,128)(2,1)}, u32[]{:S(2)}, u32[]{:S(2)}) collective-permute-start(bf16[2048,64]{1,0:T(8,128)(2,1)} %get-tuple-element.102), channel_id=1, source_target_pairs={{0,2},{1,3},{2,0},{3,1},{4,6},{5,7},{6,4},{7,5},{8,10},{9,11},{10,... | collective-permute-start | bytes 786440 | tf_op jit(solution)/shard_map/ppermute | solution.py:443
  515.4 51.3 %collective-permute-start.22 = (bf16[2048,64]{1,0:T(8,128)(2,1)}, bf16[2048,64]{1,0:T(8,128)(2,1)}, u32[]{:S(2)}, u32[]{:S(2)}) collective-permute-start(bf16[2048,64]{1,0:T(8,128)(2,1)} %get-tuple-element.103), channel_id=1, source_target_pairs={{0,3},{1,2},{2,1},{3,0},{4,7},{5,6},{6,5},{7,4},{8,11},{9,10},{10,... | collective-permute-start | bytes 786440 | tf_op jit(solution)/shard_map/ppermute | solution.py:443
  554.4 31.9 %collective-permute-start.26 = (bf16[256,2560]{1,0:T(8,128)(2,1)}, bf16[256,2560]{1,0:T(8,128)(2,1)S(1)}, u32[]{:S(2)}, u32[]{:S(2)}) collective-permute-start(bf16[256,2560]{1,0:T(8,128)(2,1)} %get-tuple-element.109), channel_id=1, source_target_pairs={{0,2},{1,3},{2,0},{3,1},{4,6},{5,7},{6,4},{7,5},{8,10},{9,11},{10,... | collective-permute-start | bytes 3932168 | tf_op jit(solution)/shard_map/ppermute | solution.py:443
  604.5 39.3 %collective-permute-start.29 = (bf16[256,2560]{1,0:T(8,128)(2,1)}, bf16[256,2560]{1,0:T(8,128)(2,1)}, u32[]{:S(2)}, u32[]{:S(2)}) collective-permute-start(bf16[256,2560]{1,0:T(8,128)(2,1)} %get-tuple-element.118), channel_id=1, source_target_pairs={{0,1},{1,0},{2,3},{3,2},{4,5},{5,4},{6,7},{7,6},{8,9},{9,8},{10,11... | collective-permute-start | bytes 3932168 | tf_op jit(solution)/shard_map/ppermute | solution.py:443
  617.5 29.5 %collective-permute-start.28 = (bf16[256,2560]{1,0:T(8,128)(2,1)}, bf16[256,2560]{1,0:T(8,128)(2,1)}, u32[]{:S(2)}, u32[]{:S(2)}) collective-permute-start(bf16[256,2560]{1,0:T(8,128)(2,1)} %get-tuple-element.130), channel_id=1, source_target_pairs={{0,2},{1,3},{2,0},{3,1},{4,6},{5,7},{6,4},{7,5},{8,10},{9,11},{10,... | collective-permute-start | bytes 3932168 | tf_op jit(solution)/shard_map/ppermute | solution.py:443
  657.8 34.7 %collective-permute-start.38 = (bf16[1280,128]{1,0:T(8,128)(2,1)S(1)}, bf16[1280,128]{1,0:T(8,128)(2,1)S(1)}, u32[]{:S(2)}, u32[]{:S(2)}) collective-permute-start(bf16[1280,128]{1,0:T(8,128)(2,1)S(1)} %select_convert_fusion), channel_id=1, source_target_pairs={{0,16},{4,20},{8,24},{12,28},{16,0},{20,4},{24,8},{28,12},{1,17},{... | collective-permute-start | bytes 983048 | tf_op jit(solution)/shard_map/ppermute | solution.py:443
  686.3 32.0 %collective-permute-start.27 = (bf16[256,2560]{1,0:T(8,128)(2,1)}, bf16[256,2560]{1,0:T(8,128)(2,1)}, u32[]{:S(2)}, u32[]{:S(2)}) collective-permute-start(bf16[256,2560]{1,0:T(8,128)(2,1)} %get-tuple-element.120), channel_id=1, source_target_pairs={{0,1},{1,0},{2,3},{3,2},{4,5},{5,4},{6,7},{7,6},{8,9},{9,8},{10,11... | collective-permute-start | bytes 3932168 | tf_op jit(solution)/shard_map/ppermute | solution.py:443
  687.6 60.1 %collective-permute-start.32 = (bf16[256,2560]{1,0:T(8,128)(2,1)}, bf16[256,2560]{1,0:T(8,128)(2,1)}, u32[]{:S(2)}, u32[]{:S(2)}) collective-permute-start(bf16[256,2560]{1,0:T(8,128)(2,1)} %get-tuple-element.134), channel_id=1, source_target_pairs={{0,2},{1,3},{2,0},{3,1},{4,6},{5,7},{6,4},{7,5},{8,10},{9,11},{10,... | collective-permute-start | bytes 3932168 | tf_op jit(solution)/shard_map/ppermute | solution.py:443
  690.2 55.0 %collective-permute-start.30 = (bf16[256,2560]{1,0:T(8,128)(2,1)}, bf16[256,2560]{1,0:T(8,128)(2,1)}, u32[]{:S(2)}, u32[]{:S(2)}) collective-permute-start(bf16[256,2560]{1,0:T(8,128)(2,1)} %add_convert_fusion), channel_id=1, source_target_pairs={{0,2},{1,3},{2,0},{3,1},{4,6},{5,7},{6,4},{7,5},{8,10},{9,11},{10,... | collective-permute-start | bytes 3932168 | tf_op jit(solution)/shard_map/ppermute | solution.py:443
  691.1 56.6 %collective-permute-start.31 = (bf16[256,2560]{1,0:T(8,128)(2,1)}, bf16[256,2560]{1,0:T(8,128)(2,1)}, u32[]{:S(2)}, u32[]{:S(2)}) collective-permute-start(bf16[256,2560]{1,0:T(8,128)(2,1)} %add_convert_fusion.1), channel_id=1, source_target_pairs={{0,1},{1,0},{2,3},{3,2},{4,5},{5,4},{6,7},{7,6},{8,9},{9,8},{10,11... | collective-permute-start | bytes 3932168 | tf_op jit(solution)/shard_map/ppermute | solution.py:443
  (69 other events, 1331.0 us)
Sparse Core Ops, SparseCore 0:
  12.9 74.9 all-gather.3
  89.6 65.4 all-gather.5
  156.7 65.4 all-gather.7
  337.4 73.4 reduce-scatter.7
  511.1 73.3 reduce-scatter.5
  586.7 70.6 reduce-scatter.3

commit v3 on v2

--- a/solution.py
+++ b/solution.py
@@ -47,29 +47,40 @@
     return jnp.concatenate([jnp.where(low_half, v, zero), jnp.where(low_half, zero, v)], axis=0)
 
 
-def conv_at(halo, taps_ref, bias_ref, cols, start):
-    total = bias_ref[:, cols] + taps_ref[0:1, cols] * halo[start : start + Q, cols]
+def shifts(first_row, count, step):
+    rows = lax.broadcasted_iota(jnp.int32, (count * Q, Q + 16), 0)
+    lanes = lax.broadcasted_iota(jnp.int32, (count * Q, Q + 16), 1)
+    part = lax.div(rows, Q)
+    return (lanes == first_row + step * part + lax.rem(rows, Q)).astype(F32).astype(BF16)
+
+
+def open_chunk(taps_ref, back_ref, prior, vp_ref, cols):
+    now = vp_ref[:, cols]
+    moved = mm(back_ref[...], jnp.concatenate([prior[:, cols], now], axis=0))
+    seen = [moved[k * Q : (k + 1) * Q] for k in range(3)] + [now.astype(F32)]
+    half = taps_ref[4:5, cols] + taps_ref[0:1, cols] * seen[0]
     for k in range(1, 4):
-        total = total + taps_ref[k : k + 1, cols] * halo[start + k : start + k + Q, cols]
-    return total
+        half = half + taps_ref[k : k + 1, cols] * seen[k]
+    return seen, half, jnp.tanh(half)
 
 
 def scan_forward(
-    seat_ref, vp_ref, bc_ref, st_ref, taps_ref, bias_ref, rate_ref, skip_ref,
-    y_ref, hold_ref, state, halo, *, pairs
+    seat_ref, vp_ref, bc_ref, st_ref, taps_ref, rate_ref, skip_ref,
+    y_ref, hold_ref, state, halo, shut, *, pairs
 ):
+    rows = lax.broadcasted_iota(jnp.int32, (Q, Q), 0)
+    lanes = lax.broadcasted_iota(jnp.int32, (Q, Q), 1)
+
     @pl.when(pl.program_id(0) == 0)
     def _():
         state[...] = jnp.zeros_like(state)
         halo[0:8, :] = jnp.zeros_like(halo[0:8, :])
+        shut[...] = jnp.where(rows >= lanes, 0.0, NEG)
 
     halo[8 : 8 + Q, :] = vp_ref[...].astype(F32)
-    rows = lax.broadcasted_iota(jnp.int32, (Q, Q), 0)
-    lanes = lax.broadcasted_iota(jnp.int32, (Q, Q), 1)
-    causal = rows >= lanes
     low_half = lanes < P_SIZE
     steps = st_ref[...]
-    lam = mm_exact(causal.astype(F32), steps * rate_ref[...])
+    lam = mm_exact((rows >= lanes).astype(F32), steps * rate_ref[...])
     source_t = (lam - jnp.log(steps)).T
     grown = jnp.exp(lam)
     last = lam[Q - 1 : Q, :]
@@ -82,11 +93,13 @@
     for pair in range(pairs):
         cols = slice(pair * LANES, (pair + 1) * LANES)
         first = 2 * pair
-        conv = conv_at(halo, taps_ref, bias_ref, cols, 5)
-        x = conv * sigmoid(conv)
+        half = taps_ref[4:5, cols] + taps_ref[0:1, cols] * halo[5 : 5 + Q, cols]
+        for k in range(1, 4):
+            half = half + taps_ref[k : k + 1, cols] * halo[5 + k : 5 + k + Q, cols]
+        x = half * jnp.tanh(half) + half
         mixing = []
         for h in (first, first + 1):
-            gap = jnp.where(causal, lam[:, h : h + 1] - source_t[h : h + 1, :], NEG)
+            gap = lam[:, h : h + 1] - source_t[h : h + 1, :] + shut[...]
             mixing.append((scores * jnp.exp(gap)).astype(BF16))
         y = mm(jnp.concatenate(mixing, axis=1), halves(low_half, x).astype(BF16))
         held = state[:, cols]
@@ -101,44 +114,45 @@
 
 
 def scan_backward(
-    seat_ref, vp_ref, before_ref, dy_ref, bc_ref, st_ref, hold_ref, taps_ref, bias_ref, rate_ref, skip_ref, pick_ref,
+    seat_ref, vp_ref, before_ref, dy_ref, bc_ref, st_ref, hold_ref, taps_ref, rate_ref, skip_ref, pick_ref,
     dvp_ref, dbc_ref, dst_ref, gconv_ref, gdecay_ref,
-    halo, gbuf, ds, ds_low, across, r_cols, w_rows, state_terms, inter_terms, fed_all, dyl_all, e_rows, *, pairs, blocks
+    prior, g_next, back, ahead, shut, ds, ds_low, across, w_cols, w_rows, state_terms, inter_terms, fed_all, dyl_all,
+    e_rows, *, pairs, blocks
 ):
     step_id = pl.program_id(0)
+    rows = lax.broadcasted_iota(jnp.int32, (Q, Q), 0)
+    lanes = lax.broadcasted_iota(jnp.int32, (Q, Q), 1)
 
     @pl.when(step_id == 0)
     def _():
         ds[...] = jnp.zeros_like(ds)
-        gbuf[Q : Q + 8, :] = jnp.zeros_like(gbuf[Q : Q + 8, :])
+        g_next[...] = jnp.zeros_like(g_next)
         gconv_ref[...] = jnp.zeros_like(gconv_ref)
         gdecay_ref[...] = jnp.zeros_like(gdecay_ref)
-        r_cols[...] = jnp.zeros_like(r_cols)
+        w_cols[...] = jnp.zeros_like(w_cols)
         w_rows[...] = jnp.zeros_like(w_rows)
         e_rows[...] = jnp.zeros_like(e_rows)
-
-    halo[16 : 16 + Q, :] = vp_ref[...].astype(F32)
+        back[...] = shifts(13, 3, 1)
+        ahead[...] = shifts(1, 3, 1)
+        shut[...] = jnp.where(lanes >= rows, 0.0, NEG)
 
     @pl.when(step_id < blocks - 1)
     def _():
-        halo[0:16, :] = before_ref[...].astype(F32)
+        prior[...] = before_ref[...]
 
     @pl.when(step_id == blocks - 1)
     def _():
-        halo[0:16, :] = jnp.zeros_like(halo[0:16, :])
-
-    rows = lax.broadcasted_iota(jnp.int32, (Q, Q), 0)
-    lanes = lax.broadcasted_iota(jnp.int32, (Q, Q), 1)
-    causal = rows >= lanes
-    later = lanes >= rows
+        prior[...] = jnp.zeros_like(prior)
+
     low_half = lanes < P_SIZE
     steps = st_ref[...]
     rate = rate_ref[...]
-    lam = mm_exact(causal.astype(F32), steps * rate)
+    lam = mm_exact((rows >= lanes).astype(F32), steps * rate)
     lam_t = lam.T
+    source = lam - jnp.log(steps)
     grown = jnp.exp(lam)
     last = lam[Q - 1 : Q, :]
-    reach = jnp.exp(last - lam)
+    weight = jnp.exp(last - lam) * steps
     fade = jnp.exp(last)
     b_rows = bc_ref[:, :N]
     c_rows = bc_ref[:, N:]
@@ -147,22 +161,20 @@
     for pair in range(pairs):
         cols = slice(pair * LANES, (pair + 1) * LANES)
         first = 2 * pair
-        conv = conv_at(halo, taps_ref, bias_ref, cols, 13)
-        gate = sigmoid(conv)
-        x = conv * gate
+        seen, half, bend = open_chunk(taps_ref, back, prior, vp_ref, cols)
+        x = half * bend + half
         dy = dy_ref[:, cols]
         dy_wide = dy.astype(F32)
         q_t = nt_dot(halves(low_half, x).astype(BF16), dy)
         mixing = []
         crossed = None
         for at, h in enumerate((first, first + 1)):
-            step_col = steps[:, h : h + 1]
-            decay = jnp.exp(jnp.where(later, lam_t[h : h + 1, :] - lam[:, h : h + 1], NEG))
-            seen = decay * q_t[at * Q : (at + 1) * Q]
-            stepped = seen * step_col
+            decay = jnp.exp(lam_t[h : h + 1, :] - source[:, h : h + 1] + shut[...])
+            stepped = decay * q_t[at * Q : (at + 1) * Q]
             crossed = stepped if crossed is None else crossed + stepped
-            r_cols[:, h : h + 1] = jnp.sum(seen * scores_t, axis=1, keepdims=True)
-            w_rows[h : h + 1, :] = jnp.sum(stepped * scores_t, axis=0, keepdims=True)
+            both = stepped * scores_t
+            w_cols[:, h : h + 1] = jnp.sum(both, axis=1, keepdims=True)
+            w_rows[h : h + 1, :] = jnp.sum(both, axis=0, keepdims=True)
             mixing.append((decay * scores_t).astype(BF16))
         if pair == 0:
             across[...] = crossed
@@ -172,12 +184,11 @@
         d_state = ds[:, cols]
         d_state_low = d_state.astype(BF16)
         ds_low[:, cols] = d_state_low
-        step_pair = pair_cols(low_half, steps, first)
-        reach_pair = pair_cols(low_half, reach, first)
-        carried = reach_pair * mm(b_rows, d_state_low)
-        dx = step_pair * (dx + carried) + skip_ref[:, cols] * dy_wide
+        weight_pair = pair_cols(low_half, weight, first)
+        carried = weight_pair * mm(b_rows, d_state_low)
+        dx = dx + carried + skip_ref[:, cols] * dy_wide
         state_terms[:, cols] = (x * carried).astype(BF16)
-        fed_all[:, cols] = (x * (reach_pair * step_pair)).astype(BF16)
+        fed_all[:, cols] = (x * weight_pair).astype(BF16)
         held = hold_ref[0, :, cols]
         dyl = dy_wide * pair_cols(low_half, grown, first)
         dyl_low = dyl.astype(BF16)
@@ -185,19 +196,18 @@
         inter_terms[:, cols] = (dyl * mm(c_rows, held)).astype(BF16)
         e_rows[0:1, cols] = jnp.sum(d_state * held.astype(F32), axis=0, keepdims=True)
         ds[:, cols] = d_state * pair_cols(low_half[0:1], fade, first) + mm(c_t, dyl_low)
-        g = dx * (gate * (1.0 + conv * (1.0 - gate)))
-        gbuf[0:Q, cols] = g
+        g = dx * ((0.5 + 0.5 * bend) * (1.0 + half * (1.0 - bend)))
         for k in range(4):
-            gconv_ref[k : k + 1, cols] += jnp.sum(g * halo[13 + k : 13 + k + Q, cols], axis=0, keepdims=True)
+            gconv_ref[k : k + 1, cols] += jnp.sum(g * seen[k], axis=0, keepdims=True)
         gconv_ref[4:5, cols] += jnp.sum(g, axis=0, keepdims=True)
         gconv_ref[5:6, cols] += jnp.sum(dy_wide * x, axis=0, keepdims=True)
+        g_low = g.astype(BF16)
+        moved = mm(ahead[...], jnp.concatenate([g_low, g_next[:, cols]], axis=0))
         d_pre = taps_ref[3:4, cols] * g
-        for k in range(1, 4):
-            d_pre = d_pre + taps_ref[3 - k : 4 - k, cols] * gbuf[k : k + Q, cols]
-        dvp_ref[:, cols] = d_pre.astype(dvp_ref.dtype)
-        gbuf[Q : Q + 8, cols] = g[0:8]
-    if dvp_ref.shape[1] > pairs * LANES:
-        dvp_ref[:, pairs * LANES :] = jnp.zeros_like(dvp_ref[:, pairs * LANES :])
+        for k in range(3):
+            d_pre = d_pre + taps_ref[2 - k : 3 - k, cols] * moved[k * Q : (k + 1) * Q]
+        dvp_ref[:, cols] = (2.0 * d_pre).astype(dvp_ref.dtype)
+        g_next[:, cols] = g_low[0:16]
     cross = across[...]
     d_b = mm(cross.astype(BF16), c_rows) + nt_dot(fed_all[...], ds_low[...])
     d_c = mm(turned(cross), b_rows) + nt_dot(dyl_all[...], hold_ref[0])
@@ -209,14 +219,14 @@
     e_high = e_rows[...].astype(BF16)
     e_rest = (e_rows[...] - e_high.astype(F32)).astype(BF16)
     through = (mm(e_high, pick) + mm(e_rest, pick))[0:1]
-    r_all = r_cols[...]
-    d_lam = w_rows[...].T - steps * r_all + from_carry
+    w_all = w_cols[...]
+    d_lam = w_rows[...].T - w_all + from_carry
     d_log = (
-        mm_exact(later.astype(F32), d_lam)
-        + mm_exact((rows > lanes).astype(F32), steps * from_state)
+        mm_exact((lanes >= rows).astype(F32), d_lam)
+        + mm_exact((rows > lanes).astype(F32), from_state)
         + fade * through
     )
-    dst_ref[...] = r_all + from_state + rate * d_log
+    dst_ref[...] = (w_all + from_state) / jnp.maximum(steps, 1e-37) + rate * d_log
     gdecay_ref[...] += jnp.sum(steps * d_log, axis=0, keepdims=True)
 
 
@@ -224,7 +234,7 @@
     return (lax.div(i, per) ^ seat[0]) * per + lax.rem(i, per)
 
 
-def run_forward(seat, pre, states_in, steps, taps, bias, rate, skip, shards):
+def run_forward(seat, pre, states_in, steps, taps, rate, skip, shards):
     tokens = steps.shape[0]
     width = taps.shape[1]
     blocks = tokens // Q
@@ -245,8 +255,7 @@
                 pl.BlockSpec((Q, width), moved),
                 pl.BlockSpec((Q, 2 * N), plain),
                 pl.BlockSpec((Q, LANES), plain),
-                pl.BlockSpec((4, width), fixed),
-                pl.BlockSpec((1, width), fixed),
+                pl.BlockSpec((8, width), fixed),
                 pl.BlockSpec((1, LANES), fixed),
                 pl.BlockSpec((1, width), fixed),
             ],
@@ -254,16 +263,20 @@
                 pl.BlockSpec((Q, width), moved),
                 pl.BlockSpec((1, N, width), lambda i, seat: (i, 0, 0)),
             ],
-            scratch_shapes=[pltpu.VMEM((N, width), F32), pltpu.VMEM((Q + 8, width), F32)],
+            scratch_shapes=[
+                pltpu.VMEM((N, width), F32),
+                pltpu.VMEM((Q + 8, width), F32),
+                pltpu.VMEM((Q, Q), F32),
+            ],
         ),
         cost_estimate=pl.CostEstimate(
             flops=tokens * width * 1200, bytes_accessed=tokens * width * 10, transcendentals=tokens * width * 3
         ),
         name="scan_forward",
-    )(seat, pre, states_in, steps, taps, bias, rate, skip)
-
-
-def run_backward(seat, pre, dy, states_in, steps, held, taps, bias, rate, skip, pick, shards, out_width):
+    )(seat, pre, states_in, steps, taps, rate, skip)
+
+
+def run_backward(seat, pre, dy, states_in, steps, held, taps, rate, skip, pick, shards):
     tokens = steps.shape[0]
     width = taps.shape[1]
     blocks = tokens // Q
@@ -279,7 +292,7 @@
     return pl.pallas_call(
         functools.partial(scan_backward, pairs=width // LANES, blocks=blocks),
         out_shape=(
-            jax.ShapeDtypeStruct((tokens, out_width), BF16),
+            jax.ShapeDtypeStruct((tokens, width), BF16),
             jax.ShapeDtypeStruct((tokens, 2 * N), BF16),
             jax.ShapeDtypeStruct((tokens, LANES), F32),
             jax.ShapeDtypeStruct((8, width), F32),
@@ -295,22 +308,24 @@
                 pl.BlockSpec((Q, 2 * N), plain),
                 pl.BlockSpec((Q, LANES), plain),
                 pl.BlockSpec((1, N, width), lambda i, seat: (blocks - 1 - i, 0, 0)),
-                pl.BlockSpec((4, width), fixed),
-                pl.BlockSpec((1, width), fixed),
+                pl.BlockSpec((8, width), fixed),
                 pl.BlockSpec((1, LANES), fixed),
                 pl.BlockSpec((1, width), fixed),
                 pl.BlockSpec((width, LANES), fixed),
             ],
             out_specs=[
-                pl.BlockSpec((Q, out_width), moved),
+                pl.BlockSpec((Q, width), moved),
                 pl.BlockSpec((Q, 2 * N), plain),
                 pl.BlockSpec((Q, LANES), plain),
                 pl.BlockSpec((8, width), fixed),
                 pl.BlockSpec((1, LANES), fixed),
             ],
             scratch_shapes=[
-                pltpu.VMEM((Q + 16, width), F32),
-                pltpu.VMEM((Q + 8, width), F32),
+                pltpu.VMEM((16, width), BF16),
+                pltpu.VMEM((16, width), BF16),
+                pltpu.VMEM((3 * Q, Q + 16), BF16),
+                pltpu.VMEM((3 * Q, Q + 16), BF16),
+                pltpu.VMEM((Q, Q), F32),
                 pltpu.VMEM((N, width), F32),
                 pltpu.VMEM((N, width), BF16),
                 pltpu.VMEM((Q, Q), F32),
@@ -327,7 +342,7 @@
             flops=tokens * width * 3000, bytes_accessed=tokens * width * 14, transcendentals=tokens * width * 4
         ),
         name="scan_backward",
-    )(seat, pre, pre, dy, states_in, steps, held, taps, bias, rate, skip, pick)
+    )(seat, pre, pre, dy, states_in, steps, held, taps, rate, skip, pick)
 
 
 EPSILON = 1e-05
@@ -342,25 +357,30 @@
 
 
 def fill_kernel(x_ref, w_ref, *refs):
-    refs[-1][...] = mm(x_ref[...], w_ref[...])
+    value_ref, small_ref = refs[-2:]
+    wide = value_ref.shape[1]
+    small_ref[...] = mm(x_ref[...], w_ref[:, wide:])
+    value_ref[...] = mm(x_ref[...], w_ref[:, :wide]).astype(BF16)
 
 
 def run_fill(x, w, into, rows, first, block):
     depth, width = w.shape
+    wide = width - LANES
+    place = lambda i: (i + first, 0)
     return pl.pallas_call(
         fill_kernel,
-        out_shape=jax.ShapeDtypeStruct((rows, width), F32),
+        out_shape=(jax.ShapeDtypeStruct((rows, wide), BF16), jax.ShapeDtypeStruct((rows, LANES), F32)),
         grid=(x.shape[0] // block,),
         in_specs=[
             pl.BlockSpec((block, depth), lambda i: (i, 0)),
             pl.BlockSpec((depth, width), lambda i: (0, 0), pipeline_mode=pl.Buffered(1)),
         ]
         + [pl.BlockSpec(memory_space=pl.ANY)] * len(into),
-        out_specs=pl.BlockSpec((block, width), lambda i: (i + first, 0)),
-        input_output_aliases={2: 0} if into else {},
+        out_specs=(pl.BlockSpec((block, wide), place), pl.BlockSpec((block, LANES), place)),
+        input_output_aliases={2: 0, 3: 1} if into else {},
         cost_estimate=pl.CostEstimate(
             flops=2 * x.shape[0] * depth * width,
-            bytes_accessed=2 * (x.shape[0] + width) * depth + 4 * x.shape[0] * width,
+            bytes_accessed=2 * (x.shape[0] + width) * (depth + width),
             transcendentals=0,
         ),
         name="value_product",
@@ -466,15 +486,27 @@
         parts = jnp.where(self.x, parts[:, ::-1], parts)
         return parts.reshape(v.shape)
 
-    def gather_begin(self, v):
-        return [v, swap(v, 1), swap(v, 2)]
-
-    def gather_end(self, pieces):
-        half = pieces[0].shape[0] // 2
-        return pieces + [swap(pieces[1][:half], 2), swap(pieces[2][half:], 1)]
+    def gather_whole(self, v):
+        from_x, from_y = swap(v, 1), swap(v, 2)
+        half = v.shape[0] // 2
+        relay_y = swap(from_x[:half], 2)
+        relay_x = swap(from_y[half:], 1)
+        return [v, from_x, from_y, relay_y, relay_x]
+
+    def gather_top(self, v):
+        half = v.shape[0] // 2
+        top, low = v[:half], v[half:]
+        return [v, low, swap(top, 1), swap(top, 2)]
+
+    def gather_low(self, parts):
+        v, low, x_top, y_top = parts
+        x_low, y_low = swap(low, 1), swap(low, 2)
+        relay_y = swap(x_top, 2)
+        return [v, x_top, x_low, y_top, y_low, relay_y, swap(y_low, 1)]
 
     def gather_flat(self, v):
-        return self.settle(jnp.concatenate([v, swap(v, 1), swap(v, 2), swap(v, 3)]))
+        others = [swap(v, bit) for bit in (1, 2, 3)]
+        return self.settle(jnp.concatenate([v] + others))
 
     def token_sum(self, v):
         parts = v.reshape(2, 2, -1)
@@ -539,11 +571,14 @@
     def settle(self, v):
         return v
 
-    def gather_begin(self, v):
+    def gather_whole(self, v):
         return [lax.all_gather(v, "col", axis=0, tiled=True)]
 
-    def gather_end(self, pieces):
-        return pieces
+    def gather_top(self, v):
+        return self.gather_whole(v)
+
+    def gather_low(self, parts):
+        return parts
 
     def gather_flat(self, v):
         return lax.all_gather(v, "col", axis=0, tiled=True)
@@ -631,7 +666,6 @@
     bc_width = w_bc.shape[1]
     wide = -(-channels // LANES) * LANES
     full_width = wide + LANES
-    step_at = wide + bc_width
     piece_rows = hidden.shape[0]
 
     w_cat = lax.all_gather(
@@ -647,23 +681,24 @@
         scale = lax.rsqrt(jnp.mean(rows * rows, axis=1, keepdims=True) + EPSILON)
         return (rows * scale * full_gain).astype(BF16)
 
-    hidden_pieces = lines.gather_end(lines.gather_begin(hidden))
+    hidden_pieces = lines.gather_whole(hidden)
     near = jnp.concatenate([normalized(piece) for piece in hidden_pieces[:3]])
     far = [normalized(piece) for piece in hidden_pieces[3:]]
     grad_source, _ = tied(grad_out, hidden_pieces[-1])
-    grad_pieces = lines.gather_begin(grad_source)
+    grad_pieces = lines.gather_top(grad_source)
 
     if far:
         far = jnp.concatenate(far)
         tokens_here = near.shape[0] + far.shape[0]
-        pre = run_fill(near, w_cat, (), tokens_here, 0, 256)
-        pre = run_fill(far, w_cat, (pre,), tokens_here, near.shape[0] // 256, 256)
+        filled = run_fill(near, w_cat, (), tokens_here, 0, 256)
+        pre, pre_small = run_fill(far, w_cat, filled, tokens_here, near.shape[0] // 256, 256)
         normal_in = jnp.concatenate([near, far])
     else:
         normal_in = near
-        pre = mm(normal_in, w_cat)
-    bc_pre = lines.settle(pre[:, wide : wide + bc_width])
-    step_sum = lines.settle(pre[:, step_at : step_at + heads]) + step_bias
+        pre = mm(normal_in, w_cat[:, :wide]).astype(BF16)
+        pre_small = mm(normal_in, w_cat[:, wide:])
+    bc_pre = lines.settle(pre_small[:, :bc_width])
+    step_sum = lines.settle(pre_small[:, bc_width : bc_width + heads]) + step_bias
 
     def state_branch(pre_vals, conv_weight, conv_offset):
         return swish(causal_conv(pre_vals, conv_weight, conv_offset))
@@ -673,18 +708,19 @@
     steps = widened(jax.nn.softplus(step_sum), LANES)
     rate = widened(-jnp.exp(decay_log), LANES)[None]
     skip = widened(jnp.repeat(skip_gain, P_SIZE), wide)[None]
-    taps = widened(conv_value, wide)
-    offsets = widened(conv_value_bias, wide)[None]
+    taps = 0.5 * jnp.concatenate([conv_value, conv_value_bias[None], jnp.zeros((3, channels), F32)])
+    taps = widened(taps, wide)
     pick = (jnp.arange(wide)[:, None] // P_SIZE == jnp.arange(LANES)[None]).astype(BF16)
-    heads_out, held = run_forward(lines.seat, pre, states, steps, taps, offsets, rate, skip, lines.shards)
-
-    heads_out, *grad_pieces = tied(heads_out, *grad_pieces)
-    grad_pieces = lines.gather_end(grad_pieces)
+    states, *grad_pieces = tied(states, *grad_pieces)
+    grad_pieces = lines.gather_low(grad_pieces)
+    heads_out, held = run_forward(lines.seat, pre, states, steps, taps, rate, skip, lines.shards)
+
     gate_pre = mm(normal_in, w_gate_full).astype(BF16)
     ho = heads_out[:, :channels].astype(F32)
     gate = gate_pre.astype(F32)
     gated = ho * swish(gate)
-    squares = lines.token_sum(jnp.sum(gated * gated, axis=1))
+    squares = jnp.sum(gated * gated, axis=1)
+    squares = lines.token_sum(squares)
     mix = lax.rsqrt(squares / inner_width + EPSILON)[:, None]
     normed = (gated * mix * norm_gain).astype(BF16)
     normed, *grad_pieces = tied(normed, *grad_pieces)
@@ -711,16 +747,17 @@
     g_gate_part = row_major(tn_dot(normal_in, d_gate).astype(BF16))
     sent, came = lines.scatter_relay(kept, came)
     d_heads, g_gate_part, *sent = tied(d_heads, g_gate_part, *sent)
-    g_gate = row_scatter(g_gate_part)
+    g_gate_sent, g_out_t = tied(g_gate_part, g_out_t)
+    g_gate = row_scatter(g_gate_sent)
 
     d_value, d_states, d_steps, g_conv, g_decay = run_backward(
-        lines.seat, pre, widened(d_heads, wide), states, steps, held, taps, offsets, rate, skip, pick,
-        lines.shards, wide,
+        lines.seat, pre, widened(d_heads, wide), states, steps, held, taps, rate, skip, pick, lines.shards
     )
     state_parts = lines.split_states(d_states)
     normal_in, *state_parts = tied(normal_in, *state_parts)
     g_value_part = row_major(tn_dot(normal_in, d_value).astype(BF16))
-    g_value = row_scatter(g_value_part)
+    g_value_sent, g_gate = tied(g_value_part, g_gate)
+    g_value = row_scatter(g_value_sent)
     branch_out = lines.scatter_end(sent, came)
     result = (hidden.astype(F32) + branch_out).astype(BF16)
     d_state_local, result, g_value_part = tied(lines.scatter_states(state_parts), result, g_value_part)

time: 782 us -> 753 us (0.963)
  Pallas kernels: 218 us -> 197 us
    pallas_call x1, Pallas kernels: 88.3 us -> 69.4 us  [run_backward(): pl.pallas_call(functools.partial(scan_backward, pairs=width // LANES, blo...]
    ppermute x44 -> x46, waiting for transfers between devices: 245 us -> 239 us  [swap(): return lax.ppermute(v, axis, [(i, i ^ bit) for i in range(size)])]
    ppermute x44 -> x46, starting transfers between devices: 45.3 us -> 45.6 us  [swap(): return lax.ppermute(v, axis, [(i, i ^ bit) for i in range(size)])]
  transfers between devices with their start and end apart: 50 -> 52, of which waited for: 20 -> 19; matrix products, arithmetic and copies ran while one was open for 26% -> 30% of each run, Pallas kernels for 28% -> 26%
where the time goes in v3:
time: 753 us; the launch traced here: 744 us
  waiting for transfers between devices  240 us (32%)
  Pallas kernels  197 us (26%)
  matrix products  108 us (14%)
  other arithmetic  102 us (14%)
  starting transfers between devices  45.8 us (6%)
  local copies, waits for them, and re-layouts  37.3 us (5%)
  between operations  15.5 us (2%)
    ppermute x46, waiting for transfers between devices, swap(): return lax.ppermute(v, axis, [(i, i ^ bit) for i in range(size)])  239 us
    pallas_call x1, Pallas kernels, run_backward(): pl.pallas_call(functools.partial(scan_backward, pairs=width // LANES, blo...  69.4 us
    dot_general x4, matrix products, tn_dot(): lax.dot_general(a, b, (((0,), (0,)), ((), ())), preferred_element_type=F32)  61.2 us
    pallas_call x4, Pallas kernels, run_rows(): pl.pallas_call(rows_kernel, out_shape=[jax.ShapeDtypeStruct((rows // 2, w...  49.3 us
    dot_general x2, matrix products, mm(): return jnp.dot(a, b, preferred_element_type=F32)  46.4 us
    ppermute x46, starting transfers between devices, swap(): return lax.ppermute(v, axis, [(i, i ^ bit) for i in range(size)])  45.6 us
    pallas_call x1, Pallas kernels, run_forward(): pl.pallas_call(functools.partial(scan_forward, pairs=width // LANES), out...  33 us
    pallas_call x2, Pallas kernels, run_fill(): pl.pallas_call(fill_kernel, out_shape=(jax.ShapeDtypeStruct((rows, wide),...  26.4 us
  transfers between devices with their start and end apart: 52, of which 19 were waited for; matrix products, arithmetic and copies ran while one was open for 30% of the time, Pallas kernels for 26%

profile of v3, /device:TPU:0, one launch (start us, length us, event | category | flops | bytes accessed | tf_op | source)
XLA Modules:
  0.0 743.9 jit_solution(15370003329431080967)
XLA Ops:
  26.9 49.5 %collective-permute-done.3 = bf16[512,2560]{1,0:T(8,128)(2,1)} collective-permute-done((bf16[512,2560]{1,0:T(8,128)(2,1)S(1)}, bf16[512,2560]{1,0:T(8,128)(2,1)}, u32[]{:S(2)}, u32[]{:S(2)}) %collective-permute-start.3) | collective-permute-done | bytes 2621472 | tf_op jit(solution)/shard_map/ppermute | solution.py:463
  95.8 18.5 %collective-permute-done.6 = bf16[256,2560]{1,0:T(8,128)(2,1)S(1)} collective-permute-done((bf16[256,2560]{1,0:T(8,128)(2,1)S(1)}, bf16[256,2560]{1,0:T(8,128)(2,1)S(1)}, u32[]{:S(2)}, u32[]{:S(2)}) %collective-permute-start.6) | collective-permute-done | bytes 1310752 | tf_op jit(solution)/shard_map/ppermute | solution.py:463
  119.4 4.0 copy-done.20
  125.1 17.5 %value_product.2 = (bf16[2048,1280]{1,0:T(8,128)(2,1)}, f32[2048,128]{1,0:T(8,128)}) custom-call(bf16[1536,2560]{1,0:T(8,128)(2,1)} %pad_maximum_fusion.x_ref, bf16[2560,1408]{1,0:T(8,128)(2,1)} %all-gather.4.cloned.1.call-done.w_ref.w_cat_ref), custom_call_target="tpu_custom_call" | custom-call | flops 11072962560 | bytes 23363584 | tf_op jit(solution)/shard_map/value_product/pallas_call | solution.py:370
  142.6 8.9 %value_product.3 = (bf16[2048,1280]{1,0:T(8,128)(2,1)}, f32[2048,128]{1,0:T(8,128)}) custom-call(bf16[512,2560]{1,0:T(8,128)(2,1)} %pad_maximum_fusion.1.x_ref, bf16[2560,1408]{1,0:T(8,128)(2,1)} %all-gather.4.cloned.1.call-done.w_ref.w_cat_ref, bf16[2048,1280]{1,0:T(8,128)(2,1)} %get-tuple-element.89.refs_0_, ...), custom_call_target="tpu_custom_call", output_to_operand_aliasing={{0}: (2, {}), {1}: (3, {})} | custom-call | flops 3690987520 | bytes 15237120 | tf_op jit(solution)/shard_map/value_product/pallas_call | solution.py:370
  160.7 16.2 %collective-permute-done.7 = bf16[2048,64]{1,0:T(8,128)(2,1)S(1)} collective-permute-done((bf16[2048,64]{1,0:T(8,128)(2,1)S(1)}, bf16[2048,64]{1,0:T(8,128)(2,1)S(1)}, u32[]{:S(2)}, u32[]{:S(2)}) %collective-permute-start.7) | collective-permute-done | bytes 262176 | tf_op jit(solution)/shard_map/ppermute | solution.py:463
  181.6 33.0 %scan_forward.1 = (bf16[2048,1280]{1,0:T(8,128)(2,1)}, bf16[16,128,1280]{2,1,0:T(8,128)(2,1)}) custom-call(s32[1]{0:T(128)} %bitcast.seat_ref, bf16[2048,1280]{1,0:T(8,128)(2,1)} %get-tuple-element.91.vp_ref.before_ref, bf16[2048,256]{1,0:T(8,128)(2,1)} %pad_maximum_fusion.2.bc_ref, f32[2048,128]{1,0:T(8,128)} %pad.51.st_ref, ...), custom_call_target="tpu_custom_call" | custom-call | flops 3145728000 | bytes 26214400 | tf_op jit(solution)/shard_map/scan_forward/pallas_call | solution.py:245
  214.7 21.6 %multiply_reduce_fusion.2 = (f32[2048]{0:T(1024)S(1)}, bf16[2048,1280]{1,0:T(8,128)(2,1)}) fusion(bf16[2048,1280]{1,0:T(8,128)(2,1)} %get-tuple-element.95, bf16[2048,2560]{1,0:T(8,128)(2,1)} %copy-done.20, bf16[2560,1280]{1,0:T(8,128)(2,1)} %all-gather.6.cloned.1.call-done.w_gate_ref), kind=kOutput, calls=%fused_computation.30 | convolution fusion | flops 13447985152 | bytes 27533312 | tf_op jit(solution)/shard_map/dot_general | solution.py:30
  244.6 7.5 %multiply_convert_fusion.x_ref = bf16[2048,1280]{1,0:T(8,128)(2,1)S(1)} fusion(f32[1280]{0:T(1024)S(1)} %copy-done.23, f32[2048]{0:T(1024)S(1)} %bitcast.69, bf16[2048,1280]{1,0:T(8,128)(2,1)} %get-tuple-element.228, bf16[2048,1280]{1,0:T(8,128)(2,1)} %get-tuple-element.95), kind=kLoop, calls=%fused_computation.29 | loop fusion | flops 26214400 | bytes 15741952 | tf_op jit(solution)/shard_map/convert_element_type | solution.py:725
  252.1 20.4 %collective-permute-done.14 = bf16[256,2560]{1,0:T(8,128)(2,1)S(1)} collective-permute-done((bf16[256,2560]{1,0:T(8,128)(2,1)}, bf16[256,2560]{1,0:T(8,128)(2,1)S(1)}, u32[]{:S(2)}, u32[]{:S(2)}) %collective-permute-start.14) | collective-permute-done | bytes 1310752 | tf_op jit(solution)/shard_map/ppermute | solution.py:463
  272.5 23.3 %collective-permute-done.17 = bf16[256,2560]{1,0:T(8,128)(2,1)S(1)} collective-permute-done((bf16[256,2560]{1,0:T(8,128)(2,1)}, bf16[256,2560]{1,0:T(8,128)(2,1)S(1)}, u32[]{:S(2)}, u32[]{:S(2)}) %collective-permute-start.17) | collective-permute-done | bytes 1310752 | tf_op jit(solution)/shard_map/ppermute | solution.py:463
  300.5 3.8 copy-done.21
  304.3 15.9 %convolution_convert_fusion.2 = bf16[2560,1280]{1,0:T(8,128)(2,1)} fusion(bf16[2048,2560]{1,0:T(8,128)(2,1)S(1)} %constant_dynamic-update-slice_fusion.5, bf16[2048,1280]{1,0:T(8,128)(2,1)S(1)} %multiply_convert_fusion.x_ref), kind=kOutput, calls=%fused_computation.14 | convolution fusion | flops 13425049600 | bytes 22282240 | tf_op jit(solution)/shard_map/dot_general | solution.py:356
  320.3 24.7 %fusion.7 = (f32[1280]{0:T(1024)S(1)}, f32[2048]{0:T(1024)S(1)}, bf16[2048,1280]{1,0:T(8,128)(2,1)}) fusion(f32[2048]{0:T(1024)S(1)} %bitcast.70, bf16[2048,1280]{1,0:T(8,128)(2,1)} %get-tuple-element.228, bf16[2048,1280]{1,0:T(8,128)(2,1)} %get-tuple-element.95, f32[1280]{0:T(1024)S(1)} %copy-done.23, bf16[2048,2560]{1,0:T(8,128)(2,1)} %copy-done.21, ...), kind=kOutput, calls=%fused_computation.20 | convolution fusion | flops 13461091328 | bytes 32794624 | tf_op jit(solution)/shard_map/dot_general | solution.py:30
  350.5 18.4 %split_product.1 = (bf16[256,2560]{1,0:T(8,128)(2,1)}, bf16[256,2560]{1,0:T(8,128)(2,1)}, bf16[256,2560]{1,0:T(8,128)(2,1)}, bf16[256,2560]{1,0:T(8,128)(2,1)}, ...) custom-call(bf16[2048,1280]{1,0:T(8,128)(2,1)} %copy-done.9, ...), custom_call_target="tpu_custom_call" | custom-call | flops 13421772800 | bytes 22282240 | tf_op jit(solution)/shard_map/split_product/pallas_call | solution.py:400
  369.6 13.1 %fusion.5 = (bf16[2048,1280]{1,0:T(8,128)(2,1)S(1)}, bf16[2048,1280]{1,0:T(8,128)(2,1)}) fusion(bf16[2048,1280]{1,0:T(8,128)(2,1)} %get-tuple-element.95, bf16[2048,1280]{1,0:T(8,128)(2,1)} %get-tuple-element.228, bf16[2048,1280]{1,0:T(8,128)(2,1)} %get-tuple-element.229, f32[2048]{0:T(1024)S(1)} %fusion.39, f32[1280]{0:T(1024)S(1)} %copy-done.23, ...), kind=kLoop, calls=%fused_computation.18 | loop fusion | flops 57671680 | bytes 26235904 | tf_op jit(solution)/shard_map/convert_element_type | solution.py:746
  385.0 18.6 %convolution_convert_fusion.1 = bf16[2560,1280]{1,0:T(8,128)(2,1)} fusion(bf16[2048,2560]{1,0:T(8,128)(2,1)} %copy-done.20, bf16[2048,1280]{1,0:T(8,128)(2,1)S(1)} %get-tuple-element.202.gate_ref), kind=kOutput, calls=%fused_computation.13 | convolution fusion | flops 13425049600 | bytes 22282240 | tf_op jit(solution)/shard_map/dot_general | solution.py:356
  414.4 69.4 %scan_backward.1 = (bf16[2048,1280]{1,0:T(8,128)(2,1)}, bf16[2048,256]{1,0:T(8,128)(2,1)}, f32[2048,128]{1,0:T(8,128)}, f32[8,1280]{1,0:T(8,128)}, f32[1,128]{1,0:T(1,128)}) custom-call(s32[1]{0:T(128)} %bitcast.seat_ref, bf16[2048,1280]{1,0:T(8,128)(2,1)} %get-tuple-element.91.vp_ref.before_ref, bf16[2048,1280]{1,0:T(8,128)(2,1)} %get-tuple-element.91.vp_ref.before_ref, ...), custom_call_target="tpu_custom_call" | custom-call | flops 7864320000 | bytes 36700160 | tf_op jit(solution)/shard_map/scan_backward/pallas_call | solution.py:292
  491.7 19.1 %convolution_convert_fusion = bf16[2560,1280]{1,0:T(8,128)(2,1)} fusion(bf16[2048,2560]{1,0:T(8,128)(2,1)} %copy-done.20, bf16[2048,1280]{1,0:T(8,128)(2,1)S(1)} %copy-done.47), kind=kOutput, calls=%fused_computation.12 | convolution fusion | flops 13425049600 | bytes 22282240 | tf_op jit(solution)/shard_map/dot_general | solution.py:356
  512.1 27.9 %collective-permute-done.23 = bf16[2048,64]{1,0:T(8,128)(2,1)} collective-permute-done((bf16[2048,64]{1,0:T(8,128)(2,1)}, bf16[2048,64]{1,0:T(8,128)(2,1)}, u32[]{:S(2)}, u32[]{:S(2)}) %collective-permute-start.23) | collective-permute-done | bytes 262176 | tf_op jit(solution)/shard_map/ppermute | solution.py:463
  544.6 16.5 %collective-permute-done.28 = bf16[256,2560]{1,0:T(8,128)(2,1)S(1)} collective-permute-done((bf16[256,2560]{1,0:T(8,128)(2,1)}, bf16[256,2560]{1,0:T(8,128)(2,1)S(1)}, u32[]{:S(2)}, u32[]{:S(2)}) %collective-permute-start.28) | collective-permute-done | bytes 1310752 | tf_op jit(solution)/shard_map/ppermute | solution.py:463
  569.7 12.6 %rows_product.4 = (bf16[256,2560]{1,0:T(8,128)(2,1)}, bf16[256,2560]{1,0:T(8,128)(2,1)}) custom-call(bf16[2048,1280]{1,0:T(8,128)(2,1)} %copy-done.10, bf16[2048,1280]{1,0:T(8,128)(2,1)} %get-tuple-element.141.value_ref, bf16[2048,128]{1,0:T(8,128)(2,1)} %bitcast.64, bf16[2560,1280]{1,0:T(8,128)(2,1)} %all-gather.6.cloned.1.call-done.w_gate_ref, ...), custom_call_target="tpu_custom_call" | custom-call | flops 7046430720 | bytes 19136512 | tf_op jit(solution)/shard_map/rows_product/pallas_call | solution.py:432
  582.5 12.2 %rows_product.5 = (bf16[256,2560]{1,0:T(8,128)(2,1)}, bf16[256,2560]{1,0:T(8,128)(2,1)}) custom-call(bf16[2048,1280]{1,0:T(8,128)(2,1)} %copy-done.10, bf16[2048,1280]{1,0:T(8,128)(2,1)} %get-tuple-element.141.value_ref, bf16[2048,128]{1,0:T(8,128)(2,1)} %bitcast.65, bf16[2560,1280]{1,0:T(8,128)(2,1)} %all-gather.6.cloned.1.call-done.w_gate_ref, ...), custom_call_target="tpu_custom_call" | custom-call | flops 7046430720 | bytes 19136512 | tf_op jit(solution)/shard_map/rows_product/pallas_call | solution.py:432
  596.1 12.2 %rows_product.6 = (bf16[256,2560]{1,0:T(8,128)(2,1)}, bf16[256,2560]{1,0:T(8,128)(2,1)}) custom-call(bf16[2048,1280]{1,0:T(8,128)(2,1)} %copy-done.10, bf16[2048,1280]{1,0:T(8,128)(2,1)} %get-tuple-element.141.value_ref, bf16[2048,128]{1,0:T(8,128)(2,1)} %bitcast.66, bf16[2560,1280]{1,0:T(8,128)(2,1)} %all-gather.6.cloned.1.call-done.w_gate_ref, ...), custom_call_target="tpu_custom_call" | custom-call | flops 7046430720 | bytes 19136512 | tf_op jit(solution)/shard_map/rows_product/pallas_call | solution.py:432
  608.5 12.3 %rows_product.7 = (bf16[256,2560]{1,0:T(8,128)(2,1)}, bf16[256,2560]{1,0:T(8,128)(2,1)}) custom-call(bf16[2048,1280]{1,0:T(8,128)(2,1)} %copy-done.10, bf16[2048,1280]{1,0:T(8,128)(2,1)} %get-tuple-element.141.value_ref, bf16[2048,128]{1,0:T(8,128)(2,1)} %bitcast.67, bf16[2560,1280]{1,0:T(8,128)(2,1)} %all-gather.6.cloned.1.call-done.w_gate_ref, ...), custom_call_target="tpu_custom_call" | custom-call | flops 7046430720 | bytes 19136512 | tf_op jit(solution)/shard_map/rows_product/pallas_call | solution.py:432
  627.1 7.5 %multiply_reduce_fusion.3 = (f32[2560]{0:T(1024)S(1)}, f32[2560,128]{1,0:T(8,128)S(1)}) fusion(bf16[2560,1408]{1,0:T(8,128)(2,1)} %all-gather.4.cloned.1.call-done.w_ref.w_cat_ref, bf16[2048,2560]{1,0:T(8,128)(2,1)} %copy-done.20, bf16[2048,128]{1,0:T(8,128)(2,1)S(1)} %bitcast.68), kind=kOutput, calls=%fused_computation.84 | convolution fusion | flops 1343157760 | bytes 12986368 | tf_op jit(solution)/shard_map/dot_general | solution.py:356
  638.2 4.8 multiply_reduce_fusion
  643.0 6.6 multiply_reduce_fusion.1
  673.0 4.6 collective-permute-done.41
  681.8 14.0 %collective-permute-done.29 = bf16[256,2560]{1,0:T(8,128)(2,1)} collective-permute-done((bf16[256,2560]{1,0:T(8,128)(2,1)}, bf16[256,2560]{1,0:T(8,128)(2,1)}, u32[]{:S(2)}, u32[]{:S(2)}) %collective-permute-start.29) | collective-permute-done | bytes 1310752 | tf_op jit(solution)/shard_map/ppermute | solution.py:463
  695.7 27.3 %collective-permute-done.32 = bf16[256,2560]{1,0:T(8,128)(2,1)} collective-permute-done((bf16[256,2560]{1,0:T(8,128)(2,1)}, bf16[256,2560]{1,0:T(8,128)(2,1)}, u32[]{:S(2)}, u32[]{:S(2)}) %collective-permute-start.32) | collective-permute-done | bytes 1310752 | tf_op jit(solution)/shard_map/ppermute | solution.py:463
  729.6 4.8 fusion.29
  (327 shorter events, 161.4 us)
Async XLA Ops:
  7.2 117.9 %all-gather.4.cloned.1.call-start = ((), (), s32[]{:S(2)}) async-start(), calls=%async_computation.3 | async-start | bytes 8110080 | tf_op jit(solution)/shard_map/all_gather | solution.py:671
  12.8 201.9 %all-gather.6.cloned.1.call-start = ((), (), s32[]{:S(2)}) async-start(), calls=%async_computation.4 | async-start | bytes 7372800 | tf_op jit(solution)/shard_map/all_gather | solution.py:675
  13.5 306.7 %all-gather.8.cloned.1.call-start = ((), (), s32[]{:S(2)}) async-start(), calls=%async_computation.5 | async-start | bytes 7372800 | tf_op jit(solution)/shard_map/all_gather | solution.py:676
  18.2 58.2 %collective-permute-start.3 = (bf16[512,2560]{1,0:T(8,128)(2,1)S(1)}, bf16[512,2560]{1,0:T(8,128)(2,1)}, u32[]{:S(2)}, u32[]{:S(2)}) collective-permute-start(bf16[512,2560]{1,0:T(8,128)(2,1)S(1)} %copy-done), channel_id=1, source_target_pairs={{0,1},{1,0},{2,3},{3,2},{4,5},{5,4},{6,7},{7,6},{8,9},{9,8},{10,11... | collective-permute-start | bytes 7864328 | tf_op jit(solution)/shard_map/ppermute | solution.py:463
  20.1 58.6 %collective-permute-start.4 = (bf16[512,2560]{1,0:T(8,128)(2,1)S(1)}, bf16[512,2560]{1,0:T(8,128)(2,1)}, u32[]{:S(2)}, u32[]{:S(2)}) collective-permute-start(bf16[512,2560]{1,0:T(8,128)(2,1)S(1)} %copy-done), channel_id=1, source_target_pairs={{0,2},{1,3},{2,0},{3,1},{4,6},{5,7},{6,4},{7,5},{8,10},{9,11},{10,... | collective-permute-start | bytes 7864328 | tf_op jit(solution)/shard_map/ppermute | solution.py:463
  21.6 387.4 %reduce-scatter.4.cloned.1.call-start = ((), (), s32[]{:S(2)}) async-start(), calls=%async_computation.6 | async-start | bytes 7372800 | tf_op jit(solution)/shard_map/reduce_scatter | solution.py:641
  82.5 35.5 %collective-permute-start.5 = (bf16[256,2560]{1,0:T(8,128)(2,1)S(1)}, bf16[256,2560]{1,0:T(8,128)(2,1)S(1)}, u32[]{:S(2)}, u32[]{:S(2)}) collective-permute-start(bf16[256,2560]{1,0:T(8,128)(2,1)S(1)} %slice.176), channel_id=1, source_target_pairs={{0,2},{1,3},{2,0},{3,1},{4,6},{5,7},{6,4},{7,5},{8,10},{9,11},{10,... | collective-permute-start | bytes 3932168 | tf_op jit(solution)/shard_map/ppermute | solution.py:463
  85.6 28.7 %collective-permute-start.6 = (bf16[256,2560]{1,0:T(8,128)(2,1)S(1)}, bf16[256,2560]{1,0:T(8,128)(2,1)S(1)}, u32[]{:S(2)}, u32[]{:S(2)}) collective-permute-start(bf16[256,2560]{1,0:T(8,128)(2,1)S(1)} %slice.177), channel_id=1, source_target_pairs={{0,1},{1,0},{2,3},{3,2},{4,5},{5,4},{6,7},{7,6},{8,9},{9,8},{10,11... | collective-permute-start | bytes 3932168 | tf_op jit(solution)/shard_map/ppermute | solution.py:463
  116.0 64.0 %collective-permute-start.10 = (bf16[256,2560]{1,0:T(8,128)(2,1)}, bf16[256,2560]{1,0:T(8,128)(2,1)}, u32[]{:S(2)}, u32[]{:S(2)}) collective-permute-start(bf16[256,2560]{1,0:T(8,128)(2,1)} %get-tuple-element.204), channel_id=1, source_target_pairs={{0,1},{1,0},{2,3},{3,2},{4,5},{5,4},{6,7},{7,6},{8,9},{9,8},{10,11... | collective-permute-start | bytes 3932168 | tf_op jit(solution)/shard_map/ppermute | solution.py:463
  117.5 62.5 %collective-permute-start.11 = (bf16[256,2560]{1,0:T(8,128)(2,1)}, bf16[256,2560]{1,0:T(8,128)(2,1)}, u32[]{:S(2)}, u32[]{:S(2)}) collective-permute-start(bf16[256,2560]{1,0:T(8,128)(2,1)} %get-tuple-element.204), channel_id=1, source_target_pairs={{0,2},{1,3},{2,0},{3,1},{4,6},{5,7},{6,4},{7,5},{8,10},{9,11},{10,... | collective-permute-start | bytes 3932168 | tf_op jit(solution)/shard_map/ppermute | solution.py:463
  180.0 64.0 %collective-permute-start.15 = (bf16[256,2560]{1,0:T(8,128)(2,1)}, bf16[256,2560]{1,0:T(8,128)(2,1)}, u32[]{:S(2)}, u32[]{:S(2)}) collective-permute-start(bf16[256,2560]{1,0:T(8,128)(2,1)} %get-tuple-element.98), channel_id=1, source_target_pairs={{0,2},{1,3},{2,0},{3,1},{4,6},{5,7},{6,4},{7,5},{8,10},{9,11},{10,... | collective-permute-start | bytes 3932168 | tf_op jit(solution)/shard_map/ppermute | solution.py:463
  240.6 31.9 %collective-permute-start.14 = (bf16[256,2560]{1,0:T(8,128)(2,1)}, bf16[256,2560]{1,0:T(8,128)(2,1)S(1)}, u32[]{:S(2)}, u32[]{:S(2)}) collective-permute-start(bf16[256,2560]{1,0:T(8,128)(2,1)} %get-tuple-element.98), channel_id=1, source_target_pairs={{0,1},{1,0},{2,3},{3,2},{4,5},{5,4},{6,7},{7,6},{8,9},{9,8},{10,11... | collective-permute-start | bytes 3932168 | tf_op jit(solution)/shard_map/ppermute | solution.py:463
  241.6 30.9 %collective-permute-start.16 = (bf16[256,2560]{1,0:T(8,128)(2,1)}, bf16[256,2560]{1,0:T(8,128)(2,1)S(1)}, u32[]{:S(2)}, u32[]{:S(2)}) collective-permute-start(bf16[256,2560]{1,0:T(8,128)(2,1)} %collective-permute-done.10), channel_id=1, source_target_pairs={{0,2},{1,3},{2,0},{3,1},{4,6},{5,7},{6,4},{7,5},{8,10},{9,11},{10,... | collective-permute-start | bytes 3932168 | tf_op jit(solution)/shard_map/ppermute | solution.py:463
  244.1 51.7 %collective-permute-start.17 = (bf16[256,2560]{1,0:T(8,128)(2,1)}, bf16[256,2560]{1,0:T(8,128)(2,1)S(1)}, u32[]{:S(2)}, u32[]{:S(2)}) collective-permute-start(bf16[256,2560]{1,0:T(8,128)(2,1)} %collective-permute-done.15), channel_id=1, source_target_pairs={{0,1},{1,0},{2,3},{3,2},{4,5},{5,4},{6,7},{7,6},{8,9},{9,8},{10,11... | collective-permute-start | bytes 3932168 | tf_op jit(solution)/shard_map/ppermute | solution.py:463
  320.3 246.0 %reduce-scatter.6.cloned.1.call-start = ((), (), s32[]{:S(2)}) async-start(), calls=%async_computation.7 | async-start | bytes 7372800 | tf_op jit(solution)/shard_map/reduce_scatter | solution.py:641
  368.9 34.8 %collective-permute-start.21 = (bf16[256,2560]{1,0:T(8,128)(2,1)}, bf16[256,2560]{1,0:T(8,128)(2,1)}, u32[]{:S(2)}, u32[]{:S(2)}) collective-permute-start(bf16[256,2560]{1,0:T(8,128)(2,1)} %get-tuple-element.114), channel_id=1, source_target_pairs={{0,1},{1,0},{2,3},{3,2},{4,5},{5,4},{6,7},{7,6},{8,9},{9,8},{10,11... | collective-permute-start | bytes 3932168 | tf_op jit(solution)/shard_map/ppermute | solution.py:463
  368.9 37.4 %collective-permute-start.20 = (bf16[256,2560]{1,0:T(8,128)(2,1)}, bf16[256,2560]{1,0:T(8,128)(2,1)}, u32[]{:S(2)}, u32[]{:S(2)}) collective-permute-start(bf16[256,2560]{1,0:T(8,128)(2,1)} %get-tuple-element.112), channel_id=1, source_target_pairs={{0,2},{1,3},{2,0},{3,1},{4,6},{5,7},{6,4},{7,5},{8,10},{9,11},{10,... | collective-permute-start | bytes 3932168 | tf_op jit(solution)/shard_map/ppermute | solution.py:463
  411.5 322.9 %reduce-scatter.8.cloned.1.call-start = ((), (), s32[]{:S(2)}) async-start(), calls=%async_computation.8 | async-start | bytes 7372800 | tf_op jit(solution)/shard_map/reduce_scatter | solution.py:641
  412.5 129.3 %collective-permute-start.25 = (bf16[256,2560]{1,0:T(8,128)(2,1)}, bf16[256,2560]{1,0:T(8,128)(2,1)}, u32[]{:S(2)}, u32[]{:S(2)}) collective-permute-start(bf16[256,2560]{1,0:T(8,128)(2,1)} %get-tuple-element.123), channel_id=1, source_target_pairs={{0,1},{1,0},{2,3},{3,2},{4,5},{5,4},{6,7},{7,6},{8,9},{9,8},{10,11... | collective-permute-start | bytes 3932168 | tf_op jit(solution)/shard_map/ppermute | solution.py:463
  486.7 55.1 %collective-permute-start.26 = (bf16[256,2560]{1,0:T(8,128)(2,1)}, bf16[256,2560]{1,0:T(8,128)(2,1)}, u32[]{:S(2)}, u32[]{:S(2)}) collective-permute-start(bf16[256,2560]{1,0:T(8,128)(2,1)} %add_convert_fusion.2), channel_id=1, source_target_pairs={{0,2},{1,3},{2,0},{3,1},{4,6},{5,7},{6,4},{7,5},{8,10},{9,11},{10,... | collective-permute-start | bytes 3932168 | tf_op jit(solution)/shard_map/ppermute | solution.py:463
  488.2 23.3 %collective-permute-start.22 = (bf16[2048,64]{1,0:T(8,128)(2,1)}, bf16[2048,64]{1,0:T(8,128)(2,1)S(1)}, u32[]{:S(2)}, u32[]{:S(2)}) collective-permute-start(bf16[2048,64]{1,0:T(8,128)(2,1)} %get-tuple-element.119), channel_id=1, source_target_pairs={{0,1},{1,0},{2,3},{3,2},{4,5},{5,4},{6,7},{7,6},{8,9},{9,8},{10,11... | collective-permute-start | bytes 786440 | tf_op jit(solution)/shard_map/ppermute | solution.py:463
  488.4 51.7 %collective-permute-start.23 = (bf16[2048,64]{1,0:T(8,128)(2,1)}, bf16[2048,64]{1,0:T(8,128)(2,1)}, u32[]{:S(2)}, u32[]{:S(2)}) collective-permute-start(bf16[2048,64]{1,0:T(8,128)(2,1)} %get-tuple-element.120), channel_id=1, source_target_pairs={{0,2},{1,3},{2,0},{3,1},{4,6},{5,7},{6,4},{7,5},{8,10},{9,11},{10,... | collective-permute-start | bytes 786440 | tf_op jit(solution)/shard_map/ppermute | solution.py:463
  488.9 51.5 %collective-permute-start.24 = (bf16[2048,64]{1,0:T(8,128)(2,1)}, bf16[2048,64]{1,0:T(8,128)(2,1)}, u32[]{:S(2)}, u32[]{:S(2)}) collective-permute-start(bf16[2048,64]{1,0:T(8,128)(2,1)} %get-tuple-element.121), channel_id=1, source_target_pairs={{0,3},{1,2},{2,1},{3,0},{4,7},{5,6},{6,5},{7,4},{8,11},{9,10},{10,... | collective-permute-start | bytes 786440 | tf_op jit(solution)/shard_map/ppermute | solution.py:463
  511.5 49.6 %collective-permute-start.28 = (bf16[256,2560]{1,0:T(8,128)(2,1)}, bf16[256,2560]{1,0:T(8,128)(2,1)S(1)}, u32[]{:S(2)}, u32[]{:S(2)}) collective-permute-start(bf16[256,2560]{1,0:T(8,128)(2,1)} %get-tuple-element.127), channel_id=1, source_target_pairs={{0,2},{1,3},{2,0},{3,1},{4,6},{5,7},{6,4},{7,5},{8,10},{9,11},{10,... | collective-permute-start | bytes 3932168 | tf_op jit(solution)/shard_map/ppermute | solution.py:463
  582.3 38.5 %collective-permute-start.31 = (bf16[256,2560]{1,0:T(8,128)(2,1)}, bf16[256,2560]{1,0:T(8,128)(2,1)}, u32[]{:S(2)}, u32[]{:S(2)}) collective-permute-start(bf16[256,2560]{1,0:T(8,128)(2,1)} %get-tuple-element.136), channel_id=1, source_target_pairs={{0,1},{1,0},{2,3},{3,2},{4,5},{5,4},{6,7},{7,6},{8,9},{9,8},{10,11... | collective-permute-start | bytes 3932168 | tf_op jit(solution)/shard_map/ppermute | solution.py:463
  594.7 29.3 %collective-permute-start.30 = (bf16[256,2560]{1,0:T(8,128)(2,1)}, bf16[256,2560]{1,0:T(8,128)(2,1)}, u32[]{:S(2)}, u32[]{:S(2)}) collective-permute-start(bf16[256,2560]{1,0:T(8,128)(2,1)} %get-tuple-element.148), channel_id=1, source_target_pairs={{0,2},{1,3},{2,0},{3,1},{4,6},{5,7},{6,4},{7,5},{8,10},{9,11},{10,... | collective-permute-start | bytes 3932168 | tf_op jit(solution)/shard_map/ppermute | solution.py:463
  627.1 22.5 %collective-permute-start.43 = (f32[8060]{0:T(1024)S(1)}, f32[8060]{0:T(1024)S(1)}, u32[]{:S(2)}, u32[]{:S(2)}) collective-permute-start(f32[8060]{0:T(1024)S(1)} %concatenate.55), channel_id=1, source_target_pairs={{0,4},{4,0},{8,12},{12,8},{16,20},{20,16},{24,28},{28,24},{1,5},{5... | collective-permute-start | bytes 96728 | tf_op jit(solution)/shard_map/ppermute | solution.py:463
  635.8 35.0 %collective-permute-start.40 = (bf16[1280,128]{1,0:T(8,128)(2,1)S(1)}, bf16[1280,128]{1,0:T(8,128)(2,1)S(1)}, u32[]{:S(2)}, u32[]{:S(2)}) collective-permute-start(bf16[1280,128]{1,0:T(8,128)(2,1)S(1)} %select_convert_fusion), channel_id=1, source_target_pairs={{0,16},{4,20},{8,24},{12,28},{16,0},{20,4},{24,8},{28,12},{1,17},{... | collective-permute-start | bytes 983048 | tf_op jit(solution)/shard_map/ppermute | solution.py:463
  663.8 32.0 %collective-permute-start.29 = (bf16[256,2560]{1,0:T(8,128)(2,1)}, bf16[256,2560]{1,0:T(8,128)(2,1)}, u32[]{:S(2)}, u32[]{:S(2)}) collective-permute-start(bf16[256,2560]{1,0:T(8,128)(2,1)} %get-tuple-element.138), channel_id=1, source_target_pairs={{0,1},{1,0},{2,3},{3,2},{4,5},{5,4},{6,7},{7,6},{8,9},{9,8},{10,11... | collective-permute-start | bytes 3932168 | tf_op jit(solution)/shard_map/ppermute | solution.py:463
  665.3 60.3 %collective-permute-start.34 = (bf16[256,2560]{1,0:T(8,128)(2,1)}, bf16[256,2560]{1,0:T(8,128)(2,1)}, u32[]{:S(2)}, u32[]{:S(2)}) collective-permute-start(bf16[256,2560]{1,0:T(8,128)(2,1)} %get-tuple-element.152), channel_id=1, source_target_pairs={{0,2},{1,3},{2,0},{3,1},{4,6},{5,7},{6,4},{7,5},{8,10},{9,11},{10,... | collective-permute-start | bytes 3932168 | tf_op jit(solution)/shard_map/ppermute | solution.py:463
  668.2 54.9 %collective-permute-start.32 = (bf16[256,2560]{1,0:T(8,128)(2,1)}, bf16[256,2560]{1,0:T(8,128)(2,1)}, u32[]{:S(2)}, u32[]{:S(2)}) collective-permute-start(bf16[256,2560]{1,0:T(8,128)(2,1)} %add_convert_fusion), channel_id=1, source_target_pairs={{0,2},{1,3},{2,0},{3,1},{4,6},{5,7},{6,4},{7,5},{8,10},{9,11},{10,... | collective-permute-start | bytes 3932168 | tf_op jit(solution)/shard_map/ppermute | solution.py:463
  669.4 56.3 %collective-permute-start.33 = (bf16[256,2560]{1,0:T(8,128)(2,1)}, bf16[256,2560]{1,0:T(8,128)(2,1)}, u32[]{:S(2)}, u32[]{:S(2)}) collective-permute-start(bf16[256,2560]{1,0:T(8,128)(2,1)} %add_convert_fusion.1), channel_id=1, source_target_pairs={{0,1},{1,0},{2,3},{3,2},{4,5},{5,4},{6,7},{7,6},{8,9},{9,8},{10,11... | collective-permute-start | bytes 3932168 | tf_op jit(solution)/shard_map/ppermute | solution.py:463
  (70 other events, 1505.8 us)
Sparse Core Ops, SparseCore 0:
  12.9 74.9 all-gather.3
  89.6 65.4 all-gather.5
  156.7 65.4 all-gather.7
  320.4 72.3 reduce-scatter.3
  411.6 73.4 reduce-scatter.5
  568.8 72.1 reduce-scatter.7

commit v4 on v3

--- a/solution.py
+++ b/solution.py
@@ -356,35 +356,60 @@
     return lax.dot_general(a, b, (((0,), (0,)), ((), ())), preferred_element_type=F32)
 
 
-def fill_kernel(x_ref, w_ref, *refs):
-    value_ref, small_ref = refs[-2:]
+def fill_kernel(*refs, spans):
+    gain_ref, w_ref = refs[len(spans) : len(spans) + 2]
+    normal_ref, value_ref, small_ref = refs[-3:]
+    step_id = pl.program_id(0)
     wide = value_ref.shape[1]
-    small_ref[...] = mm(x_ref[...], w_ref[:, wide:])
-    value_ref[...] = mm(x_ref[...], w_ref[:, :wide]).astype(BF16)
-
-
-def run_fill(x, w, into, rows, first, block):
+    for (start, stop), piece_ref in zip(spans, refs):
+
+        @pl.when((step_id >= start) & (step_id < stop))
+        def _(piece_ref=piece_ref):
+            rows = piece_ref[...].astype(F32)
+            scale = lax.rsqrt(jnp.mean(rows * rows, axis=1, keepdims=True) + EPSILON)
+            normal_ref[...] = (rows * scale * gain_ref[...]).astype(BF16)
+
+    small_ref[...] = mm(normal_ref[...], w_ref[:, wide:])
+    value_ref[...] = mm(normal_ref[...], w_ref[:, :wide]).astype(BF16)
+
+
+def run_fill(pieces, gain, w, into, rows, first, block):
     depth, width = w.shape
     wide = width - LANES
     place = lambda i: (i + first, 0)
+    spans = []
+    specs = []
+    at = 0
+    for piece in pieces:
+        blocks = piece.shape[0] // block
+        spans.append((at, at + blocks))
+        specs.append(pl.BlockSpec((block, depth), lambda i, at=at, blocks=blocks: (jnp.clip(i - at, 0, blocks - 1), 0)))
+        at += blocks
     return pl.pallas_call(
-        fill_kernel,
-        out_shape=(jax.ShapeDtypeStruct((rows, wide), BF16), jax.ShapeDtypeStruct((rows, LANES), F32)),
-        grid=(x.shape[0] // block,),
-        in_specs=[
-            pl.BlockSpec((block, depth), lambda i: (i, 0)),
+        functools.partial(fill_kernel, spans=spans),
+        out_shape=(
+            jax.ShapeDtypeStruct((rows, depth), BF16),
+            jax.ShapeDtypeStruct((rows, wide), BF16),
+            jax.ShapeDtypeStruct((rows, LANES), F32),
+        ),
+        grid=(at,),
+        in_specs=specs
+        + [
+            pl.BlockSpec((1, depth), lambda i: (0, 0)),
             pl.BlockSpec((depth, width), lambda i: (0, 0), pipeline_mode=pl.Buffered(1)),
         ]
         + [pl.BlockSpec(memory_space=pl.ANY)] * len(into),
-        out_specs=(pl.BlockSpec((block, wide), place), pl.BlockSpec((block, LANES), place)),
-        input_output_aliases={2: 0, 3: 1} if into else {},
+        out_specs=(
+            pl.BlockSpec((block, depth), place), pl.BlockSpec((block, wide), place), pl.BlockSpec((block, LANES), place)
+        ),
+        input_output_aliases={len(pieces) + 2 + k: k for k in range(len(into))},
         cost_estimate=pl.CostEstimate(
-            flops=2 * x.shape[0] * depth * width,
-            bytes_accessed=2 * (x.shape[0] + width) * (depth + width),
+            flops=2 * at * block * depth * width,
+            bytes_accessed=2 * (at * block + width) * (depth + width),
             transcendentals=0,
         ),
         name="value_product",
-    )(x, w, *into)
+    )(*pieces, gain, w, *into)
 
 
 def split_kernel(x_ref, w_ref, *out_refs):
@@ -494,15 +519,17 @@
         return [v, from_x, from_y, relay_y, relay_x]
 
     def gather_top(self, v):
-        half = v.shape[0] // 2
-        top, low = v[:half], v[half:]
-        return [v, low, swap(top, 1), swap(top, 2)]
+        first, rest = v[: v.shape[0] // 4], v[v.shape[0] // 4 :]
+        return [v, rest, swap(first, 1), swap(first, 2)]
 
     def gather_low(self, parts):
-        v, low, x_top, y_top = parts
-        x_low, y_low = swap(low, 1), swap(low, 2)
-        relay_y = swap(x_top, 2)
-        return [v, x_top, x_low, y_top, y_low, relay_y, swap(y_low, 1)]
+        v, rest, x_first, y_first = parts
+        quarter = x_first.shape[0]
+        x_rest, y_rest = swap(rest, 1), swap(rest, 2)
+        far_first = swap(y_first, 1)
+        far_middle = swap(x_rest[: 2 * quarter], 2)
+        far_last = swap(y_rest[2 * quarter :], 1)
+        return [v, x_first, x_rest, y_first, y_rest, far_first, far_middle, far_last]
 
     def gather_flat(self, v):
         others = [swap(v, bit) for bit in (1, 2, 3)]
@@ -682,19 +709,18 @@
         return (rows * scale * full_gain).astype(BF16)
 
     hidden_pieces = lines.gather_whole(hidden)
-    near = jnp.concatenate([normalized(piece) for piece in hidden_pieces[:3]])
-    far = [normalized(piece) for piece in hidden_pieces[3:]]
+    near, far = hidden_pieces[:3], hidden_pieces[3:]
     grad_source, _ = tied(grad_out, hidden_pieces[-1])
     grad_pieces = lines.gather_top(grad_source)
 
     if far:
-        far = jnp.concatenate(far)
-        tokens_here = near.shape[0] + far.shape[0]
-        filled = run_fill(near, w_cat, (), tokens_here, 0, 256)
-        pre, pre_small = run_fill(far, w_cat, filled, tokens_here, near.shape[0] // 256, 256)
-        normal_in = jnp.concatenate([near, far])
+        tokens_here = 4 * piece_rows
+        half_rows = piece_rows // 2
+        filled = run_fill(near, full_gain[None], w_cat, (), tokens_here, 0, half_rows)
+        filled = run_fill(far, full_gain[None], w_cat, filled, tokens_here, 6, half_rows)
+        normal_in, pre, pre_small = filled
     else:
-        normal_in = near
+        normal_in = normalized(near[0])
         pre = mm(normal_in, w_cat[:, :wide]).astype(BF16)
         pre_small = mm(normal_in, w_cat[:, wide:])
     bc_pre = lines.settle(pre_small[:, :bc_width])
@@ -711,7 +737,7 @@
     taps = 0.5 * jnp.concatenate([conv_value, conv_value_bias[None], jnp.zeros((3, channels), F32)])
     taps = widened(taps, wide)
     pick = (jnp.arange(wide)[:, None] // P_SIZE == jnp.arange(LANES)[None]).astype(BF16)
-    states, *grad_pieces = tied(states, *grad_pieces)
+    states, *grad_pieces[:2] = tied(states, *grad_pieces[:2])
     grad_pieces = lines.gather_low(grad_pieces)
     heads_out, held = run_forward(lines.seat, pre, states, steps, taps, rate, skip, lines.shards)
 
@@ -745,8 +771,8 @@
     d_heads = (d_gated * gate * open_gate).astype(BF16)
     d_gate = (d_gated * ho * (open_gate * (1.0 + gate * (1.0 - open_gate)))).astype(BF16)
     g_gate_part = row_major(tn_dot(normal_in, d_gate).astype(BF16))
-    sent, came = lines.scatter_relay(kept, came)
-    d_heads, g_gate_part, *sent = tied(d_heads, g_gate_part, *sent)
+    early_sent, early_came = lines.scatter_relay(kept, came)
+    d_heads, g_gate_part, *early_sent = tied(d_heads, g_gate_part, *early_sent)
     g_gate_sent, g_out_t = tied(g_gate_part, g_out_t)
     g_gate = row_scatter(g_gate_sent)
 
@@ -758,9 +784,7 @@
     g_value_part = row_major(tn_dot(normal_in, d_value).astype(BF16))
     g_value_sent, g_gate = tied(g_value_part, g_gate)
     g_value = row_scatter(g_value_sent)
-    branch_out = lines.scatter_end(sent, came)
-    result = (hidden.astype(F32) + branch_out).astype(BF16)
-    d_state_local, result, g_value_part = tied(lines.scatter_states(state_parts), result, g_value_part)
+    d_state_local, g_value_part = tied(lines.scatter_states(state_parts), g_value_part)
     d_bc_pre, g_conv_bc, g_conv_bc_bias = state_back(d_state_local)
     d_step = d_steps[:, :heads] * sigmoid(step_sum)
     small = lines.settle(widened(jnp.concatenate([d_bc_pre, d_step], axis=1), LANES)).astype(BF16)
@@ -786,12 +810,14 @@
         jnp.sum(g_conv[5, :channels].reshape(heads, P_SIZE), axis=1),
         g_norm_gain,
     )
-    packed = jnp.concatenate([part.reshape(-1) for part in parts])
-    packed, last_part, normal_in, g_gate_part, g_value_part, *sent = tied(
-        packed, row_parts[0], normal_in, g_gate_part, g_value_part, *sent
+    sent_count = len(sent)
+    last_part, normal_in, g_gate_part, g_value_part, *held_back = tied(
+        row_parts[0], normal_in, g_gate_part, g_value_part, *sent, *early_came
     )
+    sent, early_came = held_back[:sent_count], held_back[sent_count:]
+    branch_out = lines.scatter_end(early_sent, early_came)
+    result = (hidden.astype(F32) + branch_out).astype(BF16)
     d_rows = lines.scatter_end(sent, came)
-    packed = row_sum(packed)
     g_small_part = tn_dot(normal_in, small)
     g_small = row_scatter_small(g_small_part)
     tokens = hidden.astype(F32)
@@ -802,12 +828,13 @@
     )
 
     g_in_gain = gain_sums(w_gate_full, g_gate_part, w_cat, g_value_part, g_small_part) / full_gain
-    g_in_gain = row_sum(lines.own_slice(lines.total(g_in_gain)))
+    packed = row_sum(jnp.concatenate([part.reshape(-1) for part in parts] + [g_in_gain]))
     summed = []
     at = 0
     for part in parts:
         summed.append(packed[at : at + part.size].reshape(part.shape))
         at += part.size
+    g_in_gain = lines.own_slice(lines.total(packed[at:]))
     return (
         result,
         grad_hidden,

time: 753 us -> 684 us (0.908)
  waiting for transfers between devices: 240 us -> 178 us
  other arithmetic: 102 us -> 82.4 us
    ppermute x46 -> x44, waiting for transfers between devices: 239 us -> 177 us  [swap(): return lax.ppermute(v, axis, [(i, i ^ bit) for i in range(size)])]
    unnamed x112 -> x103, local copies, waits for them, and re-layouts: 21.5 us -> 14.6 us
    ppermute x46 -> x44, starting transfers between devices: 45.6 us -> 49.9 us  [swap(): return lax.ppermute(v, axis, [(i, i ^ bit) for i in range(size)])]
    convert_element_type x2 -> x1, other arithmetic: 15.4 us -> 13 us  [body(): d_heads = (d_gated * gate * open_gate).astype(BF16)]
  transfers between devices with their start and end apart: 52 -> 50, of which waited for: 19 -> 17; matrix products, arithmetic and copies ran while one was open for 30% -> 31% of each run, Pallas kernels for 26% -> 30%
where the time goes in v4:
time: 684 us; the launch traced here: 673 us
  Pallas kernels  204 us (30%)
  waiting for transfers between devices  178 us (26%)
  matrix products  107 us (16%)
  other arithmetic  82.4 us (12%)
  starting transfers between devices  50.2 us (7%)
  local copies, waits for them, and re-layouts  36.4 us (5%)
  between operations  15.6 us (2%)
    ppermute x44, waiting for transfers between devices, swap(): return lax.ppermute(v, axis, [(i, i ^ bit) for i in range(size)])  177 us
    pallas_call x1, Pallas kernels, run_backward(): pl.pallas_call(functools.partial(scan_backward, pairs=width // LANES, blo...  69.4 us
    dot_general x4, matrix products, tn_dot(): lax.dot_general(a, b, (((0,), (0,)), ((), ())), preferred_element_type=F32)  61.1 us
    ppermute x44, starting transfers between devices, swap(): return lax.ppermute(v, axis, [(i, i ^ bit) for i in range(size)])  49.9 us
    pallas_call x4, Pallas kernels, run_rows(): pl.pallas_call(rows_kernel, out_shape=[jax.ShapeDtypeStruct((rows // 2, w...  48.9 us
    dot_general x2, matrix products, mm(): return jnp.dot(a, b, preferred_element_type=F32)  46.1 us
    pallas_call x2, Pallas kernels, run_fill(): pl.pallas_call(functools.partial(fill_kernel, spans=spans), out_shape=(ja...  33.8 us
    pallas_call x1, Pallas kernels, run_forward(): pl.pallas_call(functools.partial(scan_forward, pairs=width // LANES), out...  33.3 us
  transfers between devices with their start and end apart: 50, of which 17 were waited for; matrix products, arithmetic and copies ran while one was open for 31% of the time, Pallas kernels for 30%

profile of v4, /device:TPU:0, one launch (start us, length us, event | category | flops | bytes accessed | tf_op | source)
XLA Modules:
  0.0 673.3 jit_solution(14686115258359023958)
XLA Ops:
  21.2 51.2 %collective-permute-done.2.refs_2_ = bf16[512,2560]{1,0:T(8,128)(2,1)} collective-permute-done((bf16[512,2560]{1,0:T(8,128)(2,1)}, bf16[512,2560]{1,0:T(8,128)(2,1)}, u32[]{:S(2)}, u32[]{:S(2)}) %collective-permute-start.2) | collective-permute-done | bytes 2621472 | tf_op jit(solution)/shard_map/ppermute | solution.py:488
  84.1 21.0 %collective-permute-done.3.refs_1_ = bf16[256,2560]{1,0:T(8,128)(2,1)} collective-permute-done((bf16[256,2560]{1,0:T(8,128)(2,1)}, bf16[256,2560]{1,0:T(8,128)(2,1)}, u32[]{:S(2)}, u32[]{:S(2)}) %collective-permute-start.3) | collective-permute-done | bytes 1310752 | tf_op jit(solution)/shard_map/ppermute | solution.py:488
  108.8 23.1 %value_product.2 = (bf16[2048,2560]{1,0:T(8,128)(2,1)}, bf16[2048,1280]{1,0:T(8,128)(2,1)}, f32[2048,128]{1,0:T(8,128)}) custom-call(bf16[512,2560]{1,0:T(8,128)(2,1)} %refs_0_.1, bf16[512,2560]{1,0:T(8,128)(2,1)} %collective-permute-done.refs_1_, bf16[512,2560]{1,0:T(8,128)(2,1)} %collective-permute-done.2.refs_2_, f32[1,2560]{1,0:T(1,128)} %reshape.216.refs_3_.refs_2_, ...), custom_call_target="tpu_custom_call" | custom-call | flops 11072962560 | bytes 23363584 | tf_op jit(solution)/shard_map/value_product/pallas_call | solution.py:388
  132.0 10.6 %value_product.3 = (bf16[2048,2560]{1,0:T(8,128)(2,1)}, bf16[2048,1280]{1,0:T(8,128)(2,1)}, f32[2048,128]{1,0:T(8,128)}) custom-call(bf16[256,2560]{1,0:T(8,128)(2,1)} %collective-permute-done.1.refs_0_, bf16[256,2560]{1,0:T(8,128)(2,1)} %collective-permute-done.3.refs_1_, ...), custom_call_target="tpu_custom_call", output_to_operand_aliasing={{0}: (4, {}), {1}: (5, {}), {2}: (6, {})} | custom-call | flops 3690987520 | bytes 15237120 | tf_op jit(solution)/shard_map/value_product/pallas_call | solution.py:388
  151.9 17.4 %collective-permute-done.7 = bf16[2048,64]{1,0:T(8,128)(2,1)S(1)} collective-permute-done((bf16[2048,64]{1,0:T(8,128)(2,1)S(1)}, bf16[2048,64]{1,0:T(8,128)(2,1)S(1)}, u32[]{:S(2)}, u32[]{:S(2)}) %collective-permute-start.7) | collective-permute-done | bytes 262176 | tf_op jit(solution)/shard_map/ppermute | solution.py:488
  174.3 33.3 %scan_forward.1 = (bf16[2048,1280]{1,0:T(8,128)(2,1)}, bf16[16,128,1280]{2,1,0:T(8,128)(2,1)}) custom-call(s32[1]{0:T(128)} %bitcast.seat_ref, bf16[2048,1280]{1,0:T(8,128)(2,1)} %get-tuple-element.95.vp_ref.before_ref, bf16[2048,256]{1,0:T(8,128)(2,1)} %pad_maximum_fusion.bc_ref, f32[2048,128]{1,0:T(8,128)} %pad.51.st_ref, ...), custom_call_target="tpu_custom_call" | custom-call | flops 3145728000 | bytes 26214400 | tf_op jit(solution)/shard_map/scan_forward/pallas_call | solution.py:245
  207.6 21.6 %multiply_reduce_fusion.2 = (f32[2048]{0:T(1024)S(1)}, bf16[2048,1280]{1,0:T(8,128)(2,1)}) fusion(bf16[2048,1280]{1,0:T(8,128)(2,1)} %get-tuple-element.99, bf16[2048,2560]{1,0:T(8,128)(2,1)} %get-tuple-element.162, bf16[2560,1280]{1,0:T(8,128)(2,1)} %all-gather.6.cloned.1.call-done.w_gate_ref), kind=kOutput, calls=%fused_computation.30 | convolution fusion | flops 13447985152 | bytes 27533312 | tf_op jit(solution)/shard_map/dot_general | solution.py:30
  241.8 7.5 %multiply_convert_fusion.x_ref = bf16[2048,1280]{1,0:T(8,128)(2,1)S(1)} fusion(f32[1280]{0:T(1024)S(1)} %copy-done.21, f32[2048]{0:T(1024)S(1)} %bitcast.71, bf16[2048,1280]{1,0:T(8,128)(2,1)} %get-tuple-element.228, bf16[2048,1280]{1,0:T(8,128)(2,1)} %get-tuple-element.99), kind=kLoop, calls=%fused_computation.29 | loop fusion | flops 26214400 | bytes 15741952 | tf_op jit(solution)/shard_map/convert_element_type | solution.py:751
  252.6 14.0 %collective-permute-done.16 = bf16[128,2560]{1,0:T(8,128)(2,1)S(1)} collective-permute-done((bf16[128,2560]{1,0:T(8,128)(2,1)S(1)}, bf16[128,2560]{1,0:T(8,128)(2,1)S(1)}, u32[]{:S(2)}, u32[]{:S(2)}) %collective-permute-start.16) | collective-permute-done | bytes 655392 | tf_op jit(solution)/shard_map/ppermute | solution.py:488
  266.6 8.9 %collective-permute-done.18 = bf16[128,2560]{1,0:T(8,128)(2,1)S(1)} collective-permute-done((bf16[128,2560]{1,0:T(8,128)(2,1)S(1)}, bf16[128,2560]{1,0:T(8,128)(2,1)S(1)}, u32[]{:S(2)}, u32[]{:S(2)}) %collective-permute-start.18) | collective-permute-done | bytes 655392 | tf_op jit(solution)/shard_map/ppermute | solution.py:488
  279.4 3.9 copy-done.17
  283.2 15.9 %convolution_convert_fusion.2 = bf16[2560,1280]{1,0:T(8,128)(2,1)} fusion(bf16[2048,2560]{1,0:T(8,128)(2,1)S(1)} %constant_dynamic-update-slice_fusion, bf16[2048,1280]{1,0:T(8,128)(2,1)S(1)} %multiply_convert_fusion.x_ref), kind=kOutput, calls=%fused_computation.14 | convolution fusion | flops 13425049600 | bytes 22282240 | tf_op jit(solution)/shard_map/dot_general | solution.py:356
  299.2 24.5 %fusion.7 = (f32[1280]{0:T(1024)S(1)}, f32[2048]{0:T(1024)S(1)}, bf16[2048,1280]{1,0:T(8,128)(2,1)}) fusion(f32[2048]{0:T(1024)S(1)} %bitcast.72, bf16[2048,1280]{1,0:T(8,128)(2,1)} %get-tuple-element.228, bf16[2048,1280]{1,0:T(8,128)(2,1)} %get-tuple-element.99, f32[1280]{0:T(1024)S(1)} %copy-done.21, bf16[2048,2560]{1,0:T(8,128)(2,1)} %copy-done.17, ...), kind=kOutput, calls=%fused_computation.20 | convolution fusion | flops 13461091328 | bytes 32794624 | tf_op jit(solution)/shard_map/dot_general | solution.py:30
  323.8 3.6 collective-permute-done.19
  327.7 18.5 %split_product.1 = (bf16[256,2560]{1,0:T(8,128)(2,1)}, bf16[256,2560]{1,0:T(8,128)(2,1)}, bf16[256,2560]{1,0:T(8,128)(2,1)}, bf16[256,2560]{1,0:T(8,128)(2,1)}, ...) custom-call(bf16[2048,1280]{1,0:T(8,128)(2,1)} %copy-done.9, ...), custom_call_target="tpu_custom_call" | custom-call | flops 13421772800 | bytes 22282240 | tf_op jit(solution)/shard_map/split_product/pallas_call | solution.py:425
  348.3 13.0 %fusion.14 = (bf16[2048,1280]{1,0:T(8,128)(2,1)}, bf16[2048,1280]{1,0:T(8,128)(2,1)S(1)}) fusion(bf16[2048,1280]{1,0:T(8,128)(2,1)} %get-tuple-element.228, bf16[2048,1280]{1,0:T(8,128)(2,1)} %get-tuple-element.229, f32[2048]{0:T(1024)S(1)} %fusion.25, f32[1280]{0:T(1024)S(1)} %copy-done.21, f32[2048]{0:T(1024)S(1)} %bitcast.74, ...), kind=kLoop, calls=%fused_computation.27 | loop fusion | flops 57671680 | bytes 26235904 | tf_op jit(solution)/shard_map/convert_element_type | solution.py:771
  363.6 19.0 %convolution_convert_fusion.1 = bf16[2560,1280]{1,0:T(8,128)(2,1)} fusion(bf16[2048,2560]{1,0:T(8,128)(2,1)} %get-tuple-element.162, bf16[2048,1280]{1,0:T(8,128)(2,1)S(1)} %get-tuple-element.201.gate_ref), kind=kOutput, calls=%fused_computation.13 | convolution fusion | flops 13425049600 | bytes 22282240 | tf_op jit(solution)/shard_map/dot_general | solution.py:356
  393.6 69.4 %scan_backward.1 = (bf16[2048,1280]{1,0:T(8,128)(2,1)}, bf16[2048,256]{1,0:T(8,128)(2,1)}, f32[2048,128]{1,0:T(8,128)}, f32[8,1280]{1,0:T(8,128)}, f32[1,128]{1,0:T(1,128)}) custom-call(s32[1]{0:T(128)} %bitcast.seat_ref, bf16[2048,1280]{1,0:T(8,128)(2,1)} %get-tuple-element.95.vp_ref.before_ref, bf16[2048,1280]{1,0:T(8,128)(2,1)} %get-tuple-element.95.vp_ref.before_ref, ...), custom_call_target="tpu_custom_call" | custom-call | flops 7864320000 | bytes 36700160 | tf_op jit(solution)/shard_map/scan_backward/pallas_call | solution.py:292
  469.8 20.1 %convolution_convert_fusion = bf16[2560,1280]{1,0:T(8,128)(2,1)} fusion(bf16[2048,2560]{1,0:T(8,128)(2,1)} %get-tuple-element.162, bf16[2048,1280]{1,0:T(8,128)(2,1)} %get-tuple-element.138.value_ref), kind=kOutput, calls=%fused_computation.12 | convolution fusion | flops 13425049600 | bytes 22282240 | tf_op jit(solution)/shard_map/dot_general | solution.py:356
  498.9 12.1 %rows_product.4 = (bf16[256,2560]{1,0:T(8,128)(2,1)}, bf16[256,2560]{1,0:T(8,128)(2,1)}) custom-call(bf16[2048,1280]{1,0:T(8,128)(2,1)} %copy-done.10, bf16[2048,1280]{1,0:T(8,128)(2,1)} %get-tuple-element.138.value_ref, bf16[2048,128]{1,0:T(8,128)(2,1)} %bitcast.66, bf16[2560,1280]{1,0:T(8,128)(2,1)} %all-gather.6.cloned.1.call-done.w_gate_ref, ...), custom_call_target="tpu_custom_call" | custom-call | flops 7046430720 | bytes 19136512 | tf_op jit(solution)/shard_map/rows_product/pallas_call | solution.py:457
  511.1 12.3 %rows_product.5 = (bf16[256,2560]{1,0:T(8,128)(2,1)}, bf16[256,2560]{1,0:T(8,128)(2,1)}) custom-call(bf16[2048,1280]{1,0:T(8,128)(2,1)} %copy-done.10, bf16[2048,1280]{1,0:T(8,128)(2,1)} %get-tuple-element.138.value_ref, bf16[2048,128]{1,0:T(8,128)(2,1)} %bitcast.67, bf16[2560,1280]{1,0:T(8,128)(2,1)} %all-gather.6.cloned.1.call-done.w_gate_ref, ...), custom_call_target="tpu_custom_call" | custom-call | flops 7046430720 | bytes 19136512 | tf_op jit(solution)/shard_map/rows_product/pallas_call | solution.py:457
  526.3 12.3 %rows_product.6 = (bf16[256,2560]{1,0:T(8,128)(2,1)}, bf16[256,2560]{1,0:T(8,128)(2,1)}) custom-call(bf16[2048,1280]{1,0:T(8,128)(2,1)} %copy-done.10, bf16[2048,1280]{1,0:T(8,128)(2,1)} %get-tuple-element.138.value_ref, bf16[2048,128]{1,0:T(8,128)(2,1)} %bitcast.68, bf16[2560,1280]{1,0:T(8,128)(2,1)} %all-gather.6.cloned.1.call-done.w_gate_ref, ...), custom_call_target="tpu_custom_call" | custom-call | flops 7046430720 | bytes 19136512 | tf_op jit(solution)/shard_map/rows_product/pallas_call | solution.py:457
  538.7 12.3 %rows_product.7 = (bf16[256,2560]{1,0:T(8,128)(2,1)}, bf16[256,2560]{1,0:T(8,128)(2,1)}) custom-call(bf16[2048,1280]{1,0:T(8,128)(2,1)} %copy-done.10, bf16[2048,1280]{1,0:T(8,128)(2,1)} %get-tuple-element.138.value_ref, bf16[2048,128]{1,0:T(8,128)(2,1)} %bitcast.69, bf16[2560,1280]{1,0:T(8,128)(2,1)} %all-gather.6.cloned.1.call-done.w_gate_ref, ...), custom_call_target="tpu_custom_call" | custom-call | flops 7046430720 | bytes 19136512 | tf_op jit(solution)/shard_map/rows_product/pallas_call | solution.py:457
  552.6 3.3 add_convert_fusion
  559.4 6.8 %multiply_reduce_fusion.1 = f32[2560]{0:T(1024)S(1)} fusion(bf16[2560,1280]{1,0:T(8,128)(2,1)} %convolution_convert_fusion.1, bf16[2560,1280]{1,0:T(8,128)(2,1)} %all-gather.6.cloned.1.call-done.w_gate_ref), kind=kLoop, calls=%fused_computation.5 | loop fusion | flops 13104640 | bytes 13117440 | tf_op jit(solution)/shard_map/reduce_sum | solution.py:854
  568.0 6.1 multiply_reduce_fusion.3
  582.6 12.0 %collective-permute-done.37 = f32[10620]{0:T(1024)S(1)} collective-permute-done((f32[10620]{0:T(1024)S(1)}, f32[10620]{0:T(1024)S(1)}, u32[]{:S(2)}, u32[]{:S(2)}) %collective-permute-start.37) | collective-permute-done | bytes 42512 | tf_op jit(solution)/shard_map/ppermute | solution.py:488
  597.8 4.0 convert_add_fusion.3
  601.8 7.4 %collective-permute-done.38 = f32[10620]{0:T(1024)S(1)} collective-permute-done((f32[10620]{0:T(1024)S(1)}, f32[10620]{0:T(1024)S(1)}, u32[]{:S(2)}, u32[]{:S(2)}) %collective-permute-start.38) | collective-permute-done | bytes 42512 | tf_op jit(solution)/shard_map/ppermute | solution.py:488
  615.8 24.3 %collective-permute-done.39 = f32[2560]{0:T(1024)S(1)} collective-permute-done((f32[2560]{0:T(1024)S(1)}, f32[2560]{0:T(1024)S(1)}, u32[]{:S(2)}, u32[]{:S(2)}) %collective-permute-start.39) | collective-permute-done | bytes 10272 | tf_op jit(solution)/shard_map/ppermute | solution.py:488
  640.3 5.2 collective-permute-done.42
  659.6 4.0 fusion.21
  (299 shorter events, 139.0 us)
Async XLA Ops:
  7.2 101.6 %all-gather.4.cloned.1.call-start = ((), (), s32[]{:S(2)}) async-start(), calls=%async_computation.3 | async-start | bytes 8110080 | tf_op jit(solution)/shard_map/all_gather | solution.py:698
  11.3 196.3 %all-gather.6.cloned.1.call-start = ((), (), s32[]{:S(2)}) async-start(), calls=%async_computation.4 | async-start | bytes 7372800 | tf_op jit(solution)/shard_map/all_gather | solution.py:702
  12.1 287.1 %all-gather.8.cloned.1.call-start = ((), (), s32[]{:S(2)}) async-start(), calls=%async_computation.5 | async-start | bytes 7372800 | tf_op jit(solution)/shard_map/all_gather | solution.py:703
  12.1 60.3 %collective-permute-start.2 = (bf16[512,2560]{1,0:T(8,128)(2,1)}, bf16[512,2560]{1,0:T(8,128)(2,1)}, u32[]{:S(2)}, u32[]{:S(2)}) collective-permute-start(bf16[512,2560]{1,0:T(8,128)(2,1)} %refs_0_.1), channel_id=1, source_target_pairs={{0,2},{1,3},{2,0},{3,1},{4,6},{5,7},{6,4},{7,5},{8,10},{9,11},{10,... | collective-permute-start | bytes 7864328 | tf_op jit(solution)/shard_map/ppermute | solution.py:488
  15.2 64.1 %collective-permute-start = (bf16[512,2560]{1,0:T(8,128)(2,1)}, bf16[512,2560]{1,0:T(8,128)(2,1)}, u32[]{:S(2)}, u32[]{:S(2)}) collective-permute-start(bf16[512,2560]{1,0:T(8,128)(2,1)} %refs_0_.1), channel_id=1, source_target_pairs={{0,1},{1,0},{2,3},{3,2},{4,5},{5,4},{6,7},{7,6},{8,9},{9,8},{10,11... | collective-permute-start | bytes 7864328 | tf_op jit(solution)/shard_map/ppermute | solution.py:488
  16.7 62.5 %collective-permute-start.4 = (bf16[640]{0:T(1024)(128)(2,1)S(1)}, bf16[640]{0:T(1024)(128)(2,1)S(1)}, u32[]{:S(2)}, u32[]{:S(2)}) collective-permute-start(bf16[640]{0:T(1024)(128)(2,1)S(1)} %copy-done.35), channel_id=1, source_target_pairs={{0,1},{1,0},{2,3},{3,2},{4,5},{5,4},{6,7},{7,6},{8,9},{9,8},{10,11... | collective-permute-start | bytes 3848 | tf_op jit(solution)/shard_map/ppermute | solution.py:488
  17.2 62.0 %collective-permute-start.5 = (bf16[640]{0:T(1024)(128)(2,1)S(1)}, bf16[640]{0:T(1024)(128)(2,1)S(1)}, u32[]{:S(2)}, u32[]{:S(2)}) collective-permute-start(bf16[640]{0:T(1024)(128)(2,1)S(1)} %copy-done.35), channel_id=1, source_target_pairs={{0,2},{1,3},{2,0},{3,1},{4,6},{5,7},{6,4},{7,5},{8,10},{9,11},{10,... | collective-permute-start | bytes 3848 | tf_op jit(solution)/shard_map/ppermute | solution.py:488
  17.3 61.9 %collective-permute-start.6 = (bf16[640]{0:T(1024)(128)(2,1)S(1)}, bf16[640]{0:T(1024)(128)(2,1)S(1)}, u32[]{:S(2)}, u32[]{:S(2)}) collective-permute-start(bf16[640]{0:T(1024)(128)(2,1)S(1)} %copy-done.35), channel_id=1, source_target_pairs={{0,3},{1,2},{2,1},{3,0},{4,7},{5,6},{6,5},{7,4},{8,11},{9,10},{10,... | collective-permute-start | bytes 3848 | tf_op jit(solution)/shard_map/ppermute | solution.py:488
  20.2 367.8 %reduce-scatter.4.cloned.1.call-start = ((), (), s32[]{:S(2)}) async-start(), calls=%async_computation.6 | async-start | bytes 7372800 | tf_op jit(solution)/shard_map/reduce_scatter | solution.py:668
  74.8 30.2 %collective-permute-start.3 = (bf16[256,2560]{1,0:T(8,128)(2,1)}, bf16[256,2560]{1,0:T(8,128)(2,1)}, u32[]{:S(2)}, u32[]{:S(2)}) collective-permute-start(bf16[256,2560]{1,0:T(8,128)(2,1)} %slice.189), channel_id=1, source_target_pairs={{0,1},{1,0},{2,3},{3,2},{4,5},{5,4},{6,7},{7,6},{8,9},{9,8},{10,11... | collective-permute-start | bytes 3932168 | tf_op jit(solution)/shard_map/ppermute | solution.py:488
  81.7 50.3 %collective-permute-start.1 = (bf16[256,2560]{1,0:T(8,128)(2,1)}, bf16[256,2560]{1,0:T(8,128)(2,1)}, u32[]{:S(2)}, u32[]{:S(2)}) collective-permute-start(bf16[256,2560]{1,0:T(8,128)(2,1)} %slice.188), channel_id=1, source_target_pairs={{0,2},{1,3},{2,0},{3,1},{4,6},{5,7},{6,4},{7,5},{8,10},{9,11},{10,... | collective-permute-start | bytes 3932168 | tf_op jit(solution)/shard_map/ppermute | solution.py:488
  107.4 128.0 %collective-permute-start.14 = (bf16[128,2560]{1,0:T(8,128)(2,1)}, bf16[128,2560]{1,0:T(8,128)(2,1)S(1)}, u32[]{:S(2)}, u32[]{:S(2)}) collective-permute-start(bf16[128,2560]{1,0:T(8,128)(2,1)} %slice.155), channel_id=1, source_target_pairs={{0,2},{1,3},{2,0},{3,1},{4,6},{5,7},{6,4},{7,5},{8,10},{9,11},{10,... | collective-permute-start | bytes 1966088 | tf_op jit(solution)/shard_map/ppermute | solution.py:488
  172.3 64.6 %collective-permute-start.13 = (bf16[384,2560]{1,0:T(8,128)(2,1)}, bf16[384,2560]{1,0:T(8,128)(2,1)}, u32[]{:S(2)}, u32[]{:S(2)}) collective-permute-start(bf16[384,2560]{1,0:T(8,128)(2,1)} %slice.153), channel_id=1, source_target_pairs={{0,1},{1,0},{2,3},{3,2},{4,5},{5,4},{6,7},{7,6},{8,9},{9,8},{10,11... | collective-permute-start | bytes 5898248 | tf_op jit(solution)/shard_map/ppermute | solution.py:488
  173.8 66.2 %collective-permute-start.15 = (bf16[384,2560]{1,0:T(8,128)(2,1)}, bf16[384,2560]{1,0:T(8,128)(2,1)}, u32[]{:S(2)}, u32[]{:S(2)}) collective-permute-start(bf16[384,2560]{1,0:T(8,128)(2,1)} %slice.153), channel_id=1, source_target_pairs={{0,2},{1,3},{2,0},{3,1},{4,6},{5,7},{6,4},{7,5},{8,10},{9,11},{10,... | collective-permute-start | bytes 5898248 | tf_op jit(solution)/shard_map/ppermute | solution.py:488
  235.4 31.3 %collective-permute-start.16 = (bf16[128,2560]{1,0:T(8,128)(2,1)S(1)}, bf16[128,2560]{1,0:T(8,128)(2,1)S(1)}, u32[]{:S(2)}, u32[]{:S(2)}) collective-permute-start(bf16[128,2560]{1,0:T(8,128)(2,1)S(1)} %collective-permute-done.14), channel_id=1, source_target_pairs={{0,1},{1,0},{2,3},{3,2},{4,5},{5,4},{6,7},{7,6},{8,9},{9,8},{10,11... | collective-permute-start | bytes 1966088 | tf_op jit(solution)/shard_map/ppermute | solution.py:488
  238.3 37.2 %collective-permute-start.17 = (bf16[256,2560]{1,0:T(8,128)(2,1)S(1)}, bf16[256,2560]{1,0:T(8,128)(2,1)S(1)}, u32[]{:S(2)}, u32[]{:S(2)}) collective-permute-start(bf16[256,2560]{1,0:T(8,128)(2,1)S(1)} %slice.190), channel_id=1, source_target_pairs={{0,2},{1,3},{2,0},{3,1},{4,6},{5,7},{6,4},{7,5},{8,10},{9,11},{10,... | collective-permute-start | bytes 3932168 | tf_op jit(solution)/shard_map/ppermute | solution.py:488
  241.2 34.3 %collective-permute-start.18 = (bf16[128,2560]{1,0:T(8,128)(2,1)S(1)}, bf16[128,2560]{1,0:T(8,128)(2,1)S(1)}, u32[]{:S(2)}, u32[]{:S(2)}) collective-permute-start(bf16[128,2560]{1,0:T(8,128)(2,1)S(1)} %slice.191), channel_id=1, source_target_pairs={{0,1},{1,0},{2,3},{3,2},{4,5},{5,4},{6,7},{7,6},{8,9},{9,8},{10,11... | collective-permute-start | bytes 1966088 | tf_op jit(solution)/shard_map/ppermute | solution.py:488
  299.2 224.7 %reduce-scatter.6.cloned.1.call-start = ((), (), s32[]{:S(2)}) async-start(), calls=%async_computation.7 | async-start | bytes 7372800 | tf_op jit(solution)/shard_map/reduce_scatter | solution.py:668
  346.2 36.4 %collective-permute-start.22 = (bf16[256,2560]{1,0:T(8,128)(2,1)}, bf16[256,2560]{1,0:T(8,128)(2,1)}, u32[]{:S(2)}, u32[]{:S(2)}) collective-permute-start(bf16[256,2560]{1,0:T(8,128)(2,1)} %get-tuple-element.118), channel_id=1, source_target_pairs={{0,1},{1,0},{2,3},{3,2},{4,5},{5,4},{6,7},{7,6},{8,9},{9,8},{10,11... | collective-permute-start | bytes 3932168 | tf_op jit(solution)/shard_map/ppermute | solution.py:488
  346.3 39.0 %collective-permute-start.21 = (bf16[256,2560]{1,0:T(8,128)(2,1)}, bf16[256,2560]{1,0:T(8,128)(2,1)}, u32[]{:S(2)}, u32[]{:S(2)}) collective-permute-start(bf16[256,2560]{1,0:T(8,128)(2,1)} %get-tuple-element.116), channel_id=1, source_target_pairs={{0,2},{1,3},{2,0},{3,1},{4,6},{5,7},{6,4},{7,5},{8,10},{9,11},{10,... | collective-permute-start | bytes 3932168 | tf_op jit(solution)/shard_map/ppermute | solution.py:488
  390.5 273.2 %reduce-scatter.8.cloned.1.call-start = ((), (), s32[]{:S(2)}) async-start(), calls=%async_computation.8 | async-start | bytes 7372800 | tf_op jit(solution)/shard_map/reduce_scatter | solution.py:668
  391.5 166.2 %collective-permute-start.28 = (bf16[256,2560]{1,0:T(8,128)(2,1)}, bf16[256,2560]{1,0:T(8,128)(2,1)}, u32[]{:S(2)}, u32[]{:S(2)}) collective-permute-start(bf16[256,2560]{1,0:T(8,128)(2,1)} %get-tuple-element.146), channel_id=1, source_target_pairs={{0,1},{1,0},{2,3},{3,2},{4,5},{5,4},{6,7},{7,6},{8,9},{9,8},{10,11... | collective-permute-start | bytes 3932168 | tf_op jit(solution)/shard_map/ppermute | solution.py:488
  393.5 165.8 %collective-permute-start.29 = (bf16[256,2560]{1,0:T(8,128)(2,1)}, bf16[256,2560]{1,0:T(8,128)(2,1)}, u32[]{:S(2)}, u32[]{:S(2)}) collective-permute-start(bf16[256,2560]{1,0:T(8,128)(2,1)} %get-tuple-element.147), channel_id=1, source_target_pairs={{0,2},{1,3},{2,0},{3,1},{4,6},{5,7},{6,4},{7,5},{8,10},{9,11},{10,... | collective-permute-start | bytes 3932168 | tf_op jit(solution)/shard_map/ppermute | solution.py:488
  491.7 86.0 %collective-permute-start.30 = (bf16[256,2560]{1,0:T(8,128)(2,1)}, bf16[256,2560]{1,0:T(8,128)(2,1)}, u32[]{:S(2)}, u32[]{:S(2)}) collective-permute-start(bf16[256,2560]{1,0:T(8,128)(2,1)} %add_convert_fusion.2), channel_id=1, source_target_pairs={{0,2},{1,3},{2,0},{3,1},{4,6},{5,7},{6,4},{7,5},{8,10},{9,11},{10,... | collective-permute-start | bytes 3932168 | tf_op jit(solution)/shard_map/ppermute | solution.py:488
  511.0 40.0 %collective-permute-start.27 = (bf16[256,2560]{1,0:T(8,128)(2,1)}, bf16[256,2560]{1,0:T(8,128)(2,1)}, u32[]{:S(2)}, u32[]{:S(2)}) collective-permute-start(bf16[256,2560]{1,0:T(8,128)(2,1)} %get-tuple-element.133), channel_id=1, source_target_pairs={{0,1},{1,0},{2,3},{3,2},{4,5},{5,4},{6,7},{7,6},{8,9},{9,8},{10,11... | collective-permute-start | bytes 3932168 | tf_op jit(solution)/shard_map/ppermute | solution.py:488
  523.4 32.5 %collective-permute-start.26 = (bf16[256,2560]{1,0:T(8,128)(2,1)}, bf16[256,2560]{1,0:T(8,128)(2,1)S(1)}, u32[]{:S(2)}, u32[]{:S(2)}) collective-permute-start(bf16[256,2560]{1,0:T(8,128)(2,1)} %get-tuple-element.143), channel_id=1, source_target_pairs={{0,2},{1,3},{2,0},{3,1},{4,6},{5,7},{6,4},{7,5},{8,10},{9,11},{10,... | collective-permute-start | bytes 3932168 | tf_op jit(solution)/shard_map/ppermute | solution.py:488
  551.0 44.2 %collective-permute-start.31 = (bf16[256,2560]{1,0:T(8,128)(2,1)}, bf16[256,2560]{1,0:T(8,128)(2,1)}, u32[]{:S(2)}, u32[]{:S(2)}) collective-permute-start(bf16[256,2560]{1,0:T(8,128)(2,1)} %add_convert_fusion.3), channel_id=1, source_target_pairs={{0,1},{1,0},{2,3},{3,2},{4,5},{5,4},{6,7},{7,6},{8,9},{9,8},{10,11... | collective-permute-start | bytes 3932168 | tf_op jit(solution)/shard_map/ppermute | solution.py:488
  555.8 96.3 %collective-permute-start.32 = (bf16[256,2560]{1,0:T(8,128)(2,1)}, bf16[256,2560]{1,0:T(8,128)(2,1)}, u32[]{:S(2)}, u32[]{:S(2)}) collective-permute-start(bf16[256,2560]{1,0:T(8,128)(2,1)} %get-tuple-element.135), channel_id=1, source_target_pairs={{0,1},{1,0},{2,3},{3,2},{4,5},{5,4},{6,7},{7,6},{8,9},{9,8},{10,11... | collective-permute-start | bytes 3932168 | tf_op jit(solution)/shard_map/ppermute | solution.py:488
  557.7 97.1 %collective-permute-start.35 = (bf16[256,2560]{1,0:T(8,128)(2,1)}, bf16[256,2560]{1,0:T(8,128)(2,1)}, u32[]{:S(2)}, u32[]{:S(2)}) collective-permute-start(bf16[256,2560]{1,0:T(8,128)(2,1)} %get-tuple-element.157), channel_id=1, source_target_pairs={{0,2},{1,3},{2,0},{3,1},{4,6},{5,7},{6,4},{7,5},{8,10},{9,11},{10,... | collective-permute-start | bytes 3932168 | tf_op jit(solution)/shard_map/ppermute | solution.py:488
  575.6 38.6 %collective-permute-start.41 = (bf16[1280,128]{1,0:T(8,128)(2,1)S(1)}, bf16[1280,128]{1,0:T(8,128)(2,1)S(1)}, u32[]{:S(2)}, u32[]{:S(2)}) collective-permute-start(bf16[1280,128]{1,0:T(8,128)(2,1)S(1)} %select_convert_fusion), channel_id=1, source_target_pairs={{0,16},{4,20},{8,24},{12,28},{16,0},{20,4},{24,8},{28,12},{1,17},{... | collective-permute-start | bytes 983048 | tf_op jit(solution)/shard_map/ppermute | solution.py:488
  594.6 57.5 %collective-permute-start.33 = (bf16[256,2560]{1,0:T(8,128)(2,1)}, bf16[256,2560]{1,0:T(8,128)(2,1)}, u32[]{:S(2)}, u32[]{:S(2)}) collective-permute-start(bf16[256,2560]{1,0:T(8,128)(2,1)} %add_convert_fusion), channel_id=1, source_target_pairs={{0,2},{1,3},{2,0},{3,1},{4,6},{5,7},{6,4},{7,5},{8,10},{9,11},{10,... | collective-permute-start | bytes 3932168 | tf_op jit(solution)/shard_map/ppermute | solution.py:488
  609.3 45.6 %collective-permute-start.34 = (bf16[256,2560]{1,0:T(8,128)(2,1)}, bf16[256,2560]{1,0:T(8,128)(2,1)}, u32[]{:S(2)}, u32[]{:S(2)}) collective-permute-start(bf16[256,2560]{1,0:T(8,128)(2,1)} %add_convert_fusion.1), channel_id=1, source_target_pairs={{0,1},{1,0},{2,3},{3,2},{4,5},{5,4},{6,7},{7,6},{8,9},{9,8},{10,11... | collective-permute-start | bytes 3932168 | tf_op jit(solution)/shard_map/ppermute | solution.py:488
  (63 other events, 1408.2 us)
Sparse Core Ops, SparseCore 0:
  11.4 74.9 all-gather.3
  88.1 65.4 all-gather.5
  155.2 65.4 all-gather.7
  299.3 71.4 reduce-scatter.3
  390.6 72.7 reduce-scatter.5
  526.4 82.6 reduce-scatter.7

commit v5 on v4

--- a/solution.py
+++ b/solution.py
@@ -4,7 +4,6 @@
 from jax import lax
 from jax.experimental import pallas as pl
 from jax.experimental.pallas import tpu as pltpu
-from jax.experimental.layout import Layout, with_layout_constraint
 from jax.sharding import PartitionSpec as P
 
 
@@ -438,39 +437,64 @@
     )(x, w)
 
 
-def rows_kernel(gate_ref, value_ref, small_ref, w_gate_ref, w_cat_ref, top_ref, low_ref):
-    wide = value_ref.shape[1]
-    rows = top_ref.shape[0]
-    for at, out_ref in enumerate((top_ref, low_ref)):
-        here = slice(at * rows, (at + 1) * rows)
-        total = nt_dot(gate_ref[here], w_gate_ref[...])
-        total = total + nt_dot(value_ref[here], w_cat_ref[:, :wide])
-        total = total + nt_dot(small_ref[here], w_cat_ref[:, wide:])
-        out_ref[...] = total.astype(BF16)
-
-
-def run_rows(piece, d_gate, d_value, d_small, w_gate, w_cat, rows, block):
+def rows_kernel(*refs):
+    w_gate_ref, w_cat_ref = refs[6:8]
+    wide = refs[2].shape[1]
+    for at in range(2):
+        gate_ref, value_ref, small_ref = refs[at:6:2]
+        total = nt_dot(gate_ref[...], w_gate_ref[...])
+        total = total + nt_dot(value_ref[...], w_cat_ref[:, :wide])
+        total = total + nt_dot(small_ref[...], w_cat_ref[:, wide:])
+        refs[8 + at][...] = total.astype(BF16)
+
+
+def run_rows(blocks, d_gate, d_value, d_small, w_gate, w_cat, rows, block):
     width = w_gate.shape[0]
     depth = w_gate.shape[1] + w_cat.shape[1]
-    mine = lambda i: (piece, 0)
-    once = pl.Buffered(1)
+    given = [v for v in (d_gate, d_value, d_small) for _ in blocks]
+    specs = [
+        pl.BlockSpec((rows, v.shape[1]), lambda i, at=at: (at, 0), pipeline_mode=pl.Buffered(1))
+        for v in (d_gate, d_value, d_small)
+        for at in blocks
+    ]
     return pl.pallas_call(
         rows_kernel,
-        out_shape=[jax.ShapeDtypeStruct((rows // 2, width), BF16)] * 2,
+        out_shape=[jax.ShapeDtypeStruct((rows, width), BF16)] * 2,
         grid=(width // block,),
-        in_specs=[
-            pl.BlockSpec((rows, d_gate.shape[1]), mine, pipeline_mode=once),
-            pl.BlockSpec((rows, d_value.shape[1]), mine, pipeline_mode=once),
-            pl.BlockSpec((rows, d_small.shape[1]), mine, pipeline_mode=once),
+        in_specs=specs
+        + [
             pl.BlockSpec((block, w_gate.shape[1]), lambda i: (i, 0)),
             pl.BlockSpec((block, w_cat.shape[1]), lambda i: (i, 0)),
         ],
-        out_specs=[pl.BlockSpec((rows // 2, block), lambda i: (0, i))] * 2,
+        out_specs=[pl.BlockSpec((rows, block), lambda i: (0, i))] * 2,
         cost_estimate=pl.CostEstimate(
-            flops=2 * rows * depth * width, bytes_accessed=2 * (rows + width) * depth + 2 * rows * width, transcendentals=0
+            flops=4 * rows * depth * width, bytes_accessed=2 * (2 * rows + width) * depth + 4 * rows * width, transcendentals=0
         ),
         name="rows_product",
-    )(d_gate, d_value, d_small, w_gate, w_cat)
+    )(*given, w_gate, w_cat)
+
+
+def turned_kernel(a_ref, b_ref, out_ref):
+    out_ref[...] = tn_dot(a_ref[...], b_ref[...]).astype(BF16)
+
+
+def run_turned(a, b, block):
+    tokens, depth = a.shape
+    width = b.shape[1]
+    return pl.pallas_call(
+        turned_kernel,
+        out_shape=jax.ShapeDtypeStruct((depth, width), BF16),
+        grid=(depth // block,),
+        in_specs=[
+            pl.BlockSpec((tokens, block), lambda i: (0, i)),
+            pl.BlockSpec((tokens, width), lambda i: (0, 0), pipeline_mode=pl.Buffered(1)),
+        ],
+        out_specs=pl.BlockSpec((block, width), lambda i: (i, 0)),
+        cost_estimate=pl.CostEstimate(
+            flops=2 * tokens * depth * width, bytes_accessed=2 * (tokens * (depth + width) + depth * width), transcendentals=0
+        ),
+        name="weight_product",
+    )(a, b)
 
 
 def causal_conv(values, taps, offsets):
@@ -545,29 +569,32 @@
         v = v + swap(v, 1)
         return v + swap(v, 2)
 
-    def scatter_begin(self, halves_of):
-        top, low, x_top, x_low, y_top, y_low, far_top, far_low = halves_of
-        came = []
-        for part, bit in ((far_top, 1), (far_low, 2), (x_top, 1), (y_low, 2)):
-            came.append(swap(part, bit))
-        return [x_low, y_top, top, low], came
-
-    def scatter_relay(self, kept, came):
-        beside, above, top, low = kept
-        across_x, across_y, x_top, y_low = came
-        x_low = (beside.astype(F32) + across_y.astype(F32)).astype(BF16)
-        y_top = (above.astype(F32) + across_x.astype(F32)).astype(BF16)
-        return [x_low, y_top], [top, low, x_top, y_low]
-
-    def scatter_end(self, sent, came):
-        x_low = swap(sent[0], 1)
-        y_top = swap(sent[1], 2)
-        top, low, x_top, y_low = (v.astype(F32) for v in came)
+    def scatter_far(self, far_top, far_low):
+        return swap(far_top, 1), swap(far_low, 2)
+
+    def scatter_near(self, x_top, y_low):
+        return swap(x_top, 1), swap(y_low, 2)
+
+    def scatter_add(self, x_low, y_top, far_came):
+        across_x, across_y = far_came
+        return [
+            (x_low.astype(F32) + across_y.astype(F32)).astype(BF16),
+            (y_top.astype(F32) + across_x.astype(F32)).astype(BF16),
+        ]
+
+    def scatter_end(self, sent, own, near_came):
+        x_low, y_top = swap(sent[0], 1), swap(sent[1], 2)
+        top, low, x_top, y_low = (v.astype(F32) for v in (*own, *near_came))
         return jnp.concatenate([top + x_top + y_top.astype(F32), low + x_low.astype(F32) + y_low])
 
+    def dense_swap(self, v, bit):
+        half, width = v.shape[0] // 2, v.shape[1]
+        came = swap(jnp.concatenate([v[:half], v[half:]], axis=1), bit)
+        return jnp.concatenate([came[:, :width], came[:, width:]])
+
     def gather_states(self, s):
-        pair = jnp.concatenate([s, swap(s, 1)], axis=1)
-        other = jnp.concatenate([swap(s, 2), swap(s, 3)], axis=1)
+        pair = jnp.concatenate([s, self.dense_swap(s, 1)], axis=1)
+        other = jnp.concatenate([self.dense_swap(s, 2), self.dense_swap(s, 3)], axis=1)
         return jnp.concatenate([jnp.where(self.y, other, pair), jnp.where(self.y, pair, other)], axis=1)
 
     def split_states(self, d):
@@ -580,8 +607,7 @@
     def scatter_states(self, parts):
         own = parts[0].astype(F32)
         for bit in (1, 2, 3):
-            came = swap(parts[bit], bit)
-            own = own + came.astype(F32)
+            own = own + self.dense_swap(parts[bit], bit).astype(F32)
         return own
 
     def own_slice(self, v):
@@ -616,14 +642,8 @@
     def total(self, v):
         return lax.psum(v, "col")
 
-    def scatter_begin(self, halves_of):
-        return [], list(halves_of)
-
-    def scatter_relay(self, kept, came):
-        return came, []
-
-    def scatter_end(self, sent, came):
-        return lax.psum_scatter(sent[0], "col", scatter_dimension=0, tiled=True).astype(F32)
+    def scatter_whole(self, v):
+        return lax.psum_scatter(v, "col", scatter_dimension=0, tiled=True).astype(F32)
 
     def gather_states(self, s):
         return lax.all_gather(s, "col", axis=1, tiled=True)
@@ -645,10 +665,6 @@
 
 def tied(*values):
     return lax.optimization_barrier(values)
-
-
-def row_major(v):
-    return with_layout_constraint(v, Layout(major_to_minor=(0, 1)))
 
 
 def row_scatter_small(v):
@@ -665,7 +681,7 @@
 
 
 def row_scatter(v):
-    return lax.psum_scatter(v.astype(BF16), "row", scatter_dimension=0, tiled=True).astype(F32)
+    return lax.psum_scatter(v, "row", scatter_dimension=0, tiled=True)
 
 
 def body(
@@ -703,15 +719,18 @@
     w_out_t = lax.all_gather(w_out.T, "row", axis=0, tiled=True)
     full_gain = lines.gather_flat(in_gain).astype(F32)
 
+    def weight_grad(a, b):
+        return run_turned(a, b, 256) if lines.shards == 4 else tn_dot(a, b).astype(BF16)
+
     def normalized(rows):
         rows = rows.astype(F32)
         scale = lax.rsqrt(jnp.mean(rows * rows, axis=1, keepdims=True) + EPSILON)
         return (rows * scale * full_gain).astype(BF16)
 
     hidden_pieces = lines.gather_whole(hidden)
+    grad_source, hidden_pieces[-1] = tied(grad_out, hidden_pieces[-1])
+    grad_pieces = lines.gather_top(grad_source)
     near, far = hidden_pieces[:3], hidden_pieces[3:]
-    grad_source, _ = tied(grad_out, hidden_pieces[-1])
-    grad_pieces = lines.gather_top(grad_source)
 
     if far:
         tokens_here = 4 * piece_rows
@@ -752,7 +771,7 @@
     normed, *grad_pieces = tied(normed, *grad_pieces)
     grad_full = jnp.concatenate(grad_pieces)
 
-    g_out_part = row_major(tn_dot(grad_full, normed).astype(BF16))
+    g_out_part = weight_grad(grad_full, normed)
     w_out_t, g_out_part = tied(w_out_t, g_out_part)
     g_out_t = row_scatter(g_out_part)
     d_normed = mm(grad_full, w_out_t).astype(BF16).astype(F32)
@@ -761,18 +780,20 @@
     w_out_t, dots = tied(w_out_t, dots)
     if lines.shards == 4:
         out_parts = run_split(normed, w_out_t, 8, 512)
+        early_far = lines.scatter_far(*out_parts[6:])
+        early_near = lines.scatter_near(out_parts[2], out_parts[5])
     else:
-        out_parts = [nt_dot(normed, w_out_t).astype(BF16)]
-    kept, came = lines.scatter_begin(out_parts)
+        branch_out = lines.scatter_whole(nt_dot(normed, w_out_t).astype(BF16))
     dots = lines.token_sum(dots)[:, None]
     d_gated = mix * scaled - gated * (mix * mix * mix * dots / inner_width)
     g_norm_gain = jnp.sum(d_normed * gated * mix, axis=0)
     open_gate = sigmoid(gate)
     d_heads = (d_gated * gate * open_gate).astype(BF16)
     d_gate = (d_gated * ho * (open_gate * (1.0 + gate * (1.0 - open_gate)))).astype(BF16)
-    g_gate_part = row_major(tn_dot(normal_in, d_gate).astype(BF16))
-    early_sent, early_came = lines.scatter_relay(kept, came)
-    d_heads, g_gate_part, *early_sent = tied(d_heads, g_gate_part, *early_sent)
+    g_gate_part = weight_grad(normal_in, d_gate)
+    if lines.shards == 4:
+        early_sent = lines.scatter_add(out_parts[3], out_parts[4], early_far)
+        d_heads, g_gate_part, *early_sent = tied(d_heads, g_gate_part, *early_sent)
     g_gate_sent, g_out_t = tied(g_gate_part, g_out_t)
     g_gate = row_scatter(g_gate_sent)
 
@@ -781,7 +802,7 @@
     )
     state_parts = lines.split_states(d_states)
     normal_in, *state_parts = tied(normal_in, *state_parts)
-    g_value_part = row_major(tn_dot(normal_in, d_value).astype(BF16))
+    g_value_part = weight_grad(normal_in, d_value)
     g_value_sent, g_gate = tied(g_value_part, g_gate)
     g_value = row_scatter(g_value_sent)
     d_state_local, g_value_part = tied(lines.scatter_states(state_parts), g_value_part)
@@ -789,17 +810,6 @@
     d_step = d_steps[:, :heads] * sigmoid(step_sum)
     small = lines.settle(widened(jnp.concatenate([d_bc_pre, d_step], axis=1), LANES)).astype(BF16)
     small, d_value, g_value_part = tied(small, d_value, g_value_part)
-    if lines.shards == 4:
-        pieces = {}
-        turn = d_value
-        for piece in (3, 1, 2, 0):
-            pieces[piece] = run_rows(piece, d_gate, turn, small, w_gate_full, w_cat, piece_rows, 512)
-            turn, last_part = tied(turn, pieces[piece][0])
-        row_parts = [half for piece in range(4) for half in pieces[piece]]
-    else:
-        d_cat = jnp.concatenate([d_value, small], axis=1)
-        row_parts = [(nt_dot(d_gate, w_gate_full) + nt_dot(d_cat, w_cat)).astype(BF16)]
-    sent, came = lines.scatter_relay(*lines.scatter_begin(row_parts))
     parts = (
         g_conv[:4, :channels],
         g_conv[4, :channels],
@@ -810,14 +820,29 @@
         jnp.sum(g_conv[5, :channels].reshape(heads, P_SIZE), axis=1),
         g_norm_gain,
     )
-    sent_count = len(sent)
-    last_part, normal_in, g_gate_part, g_value_part, *held_back = tied(
-        row_parts[0], normal_in, g_gate_part, g_value_part, *sent, *early_came
-    )
-    sent, early_came = held_back[:sent_count], held_back[sent_count:]
-    branch_out = lines.scatter_end(early_sent, early_came)
+    if lines.shards == 4:
+        row_parts = {}
+        turn = d_value
+        for name, blocks in (("rows_far", (6, 7)), ("rows_near", (2, 5)), ("rows_next", (3, 4)), ("rows_own", (0, 1))):
+            row_parts[name] = run_rows(blocks, d_gate, turn, small, w_gate_full, w_cat, piece_rows // 2, 512)
+            turn, *row_parts[name] = tied(turn, *row_parts[name])
+            if name == "rows_far":
+                far_came = lines.scatter_far(*row_parts[name])
+            elif name == "rows_near":
+                near_came = lines.scatter_near(*row_parts[name])
+            elif name == "rows_next":
+                sent = lines.scatter_add(*row_parts[name], far_came)
+                turn, *sent = tied(turn, *sent)
+        own = row_parts["rows_own"]
+        own[0], normal_in, g_gate_part, g_value_part, *early_near = tied(
+            own[0], normal_in, g_gate_part, g_value_part, *early_near
+        )
+        d_rows = lines.scatter_end(sent, own, near_came)
+        branch_out = lines.scatter_end(early_sent, out_parts[:2], early_near)
+    else:
+        d_cat = jnp.concatenate([d_value, small], axis=1)
+        d_rows = lines.scatter_whole((nt_dot(d_gate, w_gate_full) + nt_dot(d_cat, w_cat)).astype(BF16))
     result = (hidden.astype(F32) + branch_out).astype(BF16)
-    d_rows = lines.scatter_end(sent, came)
     g_small_part = tn_dot(normal_in, small)
     g_small = row_scatter_small(g_small_part)
     tokens = hidden.astype(F32)
@@ -839,12 +864,12 @@
         result,
         grad_hidden,
         g_in_gain,
-        g_gate,
-        g_value[:, :channels],
+        g_gate.astype(F32),
+        g_value[:, :channels].astype(F32),
         g_small[:, :bc_width],
         g_small[:, bc_width : bc_width + heads],
         *summed,
-        g_out_t.T,
+        g_out_t.T.astype(F32),
     )
 
 

time: 684 us -> 689 us (level)
  Pallas kernels: 204 us -> 262 us
  matrix products: 107 us -> 52.5 us
  waiting for transfers between devices: 178 us -> 170 us
    pallas_call x4 -> x7, Pallas kernels: 48.9 us -> 107 us  [the longest x3 58.7 us: run_turned(): pl.pallas_call(turned_kernel, out_shape=jax.ShapeDtypeStruct((depth, widt...]
    dot_general x4 -> x1, matrix products: 61.1 us -> 6.14 us  [tn_dot(): lax.dot_general(a, b, (((0,), (0,)), ((), ())), preferred_element_type=F32)]
    ppermute x44, waiting for transfers between devices: 177 us -> 169 us  [swap(): return lax.ppermute(v, axis, [(i, i ^ bit) for i in range(size)])]
    unnamed x103 -> x97, local copies, waits for them, and re-layouts: 14.6 us -> 16.6 us
  transfers between devices with their start and end apart: 50 -> 50, of which waited for: 17 -> 18; matrix products, arithmetic and copies ran while one was open for 31% -> 25% of each run, Pallas kernels for 30% -> 39%
where the time goes in v5:
time: 689 us; the launch traced here: 679 us
  Pallas kernels  262 us (38%)
  waiting for transfers between devices  170 us (25%)
  other arithmetic  86.2 us (13%)
  matrix products  52.5 us (8%)
  starting transfers between devices  51.2 us (7%)
  local copies, waits for them, and re-layouts  41 us (6%)
  between operations  15.6 us (2%)
    ppermute x44, waiting for transfers between devices, swap(): return lax.ppermute(v, axis, [(i, i ^ bit) for i in range(size)])  169 us
    pallas_call x1, Pallas kernels, run_backward(): pl.pallas_call(functools.partial(scan_backward, pairs=width // LANES, blo...  69.6 us
    pallas_call x3, Pallas kernels, run_turned(): pl.pallas_call(turned_kernel, out_shape=jax.ShapeDtypeStruct((depth, widt...  58.7 us
    ppermute x44, starting transfers between devices, swap(): return lax.ppermute(v, axis, [(i, i ^ bit) for i in range(size)])  50.9 us
    pallas_call x4, Pallas kernels, run_rows(): pl.pallas_call(rows_kernel, out_shape=[jax.ShapeDtypeStruct((rows, width)...  48.5 us
    dot_general x2, matrix products, mm(): return jnp.dot(a, b, preferred_element_type=F32)  46.4 us
    pallas_call x2, Pallas kernels, run_fill(): pl.pallas_call(functools.partial(fill_kernel, spans=spans), out_shape=(ja...  33.8 us
    pallas_call x1, Pallas kernels, run_forward(): pl.pallas_call(functools.partial(scan_forward, pairs=width // LANES), out...  33.2 us
  transfers between devices with their start and end apart: 50, of which 18 were waited for; matrix products, arithmetic and copies ran while one was open for 25% of the time, Pallas kernels for 39%

profile of v5, /device:TPU:0, one launch (start us, length us, event | category | flops | bytes accessed | tf_op | source)
XLA Modules:
  0.0 678.7 jit_solution(2252605039713420646)
XLA Ops:
  21.2 51.2 %collective-permute-done.2.refs_2_ = bf16[512,2560]{1,0:T(8,128)(2,1)} collective-permute-done((bf16[512,2560]{1,0:T(8,128)(2,1)}, bf16[512,2560]{1,0:T(8,128)(2,1)}, u32[]{:S(2)}, u32[]{:S(2)}) %collective-permute-start.2) | collective-permute-done | bytes 2621472 | tf_op jit(solution)/shard_map/ppermute | solution.py:512
  84.1 21.0 %collective-permute-done.3.refs_1_ = bf16[256,2560]{1,0:T(8,128)(2,1)} collective-permute-done((bf16[256,2560]{1,0:T(8,128)(2,1)}, bf16[256,2560]{1,0:T(8,128)(2,1)}, u32[]{:S(2)}, u32[]{:S(2)}) %collective-permute-start.3) | collective-permute-done | bytes 1310752 | tf_op jit(solution)/shard_map/ppermute | solution.py:512
  108.8 23.1 %value_product.2 = (bf16[2048,2560]{1,0:T(8,128)(2,1)}, bf16[2048,1280]{1,0:T(8,128)(2,1)}, f32[2048,128]{1,0:T(8,128)}) custom-call(bf16[512,2560]{1,0:T(8,128)(2,1)} %refs_0_.1, bf16[512,2560]{1,0:T(8,128)(2,1)} %collective-permute-done.refs_1_, bf16[512,2560]{1,0:T(8,128)(2,1)} %collective-permute-done.2.refs_2_, f32[1,2560]{1,0:T(1,128)} %reshape.216.refs_3_.refs_2_, ...), custom_call_target="tpu_custom_call" | custom-call | flops 11072962560 | bytes 23363584 | tf_op jit(solution)/shard_map/value_product/pallas_call | solution.py:387
  132.0 10.6 %value_product.3 = (bf16[2048,2560]{1,0:T(8,128)(2,1)}, bf16[2048,1280]{1,0:T(8,128)(2,1)}, f32[2048,128]{1,0:T(8,128)}) custom-call(bf16[256,2560]{1,0:T(8,128)(2,1)} %collective-permute-done.1.refs_0_, bf16[256,2560]{1,0:T(8,128)(2,1)} %collective-permute-done.3.refs_1_, ...), custom_call_target="tpu_custom_call", output_to_operand_aliasing={{0}: (4, {}), {1}: (5, {}), {2}: (6, {})} | custom-call | flops 3690987520 | bytes 15237120 | tf_op jit(solution)/shard_map/value_product/pallas_call | solution.py:387
  152.7 5.7 collective-permute-done.7
  163.4 33.2 %scan_forward.1 = (bf16[2048,1280]{1,0:T(8,128)(2,1)}, bf16[16,128,1280]{2,1,0:T(8,128)(2,1)}) custom-call(s32[1]{0:T(128)} %bitcast.seat_ref, bf16[2048,1280]{1,0:T(8,128)(2,1)} %get-tuple-element.105.vp_ref.before_ref, bf16[2048,256]{1,0:T(8,128)(2,1)} %pad_maximum_fusion.bc_ref, f32[2048,128]{1,0:T(8,128)} %pad.51.st_ref, ...), custom_call_target="tpu_custom_call" | custom-call | flops 3145728000 | bytes 26214400 | tf_op jit(solution)/shard_map/scan_forward/pallas_call | solution.py:244
  196.6 21.6 %multiply_reduce_fusion.2 = (f32[2048]{0:T(1024)S(1)}, bf16[2048,1280]{1,0:T(8,128)(2,1)}) fusion(bf16[2048,1280]{1,0:T(8,128)(2,1)} %get-tuple-element.109, bf16[2048,2560]{1,0:T(8,128)(2,1)} %get-tuple-element.180.a_ref, bf16[2560,1280]{1,0:T(8,128)(2,1)} %all-gather.6.cloned.1.call-done.refs_6_), kind=kOutput, calls=%fused_computation.27 | convolution fusion | flops 13447985152 | bytes 27533312 | tf_op jit(solution)/shard_map/dot_general | solution.py:29
  231.0 9.3 %multiply_convert_fusion.b_ref.x_ref = bf16[2048,1280]{1,0:T(8,128)(2,1)} fusion(f32[1280]{0:T(1024)S(1)} %copy-done.21, f32[2048]{0:T(1024)S(1)} %bitcast.67, bf16[2048,1280]{1,0:T(8,128)(2,1)} %get-tuple-element.266, bf16[2048,1280]{1,0:T(8,128)(2,1)} %get-tuple-element.109), kind=kLoop, calls=%fused_computation.26 | loop fusion | flops 26214400 | bytes 15741952 | tf_op jit(solution)/shard_map/convert_element_type | solution.py:770
  241.6 14.0 %collective-permute-done.16 = bf16[128,2560]{1,0:T(8,128)(2,1)S(1)} collective-permute-done((bf16[128,2560]{1,0:T(8,128)(2,1)S(1)}, bf16[128,2560]{1,0:T(8,128)(2,1)S(1)}, u32[]{:S(2)}, u32[]{:S(2)}) %collective-permute-start.16) | collective-permute-done | bytes 655392 | tf_op jit(solution)/shard_map/ppermute | solution.py:512
  255.7 9.4 %collective-permute-done.18 = bf16[128,2560]{1,0:T(8,128)(2,1)S(1)} collective-permute-done((bf16[128,2560]{1,0:T(8,128)(2,1)S(1)}, bf16[128,2560]{1,0:T(8,128)(2,1)S(1)}, u32[]{:S(2)}, u32[]{:S(2)}) %collective-permute-start.18) | collective-permute-done | bytes 655392 | tf_op jit(solution)/shard_map/ppermute | solution.py:512
  277.5 19.5 %weight_product.3 = bf16[2560,1280]{1,0:T(8,128)(2,1)} custom-call(bf16[2048,2560]{1,0:T(8,128)(2,1)} %constant_dynamic-update-slice_fusion.a_ref, bf16[2048,1280]{1,0:T(8,128)(2,1)} %multiply_convert_fusion.b_ref.x_ref), custom_call_target="tpu_custom_call" | custom-call | flops 13421772800 | bytes 22282240 | tf_op jit(solution)/shard_map/weight_product/pallas_call | solution.py:484
  297.1 24.8 %fusion.7 = (f32[1280]{0:T(1024)S(1)}, f32[2048]{0:T(1024)S(1)}, bf16[2048,1280]{1,0:T(8,128)(2,1)}) fusion(f32[2048]{0:T(1024)S(1)} %bitcast.68, bf16[2048,1280]{1,0:T(8,128)(2,1)} %get-tuple-element.266, bf16[2048,1280]{1,0:T(8,128)(2,1)} %get-tuple-element.109, f32[1280]{0:T(1024)S(1)} %copy-done.21, ...), kind=kOutput, calls=%fused_computation.17 | convolution fusion | flops 13461091328 | bytes 32794624 | tf_op jit(solution)/shard_map/dot_general | solution.py:29
  322.1 3.5 collective-permute-done.19
  326.2 18.4 %split_product.1 = (bf16[256,2560]{1,0:T(8,128)(2,1)}, bf16[256,2560]{1,0:T(8,128)(2,1)}, bf16[256,2560]{1,0:T(8,128)(2,1)}, bf16[256,2560]{1,0:T(8,128)(2,1)}, ...) custom-call(bf16[2048,1280]{1,0:T(8,128)(2,1)} %multiply_convert_fus, ...), custom_call_target="tpu_custom_call" | custom-call | flops 13421772800 | bytes 22282240 | tf_op jit(solution)/shard_map/split_product/pallas_call | solution.py:424
  346.5 14.3 %fusion.5 = (bf16[2048,1280]{1,0:T(8,128)(2,1)}, bf16[2048,1280]{1,0:T(8,128)(2,1)}) fusion(bf16[2048,1280]{1,0:T(8,128)(2,1)} %get-tuple-element.109, bf16[2048,1280]{1,0:T(8,128)(2,1)} %get-tuple-element.266, bf16[2048,1280]{1,0:T(8,128)(2,1)} %get-tuple-element.267, f32[2048]{0:T(1024)S(1)} %fusion.25, f32[1280]{0:T(1024)S(1)} %copy-done.21, ...), kind=kLoop, calls=%fused_computation.15 | loop fusion | flops 57671680 | bytes 26235904 | tf_op jit(solution)/shard_map/convert_element_type | solution.py:792
  360.8 19.7 %weight_product.4 = bf16[2560,1280]{1,0:T(8,128)(2,1)} custom-call(bf16[2048,2560]{1,0:T(8,128)(2,1)} %get-tuple-element.180.a_ref, bf16[2048,1280]{1,0:T(8,128)(2,1)} %get-tuple-element.218.b_ref.refs_0_.refs_1_), custom_call_target="tpu_custom_call" | custom-call | flops 13421772800 | bytes 22282240 | tf_op jit(solution)/shard_map/weight_product/pallas_call | solution.py:484
  389.3 69.6 %scan_backward.1 = (bf16[2048,1280]{1,0:T(8,128)(2,1)}, bf16[2048,256]{1,0:T(8,128)(2,1)}, f32[2048,128]{1,0:T(8,128)}, f32[8,1280]{1,0:T(8,128)}, f32[1,128]{1,0:T(1,128)}) custom-call(s32[1]{0:T(128)} %bitcast.seat_ref, bf16[2048,1280]{1,0:T(8,128)(2,1)} %get-tuple-element.105.vp_ref.before_ref, bf16[2048,1280]{1,0:T(8,128)(2,1)} %get-tuple-element.105.vp_ref.before_ref, ...), custom_call_target="tpu_custom_call" | custom-call | flops 7864320000 | bytes 36700160 | tf_op jit(solution)/shard_map/scan_backward/pallas_call | solution.py:291
  467.1 19.5 %weight_product.5 = bf16[2560,1280]{1,0:T(8,128)(2,1)} custom-call(bf16[2048,2560]{1,0:T(8,128)(2,1)} %get-tuple-element.180.a_ref, bf16[2048,1280]{1,0:T(8,128)(2,1)} %get-tuple-element.157.b_ref.refs_2_.refs_3_), custom_call_target="tpu_custom_call" | custom-call | flops 13421772800 | bytes 22282240 | tf_op jit(solution)/shard_map/weight_product/pallas_call | solution.py:484
  495.0 12.2 %rows_product.4 = (bf16[256,2560]{1,0:T(8,128)(2,1)}, bf16[256,2560]{1,0:T(8,128)(2,1)}) custom-call(bf16[2048,1280]{1,0:T(8,128)(2,1)} %get-tuple-element.218.b_ref.refs_0_.refs_1_, bf16[2048,1280]{1,0:T(8,128)(2,1)} %get-tuple-element.218.b_ref.refs_0_.refs_1_, bf16[2048,1280]{1,0:T(8,128)(2,1)} %get-tuple-element.157.b_ref.refs_2_.refs_3_, ...), custom_call_target="tpu_custom_call" | custom-call | flops 7046430720 | bytes 19136512 | tf_op jit(solution)/shard_map/rows_product/pallas_call | solution.py:460
  507.5 12.0 %rows_product.5 = (bf16[256,2560]{1,0:T(8,128)(2,1)}, bf16[256,2560]{1,0:T(8,128)(2,1)}) custom-call(bf16[2048,1280]{1,0:T(8,128)(2,1)} %get-tuple-element.218.b_ref.refs_0_.refs_1_, bf16[2048,1280]{1,0:T(8,128)(2,1)} %get-tuple-element.218.b_ref.refs_0_.refs_1_, bf16[2048,1280]{1,0:T(8,128)(2,1)} %get-tuple-element.157.b_ref.refs_2_.refs_3_, ...), custom_call_target="tpu_custom_call" | custom-call | flops 7046430720 | bytes 19136512 | tf_op jit(solution)/shard_map/rows_product/pallas_call | solution.py:460
  519.9 12.1 %rows_product.6 = (bf16[256,2560]{1,0:T(8,128)(2,1)}, bf16[256,2560]{1,0:T(8,128)(2,1)}) custom-call(bf16[2048,1280]{1,0:T(8,128)(2,1)} %get-tuple-element.218.b_ref.refs_0_.refs_1_, bf16[2048,1280]{1,0:T(8,128)(2,1)} %get-tuple-element.218.b_ref.refs_0_.refs_1_, bf16[2048,1280]{1,0:T(8,128)(2,1)} %get-tuple-element.157.b_ref.refs_2_.refs_3_, ...), custom_call_target="tpu_custom_call" | custom-call | flops 7046430720 | bytes 19136512 | tf_op jit(solution)/shard_map/rows_product/pallas_call | solution.py:460
  537.1 4.8 collective-permute-done.26
  544.9 12.2 %rows_product.7 = (bf16[256,2560]{1,0:T(8,128)(2,1)}, bf16[256,2560]{1,0:T(8,128)(2,1)}) custom-call(bf16[2048,1280]{1,0:T(8,128)(2,1)} %get-tuple-element.218.b_ref.refs_0_.refs_1_, bf16[2048,1280]{1,0:T(8,128)(2,1)} %get-tuple-element.218.b_ref.refs_0_.refs_1_, bf16[2048,1280]{1,0:T(8,128)(2,1)} %get-tuple-element.157.b_ref.refs_2_.refs_3_, ...), custom_call_target="tpu_custom_call" | custom-call | flops 7046430720 | bytes 19136512 | tf_op jit(solution)/shard_map/rows_product/pallas_call | solution.py:460
  557.7 7.0 %multiply_reduce_fusion.1 = f32[2560]{0:T(1024)S(1)} fusion(bf16[2560,1280]{1,0:T(8,128)(2,1)} %weight_product.4, bf16[2560,1280]{1,0:T(8,128)(2,1)} %all-gather.6.cloned.1.call-done.refs_6_), kind=kLoop, calls=%fused_computation.5 | loop fusion | flops 13104640 | bytes 13117440 | tf_op jit(solution)/shard_map/reduce_sum | solution.py:879
  564.7 4.9 multiply_reduce_fusion
  569.6 6.1 multiply_reduce_fusion.3
  582.7 12.5 %collective-permute-done.37 = f32[10620]{0:T(1024)S(1)} collective-permute-done((f32[10620]{0:T(1024)S(1)}, f32[10620]{0:T(1024)S(1)}, u32[]{:S(2)}, u32[]{:S(2)}) %collective-permute-start.37) | collective-permute-done | bytes 42512 | tf_op jit(solution)/shard_map/ppermute | solution.py:512
  600.1 4.1 convert_add_fusion.3
  604.2 8.0 %collective-permute-done.38 = f32[10620]{0:T(1024)S(1)} collective-permute-done((f32[10620]{0:T(1024)S(1)}, f32[10620]{0:T(1024)S(1)}, u32[]{:S(2)}, u32[]{:S(2)}) %collective-permute-start.38) | collective-permute-done | bytes 42512 | tf_op jit(solution)/shard_map/ppermute | solution.py:512
  618.8 24.2 %collective-permute-done.39 = f32[2560]{0:T(1024)S(1)} collective-permute-done((f32[2560]{0:T(1024)S(1)}, f32[2560]{0:T(1024)S(1)}, u32[]{:S(2)}, u32[]{:S(2)}) %collective-permute-start.39) | collective-permute-done | bytes 10272 | tf_op jit(solution)/shard_map/ppermute | solution.py:512
  643.1 5.2 collective-permute-done.42
  662.4 4.0 fusion.21
  (306 shorter events, 145.3 us)
Async XLA Ops:
  7.2 101.6 %all-gather.4.cloned.1.call-start = ((), (), s32[]{:S(2)}) async-start(), calls=%async_computation.3 | async-start | bytes 8110080 | tf_op jit(solution)/shard_map/all_gather | solution.py:714
  11.3 185.3 %all-gather.6.cloned.1.call-start = ((), (), s32[]{:S(2)}) async-start(), calls=%async_computation.4 | async-start | bytes 7372800 | tf_op jit(solution)/shard_map/all_gather | solution.py:718
  12.1 284.9 %all-gather.8.cloned.1.call-start = ((), (), s32[]{:S(2)}) async-start(), calls=%async_computation.5 | async-start | bytes 7372800 | tf_op jit(solution)/shard_map/all_gather | solution.py:719
  12.1 60.3 %collective-permute-start.2 = (bf16[512,2560]{1,0:T(8,128)(2,1)}, bf16[512,2560]{1,0:T(8,128)(2,1)}, u32[]{:S(2)}, u32[]{:S(2)}) collective-permute-start(bf16[512,2560]{1,0:T(8,128)(2,1)} %refs_0_.1), channel_id=1, source_target_pairs={{0,2},{1,3},{2,0},{3,1},{4,6},{5,7},{6,4},{7,5},{8,10},{9,11},{10,... | collective-permute-start | bytes 7864328 | tf_op jit(solution)/shard_map/ppermute | solution.py:512
  15.2 64.1 %collective-permute-start = (bf16[512,2560]{1,0:T(8,128)(2,1)}, bf16[512,2560]{1,0:T(8,128)(2,1)}, u32[]{:S(2)}, u32[]{:S(2)}) collective-permute-start(bf16[512,2560]{1,0:T(8,128)(2,1)} %refs_0_.1), channel_id=1, source_target_pairs={{0,1},{1,0},{2,3},{3,2},{4,5},{5,4},{6,7},{7,6},{8,9},{9,8},{10,11... | collective-permute-start | bytes 7864328 | tf_op jit(solution)/shard_map/ppermute | solution.py:512
  16.7 62.5 %collective-permute-start.4 = (bf16[640]{0:T(1024)(128)(2,1)S(1)}, bf16[640]{0:T(1024)(128)(2,1)S(1)}, u32[]{:S(2)}, u32[]{:S(2)}) collective-permute-start(bf16[640]{0:T(1024)(128)(2,1)S(1)} %copy-done.34), channel_id=1, source_target_pairs={{0,1},{1,0},{2,3},{3,2},{4,5},{5,4},{6,7},{7,6},{8,9},{9,8},{10,11... | collective-permute-start | bytes 3848 | tf_op jit(solution)/shard_map/ppermute | solution.py:512
  17.2 62.0 %collective-permute-start.5 = (bf16[640]{0:T(1024)(128)(2,1)S(1)}, bf16[640]{0:T(1024)(128)(2,1)S(1)}, u32[]{:S(2)}, u32[]{:S(2)}) collective-permute-start(bf16[640]{0:T(1024)(128)(2,1)S(1)} %copy-done.34), channel_id=1, source_target_pairs={{0,2},{1,3},{2,0},{3,1},{4,6},{5,7},{6,4},{7,5},{8,10},{9,11},{10,... | collective-permute-start | bytes 3848 | tf_op jit(solution)/shard_map/ppermute | solution.py:512
  17.3 61.9 %collective-permute-start.6 = (bf16[640]{0:T(1024)(128)(2,1)S(1)}, bf16[640]{0:T(1024)(128)(2,1)S(1)}, u32[]{:S(2)}, u32[]{:S(2)}) collective-permute-start(bf16[640]{0:T(1024)(128)(2,1)S(1)} %copy-done.34), channel_id=1, source_target_pairs={{0,3},{1,2},{2,1},{3,0},{4,7},{5,6},{6,5},{7,4},{8,11},{9,10},{10,... | collective-permute-start | bytes 3848 | tf_op jit(solution)/shard_map/ppermute | solution.py:512
  20.2 365.8 %reduce-scatter.4.cloned.1.call-start = ((), (), s32[]{:S(2)}) async-start(), calls=%async_computation.6 | async-start | bytes 7372800 | tf_op jit(solution)/shard_map/reduce_scatter | solution.py:684
  74.8 30.2 %collective-permute-start.3 = (bf16[256,2560]{1,0:T(8,128)(2,1)}, bf16[256,2560]{1,0:T(8,128)(2,1)}, u32[]{:S(2)}, u32[]{:S(2)}) collective-permute-start(bf16[256,2560]{1,0:T(8,128)(2,1)} %slice.273), channel_id=1, source_target_pairs={{0,1},{1,0},{2,3},{3,2},{4,5},{5,4},{6,7},{7,6},{8,9},{9,8},{10,11... | collective-permute-start | bytes 3932168 | tf_op jit(solution)/shard_map/ppermute | solution.py:512
  81.7 50.3 %collective-permute-start.1 = (bf16[256,2560]{1,0:T(8,128)(2,1)}, bf16[256,2560]{1,0:T(8,128)(2,1)}, u32[]{:S(2)}, u32[]{:S(2)}) collective-permute-start(bf16[256,2560]{1,0:T(8,128)(2,1)} %slice.272), channel_id=1, source_target_pairs={{0,2},{1,3},{2,0},{3,1},{4,6},{5,7},{6,4},{7,5},{8,10},{9,11},{10,... | collective-permute-start | bytes 3932168 | tf_op jit(solution)/shard_map/ppermute | solution.py:512
  107.4 117.2 %collective-permute-start.14 = (bf16[128,2560]{1,0:T(8,128)(2,1)}, bf16[128,2560]{1,0:T(8,128)(2,1)S(1)}, u32[]{:S(2)}, u32[]{:S(2)}) collective-permute-start(bf16[128,2560]{1,0:T(8,128)(2,1)} %slice.227), channel_id=1, source_target_pairs={{0,2},{1,3},{2,0},{3,1},{4,6},{5,7},{6,4},{7,5},{8,10},{9,11},{10,... | collective-permute-start | bytes 1966088 | tf_op jit(solution)/shard_map/ppermute | solution.py:512
  161.5 64.4 %collective-permute-start.13 = (bf16[384,2560]{1,0:T(8,128)(2,1)}, bf16[384,2560]{1,0:T(8,128)(2,1)}, u32[]{:S(2)}, u32[]{:S(2)}) collective-permute-start(bf16[384,2560]{1,0:T(8,128)(2,1)} %slice.225), channel_id=1, source_target_pairs={{0,1},{1,0},{2,3},{3,2},{4,5},{5,4},{6,7},{7,6},{8,9},{9,8},{10,11... | collective-permute-start | bytes 5898248 | tf_op jit(solution)/shard_map/ppermute | solution.py:512
  163.0 66.1 %collective-permute-start.15 = (bf16[384,2560]{1,0:T(8,128)(2,1)}, bf16[384,2560]{1,0:T(8,128)(2,1)}, u32[]{:S(2)}, u32[]{:S(2)}) collective-permute-start(bf16[384,2560]{1,0:T(8,128)(2,1)} %slice.225), channel_id=1, source_target_pairs={{0,2},{1,3},{2,0},{3,1},{4,6},{5,7},{6,4},{7,5},{8,10},{9,11},{10,... | collective-permute-start | bytes 5898248 | tf_op jit(solution)/shard_map/ppermute | solution.py:512
  224.5 31.1 %collective-permute-start.16 = (bf16[128,2560]{1,0:T(8,128)(2,1)S(1)}, bf16[128,2560]{1,0:T(8,128)(2,1)S(1)}, u32[]{:S(2)}, u32[]{:S(2)}) collective-permute-start(bf16[128,2560]{1,0:T(8,128)(2,1)S(1)} %collective-permute-done.14), channel_id=1, source_target_pairs={{0,1},{1,0},{2,3},{3,2},{4,5},{5,4},{6,7},{7,6},{8,9},{9,8},{10,11... | collective-permute-start | bytes 1966088 | tf_op jit(solution)/shard_map/ppermute | solution.py:512
  227.3 37.8 %collective-permute-start.17 = (bf16[256,2560]{1,0:T(8,128)(2,1)S(1)}, bf16[256,2560]{1,0:T(8,128)(2,1)S(1)}, u32[]{:S(2)}, u32[]{:S(2)}) collective-permute-start(bf16[256,2560]{1,0:T(8,128)(2,1)S(1)} %slice.282), channel_id=1, source_target_pairs={{0,2},{1,3},{2,0},{3,1},{4,6},{5,7},{6,4},{7,5},{8,10},{9,11},{10,... | collective-permute-start | bytes 3932168 | tf_op jit(solution)/shard_map/ppermute | solution.py:512
  230.2 34.9 %collective-permute-start.18 = (bf16[128,2560]{1,0:T(8,128)(2,1)S(1)}, bf16[128,2560]{1,0:T(8,128)(2,1)S(1)}, u32[]{:S(2)}, u32[]{:S(2)}) collective-permute-start(bf16[128,2560]{1,0:T(8,128)(2,1)S(1)} %slice.283), channel_id=1, source_target_pairs={{0,1},{1,0},{2,3},{3,2},{4,5},{5,4},{6,7},{7,6},{8,9},{9,8},{10,11... | collective-permute-start | bytes 1966088 | tf_op jit(solution)/shard_map/ppermute | solution.py:512
  297.0 235.0 %reduce-scatter.6.cloned.1.call-start = ((), (), s32[]{:S(2)}) async-start(), calls=%async_computation.7 | async-start | bytes 7372800 | tf_op jit(solution)/shard_map/reduce_scatter | solution.py:684
  344.6 35.9 %collective-permute-start.22 = (bf16[256,2560]{1,0:T(8,128)(2,1)}, bf16[256,2560]{1,0:T(8,128)(2,1)}, u32[]{:S(2)}, u32[]{:S(2)}) collective-permute-start(bf16[256,2560]{1,0:T(8,128)(2,1)} %get-tuple-element.129), channel_id=1, source_target_pairs={{0,1},{1,0},{2,3},{3,2},{4,5},{5,4},{6,7},{7,6},{8,9},{9,8},{10,11... | collective-permute-start | bytes 3932168 | tf_op jit(solution)/shard_map/ppermute | solution.py:512
  344.6 38.6 %collective-permute-start.21 = (bf16[256,2560]{1,0:T(8,128)(2,1)}, bf16[256,2560]{1,0:T(8,128)(2,1)}, u32[]{:S(2)}, u32[]{:S(2)}) collective-permute-start(bf16[256,2560]{1,0:T(8,128)(2,1)} %get-tuple-element.127), channel_id=1, source_target_pairs={{0,2},{1,3},{2,0},{3,1},{4,6},{5,7},{6,4},{7,5},{8,10},{9,11},{10,... | collective-permute-start | bytes 3932168 | tf_op jit(solution)/shard_map/ppermute | solution.py:512
  386.0 283.0 %reduce-scatter.8.cloned.1.call-start = ((), (), s32[]{:S(2)}) async-start(), calls=%async_computation.8 | async-start | bytes 7372800 | tf_op jit(solution)/shard_map/reduce_scatter | solution.py:684
  387.1 170.0 %collective-permute-start.28 = (bf16[256,2560]{1,0:T(8,128)(2,1)}, bf16[256,2560]{1,0:T(8,128)(2,1)}, u32[]{:S(2)}, u32[]{:S(2)}) collective-permute-start(bf16[256,2560]{1,0:T(8,128)(2,1)} %get-tuple-element.163), channel_id=1, source_target_pairs={{0,1},{1,0},{2,3},{3,2},{4,5},{5,4},{6,7},{7,6},{8,9},{9,8},{10,11... | collective-permute-start | bytes 3932168 | tf_op jit(solution)/shard_map/ppermute | solution.py:512
  389.0 168.7 %collective-permute-start.29 = (bf16[256,2560]{1,0:T(8,128)(2,1)}, bf16[256,2560]{1,0:T(8,128)(2,1)}, u32[]{:S(2)}, u32[]{:S(2)}) collective-permute-start(bf16[256,2560]{1,0:T(8,128)(2,1)} %get-tuple-element.164), channel_id=1, source_target_pairs={{0,2},{1,3},{2,0},{3,1},{4,6},{5,7},{6,4},{7,5},{8,10},{9,11},{10,... | collective-permute-start | bytes 3932168 | tf_op jit(solution)/shard_map/ppermute | solution.py:512
  486.9 91.5 %collective-permute-start.30 = (bf16[256,2560]{1,0:T(8,128)(2,1)}, bf16[256,2560]{1,0:T(8,128)(2,1)}, u32[]{:S(2)}, u32[]{:S(2)}) collective-permute-start(bf16[256,2560]{1,0:T(8,128)(2,1)} %add_convert_fusion.2), channel_id=1, source_target_pairs={{0,2},{1,3},{2,0},{3,1},{4,6},{5,7},{6,4},{7,5},{8,10},{9,11},{10,... | collective-permute-start | bytes 3932168 | tf_op jit(solution)/shard_map/ppermute | solution.py:512
  507.2 26.1 %collective-permute-start.27 = (bf16[256,2560]{1,0:T(8,128)(2,1)}, bf16[256,2560]{1,0:T(8,128)(2,1)}, u32[]{:S(2)}, u32[]{:S(2)}) collective-permute-start(bf16[256,2560]{1,0:T(8,128)(2,1)} %get-tuple-element.156), channel_id=1, source_target_pairs={{0,1},{1,0},{2,3},{3,2},{4,5},{5,4},{6,7},{7,6},{8,9},{9,8},{10,11... | collective-permute-start | bytes 3932168 | tf_op jit(solution)/shard_map/ppermute | solution.py:512
  533.3 63.7 %collective-permute-start.31 = (bf16[256,2560]{1,0:T(8,128)(2,1)}, bf16[256,2560]{1,0:T(8,128)(2,1)}, u32[]{:S(2)}, u32[]{:S(2)}) collective-permute-start(bf16[256,2560]{1,0:T(8,128)(2,1)} %add_convert_fusion.3), channel_id=1, source_target_pairs={{0,1},{1,0},{2,3},{3,2},{4,5},{5,4},{6,7},{7,6},{8,9},{9,8},{10,11... | collective-permute-start | bytes 3932168 | tf_op jit(solution)/shard_map/ppermute | solution.py:512
  541.9 113.0 %collective-permute-start.32 = (bf16[256,2560]{1,0:T(8,128)(2,1)}, bf16[256,2560]{1,0:T(8,128)(2,1)}, u32[]{:S(2)}, u32[]{:S(2)}) collective-permute-start(bf16[256,2560]{1,0:T(8,128)(2,1)} %get-tuple-element.171), channel_id=1, source_target_pairs={{0,1},{1,0},{2,3},{3,2},{4,5},{5,4},{6,7},{7,6},{8,9},{9,8},{10,11... | collective-permute-start | bytes 3932168 | tf_op jit(solution)/shard_map/ppermute | solution.py:512
  557.1 100.5 %collective-permute-start.35 = (bf16[256,2560]{1,0:T(8,128)(2,1)}, bf16[256,2560]{1,0:T(8,128)(2,1)}, u32[]{:S(2)}, u32[]{:S(2)}) collective-permute-start(bf16[256,2560]{1,0:T(8,128)(2,1)} %get-tuple-element.175), channel_id=1, source_target_pairs={{0,2},{1,3},{2,0},{3,1},{4,6},{5,7},{6,4},{7,5},{8,10},{9,11},{10,... | collective-permute-start | bytes 3932168 | tf_op jit(solution)/shard_map/ppermute | solution.py:512
  577.1 38.4 %collective-permute-start.41 = (bf16[1280,128]{1,0:T(8,128)(2,1)S(1)}, bf16[1280,128]{1,0:T(8,128)(2,1)S(1)}, u32[]{:S(2)}, u32[]{:S(2)}) collective-permute-start(bf16[1280,128]{1,0:T(8,128)(2,1)S(1)} %select_convert_fusion), channel_id=1, source_target_pairs={{0,16},{4,20},{8,24},{12,28},{16,0},{20,4},{24,8},{28,12},{1,17},{... | collective-permute-start | bytes 983048 | tf_op jit(solution)/shard_map/ppermute | solution.py:512
  595.2 59.7 %collective-permute-start.33 = (bf16[256,2560]{1,0:T(8,128)(2,1)}, bf16[256,2560]{1,0:T(8,128)(2,1)}, u32[]{:S(2)}, u32[]{:S(2)}) collective-permute-start(bf16[256,2560]{1,0:T(8,128)(2,1)} %add_convert_fusion), channel_id=1, source_target_pairs={{0,2},{1,3},{2,0},{3,1},{4,6},{5,7},{6,4},{7,5},{8,10},{9,11},{10,... | collective-permute-start | bytes 3932168 | tf_op jit(solution)/shard_map/ppermute | solution.py:512
  612.2 45.4 %collective-permute-start.34 = (bf16[256,2560]{1,0:T(8,128)(2,1)}, bf16[256,2560]{1,0:T(8,128)(2,1)}, u32[]{:S(2)}, u32[]{:S(2)}) collective-permute-start(bf16[256,2560]{1,0:T(8,128)(2,1)} %add_convert_fusion.1), channel_id=1, source_target_pairs={{0,1},{1,0},{2,3},{3,2},{4,5},{5,4},{6,7},{7,6},{8,9},{9,8},{10,11... | collective-permute-start | bytes 3932168 | tf_op jit(solution)/shard_map/ppermute | solution.py:512
  615.6 27.4 %collective-permute-start.39 = (f32[2560]{0:T(1024)S(1)}, f32[2560]{0:T(1024)S(1)}, u32[]{:S(2)}, u32[]{:S(2)}) collective-permute-start(f32[2560]{0:T(1024)S(1)} %slice.296), channel_id=1, source_target_pairs={{0,1},{1,0},{2,3},{3,2},{4,5},{5,4},{6,7},{7,6},{8,9},{9,8},{10,11... | collective-permute-start | bytes 30728 | tf_op jit(solution)/shard_map/ppermute | solution.py:512
  (60 other events, 1292.6 us)
Sparse Core Ops, SparseCore 0:
  11.4 74.9 all-gather.3
  88.1 65.4 all-gather.5
  155.2 65.4 all-gather.7
  297.2 71.0 reduce-scatter.3
  386.1 72.1 reduce-scatter.5
  532.2 82.1 reduce-scatter.7

commit v6 on v5

--- a/solution.py
+++ b/solution.py
@@ -407,7 +407,7 @@
             bytes_accessed=2 * (at * block + width) * (depth + width),
             transcendentals=0,
         ),
-        name="value_product",
+        name="values",
     )(*pieces, gain, w, *into)
 
 
@@ -433,7 +433,7 @@
         cost_estimate=pl.CostEstimate(
             flops=2 * tokens * depth * width, bytes_accessed=2 * (tokens + width) * depth + 2 * tokens * width, transcendentals=0
         ),
-        name="split_product",
+        name="split",
     )(x, w)
 
 
@@ -470,7 +470,7 @@
         cost_estimate=pl.CostEstimate(
             flops=4 * rows * depth * width, bytes_accessed=2 * (2 * rows + width) * depth + 4 * rows * width, transcendentals=0
         ),
-        name="rows_product",
+        name="rows",
     )(*given, w_gate, w_cat)
 
 
@@ -493,8 +493,35 @@
         cost_estimate=pl.CostEstimate(
             flops=2 * tokens * depth * width, bytes_accessed=2 * (tokens * (depth + width) + depth * width), transcendentals=0
         ),
-        name="weight_product",
+        name="weights",
     )(a, b)
+
+
+def joined_kernel(*refs):
+    b_ref, out_ref, full_ref = refs[-3:]
+    at = 0
+    for piece_ref in refs[:-3]:
+        rows = piece_ref.shape[0]
+        full_ref[at : at + rows] = piece_ref[...]
+        at += rows
+    out_ref[...] = tn_dot(full_ref[...], b_ref[...]).astype(BF16)
+
+
+def run_joined(pieces, b, block):
+    tokens, width = b.shape
+    depth = pieces[0].shape[1]
+    return pl.pallas_call(
+        joined_kernel,
+        out_shape=(jax.ShapeDtypeStruct((depth, width), BF16), jax.ShapeDtypeStruct((tokens, depth), BF16)),
+        grid=(depth // block,),
+        in_specs=[pl.BlockSpec((piece.shape[0], block), lambda i: (0, i)) for piece in pieces]
+        + [pl.BlockSpec((tokens, width), lambda i: (0, 0), pipeline_mode=pl.Buffered(1))],
+        out_specs=(pl.BlockSpec((block, width), lambda i: (i, 0)), pl.BlockSpec((tokens, block), lambda i: (0, i))),
+        cost_estimate=pl.CostEstimate(
+            flops=2 * tokens * depth * width, bytes_accessed=2 * (tokens * (2 * depth + width) + depth * width), transcendentals=0
+        ),
+        name="joined",
+    )(*pieces, b)
 
 
 def causal_conv(values, taps, offsets):
@@ -768,10 +795,12 @@
     squares = lines.token_sum(squares)
     mix = lax.rsqrt(squares / inner_width + EPSILON)[:, None]
     normed = (gated * mix * norm_gain).astype(BF16)
-    normed, *grad_pieces = tied(normed, *grad_pieces)
-    grad_full = jnp.concatenate(grad_pieces)
-
-    g_out_part = weight_grad(grad_full, normed)
+
+    if lines.shards == 4:
+        g_out_part, grad_full = run_joined(grad_pieces, normed, 256)
+    else:
+        grad_full = grad_pieces[0]
+        g_out_part = weight_grad(grad_full, normed)
     w_out_t, g_out_part = tied(w_out_t, g_out_part)
     g_out_t = row_scatter(g_out_part)
     d_normed = mm(grad_full, w_out_t).astype(BF16).astype(F32)
@@ -820,6 +849,11 @@
         jnp.sum(g_conv[5, :channels].reshape(heads, P_SIZE), axis=1),
         g_norm_gain,
     )
+
+    def small_and_gain(normal, from_gate, from_value):
+        from_small = tn_dot(normal, small)
+        return from_small, gain_sums(w_gate_full, from_gate, w_cat, from_value, from_small) / full_gain
+
     if lines.shards == 4:
         row_parts = {}
         turn = d_value
@@ -830,21 +864,23 @@
                 far_came = lines.scatter_far(*row_parts[name])
             elif name == "rows_near":
                 near_came = lines.scatter_near(*row_parts[name])
+                turn, normal_in, g_gate_part, g_value_part = tied(turn, normal_in, g_gate_part, g_value_part)
+                g_small_part, g_in_gain = small_and_gain(normal_in, g_gate_part, g_value_part)
+                turn, g_small_part, g_in_gain = tied(turn, g_small_part, g_in_gain)
             elif name == "rows_next":
                 sent = lines.scatter_add(*row_parts[name], far_came)
-                turn, *sent = tied(turn, *sent)
+                turn, g_small_part, g_in_gain, *sent = tied(turn, g_small_part, g_in_gain, *sent)
         own = row_parts["rows_own"]
-        own[0], normal_in, g_gate_part, g_value_part, *early_near = tied(
-            own[0], normal_in, g_gate_part, g_value_part, *early_near
-        )
+        own[0], *early_near = tied(own[0], *early_near)
         d_rows = lines.scatter_end(sent, own, near_came)
         branch_out = lines.scatter_end(early_sent, out_parts[:2], early_near)
     else:
+        g_small_part, g_in_gain = small_and_gain(normal_in, g_gate_part, g_value_part)
         d_cat = jnp.concatenate([d_value, small], axis=1)
         d_rows = lines.scatter_whole((nt_dot(d_gate, w_gate_full) + nt_dot(d_cat, w_cat)).astype(BF16))
     result = (hidden.astype(F32) + branch_out).astype(BF16)
-    g_small_part = tn_dot(normal_in, small)
     g_small = row_scatter_small(g_small_part)
+
     tokens = hidden.astype(F32)
     scale = lax.rsqrt(jnp.mean(tokens * tokens, axis=1, keepdims=True) + EPSILON)
     scaled_rows = d_rows * full_gain
@@ -852,7 +888,6 @@
         scaled_rows - tokens * (scale * scale * jnp.mean(tokens * scaled_rows, axis=1, keepdims=True))
     )
 
-    g_in_gain = gain_sums(w_gate_full, g_gate_part, w_cat, g_value_part, g_small_part) / full_gain
     packed = row_sum(jnp.concatenate([part.reshape(-1) for part in parts] + [g_in_gain]))
     summed = []
     at = 0

time: 689 us -> 678 us (0.984)
  local copies, waits for them, and re-layouts: 41 us -> 29.2 us
    pallas_call x0 -> x1, Pallas kernels: none -> 20.9 us  [run_joined(): pl.pallas_call(joined_kernel, out_shape=(jax.ShapeDtypeStruct((depth, wid...]
    pallas_call x3 -> x2, Pallas kernels: 58.7 us -> 39.2 us  [run_turned(): pl.pallas_call(turned_kernel, out_shape=jax.ShapeDtypeStruct((depth, widt...]
    unnamed x97 -> x88, local copies, waits for them, and re-layouts: 16.6 us -> 4 us
  transfers between devices with their start and end apart: 50 -> 50, of which waited for: 18 -> 16; matrix products, arithmetic and copies ran while one was open for 25% -> 24% of each run, Pallas kernels for 39% -> 40%
where the time goes in v6:
time: 678 us; the launch traced here: 667 us
  Pallas kernels  264 us (39%)
  waiting for transfers between devices  164 us (24%)
  other arithmetic  90.1 us (13%)
  starting transfers between devices  52 us (8%)
  matrix products  52 us (8%)
  local copies, waits for them, and re-layouts  29.2 us (4%)
  between operations  15.6 us (2%)
    ppermute x44, waiting for transfers between devices, swap(): return lax.ppermute(v, axis, [(i, i ^ bit) for i in range(size)])  163 us
    pallas_call x1, Pallas kernels, run_backward(): pl.pallas_call(functools.partial(scan_backward, pairs=width // LANES, blo...  69.6 us
    ppermute x44, starting transfers between devices, swap(): return lax.ppermute(v, axis, [(i, i ^ bit) for i in range(size)])  51.7 us
    pallas_call x4, Pallas kernels, run_rows(): pl.pallas_call(rows_kernel, out_shape=[jax.ShapeDtypeStruct((rows, width)...  48.9 us
    dot_general x2, matrix products, mm(): return jnp.dot(a, b, preferred_element_type=F32)  46.4 us
    pallas_call x2, Pallas kernels, run_turned(): pl.pallas_call(turned_kernel, out_shape=jax.ShapeDtypeStruct((depth, widt...  39.2 us
    pallas_call x2, Pallas kernels, run_fill(): pl.pallas_call(functools.partial(fill_kernel, spans=spans), out_shape=(ja...  33.8 us
    pallas_call x1, Pallas kernels, run_forward(): pl.pallas_call(functools.partial(scan_forward, pairs=width // LANES), out...  33.2 us
  transfers between devices with their start and end apart: 50, of which 16 were waited for; matrix products, arithmetic and copies ran while one was open for 24% of the time, Pallas kernels for 40%

profile of v6, /device:TPU:0, one launch (start us, length us, event | category | flops | bytes accessed | tf_op | source)
XLA Modules:
  0.0 666.9 jit_solution(2036596751481217276)
XLA Ops:
  21.2 51.2 %collective-permute-done.2.refs_2_ = bf16[512,2560]{1,0:T(8,128)(2,1)} collective-permute-done((bf16[512,2560]{1,0:T(8,128)(2,1)}, bf16[512,2560]{1,0:T(8,128)(2,1)}, u32[]{:S(2)}, u32[]{:S(2)}) %collective-permute-start.2) | collective-permute-done | bytes 2621472 | tf_op jit(solution)/shard_map/ppermute | solution.py:539
  84.1 21.0 %collective-permute-done.3.refs_1_ = bf16[256,2560]{1,0:T(8,128)(2,1)} collective-permute-done((bf16[256,2560]{1,0:T(8,128)(2,1)}, bf16[256,2560]{1,0:T(8,128)(2,1)}, u32[]{:S(2)}, u32[]{:S(2)}) %collective-permute-start.3) | collective-permute-done | bytes 1310752 | tf_op jit(solution)/shard_map/ppermute | solution.py:539
  108.9 23.1 %values.2 = (bf16[2048,2560]{1,0:T(8,128)(2,1)}, bf16[2048,1280]{1,0:T(8,128)(2,1)}, f32[2048,128]{1,0:T(8,128)}) custom-call(bf16[512,2560]{1,0:T(8,128)(2,1)} %refs_0_.1, bf16[512,2560]{1,0:T(8,128)(2,1)} %collective-permute-done.refs_1_, bf16[512,2560]{1,0:T(8,128)(2,1)} %collective-permute-done.2.refs_2_, f32[1,2560]{1,0:T(1,128)} %reshape.216.refs_3_.refs_2_, ...), custom_call_target="tpu_custom_call" | custom-call | flops 11072962560 | bytes 23363584 | tf_op jit(solution)/shard_map/values/pallas_call | solution.py:387
  132.0 10.7 %values.3 = (bf16[2048,2560]{1,0:T(8,128)(2,1)}, bf16[2048,1280]{1,0:T(8,128)(2,1)}, f32[2048,128]{1,0:T(8,128)}) custom-call(bf16[256,2560]{1,0:T(8,128)(2,1)} %collective-permute-done.1.refs_0_, bf16[256,2560]{1,0:T(8,128)(2,1)} %collective-permute-done.3.refs_1_, ...), custom_call_target="tpu_custom_call", output_to_operand_aliasing={{0}: (4, {}), {1}: (5, {}), {2}: (6, {})} | custom-call | flops 3690987520 | bytes 15237120 | tf_op jit(solution)/shard_map/values/pallas_call | solution.py:387
  152.3 6.1 collective-permute-done.7
  163.5 33.2 %scan_forward.1 = (bf16[2048,1280]{1,0:T(8,128)(2,1)}, bf16[16,128,1280]{2,1,0:T(8,128)(2,1)}) custom-call(s32[1]{0:T(128)} %bitcast.seat_ref, bf16[2048,1280]{1,0:T(8,128)(2,1)} %get-tuple-element.104.vp_ref.before_ref, bf16[2048,256]{1,0:T(8,128)(2,1)} %pad_maximum_fusion.bc_ref, f32[2048,128]{1,0:T(8,128)} %pad.51.st_ref, ...), custom_call_target="tpu_custom_call" | custom-call | flops 3145728000 | bytes 26214400 | tf_op jit(solution)/shard_map/scan_forward/pallas_call | solution.py:244
  196.7 21.6 %multiply_reduce_fusion.2 = (f32[2048]{0:T(1024)S(1)}, bf16[2048,1280]{1,0:T(8,128)(2,1)}) fusion(bf16[2048,1280]{1,0:T(8,128)(2,1)} %get-tuple-element.108, bf16[2048,2560]{1,0:T(8,128)(2,1)} %get-tuple-element.145.a_ref, bf16[2560,1280]{1,0:T(8,128)(2,1)} %all-gather.6.cloned.1.call-done.refs_6_), kind=kOutput, calls=%fused_computation.27 | convolution fusion | flops 13447985152 | bytes 27533312 | tf_op jit(solution)/shard_map/dot_general | solution.py:29
  231.0 9.3 %multiply_convert_fusion.refs_8_.x_ref = bf16[2048,1280]{1,0:T(8,128)(2,1)} fusion(f32[1280]{0:T(1024)S(1)} %copy-done.20, f32[2048]{0:T(1024)S(1)} %bitcast.63, bf16[2048,1280]{1,0:T(8,128)(2,1)} %get-tuple-element.248, bf16[2048,1280]{1,0:T(8,128)(2,1)} %get-tuple-element.108), kind=kLoop, calls=%fused_computation.26 | loop fusion | flops 26214400 | bytes 15741952 | tf_op jit(solution)/shard_map/convert_element_type | solution.py:797
  241.7 14.0 %collective-permute-done.16.refs_5_ = bf16[128,2560]{1,0:T(8,128)(2,1)S(1)} collective-permute-done((bf16[128,2560]{1,0:T(8,128)(2,1)}, bf16[128,2560]{1,0:T(8,128)(2,1)S(1)}, u32[]{:S(2)}, u32[]{:S(2)}) %collective-permute-start.16) | collective-permute-done | bytes 655392 | tf_op jit(solution)/shard_map/ppermute | solution.py:539
  255.8 9.4 %collective-permute-done.18.refs_7_ = bf16[128,2560]{1,0:T(8,128)(2,1)S(1)} collective-permute-done((bf16[128,2560]{1,0:T(8,128)(2,1)S(1)}, bf16[128,2560]{1,0:T(8,128)(2,1)S(1)}, u32[]{:S(2)}, u32[]{:S(2)}) %collective-permute-start.18) | collective-permute-done | bytes 655392 | tf_op jit(solution)/shard_map/ppermute | solution.py:539
  266.1 20.9 %joined.1 = (bf16[2560,1280]{1,0:T(8,128)(2,1)}, bf16[2048,2560]{1,0:T(8,128)(2,1)}) custom-call(bf16[512,2560]{1,0:T(8,128)(2,1)} %refs_0_.2, bf16[128,2560]{1,0:T(8,128)(2,1)} %copy-done.36, bf16[384,2560]{1,0:T(8,128)(2,1)} %collective-permute-done.13.refs_2_, bf16[128,2560]{1,0:T(8,128)(2,1)} %collective-permute-done.14.refs_3_, ...), custom_call_target="tpu_custom_call" | custom-call | flops 13421772800 | bytes 32768000 | tf_op jit(solution)/shard_map/joined/pallas_call | solution.py:513
  287.1 24.8 %fusion.7 = (f32[1280]{0:T(1024)S(1)}, f32[2048]{0:T(1024)S(1)}, bf16[2048,1280]{1,0:T(8,128)(2,1)}) fusion(f32[2048]{0:T(1024)S(1)} %bitcast.64, bf16[2048,1280]{1,0:T(8,128)(2,1)} %get-tuple-element.248, bf16[2048,1280]{1,0:T(8,128)(2,1)} %get-tuple-element.108, f32[1280]{0:T(1024)S(1)} %copy-done.20, bf16[2048,2560]{1,0:T(8,128)(2,1)} %get-tuple-element.114, ...), kind=kOutput, calls=%fused_computation.17 | convolution fusion | flops 13461091328 | bytes 32794624 | tf_op jit(solution)/shard_map/dot_general | solution.py:29
  312.1 3.5 collective-permute-done.19
  316.1 18.4 %split.1 = (bf16[256,2560]{1,0:T(8,128)(2,1)}, bf16[256,2560]{1,0:T(8,128)(2,1)}, bf16[256,2560]{1,0:T(8,128)(2,1)}, bf16[256,2560]{1,0:T(8,128)(2,1)}, bf16[256...) custom-call(bf16[2048,1280]{1,0:T(8,128)(2,1)} %multiply_convert_fusion.re, ...), custom_call_target="tpu_custom_call" | custom-call | flops 13421772800 | bytes 22282240 | tf_op jit(solution)/shard_map/split/pallas_call | solution.py:424
  336.4 14.3 %fusion.5 = (bf16[2048,1280]{1,0:T(8,128)(2,1)}, bf16[2048,1280]{1,0:T(8,128)(2,1)}) fusion(bf16[2048,1280]{1,0:T(8,128)(2,1)} %get-tuple-element.108, bf16[2048,1280]{1,0:T(8,128)(2,1)} %get-tuple-element.248, bf16[2048,1280]{1,0:T(8,128)(2,1)} %get-tuple-element.249, f32[2048]{0:T(1024)S(1)} %fusion.25, f32[1280]{0:T(1024)S(1)} %copy-done.20, ...), kind=kLoop, calls=%fused_computation.15 | loop fusion | flops 57671680 | bytes 26235904 | tf_op jit(solution)/shard_map/convert_element_type | solution.py:821
  350.8 19.7 %weights.2 = bf16[2560,1280]{1,0:T(8,128)(2,1)} custom-call(bf16[2048,2560]{1,0:T(8,128)(2,1)} %get-tuple-element.145.a_ref, bf16[2048,1280]{1,0:T(8,128)(2,1)} %get-tuple-element.200.b_ref.refs_0_.refs_1_), custom_call_target="tpu_custom_call" | custom-call | flops 13421772800 | bytes 22282240 | tf_op jit(solution)/shard_map/weights/pallas_call | solution.py:484
  379.6 69.6 %scan_backward.1 = (bf16[2048,1280]{1,0:T(8,128)(2,1)}, bf16[2048,256]{1,0:T(8,128)(2,1)}, f32[2048,128]{1,0:T(8,128)}, f32[8,1280]{1,0:T(8,128)}, f32[1,128]{1,0:T(1,128)}) custom-call(s32[1]{0:T(128)} %bitcast.seat_ref, bf16[2048,1280]{1,0:T(8,128)(2,1)} %get-tuple-element.104.vp_ref.before_ref, bf16[2048,1280]{1,0:T(8,128)(2,1)} %get-tuple-element.104.vp_ref.before_ref, ...), custom_call_target="tpu_custom_call" | custom-call | flops 7864320000 | bytes 36700160 | tf_op jit(solution)/shard_map/scan_backward/pallas_call | solution.py:291
  457.4 19.5 %weights.3 = bf16[2560,1280]{1,0:T(8,128)(2,1)} custom-call(bf16[2048,2560]{1,0:T(8,128)(2,1)} %get-tuple-element.145.a_ref, bf16[2048,1280]{1,0:T(8,128)(2,1)} %get-tuple-element.158.b_ref.refs_2_.refs_3_), custom_call_target="tpu_custom_call" | custom-call | flops 13421772800 | bytes 22282240 | tf_op jit(solution)/shard_map/weights/pallas_call | solution.py:484
  485.3 12.0 %rows.4 = (bf16[256,2560]{1,0:T(8,128)(2,1)}, bf16[256,2560]{1,0:T(8,128)(2,1)}) custom-call(bf16[2048,1280]{1,0:T(8,128)(2,1)} %get-tuple-element.200.b_ref.refs_0_.refs_1_, bf16[2048,1280]{1,0:T(8,128)(2,1)} %get-tuple-element.200.b_ref.refs_0_.refs_1_, bf16[2048,1280]{1,0:T(8,128)(2,1)} %get-tuple-element.158.b_ref.refs_2_.refs_3_, ...), custom_call_target="tpu_custom_call" | custom-call | flops 7046430720 | bytes 19136512 | tf_op jit(solution)/shard_map/rows/pallas_call | solution.py:460
  497.4 12.2 %rows.5 = (bf16[256,2560]{1,0:T(8,128)(2,1)}, bf16[256,2560]{1,0:T(8,128)(2,1)}) custom-call(bf16[2048,1280]{1,0:T(8,128)(2,1)} %get-tuple-element.200.b_ref.refs_0_.refs_1_, bf16[2048,1280]{1,0:T(8,128)(2,1)} %get-tuple-element.200.b_ref.refs_0_.refs_1_, bf16[2048,1280]{1,0:T(8,128)(2,1)} %get-tuple-element.158.b_ref.refs_2_.refs_3_, ...), custom_call_target="tpu_custom_call" | custom-call | flops 7046430720 | bytes 19136512 | tf_op jit(solution)/shard_map/rows/pallas_call | solution.py:460
  509.8 6.5 multiply_reduce_fusion
  516.4 6.6 multiply_reduce_fusion.1
  522.9 5.6 fusion.46
  531.5 12.2 %rows.6 = (bf16[256,2560]{1,0:T(8,128)(2,1)}, bf16[256,2560]{1,0:T(8,128)(2,1)}) custom-call(bf16[2048,1280]{1,0:T(8,128)(2,1)} %get-tuple-element.200.b_ref.refs_0_.refs_1_, bf16[2048,1280]{1,0:T(8,128)(2,1)} %get-tuple-element.200.b_ref.refs_0_.refs_1_, bf16[2048,1280]{1,0:T(8,128)(2,1)} %get-tuple-element.158.b_ref.refs_2_.refs_3_, ...), custom_call_target="tpu_custom_call" | custom-call | flops 7046430720 | bytes 19136512 | tf_op jit(solution)/shard_map/rows/pallas_call | solution.py:460
  548.5 4.5 collective-permute-done.26
  555.9 12.4 %rows.7 = (bf16[256,2560]{1,0:T(8,128)(2,1)}, bf16[256,2560]{1,0:T(8,128)(2,1)}) custom-call(bf16[2048,1280]{1,0:T(8,128)(2,1)} %get-tuple-element.200.b_ref.refs_0_.refs_1_, bf16[2048,1280]{1,0:T(8,128)(2,1)} %get-tuple-element.200.b_ref.refs_0_.refs_1_, bf16[2048,1280]{1,0:T(8,128)(2,1)} %get-tuple-element.158.b_ref.refs_2_.refs_3_, ...), custom_call_target="tpu_custom_call" | custom-call | flops 7046430720 | bytes 19136512 | tf_op jit(solution)/shard_map/rows/pallas_call | solution.py:460
  576.3 12.4 %collective-permute-done.37 = f32[10620]{0:T(1024)S(1)} collective-permute-done((f32[10620]{0:T(1024)S(1)}, f32[10620]{0:T(1024)S(1)}, u32[]{:S(2)}, u32[]{:S(2)}) %collective-permute-start.37) | collective-permute-done | bytes 42512 | tf_op jit(solution)/shard_map/ppermute | solution.py:539
  593.3 3.7 convert_add_fusion.3
  597.0 3.9 collective-permute-done.38
  607.5 24.3 %collective-permute-done.39 = f32[2560]{0:T(1024)S(1)} collective-permute-done((f32[2560]{0:T(1024)S(1)}, f32[2560]{0:T(1024)S(1)}, u32[]{:S(2)}, u32[]{:S(2)}) %collective-permute-start.39) | collective-permute-done | bytes 10272 | tf_op jit(solution)/shard_map/ppermute | solution.py:539
  631.9 5.2 collective-permute-done.42
  650.6 4.0 fusion.21
  (298 shorter events, 135.3 us)
Async XLA Ops:
  7.2 101.7 %all-gather.4.cloned.1.call-start = ((), (), s32[]{:S(2)}) async-start(), calls=%async_computation.3 | async-start | bytes 8110080 | tf_op jit(solution)/shard_map/all_gather | solution.py:741
  11.3 185.4 %all-gather.6.cloned.1.call-start = ((), (), s32[]{:S(2)}) async-start(), calls=%async_computation.4 | async-start | bytes 7372800 | tf_op jit(solution)/shard_map/all_gather | solution.py:745
  12.1 274.9 %all-gather.8.cloned.1.call-start = ((), (), s32[]{:S(2)}) async-start(), calls=%async_computation.5 | async-start | bytes 7372800 | tf_op jit(solution)/shard_map/all_gather | solution.py:746
  12.1 60.3 %collective-permute-start.2 = (bf16[512,2560]{1,0:T(8,128)(2,1)}, bf16[512,2560]{1,0:T(8,128)(2,1)}, u32[]{:S(2)}, u32[]{:S(2)}) collective-permute-start(bf16[512,2560]{1,0:T(8,128)(2,1)} %refs_0_.1), channel_id=1, source_target_pairs={{0,2},{1,3},{2,0},{3,1},{4,6},{5,7},{6,4},{7,5},{8,10},{9,11},{10,... | collective-permute-start | bytes 7864328 | tf_op jit(solution)/shard_map/ppermute | solution.py:539
  15.2 64.1 %collective-permute-start = (bf16[512,2560]{1,0:T(8,128)(2,1)}, bf16[512,2560]{1,0:T(8,128)(2,1)}, u32[]{:S(2)}, u32[]{:S(2)}) collective-permute-start(bf16[512,2560]{1,0:T(8,128)(2,1)} %refs_0_.1), channel_id=1, source_target_pairs={{0,1},{1,0},{2,3},{3,2},{4,5},{5,4},{6,7},{7,6},{8,9},{9,8},{10,11... | collective-permute-start | bytes 7864328 | tf_op jit(solution)/shard_map/ppermute | solution.py:539
  16.7 62.5 %collective-permute-start.4 = (bf16[640]{0:T(1024)(128)(2,1)S(1)}, bf16[640]{0:T(1024)(128)(2,1)S(1)}, u32[]{:S(2)}, u32[]{:S(2)}) collective-permute-start(bf16[640]{0:T(1024)(128)(2,1)S(1)} %copy-done.33), channel_id=1, source_target_pairs={{0,1},{1,0},{2,3},{3,2},{4,5},{5,4},{6,7},{7,6},{8,9},{9,8},{10,11... | collective-permute-start | bytes 3848 | tf_op jit(solution)/shard_map/ppermute | solution.py:539
  17.2 62.0 %collective-permute-start.5 = (bf16[640]{0:T(1024)(128)(2,1)S(1)}, bf16[640]{0:T(1024)(128)(2,1)S(1)}, u32[]{:S(2)}, u32[]{:S(2)}) collective-permute-start(bf16[640]{0:T(1024)(128)(2,1)S(1)} %copy-done.33), channel_id=1, source_target_pairs={{0,2},{1,3},{2,0},{3,1},{4,6},{5,7},{6,4},{7,5},{8,10},{9,11},{10,... | collective-permute-start | bytes 3848 | tf_op jit(solution)/shard_map/ppermute | solution.py:539
  17.3 61.9 %collective-permute-start.6 = (bf16[640]{0:T(1024)(128)(2,1)S(1)}, bf16[640]{0:T(1024)(128)(2,1)S(1)}, u32[]{:S(2)}, u32[]{:S(2)}) collective-permute-start(bf16[640]{0:T(1024)(128)(2,1)S(1)} %copy-done.33), channel_id=1, source_target_pairs={{0,3},{1,2},{2,1},{3,0},{4,7},{5,6},{6,5},{7,4},{8,11},{9,10},{10,... | collective-permute-start | bytes 3848 | tf_op jit(solution)/shard_map/ppermute | solution.py:539
  20.2 356.1 %reduce-scatter.4.cloned.1.call-start = ((), (), s32[]{:S(2)}) async-start(), calls=%async_computation.6 | async-start | bytes 7372800 | tf_op jit(solution)/shard_map/reduce_scatter | solution.py:711
  74.8 30.2 %collective-permute-start.3 = (bf16[256,2560]{1,0:T(8,128)(2,1)}, bf16[256,2560]{1,0:T(8,128)(2,1)}, u32[]{:S(2)}, u32[]{:S(2)}) collective-permute-start(bf16[256,2560]{1,0:T(8,128)(2,1)} %slice.273), channel_id=1, source_target_pairs={{0,1},{1,0},{2,3},{3,2},{4,5},{5,4},{6,7},{7,6},{8,9},{9,8},{10,11... | collective-permute-start | bytes 3932168 | tf_op jit(solution)/shard_map/ppermute | solution.py:539
  81.7 50.3 %collective-permute-start.1 = (bf16[256,2560]{1,0:T(8,128)(2,1)}, bf16[256,2560]{1,0:T(8,128)(2,1)}, u32[]{:S(2)}, u32[]{:S(2)}) collective-permute-start(bf16[256,2560]{1,0:T(8,128)(2,1)} %slice.272), channel_id=1, source_target_pairs={{0,2},{1,3},{2,0},{3,1},{4,6},{5,7},{6,4},{7,5},{8,10},{9,11},{10,... | collective-permute-start | bytes 3932168 | tf_op jit(solution)/shard_map/ppermute | solution.py:539
  107.4 117.2 %collective-permute-start.14 = (bf16[128,2560]{1,0:T(8,128)(2,1)}, bf16[128,2560]{1,0:T(8,128)(2,1)}, u32[]{:S(2)}, u32[]{:S(2)}) collective-permute-start(bf16[128,2560]{1,0:T(8,128)(2,1)} %slice.227), channel_id=1, source_target_pairs={{0,2},{1,3},{2,0},{3,1},{4,6},{5,7},{6,4},{7,5},{8,10},{9,11},{10,... | collective-permute-start | bytes 1966088 | tf_op jit(solution)/shard_map/ppermute | solution.py:539
  161.6 64.4 %collective-permute-start.13 = (bf16[384,2560]{1,0:T(8,128)(2,1)S(1)}, bf16[384,2560]{1,0:T(8,128)(2,1)}, u32[]{:S(2)}, u32[]{:S(2)}) collective-permute-start(bf16[384,2560]{1,0:T(8,128)(2,1)S(1)} %copy-done.10), channel_id=1, source_target_pairs={{0,1},{1,0},{2,3},{3,2},{4,5},{5,4},{6,7},{7,6},{8,9},{9,8},{10,11... | collective-permute-start | bytes 5898248 | tf_op jit(solution)/shard_map/ppermute | solution.py:539
  163.0 66.1 %collective-permute-start.15 = (bf16[384,2560]{1,0:T(8,128)(2,1)S(1)}, bf16[384,2560]{1,0:T(8,128)(2,1)}, u32[]{:S(2)}, u32[]{:S(2)}) collective-permute-start(bf16[384,2560]{1,0:T(8,128)(2,1)S(1)} %copy-done.10), channel_id=1, source_target_pairs={{0,2},{1,3},{2,0},{3,1},{4,6},{5,7},{6,4},{7,5},{8,10},{9,11},{10,... | collective-permute-start | bytes 5898248 | tf_op jit(solution)/shard_map/ppermute | solution.py:539
  224.6 31.2 %collective-permute-start.16 = (bf16[128,2560]{1,0:T(8,128)(2,1)}, bf16[128,2560]{1,0:T(8,128)(2,1)S(1)}, u32[]{:S(2)}, u32[]{:S(2)}) collective-permute-start(bf16[128,2560]{1,0:T(8,128)(2,1)} %collective-permute-done.14.refs_3_), channel_id=1, source_target_pairs={{0,1},{1,0},{2,3},{3,2},{4,5},{5,4},{6,7},{7,6},{8,9},{9,8},{10,11... | collective-permute-start | bytes 1966088 | tf_op jit(solution)/shard_map/ppermute | solution.py:539
  227.4 37.8 %collective-permute-start.17 = (bf16[256,2560]{1,0:T(8,128)(2,1)S(1)}, bf16[256,2560]{1,0:T(8,128)(2,1)}, u32[]{:S(2)}, u32[]{:S(2)}) collective-permute-start(bf16[256,2560]{1,0:T(8,128)(2,1)S(1)} %slice.282), channel_id=1, source_target_pairs={{0,2},{1,3},{2,0},{3,1},{4,6},{5,7},{6,4},{7,5},{8,10},{9,11},{10,... | collective-permute-start | bytes 3932168 | tf_op jit(solution)/shard_map/ppermute | solution.py:539
  230.3 34.9 %collective-permute-start.18 = (bf16[128,2560]{1,0:T(8,128)(2,1)S(1)}, bf16[128,2560]{1,0:T(8,128)(2,1)S(1)}, u32[]{:S(2)}, u32[]{:S(2)}) collective-permute-start(bf16[128,2560]{1,0:T(8,128)(2,1)S(1)} %slice.283), channel_id=1, source_target_pairs={{0,1},{1,0},{2,3},{3,2},{4,5},{5,4},{6,7},{7,6},{8,9},{9,8},{10,11... | collective-permute-start | bytes 1966088 | tf_op jit(solution)/shard_map/ppermute | solution.py:539
  287.0 229.3 %reduce-scatter.6.cloned.1.call-start = ((), (), s32[]{:S(2)}) async-start(), calls=%async_computation.7 | async-start | bytes 7372800 | tf_op jit(solution)/shard_map/reduce_scatter | solution.py:711
  334.6 35.9 %collective-permute-start.22 = (bf16[256,2560]{1,0:T(8,128)(2,1)}, bf16[256,2560]{1,0:T(8,128)(2,1)}, u32[]{:S(2)}, u32[]{:S(2)}) collective-permute-start(bf16[256,2560]{1,0:T(8,128)(2,1)} %get-tuple-element.121), channel_id=1, source_target_pairs={{0,1},{1,0},{2,3},{3,2},{4,5},{5,4},{6,7},{7,6},{8,9},{9,8},{10,11... | collective-permute-start | bytes 3932168 | tf_op jit(solution)/shard_map/ppermute | solution.py:539
  334.6 38.9 %collective-permute-start.21 = (bf16[256,2560]{1,0:T(8,128)(2,1)}, bf16[256,2560]{1,0:T(8,128)(2,1)}, u32[]{:S(2)}, u32[]{:S(2)}) collective-permute-start(bf16[256,2560]{1,0:T(8,128)(2,1)} %get-tuple-element.119), channel_id=1, source_target_pairs={{0,2},{1,3},{2,0},{3,1},{4,6},{5,7},{6,4},{7,5},{8,10},{9,11},{10,... | collective-permute-start | bytes 3932168 | tf_op jit(solution)/shard_map/ppermute | solution.py:539
  376.3 280.9 %reduce-scatter.8.cloned.1.call-start = ((), (), s32[]{:S(2)}) async-start(), calls=%async_computation.8 | async-start | bytes 7372800 | tf_op jit(solution)/shard_map/reduce_scatter | solution.py:711
  377.4 191.0 %collective-permute-start.28 = (bf16[256,2560]{1,0:T(8,128)(2,1)}, bf16[256,2560]{1,0:T(8,128)(2,1)}, u32[]{:S(2)}, u32[]{:S(2)}) collective-permute-start(bf16[256,2560]{1,0:T(8,128)(2,1)} %get-tuple-element.162), channel_id=1, source_target_pairs={{0,1},{1,0},{2,3},{3,2},{4,5},{5,4},{6,7},{7,6},{8,9},{9,8},{10,11... | collective-permute-start | bytes 3932168 | tf_op jit(solution)/shard_map/ppermute | solution.py:539
  379.3 190.8 %collective-permute-start.29 = (bf16[256,2560]{1,0:T(8,128)(2,1)}, bf16[256,2560]{1,0:T(8,128)(2,1)}, u32[]{:S(2)}, u32[]{:S(2)}) collective-permute-start(bf16[256,2560]{1,0:T(8,128)(2,1)} %get-tuple-element.163), channel_id=1, source_target_pairs={{0,2},{1,3},{2,0},{3,1},{4,6},{5,7},{6,4},{7,5},{8,10},{9,11},{10,... | collective-permute-start | bytes 3932168 | tf_op jit(solution)/shard_map/ppermute | solution.py:539
  477.2 94.7 %collective-permute-start.30 = (bf16[256,2560]{1,0:T(8,128)(2,1)}, bf16[256,2560]{1,0:T(8,128)(2,1)}, u32[]{:S(2)}, u32[]{:S(2)}) collective-permute-start(bf16[256,2560]{1,0:T(8,128)(2,1)} %add_convert_fusion.2), channel_id=1, source_target_pairs={{0,2},{1,3},{2,0},{3,1},{4,6},{5,7},{6,4},{7,5},{8,10},{9,11},{10,... | collective-permute-start | bytes 3932168 | tf_op jit(solution)/shard_map/ppermute | solution.py:539
  509.6 34.2 %collective-permute-start.27 = (bf16[256,2560]{1,0:T(8,128)(2,1)}, bf16[256,2560]{1,0:T(8,128)(2,1)}, u32[]{:S(2)}, u32[]{:S(2)}) collective-permute-start(bf16[256,2560]{1,0:T(8,128)(2,1)} %get-tuple-element.157), channel_id=1, source_target_pairs={{0,1},{1,0},{2,3},{3,2},{4,5},{5,4},{6,7},{7,6},{8,9},{9,8},{10,11... | collective-permute-start | bytes 3932168 | tf_op jit(solution)/shard_map/ppermute | solution.py:539
  543.8 46.5 %collective-permute-start.31 = (bf16[256,2560]{1,0:T(8,128)(2,1)}, bf16[256,2560]{1,0:T(8,128)(2,1)}, u32[]{:S(2)}, u32[]{:S(2)}) collective-permute-start(bf16[256,2560]{1,0:T(8,128)(2,1)} %add_convert_fusion.3), channel_id=1, source_target_pairs={{0,1},{1,0},{2,3},{3,2},{4,5},{5,4},{6,7},{7,6},{8,9},{9,8},{10,11... | collective-permute-start | bytes 3932168 | tf_op jit(solution)/shard_map/ppermute | solution.py:539
  568.4 75.1 %collective-permute-start.32 = (bf16[256,2560]{1,0:T(8,128)(2,1)}, bf16[256,2560]{1,0:T(8,128)(2,1)}, u32[]{:S(2)}, u32[]{:S(2)}) collective-permute-start(bf16[256,2560]{1,0:T(8,128)(2,1)} %get-tuple-element.170), channel_id=1, source_target_pairs={{0,1},{1,0},{2,3},{3,2},{4,5},{5,4},{6,7},{7,6},{8,9},{9,8},{10,11... | collective-permute-start | bytes 3932168 | tf_op jit(solution)/shard_map/ppermute | solution.py:539
  570.1 75.8 %collective-permute-start.35 = (bf16[256,2560]{1,0:T(8,128)(2,1)}, bf16[256,2560]{1,0:T(8,128)(2,1)}, u32[]{:S(2)}, u32[]{:S(2)}) collective-permute-start(bf16[256,2560]{1,0:T(8,128)(2,1)} %get-tuple-element.174), channel_id=1, source_target_pairs={{0,2},{1,3},{2,0},{3,1},{4,6},{5,7},{6,4},{7,5},{8,10},{9,11},{10,... | collective-permute-start | bytes 3932168 | tf_op jit(solution)/shard_map/ppermute | solution.py:539
  570.6 34.4 %collective-permute-start.41 = (bf16[1280,128]{0,1:T(8,128)(2,1)S(1)}, bf16[1280,128]{0,1:T(8,128)(2,1)S(1)}, u32[]{:S(2)}, u32[]{:S(2)}) collective-permute-start(bf16[1280,128]{0,1:T(8,128)(2,1)S(1)} %select_convert_fusion), channel_id=1, source_target_pairs={{0,16},{4,20},{8,24},{12,28},{16,0},{20,4},{24,8},{28,12},{1,17},{... | collective-permute-start | bytes 983048 | tf_op jit(solution)/shard_map/ppermute | solution.py:539
  588.7 54.8 %collective-permute-start.33 = (bf16[256,2560]{1,0:T(8,128)(2,1)}, bf16[256,2560]{1,0:T(8,128)(2,1)}, u32[]{:S(2)}, u32[]{:S(2)}) collective-permute-start(bf16[256,2560]{1,0:T(8,128)(2,1)} %add_convert_fusion), channel_id=1, source_target_pairs={{0,2},{1,3},{2,0},{3,1},{4,6},{5,7},{6,4},{7,5},{8,10},{9,11},{10,... | collective-permute-start | bytes 3932168 | tf_op jit(solution)/shard_map/ppermute | solution.py:539
  600.9 44.9 %collective-permute-start.34 = (bf16[256,2560]{1,0:T(8,128)(2,1)}, bf16[256,2560]{1,0:T(8,128)(2,1)}, u32[]{:S(2)}, u32[]{:S(2)}) collective-permute-start(bf16[256,2560]{1,0:T(8,128)(2,1)} %add_convert_fusion.1), channel_id=1, source_target_pairs={{0,1},{1,0},{2,3},{3,2},{4,5},{5,4},{6,7},{7,6},{8,9},{9,8},{10,11... | collective-permute-start | bytes 3932168 | tf_op jit(solution)/shard_map/ppermute | solution.py:539
  605.0 26.8 %collective-permute-start.39 = (f32[2560]{0:T(1024)S(1)}, f32[2560]{0:T(1024)S(1)}, u32[]{:S(2)}, u32[]{:S(2)}) collective-permute-start(f32[2560]{0:T(1024)S(1)} %slice.296), channel_id=1, source_target_pairs={{0,1},{1,0},{2,3},{3,2},{4,5},{5,4},{6,7},{7,6},{8,9},{9,8},{10,11... | collective-permute-start | bytes 30728 | tf_op jit(solution)/shard_map/ppermute | solution.py:539
  (60 other events, 1454.1 us)
Sparse Core Ops, SparseCore 0:
  11.4 74.9 all-gather.3
  88.1 65.4 all-gather.5
  155.2 65.4 all-gather.7
  287.1 71.1 reduce-scatter.3
  376.4 72.1 reduce-scatter.5
  516.5 80.3 reduce-scatter.7

commit v7 on v6

--- a/solution.py
+++ b/solution.py
@@ -575,12 +575,15 @@
 
     def gather_low(self, parts):
         v, rest, x_first, y_first = parts
-        quarter = x_first.shape[0]
         x_rest, y_rest = swap(rest, 1), swap(rest, 2)
         far_first = swap(y_first, 1)
-        far_middle = swap(x_rest[: 2 * quarter], 2)
-        far_last = swap(y_rest[2 * quarter :], 1)
-        return [v, x_first, x_rest, y_first, y_rest, far_first, far_middle, far_last]
+        return [v, x_first, x_rest, y_first, y_rest, far_first]
+
+    def gather_far(self, pieces):
+        quarter = pieces[1].shape[0]
+        far_middle = swap(pieces[2][: 2 * quarter], 2)
+        far_last = swap(pieces[4][2 * quarter :], 1)
+        return pieces + [far_middle, far_last]
 
     def gather_flat(self, v):
         others = [swap(v, bit) for bit in (1, 2, 3)]
@@ -659,6 +662,9 @@
 
     def gather_low(self, parts):
         return parts
+
+    def gather_far(self, pieces):
+        return pieces
 
     def gather_flat(self, v):
         return lax.all_gather(v, "col", axis=0, tiled=True)
@@ -792,6 +798,8 @@
     gate = gate_pre.astype(F32)
     gated = ho * swish(gate)
     squares = jnp.sum(gated * gated, axis=1)
+    squares, *grad_pieces = tied(squares, *grad_pieces)
+    grad_pieces = lines.gather_far(grad_pieces)
     squares = lines.token_sum(squares)
     mix = lax.rsqrt(squares / inner_width + EPSILON)[:, None]
     normed = (gated * mix * norm_gain).astype(BF16)

time: 678 us -> 684 us (level)
  transfers between devices with their start and end apart: 50 -> 50, of which waited for: 16 -> 17; matrix products, arithmetic and copies ran while one was open for 24% -> 24% of each run, Pallas kernels for 40% -> 39%
where the time goes in v7:
time: 684 us; the launch traced here: 673 us
  Pallas kernels  264 us (39%)
  waiting for transfers between devices  168 us (25%)
  other arithmetic  90.3 us (13%)
  matrix products  52.3 us (8%)
  starting transfers between devices  50.9 us (7%)
  local copies, waits for them, and re-layouts  31.8 us (5%)
  between operations  15.6 us (2%)
    ppermute x44, waiting for transfers between devices, swap(): return lax.ppermute(v, axis, [(i, i ^ bit) for i in range(size)])  168 us
    pallas_call x1, Pallas kernels, run_backward(): pl.pallas_call(functools.partial(scan_backward, pairs=width // LANES, blo...  69.6 us
    ppermute x44, starting transfers between devices, swap(): return lax.ppermute(v, axis, [(i, i ^ bit) for i in range(size)])  50.7 us
    pallas_call x4, Pallas kernels, run_rows(): pl.pallas_call(rows_kernel, out_shape=[jax.ShapeDtypeStruct((rows, width)...  48.8 us
    dot_general x2, matrix products, mm(): return jnp.dot(a, b, preferred_element_type=F32)  46.1 us
    pallas_call x2, Pallas kernels, run_turned(): pl.pallas_call(turned_kernel, out_shape=jax.ShapeDtypeStruct((depth, widt...  39.1 us
    pallas_call x2, Pallas kernels, run_fill(): pl.pallas_call(functools.partial(fill_kernel, spans=spans), out_shape=(ja...  33.8 us
    pallas_call x1, Pallas kernels, run_forward(): pl.pallas_call(functools.partial(scan_forward, pairs=width // LANES), out...  33.2 us
  transfers between devices with their start and end apart: 50, of which 17 were waited for; matrix products, arithmetic and copies ran while one was open for 24% of the time, Pallas kernels for 39%

profile of v7, /device:TPU:0, one launch (start us, length us, event | category | flops | bytes accessed | tf_op | source)
XLA Modules:
  0.0 673.3 jit_solution(10266329625408614519)
XLA Ops:
  18.1 55.6 %collective-permute-done.2.refs_2_ = bf16[512,2560]{1,0:T(8,128)(2,1)S(1)} collective-permute-done((bf16[512,2560]{1,0:T(8,128)(2,1)}, bf16[512,2560]{1,0:T(8,128)(2,1)S(1)}, u32[]{:S(2)}, u32[]{:S(2)}) %collective-permute-start.2) | collective-permute-done | bytes 2621472 | tf_op jit(solution)/shard_map/ppermute | solution.py:539
  84.0 22.8 %collective-permute-done.3.refs_1_ = bf16[256,2560]{1,0:T(8,128)(2,1)} collective-permute-done((bf16[256,2560]{1,0:T(8,128)(2,1)}, bf16[256,2560]{1,0:T(8,128)(2,1)}, u32[]{:S(2)}, u32[]{:S(2)}) %collective-permute-start.3) | collective-permute-done | bytes 1310752 | tf_op jit(solution)/shard_map/ppermute | solution.py:539
  117.1 8.4 %collective-permute-done.12.refs_3_ = bf16[128,2560]{1,0:T(8,128)(2,1)} collective-permute-done((bf16[128,2560]{1,0:T(8,128)(2,1)}, bf16[128,2560]{1,0:T(8,128)(2,1)}, u32[]{:S(2)}, u32[]{:S(2)}) %collective-permute-start.12) | collective-permute-done | bytes 655392 | tf_op jit(solution)/shard_map/ppermute | solution.py:539
  127.0 23.2 %values.2 = (bf16[2048,2560]{1,0:T(8,128)(2,1)}, bf16[2048,1280]{1,0:T(8,128)(2,1)}, f32[2048,128]{1,0:T(8,128)}) custom-call(bf16[512,2560]{1,0:T(8,128)(2,1)} %refs_0_.1, bf16[512,2560]{1,0:T(8,128)(2,1)} %collective-permute-done.refs_1_, bf16[512,2560]{1,0:T(8,128)(2,1)} %copy-done.18, f32[1,2560]{1,0:T(1,128)} %reshape.216.refs_3_.refs_2_, ...), custom_call_target="tpu_custom_call" | custom-call | flops 11072962560 | bytes 23363584 | tf_op jit(solution)/shard_map/values/pallas_call | solution.py:387
  151.1 10.6 %values.3 = (bf16[2048,2560]{1,0:T(8,128)(2,1)}, bf16[2048,1280]{1,0:T(8,128)(2,1)}, f32[2048,128]{1,0:T(8,128)}) custom-call(bf16[256,2560]{1,0:T(8,128)(2,1)} %collective-permute-done.1.refs_0_, bf16[256,2560]{1,0:T(8,128)(2,1)} %collective-permute-done.3.refs_1_, ...), custom_call_target="tpu_custom_call", output_to_operand_aliasing={{0}: (4, {}), {1}: (5, {}), {2}: (6, {})} | custom-call | flops 3690987520 | bytes 15237120 | tf_op jit(solution)/shard_map/values/pallas_call | solution.py:387
  171.5 5.6 collective-permute-done.7
  182.8 33.2 %scan_forward.1 = (bf16[2048,1280]{1,0:T(8,128)(2,1)}, bf16[16,128,1280]{2,1,0:T(8,128)(2,1)}) custom-call(s32[1]{0:T(128)} %bitcast.seat_ref, bf16[2048,1280]{1,0:T(8,128)(2,1)} %get-tuple-element.111.vp_ref.before_ref, bf16[2048,256]{1,0:T(8,128)(2,1)} %pad_maximum_fusion.bc_ref, f32[2048,128]{1,0:T(8,128)} %pad.51.st_ref, ...), custom_call_target="tpu_custom_call" | custom-call | flops 3145728000 | bytes 26214400 | tf_op jit(solution)/shard_map/scan_forward/pallas_call | solution.py:244
  216.0 21.6 %multiply_reduce_fusion.2 = (f32[2048]{0:T(1024)S(1)}, bf16[2048,1280]{1,0:T(8,128)(2,1)}) fusion(bf16[2048,1280]{1,0:T(8,128)(2,1)} %get-tuple-element.115, bf16[2048,2560]{1,0:T(8,128)(2,1)} %get-tuple-element.159.a_ref, bf16[2560,1280]{1,0:T(8,128)(2,1)} %all-gather.6.cloned.1.call-done.refs_6_), kind=kOutput, calls=%fused_computation.27 | convolution fusion | flops 13447985152 | bytes 27533312 | tf_op jit(solution)/shard_map/dot_general | solution.py:29
  238.2 3.1 collective-permute-done.15
  246.8 9.3 %multiply_convert_fusion.refs_8_.x_ref = bf16[2048,1280]{1,0:T(8,128)(2,1)} fusion(f32[1280]{0:T(1024)S(1)} %copy-done.21, f32[2048]{0:T(1024)S(1)} %bitcast.63, bf16[2048,1280]{1,0:T(8,128)(2,1)} %get-tuple-element.262, bf16[2048,1280]{1,0:T(8,128)(2,1)} %get-tuple-element.115), kind=kLoop, calls=%fused_computation.26 | loop fusion | flops 26214400 | bytes 15741952 | tf_op jit(solution)/shard_map/convert_element_type | solution.py:805
  259.4 10.7 %collective-permute-done.17.refs_6_ = bf16[256,2560]{1,0:T(8,128)(2,1)S(1)} collective-permute-done((bf16[256,2560]{1,0:T(8,128)(2,1)S(1)}, bf16[256,2560]{1,0:T(8,128)(2,1)S(1)}, u32[]{:S(2)}, u32[]{:S(2)}) %collective-permute-start.17) | collective-permute-done | bytes 1310752 | tf_op jit(solution)/shard_map/ppermute | solution.py:539
  271.1 20.9 %joined.1 = (bf16[2560,1280]{1,0:T(8,128)(2,1)}, bf16[2048,2560]{1,0:T(8,128)(2,1)}) custom-call(bf16[512,2560]{1,0:T(8,128)(2,1)} %refs_0_.2, bf16[128,2560]{1,0:T(8,128)(2,1)} %collective-permute-done.10.refs_1_, bf16[384,2560]{1,0:T(8,128)(2,1)} %collective-permute-done.11.refs_2_, bf16[128,2560]{1,0:T(8,128)(2,1)} %collective-permute-done.12.refs_3_, ...), custom_call_target="tpu_custom_call" | custom-call | flops 13421772800 | bytes 32768000 | tf_op jit(solution)/shard_map/joined/pallas_call | solution.py:513
  292.1 24.6 %fusion.7 = (f32[1280]{0:T(1024)S(1)}, f32[2048]{0:T(1024)S(1)}, bf16[2048,1280]{1,0:T(8,128)(2,1)}) fusion(f32[2048]{0:T(1024)S(1)} %bitcast.64, bf16[2048,1280]{1,0:T(8,128)(2,1)} %get-tuple-element.262, bf16[2048,1280]{1,0:T(8,128)(2,1)} %get-tuple-element.115, f32[1280]{0:T(1024)S(1)} %copy-done.21, bf16[2048,2560]{1,0:T(8,128)(2,1)} %get-tuple-element.128, ...), kind=kOutput, calls=%fused_computation.17 | convolution fusion | flops 13461091328 | bytes 32794624 | tf_op jit(solution)/shard_map/dot_general | solution.py:29
  316.8 3.6 collective-permute-done.19
  322.2 18.5 %split.1 = (bf16[256,2560]{1,0:T(8,128)(2,1)}, bf16[256,2560]{1,0:T(8,128)(2,1)}, bf16[256,2560]{1,0:T(8,128)(2,1)}, bf16[256,2560]{1,0:T(8,128)(2,1)}, bf16[256...) custom-call(bf16[2048,1280]{1,0:T(8,128)(2,1)} %multiply_convert_fusion.re, ...), custom_call_target="tpu_custom_call" | custom-call | flops 13421772800 | bytes 22282240 | tf_op jit(solution)/shard_map/split/pallas_call | solution.py:424
  341.2 14.4 %fusion.5 = (bf16[2048,1280]{1,0:T(8,128)(2,1)}, bf16[2048,1280]{1,0:T(8,128)(2,1)}) fusion(bf16[2048,1280]{1,0:T(8,128)(2,1)} %get-tuple-element.115, bf16[2048,1280]{1,0:T(8,128)(2,1)} %get-tuple-element.262, bf16[2048,1280]{1,0:T(8,128)(2,1)} %get-tuple-element.263, f32[2048]{0:T(1024)S(1)} %fusion.25, f32[1280]{0:T(1024)S(1)} %copy-done.21, ...), kind=kLoop, calls=%fused_computation.15 | loop fusion | flops 57671680 | bytes 26235904 | tf_op jit(solution)/shard_map/convert_element_type | solution.py:829
  355.6 19.6 %weights.2 = bf16[2560,1280]{1,0:T(8,128)(2,1)} custom-call(bf16[2048,2560]{1,0:T(8,128)(2,1)} %get-tuple-element.159.a_ref, bf16[2048,1280]{1,0:T(8,128)(2,1)} %get-tuple-element.214.b_ref.refs_0_.refs_1_), custom_call_target="tpu_custom_call" | custom-call | flops 13421772800 | bytes 22282240 | tf_op jit(solution)/shard_map/weights/pallas_call | solution.py:484
  385.8 69.6 %scan_backward.1 = (bf16[2048,1280]{1,0:T(8,128)(2,1)}, bf16[2048,256]{1,0:T(8,128)(2,1)}, f32[2048,128]{1,0:T(8,128)}, f32[8,1280]{1,0:T(8,128)}, f32[1,128]{1,0:T(1,128)}) custom-call(s32[1]{0:T(128)} %bitcast.seat_ref, bf16[2048,1280]{1,0:T(8,128)(2,1)} %get-tuple-element.111.vp_ref.before_ref, bf16[2048,1280]{1,0:T(8,128)(2,1)} %get-tuple-element.111.vp_ref.before_ref, ...), custom_call_target="tpu_custom_call" | custom-call | flops 7864320000 | bytes 36700160 | tf_op jit(solution)/shard_map/scan_backward/pallas_call | solution.py:291
  463.6 19.5 %weights.3 = bf16[2560,1280]{1,0:T(8,128)(2,1)} custom-call(bf16[2048,2560]{1,0:T(8,128)(2,1)} %get-tuple-element.159.a_ref, bf16[2048,1280]{1,0:T(8,128)(2,1)} %get-tuple-element.172.b_ref.refs_2_.refs_3_), custom_call_target="tpu_custom_call" | custom-call | flops 13421772800 | bytes 22282240 | tf_op jit(solution)/shard_map/weights/pallas_call | solution.py:484
  490.2 12.0 %rows.4 = (bf16[256,2560]{1,0:T(8,128)(2,1)}, bf16[256,2560]{1,0:T(8,128)(2,1)}) custom-call(bf16[2048,1280]{1,0:T(8,128)(2,1)} %get-tuple-element.214.b_ref.refs_0_.refs_1_, bf16[2048,1280]{1,0:T(8,128)(2,1)} %get-tuple-element.214.b_ref.refs_0_.refs_1_, bf16[2048,1280]{1,0:T(8,128)(2,1)} %get-tuple-element.172.b_ref.refs_2_.refs_3_, ...), custom_call_target="tpu_custom_call" | custom-call | flops 7046430720 | bytes 19136512 | tf_op jit(solution)/shard_map/rows/pallas_call | solution.py:460
  502.3 12.2 %rows.5 = (bf16[256,2560]{1,0:T(8,128)(2,1)}, bf16[256,2560]{1,0:T(8,128)(2,1)}) custom-call(bf16[2048,1280]{1,0:T(8,128)(2,1)} %get-tuple-element.214.b_ref.refs_0_.refs_1_, bf16[2048,1280]{1,0:T(8,128)(2,1)} %get-tuple-element.214.b_ref.refs_0_.refs_1_, bf16[2048,1280]{1,0:T(8,128)(2,1)} %get-tuple-element.172.b_ref.refs_2_.refs_3_, ...), custom_call_target="tpu_custom_call" | custom-call | flops 7046430720 | bytes 19136512 | tf_op jit(solution)/shard_map/rows/pallas_call | solution.py:460
  514.6 6.5 multiply_reduce_fusion
  521.2 6.6 multiply_reduce_fusion.1
  527.8 6.2 fusion.46
  537.5 12.2 %rows.6 = (bf16[256,2560]{1,0:T(8,128)(2,1)}, bf16[256,2560]{1,0:T(8,128)(2,1)}) custom-call(bf16[2048,1280]{1,0:T(8,128)(2,1)} %get-tuple-element.214.b_ref.refs_0_.refs_1_, bf16[2048,1280]{1,0:T(8,128)(2,1)} %get-tuple-element.214.b_ref.refs_0_.refs_1_, bf16[2048,1280]{1,0:T(8,128)(2,1)} %get-tuple-element.172.b_ref.refs_2_.refs_3_, ...), custom_call_target="tpu_custom_call" | custom-call | flops 7046430720 | bytes 19136512 | tf_op jit(solution)/shard_map/rows/pallas_call | solution.py:460
  560.9 12.4 %rows.7 = (bf16[256,2560]{1,0:T(8,128)(2,1)}, bf16[256,2560]{1,0:T(8,128)(2,1)}) custom-call(bf16[2048,1280]{1,0:T(8,128)(2,1)} %get-tuple-element.214.b_ref.refs_0_.refs_1_, bf16[2048,1280]{1,0:T(8,128)(2,1)} %get-tuple-element.214.b_ref.refs_0_.refs_1_, bf16[2048,1280]{1,0:T(8,128)(2,1)} %get-tuple-element.172.b_ref.refs_2_.refs_3_, ...), custom_call_target="tpu_custom_call" | custom-call | flops 7046430720 | bytes 19136512 | tf_op jit(solution)/shard_map/rows/pallas_call | solution.py:460
  583.6 12.4 %collective-permute-done.37 = f32[10620]{0:T(1024)S(1)} collective-permute-done((f32[10620]{0:T(1024)S(1)}, f32[10620]{0:T(1024)S(1)}, u32[]{:S(2)}, u32[]{:S(2)}) %collective-permute-start.37) | collective-permute-done | bytes 42512 | tf_op jit(solution)/shard_map/ppermute | solution.py:539
  598.6 3.7 convert_add_fusion.3
  602.3 5.1 collective-permute-done.38
  614.0 24.2 %collective-permute-done.39 = f32[2560]{0:T(1024)S(1)} collective-permute-done((f32[2560]{0:T(1024)S(1)}, f32[2560]{0:T(1024)S(1)}, u32[]{:S(2)}, u32[]{:S(2)}) %collective-permute-start.39) | collective-permute-done | bytes 10272 | tf_op jit(solution)/shard_map/ppermute | solution.py:539
  638.3 5.2 collective-permute-done.42
  657.0 4.0 fusion.21
  (298 shorter events, 140.2 us)
Async XLA Ops:
  7.2 119.8 %all-gather.4.cloned.1.call-start = ((), (), s32[]{:S(2)}) async-start(), calls=%async_computation.3 | async-start | bytes 8110080 | tf_op jit(solution)/shard_map/all_gather | solution.py:747
  12.8 203.2 %all-gather.6.cloned.1.call-start = ((), (), s32[]{:S(2)}) async-start(), calls=%async_computation.4 | async-start | bytes 7372800 | tf_op jit(solution)/shard_map/all_gather | solution.py:751
  13.5 278.5 %all-gather.8.cloned.1.call-start = ((), (), s32[]{:S(2)}) async-start(), calls=%async_computation.5 | async-start | bytes 7372800 | tf_op jit(solution)/shard_map/all_gather | solution.py:752
  13.6 60.1 %collective-permute-start.2 = (bf16[512,2560]{1,0:T(8,128)(2,1)}, bf16[512,2560]{1,0:T(8,128)(2,1)S(1)}, u32[]{:S(2)}, u32[]{:S(2)}) collective-permute-start(bf16[512,2560]{1,0:T(8,128)(2,1)} %refs_0_.1), channel_id=1, source_target_pairs={{0,2},{1,3},{2,0},{3,1},{4,6},{5,7},{6,4},{7,5},{8,10},{9,11},{10,... | collective-permute-start | bytes 7864328 | tf_op jit(solution)/shard_map/ppermute | solution.py:539
  16.6 93.8 %collective-permute-start = (bf16[512,2560]{1,0:T(8,128)(2,1)}, bf16[512,2560]{1,0:T(8,128)(2,1)}, u32[]{:S(2)}, u32[]{:S(2)}) collective-permute-start(bf16[512,2560]{1,0:T(8,128)(2,1)} %refs_0_.1), channel_id=1, source_target_pairs={{0,1},{1,0},{2,3},{3,2},{4,5},{5,4},{6,7},{7,6},{8,9},{9,8},{10,11... | collective-permute-start | bytes 7864328 | tf_op jit(solution)/shard_map/ppermute | solution.py:539
  76.3 30.4 %collective-permute-start.3 = (bf16[256,2560]{1,0:T(8,128)(2,1)}, bf16[256,2560]{1,0:T(8,128)(2,1)}, u32[]{:S(2)}, u32[]{:S(2)}) collective-permute-start(bf16[256,2560]{1,0:T(8,128)(2,1)} %slice.273), channel_id=1, source_target_pairs={{0,1},{1,0},{2,3},{3,2},{4,5},{5,4},{6,7},{7,6},{8,9},{9,8},{10,11... | collective-permute-start | bytes 3932168 | tf_op jit(solution)/shard_map/ppermute | solution.py:539
  78.1 32.3 %collective-permute-start.4 = (bf16[640]{0:T(1024)(128)(2,1)S(1)}, bf16[640]{0:T(1024)(128)(2,1)S(1)}, u32[]{:S(2)}, u32[]{:S(2)}) collective-permute-start(bf16[640]{0:T(1024)(128)(2,1)S(1)} %copy-done.34), channel_id=1, source_target_pairs={{0,1},{1,0},{2,3},{3,2},{4,5},{5,4},{6,7},{7,6},{8,9},{9,8},{10,11... | collective-permute-start | bytes 3848 | tf_op jit(solution)/shard_map/ppermute | solution.py:539
  78.4 32.0 %collective-permute-start.5 = (bf16[640]{0:T(1024)(128)(2,1)S(1)}, bf16[640]{0:T(1024)(128)(2,1)S(1)}, u32[]{:S(2)}, u32[]{:S(2)}) collective-permute-start(bf16[640]{0:T(1024)(128)(2,1)S(1)} %copy-done.34), channel_id=1, source_target_pairs={{0,2},{1,3},{2,0},{3,1},{4,6},{5,7},{6,4},{7,5},{8,10},{9,11},{10,... | collective-permute-start | bytes 3848 | tf_op jit(solution)/shard_map/ppermute | solution.py:539
  80.1 30.2 %collective-permute-start.6 = (bf16[640]{0:T(1024)(128)(2,1)S(1)}, bf16[640]{0:T(1024)(128)(2,1)S(1)}, u32[]{:S(2)}, u32[]{:S(2)}) collective-permute-start(bf16[640]{0:T(1024)(128)(2,1)S(1)} %copy-done.34), channel_id=1, source_target_pairs={{0,3},{1,2},{2,1},{3,0},{4,7},{5,6},{6,5},{7,4},{8,11},{9,10},{10,... | collective-permute-start | bytes 3848 | tf_op jit(solution)/shard_map/ppermute | solution.py:539
  81.6 299.5 %reduce-scatter.4.cloned.1.call-start = ((), (), s32[]{:S(2)}) async-start(), calls=%async_computation.6 | async-start | bytes 7372800 | tf_op jit(solution)/shard_map/reduce_scatter | solution.py:717
  112.9 38.3 %collective-permute-start.1 = (bf16[256,2560]{1,0:T(8,128)(2,1)}, bf16[256,2560]{1,0:T(8,128)(2,1)}, u32[]{:S(2)}, u32[]{:S(2)}) collective-permute-start(bf16[256,2560]{1,0:T(8,128)(2,1)} %slice.272), channel_id=1, source_target_pairs={{0,2},{1,3},{2,0},{3,1},{4,6},{5,7},{6,4},{7,5},{8,10},{9,11},{10,... | collective-permute-start | bytes 3932168 | tf_op jit(solution)/shard_map/ppermute | solution.py:539
  115.7 121.8 %collective-permute-start.10 = (bf16[128,2560]{1,0:T(8,128)(2,1)}, bf16[128,2560]{1,0:T(8,128)(2,1)}, u32[]{:S(2)}, u32[]{:S(2)}) collective-permute-start(bf16[128,2560]{1,0:T(8,128)(2,1)} %slice.227), channel_id=1, source_target_pairs={{0,1},{1,0},{2,3},{3,2},{4,5},{5,4},{6,7},{7,6},{8,9},{9,8},{10,11... | collective-permute-start | bytes 1966088 | tf_op jit(solution)/shard_map/ppermute | solution.py:539
  125.6 112.0 %collective-permute-start.14 = (bf16[128,2560]{1,0:T(8,128)(2,1)}, bf16[128,2560]{1,0:T(8,128)(2,1)}, u32[]{:S(2)}, u32[]{:S(2)}) collective-permute-start(bf16[128,2560]{1,0:T(8,128)(2,1)} %collective-permute-done.12.refs_3_), channel_id=1, source_target_pairs={{0,1},{1,0},{2,3},{3,2},{4,5},{5,4},{6,7},{7,6},{8,9},{9,8},{10,11... | collective-permute-start | bytes 1966088 | tf_op jit(solution)/shard_map/ppermute | solution.py:539
  180.4 57.2 %collective-permute-start.11 = (bf16[384,2560]{1,0:T(8,128)(2,1)S(1)}, bf16[384,2560]{1,0:T(8,128)(2,1)}, u32[]{:S(2)}, u32[]{:S(2)}) collective-permute-start(bf16[384,2560]{1,0:T(8,128)(2,1)S(1)} %copy-done.10), channel_id=1, source_target_pairs={{0,1},{1,0},{2,3},{3,2},{4,5},{5,4},{6,7},{7,6},{8,9},{9,8},{10,11... | collective-permute-start | bytes 5898248 | tf_op jit(solution)/shard_map/ppermute | solution.py:539
  181.3 56.3 %collective-permute-start.13 = (bf16[384,2560]{1,0:T(8,128)(2,1)S(1)}, bf16[384,2560]{1,0:T(8,128)(2,1)}, u32[]{:S(2)}, u32[]{:S(2)}) collective-permute-start(bf16[384,2560]{1,0:T(8,128)(2,1)S(1)} %copy-done.10), channel_id=1, source_target_pairs={{0,2},{1,3},{2,0},{3,1},{4,6},{5,7},{6,4},{7,5},{8,10},{9,11},{10,... | collective-permute-start | bytes 5898248 | tf_op jit(solution)/shard_map/ppermute | solution.py:539
  243.4 26.7 %collective-permute-start.17 = (bf16[256,2560]{1,0:T(8,128)(2,1)S(1)}, bf16[256,2560]{1,0:T(8,128)(2,1)S(1)}, u32[]{:S(2)}, u32[]{:S(2)}) collective-permute-start(bf16[256,2560]{1,0:T(8,128)(2,1)S(1)} %slice.228), channel_id=1, source_target_pairs={{0,2},{1,3},{2,0},{3,1},{4,6},{5,7},{6,4},{7,5},{8,10},{9,11},{10,... | collective-permute-start | bytes 3932168 | tf_op jit(solution)/shard_map/ppermute | solution.py:539
  292.1 229.1 %reduce-scatter.6.cloned.1.call-start = ((), (), s32[]{:S(2)}) async-start(), calls=%async_computation.7 | async-start | bytes 7372800 | tf_op jit(solution)/shard_map/reduce_scatter | solution.py:717
  340.7 34.6 %collective-permute-start.22 = (bf16[256,2560]{1,0:T(8,128)(2,1)}, bf16[256,2560]{1,0:T(8,128)(2,1)}, u32[]{:S(2)}, u32[]{:S(2)}) collective-permute-start(bf16[256,2560]{1,0:T(8,128)(2,1)} %get-tuple-element.135), channel_id=1, source_target_pairs={{0,1},{1,0},{2,3},{3,2},{4,5},{5,4},{6,7},{7,6},{8,9},{9,8},{10,11... | collective-permute-start | bytes 3932168 | tf_op jit(solution)/shard_map/ppermute | solution.py:539
  340.7 37.6 %collective-permute-start.21 = (bf16[256,2560]{1,0:T(8,128)(2,1)}, bf16[256,2560]{1,0:T(8,128)(2,1)}, u32[]{:S(2)}, u32[]{:S(2)}) collective-permute-start(bf16[256,2560]{1,0:T(8,128)(2,1)} %get-tuple-element.133), channel_id=1, source_target_pairs={{0,2},{1,3},{2,0},{3,1},{4,6},{5,7},{6,4},{7,5},{8,10},{9,11},{10,... | collective-permute-start | bytes 3932168 | tf_op jit(solution)/shard_map/ppermute | solution.py:539
  381.1 282.5 %reduce-scatter.8.cloned.1.call-start = ((), (), s32[]{:S(2)}) async-start(), calls=%async_computation.8 | async-start | bytes 7372800 | tf_op jit(solution)/shard_map/reduce_scatter | solution.py:717
  382.2 191.2 %collective-permute-start.28 = (bf16[256,2560]{1,0:T(8,128)(2,1)}, bf16[256,2560]{1,0:T(8,128)(2,1)}, u32[]{:S(2)}, u32[]{:S(2)}) collective-permute-start(bf16[256,2560]{1,0:T(8,128)(2,1)} %get-tuple-element.176), channel_id=1, source_target_pairs={{0,1},{1,0},{2,3},{3,2},{4,5},{5,4},{6,7},{7,6},{8,9},{9,8},{10,11... | collective-permute-start | bytes 3932168 | tf_op jit(solution)/shard_map/ppermute | solution.py:539
  384.2 190.8 %collective-permute-start.29 = (bf16[256,2560]{1,0:T(8,128)(2,1)}, bf16[256,2560]{1,0:T(8,128)(2,1)}, u32[]{:S(2)}, u32[]{:S(2)}) collective-permute-start(bf16[256,2560]{1,0:T(8,128)(2,1)} %get-tuple-element.177), channel_id=1, source_target_pairs={{0,2},{1,3},{2,0},{3,1},{4,6},{5,7},{6,4},{7,5},{8,10},{9,11},{10,... | collective-permute-start | bytes 3932168 | tf_op jit(solution)/shard_map/ppermute | solution.py:539
  457.9 25.4 %collective-permute-start.25 = (bf16[1024,128]{1,0:T(8,128)(2,1)}, bf16[1024,128]{1,0:T(8,128)(2,1)S(1)}, u32[]{:S(2)}, u32[]{:S(2)}) collective-permute-start(bf16[1024,128]{1,0:T(8,128)(2,1)} %pad_maximum_fusion.4), channel_id=1, source_target_pairs={{0,3},{1,2},{2,1},{3,0},{4,7},{5,6},{6,5},{7,4},{8,11},{9,10},{10,... | collective-permute-start | bytes 786440 | tf_op jit(solution)/shard_map/ppermute | solution.py:539
  483.4 95.9 %collective-permute-start.30 = (bf16[256,2560]{1,0:T(8,128)(2,1)}, bf16[256,2560]{1,0:T(8,128)(2,1)}, u32[]{:S(2)}, u32[]{:S(2)}) collective-permute-start(bf16[256,2560]{1,0:T(8,128)(2,1)} %add_convert_fusion.2), channel_id=1, source_target_pairs={{0,2},{1,3},{2,0},{3,1},{4,6},{5,7},{6,4},{7,5},{8,10},{9,11},{10,... | collective-permute-start | bytes 3932168 | tf_op jit(solution)/shard_map/ppermute | solution.py:539
  514.5 35.3 %collective-permute-start.27 = (bf16[256,2560]{1,0:T(8,128)(2,1)}, bf16[256,2560]{1,0:T(8,128)(2,1)}, u32[]{:S(2)}, u32[]{:S(2)}) collective-permute-start(bf16[256,2560]{1,0:T(8,128)(2,1)} %get-tuple-element.171), channel_id=1, source_target_pairs={{0,1},{1,0},{2,3},{3,2},{4,5},{5,4},{6,7},{7,6},{8,9},{9,8},{10,11... | collective-permute-start | bytes 3932168 | tf_op jit(solution)/shard_map/ppermute | solution.py:539
  549.8 46.6 %collective-permute-start.31 = (bf16[256,2560]{1,0:T(8,128)(2,1)}, bf16[256,2560]{1,0:T(8,128)(2,1)}, u32[]{:S(2)}, u32[]{:S(2)}) collective-permute-start(bf16[256,2560]{1,0:T(8,128)(2,1)} %add_convert_fusion.3), channel_id=1, source_target_pairs={{0,1},{1,0},{2,3},{3,2},{4,5},{5,4},{6,7},{7,6},{8,9},{9,8},{10,11... | collective-permute-start | bytes 3932168 | tf_op jit(solution)/shard_map/ppermute | solution.py:539
  573.4 76.5 %collective-permute-start.32 = (bf16[256,2560]{1,0:T(8,128)(2,1)}, bf16[256,2560]{1,0:T(8,128)(2,1)}, u32[]{:S(2)}, u32[]{:S(2)}) collective-permute-start(bf16[256,2560]{1,0:T(8,128)(2,1)} %get-tuple-element.184), channel_id=1, source_target_pairs={{0,1},{1,0},{2,3},{3,2},{4,5},{5,4},{6,7},{7,6},{8,9},{9,8},{10,11... | collective-permute-start | bytes 3932168 | tf_op jit(solution)/shard_map/ppermute | solution.py:539
  575.0 77.2 %collective-permute-start.35 = (bf16[256,2560]{1,0:T(8,128)(2,1)}, bf16[256,2560]{1,0:T(8,128)(2,1)}, u32[]{:S(2)}, u32[]{:S(2)}) collective-permute-start(bf16[256,2560]{1,0:T(8,128)(2,1)} %get-tuple-element.188), channel_id=1, source_target_pairs={{0,2},{1,3},{2,0},{3,1},{4,6},{5,7},{6,4},{7,5},{8,10},{9,11},{10,... | collective-permute-start | bytes 3932168 | tf_op jit(solution)/shard_map/ppermute | solution.py:539
  576.6 34.8 %collective-permute-start.41 = (bf16[1280,128]{0,1:T(8,128)(2,1)S(1)}, bf16[1280,128]{0,1:T(8,128)(2,1)S(1)}, u32[]{:S(2)}, u32[]{:S(2)}) collective-permute-start(bf16[1280,128]{0,1:T(8,128)(2,1)S(1)} %select_convert_fusion), channel_id=1, source_target_pairs={{0,16},{4,20},{8,24},{12,28},{16,0},{20,4},{24,8},{28,12},{1,17},{... | collective-permute-start | bytes 983048 | tf_op jit(solution)/shard_map/ppermute | solution.py:539
  596.0 53.9 %collective-permute-start.33 = (bf16[256,2560]{1,0:T(8,128)(2,1)}, bf16[256,2560]{1,0:T(8,128)(2,1)}, u32[]{:S(2)}, u32[]{:S(2)}) collective-permute-start(bf16[256,2560]{1,0:T(8,128)(2,1)} %add_convert_fusion), channel_id=1, source_target_pairs={{0,2},{1,3},{2,0},{3,1},{4,6},{5,7},{6,4},{7,5},{8,10},{9,11},{10,... | collective-permute-start | bytes 3932168 | tf_op jit(solution)/shard_map/ppermute | solution.py:539
  607.4 44.9 %collective-permute-start.34 = (bf16[256,2560]{1,0:T(8,128)(2,1)}, bf16[256,2560]{1,0:T(8,128)(2,1)}, u32[]{:S(2)}, u32[]{:S(2)}) collective-permute-start(bf16[256,2560]{1,0:T(8,128)(2,1)} %add_convert_fusion.1), channel_id=1, source_target_pairs={{0,1},{1,0},{2,3},{3,2},{4,5},{5,4},{6,7},{7,6},{8,9},{9,8},{10,11... | collective-permute-start | bytes 3932168 | tf_op jit(solution)/shard_map/ppermute | solution.py:539
  611.5 26.7 %collective-permute-start.39 = (f32[2560]{0:T(1024)S(1)}, f32[2560]{0:T(1024)S(1)}, u32[]{:S(2)}, u32[]{:S(2)}) collective-permute-start(f32[2560]{0:T(1024)S(1)} %slice.294), channel_id=1, source_target_pairs={{0,1},{1,0},{2,3},{3,2},{4,5},{5,4},{6,7},{7,6},{8,9},{9,8},{10,11... | collective-permute-start | bytes 30728 | tf_op jit(solution)/shard_map/ppermute | solution.py:539
  (60 other events, 1397.4 us)
Sparse Core Ops, SparseCore 0:
  12.9 74.9 all-gather.3
  89.6 65.4 all-gather.5
  156.7 65.5 all-gather.7
  292.2 72.6 reduce-scatter.3
  381.2 74.3 reduce-scatter.5
  521.3 82.6 reduce-scatter.7
